TPU v7x, 32 devices: a whole 2x2x4 slice. The times are simulated.
32 devices in a mesh: dp: 4 (over z), expert: 8 (over y, x, core).
Axes of the slice: x: 2, y: 2, z: 4, core: 2. Of those that a mesh axis runs over, the one named last changes fastest.
Arguments:
- hidden_in: bfloat16 [8192, 1536], P(('dp', 'expert')), may hold values from -6 to 6
- teacher: bfloat16 [8192, 1536], P(('dp', 'expert')), may hold values from -6 to 6
- valid: int32 [8192], P(('dp', 'expert')), may hold values from 0 to 1, as said below
- routes: int32 [8192, 8], P(('dp', 'expert')), may hold values from 0 to 23, all different within a row; in each aligned block of 256 rows (0 to 255, 256 to 511, ...) at most 104 rows name the same one
- gain_attn: bfloat16 [1536], P('dp'), may hold values from 0.5 to 1.5
- gain_moe: bfloat16 [1536], P('dp'), may hold values from 0.5 to 1.5
- w_query: bfloat16 [1536, 1536], P('dp'), may hold values from -0.625 to 0.625
- w_key: bfloat16 [1536, 512], P('dp'), may hold values from -0.625 to 0.625
- w_value: bfloat16 [1536, 512], P('dp'), may hold values from -0.15625 to 0.15625
- w_out: bfloat16 [1536, 1536], P('dp'), may hold values from -4 to 4
- w_router: bfloat16 [1536, 24], P('dp'), may hold values from -0.078125 to 0.078125
- w_gate_up: bfloat16 [24, 1536, 1024], P('expert', 'dp'), may hold values from -0.15625 to 0.15625
- w_down: bfloat16 [24, 512, 1536], P('expert', 'dp'), may hold values from -6 to 6
Outputs:
- activations: bfloat16 [8192, 1536], P(('dp', 'expert'))
- loss: float32 [], replicated
- grad_in: float32 [8192, 1536], P(('dp', 'expert'))
- grad_gain_attn: float32 [1536], P('dp')
- grad_gain_moe: float32 [1536], P('dp')
- grad_query: float32 [1536, 1536], P('dp')
- grad_key: float32 [1536, 512], P('dp')
- grad_value: float32 [1536, 512], P('dp')
- grad_out: float32 [1536, 1536], P('dp')
- grad_router: float32 [1536, 24], P('dp')
- grad_gate_up: float32 [24, 1536, 1024], P('expert', 'dp')
- grad_down: float32 [24, 512, 1536], P('expert', 'dp')
Inputs may be any that keep to these rules, and one draw needn't show every extreme that they name: `valid`: 1 marks a token that counts in the loss; token 0 always counts. `routes`: each row names 8 different experts. Among the rows of one device no expert is named more than 104 times, a bound that some block reaches.
All inputs are finite; a program needn't handle non-finite values.
Results may differ from a plain program's by a relative error of at most 0.02.
Values may be sent and summed in bfloat16 or wider, within the bound.
A program may use at most 256 MiB of HBM per device.

v0:
```python
import math

import jax
import jax.numpy as jnp
from jax import lax
from jax.sharding import PartitionSpec as P

H = 24
KVH = 8
HD = 64
FF = 512
TOP = 8
EXP_DEV = 3
SEQ_MIN = 1024


EPS = 1e-05
RESIDUAL = 0.22
SCORE_SCALE = 1.0 / 64.0
ROPE_BASE = 10000.0
NEG = -1000000000.0


def rms_norm(states, gain):
    return states * lax.rsqrt(jnp.mean(states * states, axis=-1, keepdims=True) + EPS) * gain


def rope_tables(positions):
    half_dim = HD // 2
    frequencies = ROPE_BASE ** (-(2.0 * jnp.arange(half_dim, dtype=jnp.float32)) / HD)
    angles = positions[:, None] * frequencies[None, :]
    return (jnp.cos(angles)[:, None, :], jnp.sin(angles)[:, None, :])


def rotary(heads_in, cosine_table, sine_table):
    half_dim = heads_in.shape[-1] // 2
    first_half = heads_in[..., :half_dim]
    second_half = heads_in[..., half_dim:]
    return jnp.concatenate(
        [
            first_half * cosine_table - second_half * sine_table,
            second_half * cosine_table + first_half * sine_table,
        ],
        axis=-1,
    )


def swiglu(gate_part, up_part):
    return gate_part * jax.nn.sigmoid(gate_part) * up_part


def soft_weights(scores):
    return jnp.exp(scores - jax.nn.logsumexp(scores, axis=-1, keepdims=True))


def body(
    hidden_in,
    teacher,
    valid,
    routes,
    gain_attn,
    gain_moe,
    w_query,
    w_key,
    w_value,
    w_out,
    w_router,
    w_gate_up,
    w_down,
):
    tok_dev, model_width = hidden_in.shape
    owners = lax.axis_size("expert")
    replicas = lax.axis_size("dp")
    owner_index = lax.axis_index("expert")
    length = min(SEQ_MIN, owners * tok_dev)
    experts_all = EXP_DEV * owners
    slot_most = 8 * ((tok_dev * TOP + experts_all * 7 - 1) // (experts_all * 7))
    slot_count = experts_all * slot_most
    keys_total = owners * tok_dev
    key_block = math.gcd(keys_total, 256)
    blocks = keys_total // key_block
    group_size = H // KVH
    first_token = owner_index * tok_dev
    offsets = first_token + jnp.arange(tok_dev, dtype=jnp.int32)
    seq_start = first_token // length * length
    last_token = first_token + tok_dev - 1
    cosine_table, sine_table = rope_tables((offsets % length).astype(jnp.float32))
    dense_full = (
        lax.all_gather(gain_attn, "dp", axis=0, tiled=True),
        lax.all_gather(gain_moe, "dp", axis=0, tiled=True),
        lax.all_gather(w_query, "dp", axis=0, tiled=True),
        lax.all_gather(w_key, "dp", axis=0, tiled=True),
        lax.all_gather(w_value, "dp", axis=0, tiled=True),
        lax.all_gather(w_out, "dp", axis=0, tiled=True),
        lax.all_gather(w_router, "dp", axis=0, tiled=True),
    )
    gain_one, gain_two, query_full, key_full, value_full, out_full, router_full = dense_full
    expert_full = (
        lax.all_gather(w_gate_up, "dp", axis=1, tiled=True),
        lax.all_gather(w_down, "dp", axis=1, tiled=True),
    )
    gate_up_full, down_full = expert_full
    inputs = hidden_in.astype(jnp.float32)
    normed_f, norm_one_pull = jax.vjp(rms_norm, inputs, gain_one.astype(jnp.float32))
    normed = normed_f.astype(jnp.bfloat16)
    query_lin = jnp.dot(normed, query_full, preferred_element_type=jnp.float32)
    key_lin = jnp.dot(normed, key_full, preferred_element_type=jnp.float32)
    value_lin = jnp.dot(normed, value_full, preferred_element_type=jnp.float32)
    queries = (
        rotary(query_lin.reshape(tok_dev, H, HD), cosine_table, sine_table)
        .astype(jnp.bfloat16)
        .reshape(tok_dev, KVH, group_size, HD)
    )
    keys_own = (
        rotary(key_lin.reshape(tok_dev, KVH, HD), cosine_table, sine_table)
        .astype(jnp.bfloat16)
        .reshape(tok_dev, KVH * HD)
    )
    values_own = value_lin.astype(jnp.bfloat16)
    keys_all, values_all = (
        lax.all_gather(keys_own, "expert", axis=0, tiled=True),
        lax.all_gather(values_own, "expert", axis=0, tiled=True),
    )

    def relevant(block_index):
        key_start = block_index * key_block
        return (key_start <= last_token) & (key_start + key_block > seq_start)

    def scores_at(block_index):
        key_start = block_index * key_block
        key_rows = lax.dynamic_slice_in_dim(keys_all, key_start, key_block, 0).reshape(
            key_block, KVH, HD
        )
        raw_scores = (
            jnp.einsum("qhgd,khd->hgqk", queries, key_rows, preferred_element_type=jnp.float32)
            * SCORE_SCALE
        )
        key_pos = key_start + jnp.arange(key_block, dtype=jnp.int32)
        allowed = (key_pos[None, :] <= offsets[:, None]) & (
            key_pos[None, :] // length == offsets[:, None] // length
        )
        return (jnp.where(allowed[None, None], raw_scores, NEG), key_rows)

    def value_rows(block_index):
        return lax.dynamic_slice_in_dim(values_all, block_index * key_block, key_block, 0).reshape(
            key_block, KVH, HD
        )

    def stats_step(block_index, carried):

        def stats_update(stats_state):
            running_max, totals = stats_state
            scores, key_rows = scores_at(block_index)
            new_max = jnp.maximum(running_max, jnp.max(scores, axis=-1))
            totals = totals * jnp.exp(running_max - new_max) + jnp.sum(
                jnp.exp(scores - new_max[..., None]), axis=-1
            )
            return (new_max, totals)

        return lax.cond(relevant(block_index), stats_update, lambda kept_state: kept_state, carried)

    start_max = jnp.full((KVH, group_size, tok_dev), NEG, jnp.float32)
    running_max, totals = lax.fori_loop(
        0, blocks, stats_step, (start_max, jnp.zeros_like(start_max))
    )
    log_total = running_max + jnp.log(totals)

    def output_step(block_index, carried):

        def output_update(accumulated):
            scores, key_rows = scores_at(block_index)
            attn_probs = jnp.exp(scores - log_total[..., None]).astype(jnp.bfloat16)
            return accumulated + jnp.einsum(
                "hgqk,khd->qhgd",
                attn_probs,
                value_rows(block_index),
                preferred_element_type=jnp.float32,
            )

        return lax.cond(
            relevant(block_index), output_update, lambda kept_state: kept_state, carried
        )

    context = lax.fori_loop(
        0, blocks, output_step, jnp.zeros((tok_dev, KVH, group_size, HD), jnp.float32)
    )
    context_b = context.reshape(tok_dev, H * HD).astype(jnp.bfloat16)
    mid = inputs + RESIDUAL * jnp.dot(context_b, out_full, preferred_element_type=jnp.float32)
    moe_f, norm_two_pull = jax.vjp(rms_norm, mid, gain_two.astype(jnp.float32))
    moe_input = moe_f.astype(jnp.bfloat16)
    logits = jnp.dot(moe_input, router_full, preferred_element_type=jnp.float32)
    route_hot = routes[:, :, None] == jnp.arange(experts_all, dtype=jnp.int32)[None, None, :]
    chosen = jnp.sum(jnp.where(route_hot, logits[:, None, :], 0.0), axis=-1)
    gate_weights, gate_pull = jax.vjp(soft_weights, chosen)
    flat_routes = routes.reshape(-1)
    flat_hot = (flat_routes[:, None] == jnp.arange(experts_all, dtype=jnp.int32)[None, :]).astype(
        jnp.int32
    )
    ranking = jnp.sum((jnp.cumsum(flat_hot, axis=0) - flat_hot) * flat_hot, axis=1)
    slot_index = flat_routes * slot_most + ranking
    row_of_slot = (
        jnp.zeros((slot_count,), jnp.int32)
        .at[slot_index]
        .set(jnp.arange(tok_dev * TOP, dtype=jnp.int32))
    )
    filled = jnp.zeros((slot_count,), jnp.int32).at[slot_index].set(1) > 0
    empty_row = jnp.zeros((), jnp.bfloat16)
    outgoing = jnp.where(filled[:, None], moe_input[row_of_slot // TOP], empty_row).reshape(
        owners, EXP_DEV, slot_most, model_width
    )
    arrived = lax.all_to_all(outgoing, "expert", split_axis=0, concat_axis=0, tiled=True)
    gate_up = jnp.einsum(
        "semd,edf->semf", arrived, gate_up_full, preferred_element_type=jnp.float32
    )
    hidden = swiglu(gate_up[..., :FF], gate_up[..., FF:]).astype(jnp.bfloat16)
    produced = jnp.einsum(
        "semf,efd->semd", hidden, down_full, preferred_element_type=jnp.float32
    ).astype(jnp.bfloat16)
    returned = lax.all_to_all(produced, "expert", split_axis=0, concat_axis=0, tiled=True)
    returned, gate_up_kept, arrived_kept = (returned, gate_up, arrived)
    picked = returned.reshape(slot_count, model_width)[slot_index].reshape(
        tok_dev, TOP, model_width
    )
    experts_sum = jnp.sum(gate_weights[:, :, None] * picked, axis=1)
    final_state = mid + RESIDUAL * experts_sum
    activations = final_state.astype(jnp.bfloat16)
    valid_float = valid.astype(jnp.float32)
    mismatch = final_state - teacher.astype(jnp.float32)
    valid_count, squares = lax.psum(
        (jnp.sum(valid_float), 0.5 * jnp.sum(valid_float[:, None] * mismatch * mismatch)),
        ("dp", "expert"),
    )
    loss_value = squares / (valid_count * model_width)
    tokens_all = tok_dev * replicas * owners
    grad_final = tokens_all / valid_count * valid_float[:, None] * mismatch
    regathered = (
        lax.all_gather(w_query, "dp", axis=0, tiled=True),
        lax.all_gather(w_key, "dp", axis=0, tiled=True),
        lax.all_gather(w_value, "dp", axis=0, tiled=True),
        lax.all_gather(w_out, "dp", axis=0, tiled=True),
        lax.all_gather(w_router, "dp", axis=0, tiled=True),
        lax.all_gather(w_gate_up, "dp", axis=1, tiled=True),
        lax.all_gather(w_down, "dp", axis=1, tiled=True),
    )
    query_full, key_full, value_full, out_full, router_full, gate_up_full, down_full = regathered
    grad_experts = RESIDUAL * grad_final
    grad_picked = (gate_weights[:, :, None] * grad_experts[:, None, :]).astype(jnp.bfloat16)
    grad_gates = jnp.sum(picked * grad_experts[:, None, :], axis=-1)
    outgoing_grad = jnp.where(
        filled[:, None], grad_picked.reshape(tok_dev * TOP, model_width)[row_of_slot], empty_row
    ).reshape(owners, EXP_DEV, slot_most, model_width)
    arrived_grad = lax.all_to_all(outgoing_grad, "expert", split_axis=0, concat_axis=0, tiled=True)
    hidden_grad = jnp.einsum(
        "semd,efd->semf", arrived_grad, down_full, preferred_element_type=jnp.float32
    )
    hidden_again, swiglu_pull = jax.vjp(swiglu, gate_up_kept[..., :FF], gate_up_kept[..., FF:])
    grad_gate_part, grad_up_part = swiglu_pull(hidden_grad)
    grad_gate_rows = jnp.concatenate([grad_gate_part, grad_up_part], axis=-1).astype(jnp.bfloat16)
    row_grad = jnp.einsum(
        "semf,edf->semd", grad_gate_rows, gate_up_full, preferred_element_type=jnp.float32
    ).astype(jnp.bfloat16)
    home_grad = lax.all_to_all(row_grad, "expert", split_axis=0, concat_axis=0, tiled=True)
    grad_down_local = jnp.einsum(
        "semf,semd->efd",
        hidden_again.astype(jnp.bfloat16),
        arrived_grad,
        preferred_element_type=jnp.float32,
    )
    grad_gate_up_local = jnp.einsum(
        "semd,semf->edf", arrived_kept, grad_gate_rows, preferred_element_type=jnp.float32
    )
    grad_gate_up_shard, grad_down_shard = (
        lax.psum_scatter(
            grad_gate_up_local.astype(jnp.bfloat16), "dp", scatter_dimension=1, tiled=True
        ).astype(jnp.float32),
        lax.psum_scatter(
            grad_down_local.astype(jnp.bfloat16), "dp", scatter_dimension=1, tiled=True
        ).astype(jnp.float32),
    )
    grad_chosen = gate_pull(grad_gates)[0]
    grad_logits = jnp.sum(jnp.where(route_hot, grad_chosen[:, :, None], 0.0), axis=1).astype(
        jnp.bfloat16
    )
    grad_router_local = jnp.einsum(
        "td,te->de", moe_input, grad_logits, preferred_element_type=jnp.float32
    )
    home_rows = home_grad.reshape(slot_count, model_width)[slot_index].reshape(
        tok_dev, TOP, model_width
    )
    grad_moe_input = jnp.sum(home_rows, axis=1, dtype=jnp.float32) + jnp.einsum(
        "te,de->td", grad_logits, router_full, preferred_element_type=jnp.float32
    )
    grad_mid_norm, grad_gain_two = norm_two_pull(grad_moe_input)
    grad_mid = grad_final + grad_mid_norm
    grad_branch = (RESIDUAL * grad_mid).astype(jnp.bfloat16)
    grad_out_local = jnp.einsum(
        "tc,td->cd", context_b, grad_branch, preferred_element_type=jnp.float32
    )
    grad_context = (
        jnp.einsum("td,cd->tc", grad_branch, out_full, preferred_element_type=jnp.float32)
        .astype(jnp.bfloat16)
        .reshape(tok_dev, KVH, group_size, HD)
    )

    def delta_step(block_index, carried):

        def delta_update(accumulated):
            scores, key_rows = scores_at(block_index)
            attn_probs = jnp.exp(scores - log_total[..., None])
            grad_probs = jnp.einsum(
                "qhgd,khd->hgqk",
                grad_context,
                value_rows(block_index),
                preferred_element_type=jnp.float32,
            )
            return accumulated + jnp.sum(attn_probs * grad_probs, axis=-1)

        return lax.cond(relevant(block_index), delta_update, lambda kept_state: kept_state, carried)

    row_delta = lax.fori_loop(
        0, blocks, delta_step, jnp.zeros((KVH, group_size, tok_dev), jnp.float32)
    )

    def grad_step(block_index, carried):

        def grad_update(grad_state):
            grad_queries, grad_keys_all, grad_values_all = grad_state
            scores, key_rows = scores_at(block_index)
            value_block = value_rows(block_index)
            attn_probs = jnp.exp(scores - log_total[..., None])
            grad_probs = jnp.einsum(
                "qhgd,khd->hgqk", grad_context, value_block, preferred_element_type=jnp.float32
            )
            grad_scores = (attn_probs * (grad_probs - row_delta[..., None])).astype(jnp.bfloat16)
            grad_queries = (
                grad_queries
                + jnp.einsum(
                    "hgqk,khd->qhgd", grad_scores, key_rows, preferred_element_type=jnp.float32
                )
                * SCORE_SCALE
            )
            key_part = (
                jnp.einsum(
                    "hgqk,qhgd->khd", grad_scores, queries, preferred_element_type=jnp.float32
                )
                * SCORE_SCALE
            )
            value_part = jnp.einsum(
                "hgqk,qhgd->khd",
                attn_probs.astype(jnp.bfloat16),
                grad_context,
                preferred_element_type=jnp.float32,
            )
            key_start = block_index * key_block
            grad_keys_all = lax.dynamic_update_slice_in_dim(
                grad_keys_all, key_part.reshape(key_block, KVH * HD), key_start, 0
            )
            grad_values_all = lax.dynamic_update_slice_in_dim(
                grad_values_all, value_part.reshape(key_block, KVH * HD), key_start, 0
            )
            return (grad_queries, grad_keys_all, grad_values_all)

        return lax.cond(relevant(block_index), grad_update, lambda kept_state: kept_state, carried)

    zero_keys = jnp.zeros((keys_total, KVH * HD), jnp.float32)
    grad_queries, grad_keys_all, grad_values_all = lax.fori_loop(
        0,
        blocks,
        grad_step,
        (jnp.zeros((tok_dev, KVH, group_size, HD), jnp.float32), zero_keys, zero_keys),
    )
    grad_keys, grad_values = (
        lax.psum_scatter(
            grad_keys_all.astype(jnp.bfloat16), "expert", scatter_dimension=0, tiled=True
        ).astype(jnp.float32),
        lax.psum_scatter(
            grad_values_all.astype(jnp.bfloat16), "expert", scatter_dimension=0, tiled=True
        ).astype(jnp.float32),
    )
    rotated_heads, query_rope_pull = jax.vjp(
        lambda heads_in: rotary(heads_in, cosine_table, sine_table),
        query_lin.reshape(tok_dev, H, HD),
    )
    rotated_kv, key_rope_pull = jax.vjp(
        lambda heads_in: rotary(heads_in, cosine_table, sine_table),
        key_lin.reshape(tok_dev, KVH, HD),
    )
    grad_query_lin = (
        query_rope_pull(grad_queries.reshape(tok_dev, H, HD))[0]
        .reshape(tok_dev, H * HD)
        .astype(jnp.bfloat16)
    )
    grad_key_lin = (
        key_rope_pull(grad_keys.reshape(tok_dev, KVH, HD))[0]
        .reshape(tok_dev, KVH * HD)
        .astype(jnp.bfloat16)
    )
    grad_value_lin = grad_values.astype(jnp.bfloat16)
    grad_query_local = jnp.einsum(
        "td,tc->dc", normed, grad_query_lin, preferred_element_type=jnp.float32
    )
    grad_key_local = jnp.einsum(
        "td,tc->dc", normed, grad_key_lin, preferred_element_type=jnp.float32
    )
    grad_value_local = jnp.einsum(
        "td,tc->dc", normed, grad_value_lin, preferred_element_type=jnp.float32
    )
    grad_normed = (
        jnp.einsum("tc,dc->td", grad_query_lin, query_full, preferred_element_type=jnp.float32)
        + jnp.einsum("tc,dc->td", grad_key_lin, key_full, preferred_element_type=jnp.float32)
        + jnp.einsum("tc,dc->td", grad_value_lin, value_full, preferred_element_type=jnp.float32)
    )
    grad_in_norm, grad_gain_one = norm_one_pull(grad_normed)
    grad_in = grad_mid + grad_in_norm
    g_one, g_two, g_query, g_key, g_value, g_out, g_router = (
        lax.psum_scatter(
            grad_gain_one.astype(jnp.bfloat16), "dp", scatter_dimension=0, tiled=True
        ).astype(jnp.float32),
        lax.psum_scatter(
            grad_gain_two.astype(jnp.bfloat16), "dp", scatter_dimension=0, tiled=True
        ).astype(jnp.float32),
        lax.psum_scatter(
            grad_query_local.astype(jnp.bfloat16), "dp", scatter_dimension=0, tiled=True
        ).astype(jnp.float32),
        lax.psum_scatter(
            grad_key_local.astype(jnp.bfloat16), "dp", scatter_dimension=0, tiled=True
        ).astype(jnp.float32),
        lax.psum_scatter(
            grad_value_local.astype(jnp.bfloat16), "dp", scatter_dimension=0, tiled=True
        ).astype(jnp.float32),
        lax.psum_scatter(
            grad_out_local.astype(jnp.bfloat16), "dp", scatter_dimension=0, tiled=True
        ).astype(jnp.float32),
        lax.psum_scatter(
            grad_router_local.astype(jnp.bfloat16), "dp", scatter_dimension=0, tiled=True
        ).astype(jnp.float32),
    )
    g_one, g_two, g_query, g_key, g_value, g_out, g_router = (
        lax.psum(g_one.astype(jnp.bfloat16), "expert").astype(jnp.float32),
        lax.psum(g_two.astype(jnp.bfloat16), "expert").astype(jnp.float32),
        lax.psum(g_query.astype(jnp.bfloat16), "expert").astype(jnp.float32),
        lax.psum(g_key.astype(jnp.bfloat16), "expert").astype(jnp.float32),
        lax.psum(g_value.astype(jnp.bfloat16), "expert").astype(jnp.float32),
        lax.psum(g_out.astype(jnp.bfloat16), "expert").astype(jnp.float32),
        lax.psum(g_router.astype(jnp.bfloat16), "expert").astype(jnp.float32),
    )
    return (
        activations,
        loss_value,
        grad_in,
        g_one,
        g_two,
        g_query,
        g_key,
        g_value,
        g_out,
        g_router,
        grad_gate_up_shard,
        grad_down_shard,
    )


def solution(mesh):
    placed = (
        P(("dp", "expert"), None),
        P(("dp", "expert"), None),
        P(("dp", "expert")),
        P(("dp", "expert"), None),
        P("dp"),
        P("dp"),
        P("dp", None),
        P("dp", None),
        P("dp", None),
        P("dp", None),
        P("dp", None),
        P("expert", "dp", None),
        P("expert", "dp", None),
    )
    return jax.shard_map(
        body,
        mesh=mesh,
        in_specs=placed,
        out_specs=(
            P(("dp", "expert"), None),
            P(),
            P(("dp", "expert"), None),
            P("dp"),
            P("dp"),
            P("dp", None),
            P("dp", None),
            P("dp", None),
            P("dp", None),
            P("dp", None),
            P("expert", "dp", None),
            P("expert", "dp", None),
        ),
        check_vma=False,
    )
```

profile of v0, /device:TPU:0, one launch (start us, length us, event | category | flops | bytes accessed | tf_op | source)
XLA Modules:
  0.0 1785.9 jit_solution(9261462877564857401)
XLA Ops:
  9.4 13.6 all-gather
  24.5 24.9 %all-gather.11.cloned.1.call-done = bf16[1536,512]{1,0:T(8,128)(2,1)} async-done(((bf16[384,512]{1,0:T(8,128)(2,1)}), bf16[1536,512]{1,0:T(8,128)(2,1)}) %all-gather.11.cloned.1.call-update) | async-done | bytes 1572880 | tf_op jit(solution)/shard_map/all_gather | solution.py:93
  53.2 33.6 %all-gather.15.cloned.1.call-done = bf16[1536,512]{1,0:T(8,128)(2,1)} async-done(((bf16[384,512]{1,0:T(8,128)(2,1)}), bf16[1536,512]{1,0:T(8,128)(2,1)}) %all-gather.15.cloned.1.call-update) | async-done | bytes 1572880 | tf_op jit(solution)/shard_map/all_gather | solution.py:92
  91.6 11.9 all-gather.1
  103.9 6.8 reduce-window.6
  111.5 8.1 scatter_custom_fusion.1
  119.5 8.5 scatter_custom_fusion
  128.3 3.9 copy.118
  132.2 74.7 %all-gather.19.cloned.1.call-done = bf16[1536,1536]{1,0:T(8,128)(2,1)} async-done(((bf16[384,1536]{1,0:T(8,128)(2,1)}), bf16[1536,1536]{1,0:T(8,128)(2,1)}) %all-gather.19.cloned.1.call-update) | async-done | bytes 4718608 | tf_op jit(solution)/shard_map/all_gather | solution.py:91
  206.9 4.3 fusion.99
  211.6 24.1 %all-gather.17.cloned.1.call-done = bf16[2048,512]{0,1:T(8,128)(2,1)} async-done(((bf16[256,512]{0,1:T(8,128)(2,1)}), bf16[2048,512]{0,1:T(8,128)(2,1)}) %all-gather.17.cloned.1.call-update) | async-done | bytes 2097168 | tf_op jit(solution)/shard_map/all_gather | solution.py:121
  235.7 4.1 while.68
  241.2 6.3 while.69
  241.2 6.0 conditional.13
  242.5 4.8 bitcast_add_fusion
  250.2 76.3 %all-gather.21.cloned.1.call-done = bf16[1536,1536]{1,0:T(8,128)(2,1)} async-done(((bf16[384,1536]{1,0:T(8,128)(2,1)}), bf16[1536,1536]{1,0:T(8,128)(2,1)}) %all-gather.21.cloned.1.call-update) | async-done | bytes 4718608 | tf_op jit(solution)/shard_map/all_gather | solution.py:94
  326.5 4.1 multiply_reduce_fusion.2
  330.9 9.6 gather_fusion
  340.5 6.8 broadcast_select_fusion.1
  347.3 4.9 all-to-all-start
  353.0 85.6 %all-to-all-done = bf16[8,3,104,1536]{3,2,1,0:T(8,128)(2,1)} async-done(((bf16[8,3,104,1536]{3,2,1,0:T(8,128)(2,1)}), bf16[8,3,104,1536]{3,2,1,0:T(8,128)(2,1)}, u32[]{:S(2)}, u32[]{:S(2)}) %all-to-all-start) | async-done | bytes 7667744 | tf_op jit(solution)/shard_map/all_to_all | solution.py:211
  438.6 54.7 %all-gather.23.cloned.1.call-done = bf16[3,1536,1024]{2,1,0:T(8,128)(2,1)} async-done(((bf16[3,384,1024]{2,1,0:T(8,128)(2,1)}), bf16[3,1536,1024]{2,1,0:T(8,128)(2,1)}) %all-gather.23.cloned.1.call-update) | async-done | bytes 9437200 | tf_op jit(solution)/shard_map/all_gather | solution.py:99
  493.3 13.1 fusion.62
  506.4 3.9 copy-done.13
  513.2 69.3 %all-gather.25.cloned.1.call-done = bf16[3,512,1536]{2,1,0:T(8,128)(2,1)} async-done(((bf16[3,128,1536]{2,1,0:T(8,128)(2,1)}), bf16[3,512,1536]{2,1,0:T(8,128)(2,1)}) %all-gather.25.cloned.1.call-update) | async-done | bytes 4718608 | tf_op jit(solution)/shard_map/all_gather | solution.py:100
  582.5 7.2 convert_bitcast_fusion.1
  593.3 5.0 all-to-all-start.1
  598.9 117.0 %psum.64 = f32[]{:T(128)} all-reduce(f32[]{:T(128)} %convert_reduce_fusion.3), channel_id=1, replica_groups=mesh['dp'=4,'expert'=8] {'dp','expert'}, use_global_device_ids=true, to_apply=%region_24.25 | all-reduce | flops 1 | bytes 8 | tf_op jit(solution)/shard_map/psum | solution.py:229
  716.5 13.2 all_gather.48
  730.4 17.6 gather_fusion.1
  748.1 8.9 fusion.38
  758.2 3.9 fusion.40
  762.0 19.9 %gather_fusion.2 = bf16[2496,1536]{1,0:T(8,128)(2,1)} fusion(bf16[2048,1536]{1,0:T(8,128)(2,1)} %fusion.40, s32[3072]{0:T(1024)S(1)} %get-tuple-element.1242), kind=kCustom, calls=%fused_computation.2 | custom fusion | bytes 15345408 | tf_op jit(solution)/shard_map/gather | solution.py:250
  785.7 90.4 %all_to_all.20 = bf16[8,3,104,1536]{3,2,1,0:T(8,128)(2,1)} all-to-all(bf16[8,3,104,1536]{3,2,1,0:T(8,128)(2,1)S(1)} %broadcast_select_fusion), channel_id=1, replica_groups=mesh['dp'=4,'expert'=8] {'expert'}, dimensions={0} | all-to-all | bytes 15335424 | tf_op jit(solution)/shard_map/all_to_all | solution.py:252
  876.2 12.4 fusion.54
  888.5 14.7 convert_bitcast_fusion
  903.2 6.8 copy.129
  910.0 5.0 all-to-all-start.3
  915.1 4.1 fusion.39
  919.4 82.0 %all-to-all-done.3 = bf16[8,3,104,1536]{3,2,1,0:T(8,128)(2,1)} async-done(((bf16[8,3,104,1536]{3,2,1,0:T(8,128)(2,1)}), bf16[8,3,104,1536]{3,2,1,0:T(8,128)(2,1)}, u32[]{:S(2)}, u32[]{:S(2)}) %all-to-all-start.3) | async-done | bytes 7667744 | tf_op jit(solution)/shard_map/all_to_all | solution.py:262
  1001.4 17.6 gather_fusion.3
  1019.0 7.2 convert_reduce_fusion
  1032.4 4.8 while.70
  1032.5 4.3 conditional.14
  1040.5 9.8 while.71
  1040.8 9.3 conditional.15
  1051.1 78.7 %reduce-scatter.14.cloned.1.call-done = bf16[256,512]{0,1:T(8,128)(2,1)} async-done(((bf16[2048,512]{0,1:T(8,128)(2,1)}), bf16[256,512]{0,1:T(8,128)(2,1)}) %reduce-scatter.14.cloned.1.call-update) | async-done | bytes 262160 | tf_op jit(solution)/shard_map/reduce_scatter | solution.py:376
  1132.7 41.9 %reduce-scatter.12.cloned.1.call-done = bf16[256,512]{0,1:T(8,128)(2,1)} async-done(((bf16[2048,512]{0,1:T(8,128)(2,1)}), bf16[256,512]{0,1:T(8,128)(2,1)}) %reduce-scatter.12.cloned.1.call-update) | async-done | bytes 262160 | tf_op jit(solution)/shard_map/reduce_scatter | solution.py:373
  1177.7 4.9 convolution_convert_fusion
  1189.2 10.6 bitcast_convert_fusion.1
  1199.9 13.1 reduce-scatter.20.cloned.1.call-done
  1212.9 37.1 %reduce-scatter.18.cloned.1.call-done = bf16[384,512]{1,0:T(8,128)(2,1)} async-done(((bf16[1536,512]{1,0:T(8,128)(2,1)}), bf16[384,512]{1,0:T(8,128)(2,1)}) %reduce-scatter.18.cloned.1.call-update) | async-done | bytes 393232 | tf_op jit(solution)/shard_map/reduce_scatter | solution.py:425
  1250.0 86.5 %reduce-scatter.22.cloned.1.call-done = bf16[384,1536]{1,0:T(8,128)(2,1)} async-done(((bf16[1536,1536]{1,0:T(8,128)(2,1)}), bf16[384,1536]{1,0:T(8,128)(2,1)}) %reduce-scatter.22.cloned.1.call-update) | async-done | bytes 1179664 | tf_op jit(solution)/shard_map/reduce_scatter | solution.py:431
  1336.5 88.6 %reduce-scatter.16.cloned.1.call-done = bf16[384,1536]{1,0:T(8,128)(2,1)} async-done(((bf16[1536,1536]{1,0:T(8,128)(2,1)}), bf16[384,1536]{1,0:T(8,128)(2,1)}) %reduce-scatter.16.cloned.1.call-update) | async-done | bytes 1179664 | tf_op jit(solution)/shard_map/reduce_scatter | solution.py:422
  1425.1 16.1 bitcast_convert_fusion
  1443.7 5.4 reduce-scatter.28.cloned.1.call-done
  1450.1 43.3 %psum.63 = f32[]{:T(128)} all-reduce(f32[]{:T(128)S(6)} %mul_shard_map.3), channel_id=1, replica_groups=mesh['dp'=4,'expert'=8] {'dp','expert'}, use_global_device_ids=true, to_apply=%region_22.23 | all-reduce | flops 1 | bytes 8 | tf_op jit(solution)/shard_map/psum | solution.py:229
  1494.0 5.0 fusion.108
  1499.0 36.9 %reduce-scatter.26.cloned.1.call-done = bf16[3,128,1536]{2,1,0:T(8,128)(2,1)} async-done(((bf16[3,512,1536]{2,1,0:T(8,128)(2,1)}), bf16[3,128,1536]{2,1,0:T(8,128)(2,1)}) %reduce-scatter.26.cloned.1.call-update) | async-done | bytes 1179664 | tf_op jit(solution)/shard_map/reduce_scatter | solution.py:276
  1542.5 11.1 all-reduce.8
  1553.7 22.8 %all-reduce.6 = (bf16[384]{0:T(512)(128)(2,1)S(1)}, bf16[384]{0:T(512)(128)(2,1)S(1)}, bf16[384,24]{0,1:T(8,128)(2,1)S(1)}) all-reduce(bf16[384]{0:T(512)(128)(2,1)S(1)} %dynamic-slice.1, bf16[384]{0:T(512)(128)(2,1)S(1)} %dynamic-slice.3, bf16[384,24]{0,1:T(8,128)(2,1)S(1)} %copy.156), channel_id=1, replica_groups=mesh['dp'=4,'expert'=8] {'expert'}, use_global_device_ids=true, to_apply=%region_44.45 | all-reduce | flops 9984 | bytes 39936 | tf_op jit(solution)/shard_map/psum | solution.py:439
  1581.3 28.2 %all-reduce.11.cloned.1.call-done = (bf16[384,1536]{1,0:T(8,128)(2,1)}, bf16[384,512]{1,0:T(8,128)(2,1)}, bf16[384,512]{1,0:T(8,128)(2,1)}, bf16[384,1536]{1,0:T(8,128)(2,1)}) async-done(((bf16[384,1536]{1,0:T(8,128)(2,1)}, bf16[384,512]{1,0:T(8,128)(2,1)}, bf16[384,512]{1,0:T(8,128)(2,1)}, bf16[384,1536]{1,0:T(8,128)(2,1)}), (bf16[384,1536]{1,0:T(8,128)(2,1)}, bf16[384,512]{1,0:T(8,128)(2,1)}, ...) | async-done | bytes 3145744 | tf_op jit(solution)/shard_map/psum | solution.py:441
  1617.1 156.0 %reduce-scatter.24.cloned.1.call-done = bf16[3,384,1024]{2,1,0:T(8,128)(2,1)} async-done(((bf16[3,1536,1024]{2,1,0:T(8,128)(2,1)}), bf16[3,384,1024]{2,1,0:T(8,128)(2,1)}) %reduce-scatter.24.cloned.1.call-update) | async-done | bytes 2359312 | tf_op jit(solution)/shard_map/reduce_scatter | solution.py:273
  1773.1 4.4 convert_element_type.276
  (325 shorter events, 96.9 us)
Async XLA Ops:
  7.2 42.2 %all-gather.11.cloned.1.call-start = ((), (), s32[]{:S(2)}) async-start(), calls=%async_computation.13 | async-start | bytes 1966080 | tf_op jit(solution)/shard_map/all_gather | solution.py:93
  7.9 78.9 %all-gather.15.cloned.1.call-start = ((), (), s32[]{:S(2)}) async-start(), calls=%async_computation.15 | async-start | bytes 1966080 | tf_op jit(solution)/shard_map/all_gather | solution.py:92
  8.7 119.6 %all-gather.13.cloned.1.call-start = ((), (), s32[]{:S(2)}) async-start(), calls=%async_computation.14 | async-start | bytes 2359296 | tf_op jit(solution)/shard_map/all_gather | solution.py:122
  23.0 183.8 %copy-start.26 = (f32[1536]{0:T(1024)}, f32[1536]{0:T(1024)S(1)}, u32[]{:S(2)}) copy-start(f32[1536]{0:T(1024)S(1)} %reshape.899) | copy-start | bytes 18436
  24.4 64.6 %copy-start.38 = (f32[256]{0:T(256)}, f32[256]{0:T(256)S(1)}, u32[]{:S(2)}) copy-start(f32[256]{0:T(256)S(1)} %fusion.74) | copy-start | bytes 3076
  24.4 62.4 %copy-start.4 = (bf16[256,1536]{1,0:T(8,128)(2,1)S(1)}, bf16[256,1536]{1,0:T(8,128)(2,1)}, u32[]{:S(2)}) copy-start(bf16[256,1536]{1,0:T(8,128)(2,1)} %param.29) | copy-start | bytes 2359300
  24.5 182.4 %copy-start.31 = (f32[256]{0:T(256)}, f32[256]{0:T(256)S(1)}, u32[]{:S(2)}) copy-start(f32[256]{0:T(256)S(1)} %fusion.92) | copy-start | bytes 3076
  52.3 154.5 %all-gather.19.cloned.1.call-start = ((), (), s32[]{:S(2)}) async-start(), calls=%async_computation.17 | async-start | bytes 5898240 | tf_op jit(solution)/shard_map/all_gather | solution.py:91
  52.9 182.8 %all-gather.17.cloned.1.call-start = ((), (), s32[]{:S(2)}) async-start(), calls=%async_computation.16 | async-start | bytes 2359296 | tf_op jit(solution)/shard_map/all_gather | solution.py:121
  53.2 158.0 %copy-start.22 = (f32[256,32]{0,1:T(8,128)}, f32[256,32]{0,1:T(8,128)S(1)}, u32[]{:S(2)}) copy-start(f32[256,32]{0,1:T(8,128)S(1)} %get-tuple-element.1236) | copy-start | bytes 98308
  53.2 158.0 %copy-start.24 = (f32[256,32]{0,1:T(8,128)}, f32[256,32]{0,1:T(8,128)S(1)}, u32[]{:S(2)}) copy-start(f32[256,32]{0,1:T(8,128)S(1)} %get-tuple-element.1237) | copy-start | bytes 98308
  89.1 2.2 copy-start.28
  89.1 2.5 copy-start.43
  89.9 236.6 %all-gather.21.cloned.1.call-start = ((), (), s32[]{:S(2)}) async-start(), calls=%async_computation.18 | async-start | bytes 5898240 | tf_op jit(solution)/shard_map/all_gather | solution.py:94
  90.5 402.8 %all-gather.23.cloned.1.call-start = ((), (), s32[]{:S(2)}) async-start(), calls=%async_computation.19 | async-start | bytes 11796480 | tf_op jit(solution)/shard_map/all_gather | solution.py:99
  103.6 227.1 %copy-start.29 = (f32[1536]{0:T(1024)}, f32[1536]{0:T(1024)S(1)}, u32[]{:S(2)}) copy-start(f32[1536]{0:T(1024)S(1)} %reshape.900) | copy-start | bytes 18436
  247.5 83.2 %copy-start.2 = (bf16[256,8,3,64]{0,3,2,1:T(8,128)(2,1)}, bf16[256,8,3,64]{0,3,2,1:T(8,128)(2,1)S(1)}, u32[]{:S(2)}) copy-start(bf16[256,8,3,64]{0,3,2,1:T(8,128)(2,1)S(1)} %get-tuple-element.1682) | copy-start | bytes 2359300
  247.5 83.2 %copy-start.33 = (f32[8,3,256]{2,1,0:T(4,128)}, f32[8,3,256]{2,1,0:T(4,128)S(1)}, u32[]{:S(2)}) copy-start(f32[8,3,256]{2,1,0:T(4,128)S(1)} %get-tuple-element.1759) | copy-start | bytes 73732
  330.7 9.8 copy-start.40
  330.7 9.8 copy-start.36
  330.9 398.8 %copy-start = (bf16[256,1536]{1,0:T(8,128)(2,1)}, bf16[256,1536]{1,0:T(8,128)(2,1)S(1)}, u32[]{:S(2)}) copy-start(bf16[256,1536]{1,0:T(8,128)(2,1)S(1)} %multiply_convert_fusion.2) | copy-start | bytes 2359300
  347.3 91.2 %all-to-all-start = ((bf16[8,3,104,1536]{3,2,1,0:T(8,128)(2,1)}), bf16[8,3,104,1536]{3,2,1,0:T(8,128)(2,1)}, u32[]{:S(2)}, u32[]{:S(2)}) async-start(bf16[8,3,104,1536]{3,2,1,0:T(8,128)(2,1)} %broadcast_select_fusion.1), calls=%async_computation | async-start | bytes 15335424 | tf_op jit(solution)/shard_map/all_to_all | solution.py:211
  352.3 230.2 %all-gather.25.cloned.1.call-start = ((), (), s32[]{:S(2)}) async-start(), calls=%async_computation.20 | async-start | bytes 5898240 | tf_op jit(solution)/shard_map/all_gather | solution.py:100
  506.4 3.9 copy-start.13
  593.3 5.0 copy-start.42
  593.3 123.2 %copy-start.35 = (bf16[384,24]{0,1:T(8,128)(2,1)S(1)}, bf16[384,24]{0,1:T(8,128)(2,1)}, u32[]{:S(2)}) copy-start(bf16[384,24]{0,1:T(8,128)(2,1)} %param.39) | copy-start | bytes 55300
  593.3 137.1 %all-to-all-start.1 = ((bf16[8,3,104,1536]{3,2,1,0:T(8,128)(2,1)}), bf16[8,3,104,1536]{3,2,1,0:T(8,128)(2,1)}, u32[]{:S(2)}, u32[]{:S(2)}) async-start(bf16[8,3,104,1536]{3,2,1,0:T(8,128)(2,1)} %copy.126), calls=%async_computation.1 | async-start | bytes 15335424 | tf_op jit(solution)/shard_map/all_to_all | solution.py:219
  748.1 9.0 copy-start.14
  758.2 3.9 copy-start.9
  910.0 5.1 copy-start.10
  910.0 91.3 %all-to-all-start.3 = ((bf16[8,3,104,1536]{3,2,1,0:T(8,128)(2,1)}), bf16[8,3,104,1536]{3,2,1,0:T(8,128)(2,1)}, u32[]{:S(2)}, u32[]{:S(2)}) async-start(bf16[8,3,104,1536]{3,2,1,0:T(8,128)(2,1)} %copy.129), calls=%async_computation.3 | async-start | bytes 15335424 | tf_op jit(solution)/shard_map/all_to_all | solution.py:262
  915.1 214.7 %reduce-scatter.14.cloned.1.call-start = ((), (), s32[]{:S(2)}) async-start(), calls=%async_computation.22 | async-start | bytes 2359296 | tf_op jit(solution)/shard_map/reduce_scatter | solution.py:376
  1019.0 7.2 copy-start.7
  1019.0 7.2 copy-start.15
  1019.0 7.2 copy-start.30
  1019.0 7.2 copy-start.37
  1026.3 1.6 copy-start.41
  1026.3 4.4 slice-start
  1027.9 2.8 slice-start.1
  1030.7 1.7 copy-start.3
  1030.7 1.7 copy-start.34
  1050.4 79.4 %copy-start.5 = (bf16[256,1536]{1,0:T(8,128)(2,1)S(1)}, bf16[256,1536]{1,0:T(8,128)(2,1)}, u32[]{:S(2)}) copy-start(bf16[256,1536]{1,0:T(8,128)(2,1)} %param.29) | copy-start | bytes 2359300
  1050.4 79.4 %copy-start.27 = (f32[1536]{0:T(1024)S(1)}, f32[1536]{0:T(1024)}, u32[]{:S(2)}) copy-start(f32[1536]{0:T(1024)} %copy-done.26) | copy-start | bytes 18436
  1050.4 79.4 %copy-start.32 = (f32[256]{0:T(256)S(1)}, f32[256]{0:T(256)}, u32[]{:S(2)}) copy-start(f32[256]{0:T(256)} %copy-done.31) | copy-start | bytes 3076
  1050.4 124.2 %reduce-scatter.12.cloned.1.call-start = ((), (), s32[]{:S(2)}) async-start(), calls=%async_computation.21 | async-start | bytes 2359296 | tf_op jit(solution)/shard_map/reduce_scatter | solution.py:373
  1051.0 124.6 %copy-start.23 = (f32[256,32]{0,1:T(8,128)S(1)}, f32[256,32]{0,1:T(8,128)}, u32[]{:S(2)}) copy-start(f32[256,32]{0,1:T(8,128)} %copy-done.22) | copy-start | bytes 98308
  1051.0 124.6 %copy-start.25 = (f32[256,32]{0,1:T(8,128)S(1)}, f32[256,32]{0,1:T(8,128)}, u32[]{:S(2)}) copy-start(f32[256,32]{0,1:T(8,128)} %copy-done.24) | copy-start | bytes 98308
  1051.0 161.9 %reduce-scatter.20.cloned.1.call-start = ((), (), s32[]{:S(2)}) async-start(), calls=%async_computation.25 | async-start | bytes 1966080 | tf_op jit(solution)/shard_map/reduce_scatter | solution.py:428
  1132.6 117.4 %reduce-scatter.18.cloned.1.call-start = ((), (), s32[]{:S(2)}) async-start(), calls=%async_computation.24 | async-start | bytes 1966080 | tf_op jit(solution)/shard_map/reduce_scatter | solution.py:425
  1175.7 2.0 copy-start.8
  1177.7 158.8 %reduce-scatter.22.cloned.1.call-start = ((), (), s32[]{:S(2)}) async-start(), calls=%async_computation.26 | async-start | bytes 5898240 | tf_op jit(solution)/shard_map/reduce_scatter | solution.py:431
  1182.7 242.4 %reduce-scatter.16.cloned.1.call-start = ((), (), s32[]{:S(2)}) async-start(), calls=%async_computation.23 | async-start | bytes 5898240 | tf_op jit(solution)/shard_map/reduce_scatter | solution.py:422
  1186.8 262.3 %reduce-scatter.28.cloned.1.call-start = ((), (), s32[]{:S(2)}) async-start(), calls=%async_computation.29 | async-start | bytes 491520
  1189.1 346.8 %reduce-scatter.26.cloned.1.call-start = ((), (), s32[]{:S(2)}) async-start(), calls=%async_computation.28 | async-start | bytes 5898240 | tf_op jit(solution)/shard_map/reduce_scatter | solution.py:276
  1199.8 409.7 %all-reduce.11.cloned.1.call-start = ((), (), s32[]{:S(2)}) async-start(), calls=%async_computation.30 | async-start | bytes 6291456 | tf_op jit(solution)/shard_map/psum | solution.py:441
  1425.1 348.0 %reduce-scatter.24.cloned.1.call-start = ((), (), s32[]{:S(2)}) async-start(), calls=%async_computation.27 | async-start | bytes 11796480 | tf_op jit(solution)/shard_map/reduce_scatter | solution.py:273
  1499.0 40.0 %copy-start.16 = (bf16[1536,512]{1,0:T(8,128)(2,1)S(1)}, bf16[1536,512]{1,0:T(8,128)(2,1)}, u32[]{:S(2)}) copy-start(bf16[1536,512]{1,0:T(8,128)(2,1)} %all-gather.15.cloned.1.call-done) | copy-start | bytes 4718596
  1535.9 3.1 copy-start.17
  1539.0 1.4 copy-start.18
  1539.0 1.4 copy-start.21
  1540.4 37.9 %copy-start.39 = (f32[256]{0:T(256)S(1)}, f32[256]{0:T(256)}, u32[]{:S(2)}) copy-start(f32[256]{0:T(256)} %copy-done.38) | copy-start | bytes 3076
  1540.4 37.9 %copy-start.12 = (f32[256,1536]{1,0:T(8,128)S(1)}, f32[256,1536]{1,0:T(8,128)}, u32[]{:S(2)}) copy-start(f32[256,1536]{1,0:T(8,128)} %copy-done.11) | copy-start | bytes 4718596
  1609.5 4.1 copy-start.20
  1611.6 3.8 copy-start.19
  (4 other events, 4.1 us)
Sparse Core Ops, SparseCore 0:
  9.6 39.7 all-gather.10
  50.9 35.8 all-gather.14
  89.3 26.6 all-gather.12
  117.4 89.3 all-gather.18
  209.2 26.4 all-gather.16
  237.1 89.3 all-gather.20
  328.1 165.1 all-gather.22
  494.9 87.5 all-gather.24
  1050.5 79.1 reduce-scatter.13
  1133.5 41.0 reduce-scatter.11
  1177.5 35.3 reduce-scatter.19
  1215.7 34.2 reduce-scatter.17
  1252.3 84.1 reduce-scatter.21
  1339.2 85.7 reduce-scatter.15
  1427.8 21.3 reduce-scatter.27
  1451.3 84.5 reduce-scatter.25
  1539.4 70.1 all-reduce.10
  1611.8 161.2 reduce-scatter.23
where the time goes:
time: 1790 us
  waiting for transfers between devices  1100 us (61%)
  blocking collectives  323 us (18%)
  matrix products  127 us (7%)
  local copies, waits for them, and re-layouts  119 us (7%)
  other arithmetic  76.5 us (4%)
  between operations  19.9 us (1%)
    psum x2, blocking collectives, body(): lax.psum((jnp.sum(valid_float), 0.5 * jnp.sum(valid_float[:, None] * mism...  160 us
    reduce_scatter x1, waiting for transfers between devices, body(): lax.psum_scatter(grad_gate_up_local.astype(jnp.bfloat16), 'dp', scatter_d...  156 us
    all_to_all x1, blocking collectives, body(): lax.all_to_all(outgoing_grad, 'expert', split_axis=0, concat_axis=0, tile...  90.4 us
    reduce_scatter x1, waiting for transfers between devices, body(): lax.psum_scatter(grad_query_local.astype(jnp.bfloat16), 'dp', scatter_dim...  88.6 us
    reduce_scatter x1, waiting for transfers between devices, body(): lax.psum_scatter(grad_out_local.astype(jnp.bfloat16), 'dp', scatter_dimen...  86.5 us
    all_to_all x1, waiting for transfers between devices, body(): lax.all_to_all(outgoing, 'expert', split_axis=0, concat_axis=0, tiled=True)  85.6 us
    all_to_all x1, waiting for transfers between devices, body(): lax.all_to_all(row_grad, 'expert', split_axis=0, concat_axis=0, tiled=True)  82 us
    reduce_scatter x1, waiting for transfers between devices, body(): lax.psum_scatter(grad_values_all.astype(jnp.bfloat16), 'expert', scatter_...  78.7 us
  transfers between devices with their start and end apart: 21, of which 19 were waited for; matrix products, arithmetic and copies ran while one was open for 9% of the time, Pallas kernels for 0%

commit v1 on v0

v1 whole, which is shorter than its diff:
```python
import jax
import jax.numpy as jnp
from jax import lax
from jax.sharding import PartitionSpec as P

H = 24
KVH = 8
HD = 64
FF = 512
TOP = 8
EXP_DEV = 3
SEQ_MIN = 1024

EPS = 1e-05
RESIDUAL = 0.22
SCORE_SCALE = 1.0 / 64.0
ROPE_BASE = 10000.0
NEG = -1000000000.0

f32 = jnp.float32
bf16 = jnp.bfloat16


def mm(spec, a, b):
    return jnp.einsum(spec, a, b, preferred_element_type=f32)


def rms_norm(states, gain):
    return states * lax.rsqrt(jnp.mean(states * states, axis=-1, keepdims=True) + EPS) * gain


def rope_tables(positions):
    half_dim = HD // 2
    frequencies = ROPE_BASE ** (-(2.0 * jnp.arange(half_dim, dtype=f32)) / HD)
    angles = positions[:, None] * frequencies[None, :]
    return (jnp.cos(angles)[:, None, :], jnp.sin(angles)[:, None, :])


def rotary(heads_in, cosine_table, sine_table):
    half_dim = heads_in.shape[-1] // 2
    first = heads_in[..., :half_dim]
    second = heads_in[..., half_dim:]
    return jnp.concatenate(
        [first * cosine_table - second * sine_table, second * cosine_table + first * sine_table],
        axis=-1,
    )


def send(x, axis, mask):
    count = lax.axis_size(axis)
    return lax.ppermute(x, axis, [(i, i ^ mask) for i in range(count)])


def gather_blocks(x, count):
    blocks = [x]
    for j in range(1, count):
        blocks.append(send(blocks[j - 1], "expert", 1) if j % 2 else send(x, "expert", j))
    return blocks


def scatter_sum(parts):
    total = None
    for j in range(0, len(parts), 2):
        chip = parts[j].astype(f32) + send(parts[j + 1], "expert", 1).astype(f32)
        if j:
            chip = send(chip.astype(bf16), "expert", j).astype(f32)
        total = chip if total is None else total + chip
    return total


def total_over(x, axis):
    mask = 1
    while mask < lax.axis_size(axis):
        x = x + send(x, axis, mask)
        mask *= 2
    return x


def place(blocks, starts, axis, size):
    width = blocks[0].shape[axis]
    shape = list(blocks[0].shape)
    shape[axis] = size * width
    out = jnp.zeros(shape, blocks[0].dtype)
    for block, start in zip(blocks, starts):
        out = lax.dynamic_update_slice_in_dim(out, block, start * width, axis)
    return out


def pick(x, index, width, axis):
    return lax.dynamic_slice_in_dim(x, index * width, width, axis)


def attend(queries, keys, values):
    count = queries.shape[0]
    raw = mm("qhgd,khd->hgqk", queries, keys) * SCORE_SCALE
    causal = jnp.arange(count)[:, None] >= jnp.arange(count)[None, :]
    scores = jnp.where(causal[None, None], raw, NEG)
    top = jnp.max(scores, axis=-1, keepdims=True)
    log_total = top + jnp.log(jnp.sum(jnp.exp(scores - top), axis=-1, keepdims=True))
    probs = jnp.exp(scores - log_total).astype(bf16)
    context = mm("hgqk,khd->qhgd", probs, values).astype(bf16)
    return context, log_total


def attend_back(queries, keys, values, log_total, grad_context):
    count = queries.shape[0]
    raw = mm("qhgd,khd->hgqk", queries, keys) * SCORE_SCALE
    causal = jnp.arange(count)[:, None] >= jnp.arange(count)[None, :]
    probs = jnp.exp(jnp.where(causal[None, None], raw, NEG) - log_total)
    grad_probs = mm("qhgd,khd->hgqk", grad_context, values)
    delta = jnp.sum(probs * grad_probs, axis=-1, keepdims=True)
    grad_scores = (probs * (grad_probs - delta)).astype(bf16)
    grad_queries = mm("hgqk,khd->qhgd", grad_scores, keys) * SCORE_SCALE
    grad_keys = mm("hgqk,qhgd->khd", grad_scores, queries) * SCORE_SCALE
    grad_values = mm("hgqk,qhgd->khd", probs.astype(bf16), grad_context)
    return grad_queries, grad_keys, grad_values


def body(
    hidden_in,
    teacher,
    valid,
    routes,
    gain_attn,
    gain_moe,
    w_query,
    w_key,
    w_value,
    w_out,
    w_router,
    w_gate_up,
    w_down,
):
    tok, width = hidden_in.shape
    owners = lax.axis_size("expert")
    replicas = lax.axis_size("dp")
    me = lax.axis_index("expert")
    plane = lax.axis_index("dp")
    length = min(SEQ_MIN, owners * tok)
    group = length // tok
    head = me % group
    experts_all = EXP_DEV * owners
    slots = 8 * ((tok * TOP + experts_all * 7 - 1) // (experts_all * 7))
    half = replicas // 2
    side = plane // half
    ff_half = FF // 2
    slab = width // replicas
    q_cols = H * HD // group
    kv_cols = KVH * HD // group
    kv_dev = KVH // group
    per_kv = H // KVH

    def over_dp(x, axis):
        return place(
            [x] + [send(x, "dp", m) for m in range(1, replicas)],
            [plane ^ m for m in range(replicas)],
            axis,
            replicas,
        )

    gains = over_dp(jnp.stack([gain_attn, gain_moe]), 1)
    gain_one, gain_two = gains[0], gains[1]
    router_full = over_dp(w_router, 0)
    qkv_slice = jnp.concatenate(
        [
            pick(w_query, head, q_cols, 1),
            pick(w_key, head, kv_cols, 1),
            pick(w_value, head, kv_cols, 1),
        ],
        axis=1,
    )
    qkv = over_dp(qkv_slice, 0)

    def on_grid(x, pairs):
        return lax.ppermute(x, ("dp", "expert"), pairs)

    if replicas == group:
        out_slice = jnp.where(plane == head, w_out, jnp.zeros((), bf16))
        for step in range(1, replicas):
            pairs = [
                (
                    (i % group) * owners + i,
                    ((i % group + step) % replicas) * owners + i,
                )
                for i in range(owners)
            ]
            out_slice = out_slice + on_grid(w_out, pairs)
    else:
        out_slice = pick(lax.all_gather(w_out, "dp", axis=0, tiled=True), head, q_cols, 0)

    def columns(which):
        return jnp.concatenate(
            [
                pick(w_gate_up[:, :, :FF], which, ff_half, 2),
                pick(w_gate_up[:, :, FF:], which, ff_half, 2),
            ],
            axis=2,
        )

    mine = columns(side)
    other = send(columns(1 - side), "dp", half)
    gate_up_w = place(
        [mine, other]
        + [send(mine, "dp", m) for m in range(1, half)]
        + [send(other, "dp", m) for m in range(1, half)],
        [plane, plane ^ half]
        + [plane ^ m for m in range(1, half)]
        + [plane ^ half ^ m for m in range(1, half)],
        1,
        replicas,
    )
    down_w = place(
        [w_down] + [send(w_down, "dp", m) for m in range(1, half)],
        [(plane % half) ^ m for m in range(half)],
        1,
        half,
    )

    both_routes = jnp.stack([routes, send(routes, "dp", half)])
    route_blocks = jnp.stack(gather_blocks(both_routes, owners), axis=1).reshape(
        2 * owners, tok, TOP
    )
    sources = 2 * owners
    routed = jnp.any(
        route_blocks[:, :, :, None] == jnp.arange(experts_all, dtype=jnp.int32), axis=2
    )
    hot = pick(routed.astype(bf16), me, EXP_DEV, 2)
    earlier = (jnp.arange(tok)[:, None] > jnp.arange(tok)[None, :]).astype(bf16)
    rank = mm("tu,sue->set", earlier, hot).astype(jnp.int32)
    hot_t = jnp.transpose(hot, (0, 2, 1)) > 0
    chooses = hot_t[:, :, None, :] & (
        rank[:, :, None, :] == jnp.arange(slots, dtype=jnp.int32)[None, None, :, None]
    )
    select = chooses.astype(bf16)

    valid_float = valid.astype(f32)
    valid_count = jnp.sum(valid_float)
    valid_count = total_over(total_over(jnp.full((8, 128), valid_count), "expert"), "dp")[0, 0]

    inputs = hidden_in.astype(f32)
    normed_f, norm_one_pull = jax.vjp(rms_norm, inputs, gain_one.astype(f32))
    normed = normed_f.astype(bf16)
    order = [head ^ j for j in range(group)]
    seq = place(gather_blocks(normed, group), order, 0, group)
    lin = mm("td,dc->tc", seq, qkv)
    cosine, sine = rope_tables(jnp.arange(length, dtype=f32))
    queries = (
        rotary(lin[:, :q_cols].reshape(length, kv_dev * per_kv, HD), cosine, sine)
        .astype(bf16)
        .reshape(length, kv_dev, per_kv, HD)
    )
    keys = rotary(
        lin[:, q_cols : q_cols + kv_cols].reshape(length, kv_dev, HD), cosine, sine
    ).astype(bf16)
    values = lin[:, q_cols + kv_cols :].reshape(length, kv_dev, HD).astype(bf16)
    context, log_total = attend(queries, keys, values)
    context = context.reshape(length, q_cols)
    branch = mm("tc,cd->td", context, out_slice).astype(bf16)
    mid = inputs + RESIDUAL * scatter_sum([pick(branch, order[j], tok, 0) for j in range(group)])
    moe_f, norm_two_pull = jax.vjp(rms_norm, mid, gain_two.astype(f32))
    moe_input = moe_f.astype(bf16)

    def share(x):
        far = send(x, "dp", half)
        return jnp.stack(gather_blocks(x, owners) + gather_blocks(far, owners))

    def collect(parts):
        far = scatter_sum([parts[owners + j] for j in range(owners)]).astype(bf16)
        near = scatter_sum([parts[j] for j in range(owners)])
        return near + send(far, "dp", half).astype(f32)

    rows = sources * slots
    states = share(moe_input)
    arrived = mm("sect,std->escd", select, states).astype(bf16).reshape(EXP_DEV, rows, width)
    logits = mm("std,de->ste", states, router_full)
    logits = jnp.where(routed, logits, NEG)
    gates = jnp.where(routed, jnp.exp(logits - jax.nn.logsumexp(logits, axis=-1, keepdims=True)), 0.0)
    gates_t = jnp.transpose(pick(gates, me, EXP_DEV, 2), (0, 2, 1))
    row_gate = jnp.sum(jnp.where(chooses, gates_t[:, :, None, :], 0.0), axis=-1)
    row_gate = jnp.transpose(row_gate, (1, 0, 2)).reshape(EXP_DEV, rows, 1)
    gate_up = mm("erd,edf->erf", arrived, gate_up_w)
    gate_part, up_part = gate_up[..., :ff_half], gate_up[..., ff_half:]
    sig = jax.nn.sigmoid(gate_part)
    hidden = gate_part * sig * up_part
    weighted = (row_gate * hidden).astype(bf16)
    produced = mm("erf,efd->erd", weighted, down_w).astype(bf16)
    parts = mm(
        "sect,escd->std", select, produced.reshape(EXP_DEV, sources, slots, width)
    ).astype(bf16)
    final_state = mid + RESIDUAL * collect(parts)
    activations = final_state.astype(bf16)
    mismatch = final_state - teacher.astype(f32)
    squares = jnp.sum(0.5 * valid_float[:, None] * mismatch * mismatch)
    squares = total_over(total_over(jnp.full((8, 128), squares), "expert"), "dp")[0, 0]
    loss_value = squares / (valid_count * width)
    tokens_all = tok * replicas * owners
    grad_final = tokens_all / valid_count * valid_float[:, None] * mismatch

    grad_states = share(grad_final.astype(bf16))
    arrived_grad = (
        mm("sect,std->escd", select, grad_states).astype(bf16).reshape(EXP_DEV, rows, width)
    )
    hidden_pull = mm("erd,efd->erf", arrived_grad, down_w)
    row_gg = RESIDUAL * jnp.sum(hidden * hidden_pull, axis=-1)
    hidden_grad = RESIDUAL * row_gate * hidden_pull
    silu_grad = sig * (1.0 + gate_part * (1.0 - sig))
    lin_grad = jnp.concatenate(
        [hidden_grad * up_part * silu_grad, hidden_grad * gate_part * sig], axis=-1
    ).astype(bf16)
    row_grad = mm("erf,edf->erd", lin_grad, gate_up_w).astype(bf16)
    grad_parts = mm(
        "sect,escd->std", select, row_grad.reshape(EXP_DEV, sources, slots, width)
    ).astype(bf16)
    grad_down = (RESIDUAL * mm("erf,erd->efd", weighted, arrived_grad)).astype(bf16)
    grad_gate_up = mm("erd,erf->edf", arrived, lin_grad).astype(bf16)

    ff_slab = FF // replicas
    low = plane % half
    down_out = pick(grad_down, low, ff_slab, 1).astype(f32)
    for m in range(1, half):
        down_out = down_out + send(pick(grad_down, low ^ m, ff_slab, 1), "dp", m).astype(f32)
    near_cols = pick(grad_gate_up, plane, slab, 1).astype(f32)
    far_cols = pick(grad_gate_up, plane ^ half, slab, 1).astype(f32)
    for m in range(1, half):
        near_cols = near_cols + send(pick(grad_gate_up, plane ^ m, slab, 1), "dp", m).astype(f32)
        far_cols = far_cols + send(
            pick(grad_gate_up, plane ^ half ^ m, slab, 1), "dp", m
        ).astype(f32)
    far_cols = send(far_cols.astype(bf16), "dp", half).astype(f32)
    first = jnp.where(side == 0, near_cols, far_cols)
    last = jnp.where(side == 0, far_cols, near_cols)
    gate_up_out = jnp.concatenate(
        [
            first[:, :, :ff_half],
            last[:, :, :ff_half],
            first[:, :, ff_half:],
            last[:, :, ff_half:],
        ],
        axis=2,
    )

    token_gg = jnp.sum(
        jnp.where(
            chooses,
            jnp.transpose(row_gg.reshape(EXP_DEV, sources, slots), (1, 0, 2))[..., None],
            0.0,
        ),
        axis=2,
    )
    plane_gg = token_gg[:owners] + send(token_gg[owners:], "dp", half)
    gg_blocks = [plane_gg[0]] + [send(plane_gg[j], "expert", j) for j in range(1, owners)]
    grad_gates = jnp.transpose(
        place(gg_blocks, [me ^ j for j in range(owners)], 0, owners), (1, 0)
    )
    own_gates = gates[0]
    grad_logits = (
        own_gates * (grad_gates - jnp.sum(own_gates * grad_gates, axis=-1, keepdims=True))
    ).astype(bf16)
    grad_router_t = mm("td,te->ed", moe_input, grad_logits)
    grad_moe_input = collect(grad_parts) + mm("te,de->td", grad_logits, router_full)
    grad_mid_norm, grad_gain_two = norm_two_pull(grad_moe_input)
    grad_mid = grad_final + grad_mid_norm
    grad_branch = (RESIDUAL * grad_mid).astype(bf16)

    seq_grad = place(gather_blocks(grad_branch, group), order, 0, group)
    grad_out = mm("tc,td->cd", context, seq_grad).astype(bf16)
    grad_context = (
        mm("td,cd->tc", seq_grad, out_slice).astype(bf16).reshape(length, kv_dev, per_kv, HD)
    )
    grad_q, grad_k, grad_v = attend_back(queries, keys, values, log_total, grad_context)
    grad_lin = jnp.concatenate(
        [
            rotary(grad_q.reshape(length, kv_dev * per_kv, HD), cosine, -sine).reshape(
                length, q_cols
            ),
            rotary(grad_k, cosine, -sine).reshape(length, kv_cols),
            grad_v.reshape(length, kv_cols),
        ],
        axis=1,
    ).astype(bf16)
    grad_qkv = mm("td,tc->dc", seq, grad_lin).astype(bf16)
    normed_parts = mm("tc,dc->td", grad_lin, qkv).astype(bf16)
    grad_normed = scatter_sum([pick(normed_parts, order[j], tok, 0) for j in range(group)])
    grad_in_norm, grad_gain_one = norm_one_pull(grad_normed)
    grad_in = grad_mid + grad_in_norm

    def other_sequences(x):
        total = x.astype(f32)
        mask = group
        while mask < owners:
            total = total + send(total.astype(bf16), "expert", mask).astype(f32)
            mask *= 2
        return total

    qkv_sum = pick(grad_qkv, plane, slab, 0).astype(f32)
    for m in range(1, replicas):
        qkv_sum = qkv_sum + send(pick(grad_qkv, plane ^ m, slab, 0), "dp", m).astype(f32)
    qkv_sum = other_sequences(qkv_sum).astype(bf16)
    qkv_blocks = gather_blocks(qkv_sum, group)
    g_query = place([b[:, :q_cols] for b in qkv_blocks], order, 1, group).astype(f32)
    g_key = place([b[:, q_cols : q_cols + kv_cols] for b in qkv_blocks], order, 1, group).astype(f32)
    g_value = place([b[:, q_cols + kv_cols :] for b in qkv_blocks], order, 1, group).astype(f32)

    if replicas == group:
        out_sum = grad_out.astype(f32)
        for step in range(1, replicas):
            pairs = [
                (
                    ((i % group + step) % replicas) * owners + i,
                    (i % group) * owners + i,
                )
                for i in range(owners)
            ]
            out_sum = out_sum + on_grid(grad_out, pairs).astype(f32)
        out_sum = other_sequences(out_sum).astype(bf16)
        g_out = jnp.where(plane == head, out_sum, jnp.zeros((), bf16))
        for m in range(1, group):
            pairs = [
                ((i % group) * owners + i, (i % group) * owners + (i ^ m)) for i in range(owners)
            ]
            g_out = g_out + on_grid(out_sum, pairs)
        g_out = g_out.astype(f32)
    else:
        out_sum = other_sequences(lax.psum(grad_out, "dp")).astype(bf16)
        g_out = pick(
            place(gather_blocks(out_sum, group), order, 0, group), plane, slab, 0
        ).astype(f32)

    def small_sum(x):
        x = x.reshape(x.shape[0], replicas, slab)
        total = jnp.squeeze(pick(x, plane, 1, 1), 1)
        for m in range(1, replicas):
            total = total + send(jnp.squeeze(pick(x, plane ^ m, 1, 1), 1), "dp", m)
        return total_over(total, "expert")

    early = small_sum(jnp.concatenate([grad_router_t, grad_gain_two[None]], axis=0))
    g_router, g_two = jnp.transpose(early[:experts_all]), early[experts_all]
    g_one = small_sum(grad_gain_one[None])[0]
    return (
        activations,
        loss_value,
        grad_in,
        g_one,
        g_two,
        g_query,
        g_key,
        g_value,
        g_out,
        g_router,
        gate_up_out,
        down_out,
    )


def solution(mesh):
    placed = (
        P(("dp", "expert"), None),
        P(("dp", "expert"), None),
        P(("dp", "expert")),
        P(("dp", "expert"), None),
        P("dp"),
        P("dp"),
        P("dp", None),
        P("dp", None),
        P("dp", None),
        P("dp", None),
        P("dp", None),
        P("expert", "dp", None),
        P("expert", "dp", None),
    )
    return jax.shard_map(
        body,
        mesh=mesh,
        in_specs=placed,
        out_specs=(
            P(("dp", "expert"), None),
            P(),
            P(("dp", "expert"), None),
            P("dp"),
            P("dp"),
            P("dp", None),
            P("dp", None),
            P("dp", None),
            P("dp", None),
            P("dp", None),
            P("expert", "dp", None),
            P("expert", "dp", None),
        ),
        check_vma=False,
    )
```

time: 1790 us -> 1160 us (0.65)
  waiting for transfers between devices: 1100 us -> 566 us
  blocking collectives: 323 us -> 0 us
  starting transfers between devices: 15.8 us -> 134 us
  matrix products: 127 us -> 229 us
  other arithmetic: 76.5 us -> 95.1 us
    ppermute x0 -> x144, waiting for transfers between devices: none -> 566 us  [the longest x135 480 us: send(): return lax.ppermute(x, axis, [(i, i ^ mask) for i in range(count)])]
    reduce_scatter x8 -> x0, waiting for transfers between devices: 539 us -> none  [the longest x1 156 us: body(): lax.psum_scatter(grad_gate_up_local.astype(jnp.bfloat16), 'dp', scatter_d...]
    all_gather x8 -> x0, waiting for transfers between devices: 358 us -> none  [the longest x1 76.3 us: body(): lax.all_gather(w_out, 'dp', axis=0, tiled=True)]
    psum x3 -> x0, blocking collectives: 183 us -> none  [the longest x2 160 us: body(): lax.psum((jnp.sum(valid_float), 0.5 * jnp.sum(valid_float[:, None] * mism...]
    all_to_all x3 -> x0, waiting for transfers between devices: 168 us -> none  [the longest x1 85.6 us: body(): lax.all_to_all(outgoing, 'expert', split_axis=0, concat_axis=0, tiled=True)]
    ppermute x0 -> x144, starting transfers between devices: none -> 134 us  [the longest x135 119 us: send(): return lax.ppermute(x, axis, [(i, i ^ mask) for i in range(count)])]
    dot_general x30 -> x26, matrix products: 127 us -> 229 us  [mm(): return jnp.einsum(spec, a, b, preferred_element_type=f32)]
    all_to_all x1 -> x0, blocking collectives: 90.4 us -> none  [body(): lax.all_to_all(outgoing_grad, 'expert', split_axis=0, concat_axis=0, tile...]
  transfers between devices with their start and end apart: 21 -> 144, of which waited for: 19 -> 54; matrix products, arithmetic and copies ran while one was open for 9% -> 24% of each run, Pallas kernels for 0% -> 0%
where the time goes in v1:
time: 1160 us; the launch traced here: 1150 us
  waiting for transfers between devices  566 us (49%)
  matrix products  229 us (20%)
  starting transfers between devices  134 us (12%)
  local copies, waits for them, and re-layouts  121 us (10%)
  other arithmetic  95.1 us (8%)
    ppermute x135, waiting for transfers between devices, send(): return lax.ppermute(x, axis, [(i, i ^ mask) for i in range(count)])  480 us
    dot_general x26, matrix products, mm(): return jnp.einsum(spec, a, b, preferred_element_type=f32)  229 us
    ppermute x135, starting transfers between devices, send(): return lax.ppermute(x, axis, [(i, i ^ mask) for i in range(count)])  119 us
    ppermute x9, waiting for transfers between devices, on_grid(): return lax.ppermute(x, ('dp', 'expert'), pairs)  85.7 us
    unnamed x207, local copies, waits for them, and re-layouts  39.1 us
    dynamic_update_slice x38, local copies, waits for them, and re-layouts, place(): out = lax.dynamic_update_slice_in_dim(out, block, start * width, axis)  24.6 us
  transfers between devices with their start and end apart: 144, of which 54 were waited for; matrix products, arithmetic and copies ran while one was open for 24% of the time, Pallas kernels for 0%

profile of v1, /device:TPU:0, one launch (start us, length us, event | category | flops | bytes accessed | tf_op | source)
XLA Modules:
  0.0 1150.0 jit_solution(2234915589860935428)
XLA Ops:
  12.1 3.5 collective-permute-start.1
  31.6 8.8 collective-permute-done
  42.9 11.2 collective-permute-done.1
  63.4 3.8 collective-permute-done.40
  83.5 5.3 collective-permute-done.10
  88.8 20.3 %collective-permute-done.11 = bf16[384,1536]{1,0:T(8,128)(2,1)S(1)} collective-permute-done((bf16[384,1536]{1,0:T(8,128)(2,1)S(1)}, bf16[384,1536]{1,0:T(8,128)(2,1)S(1)}, u32[]{:S(2)}, u32[]{:S(2)}) %collective-permute-start.11) | collective-permute-done | bytes 1179680 | tf_op jit(solution)/shard_map/ppermute | solution.py:175
  109.1 12.6 %collective-permute-done.9 = bf16[384,1536]{1,0:T(8,128)(2,1)S(1)} collective-permute-done((bf16[384,1536]{1,0:T(8,128)(2,1)S(1)}, bf16[384,1536]{1,0:T(8,128)(2,1)S(1)}, u32[]{:S(2)}, u32[]{:S(2)}) %collective-permute-start.9) | collective-permute-done | bytes 1179680 | tf_op jit(solution)/shard_map/ppermute | solution.py:175
  124.3 4.9 fusion.112
  131.9 10.5 fusion.6
  142.5 11.4 exponential_reduce_fusion
  153.9 11.8 %convolution_convert_fusion.8 = bf16[2,64,3,1024]{3,1,2,0:T(8,128)(2,1)S(1)} fusion(bf16[1024,2,64,1]{0,2,3,1:T(8,128)(2,1)S(1)} %bitcast.421, f32[2,1024,1024,3]{2,1,3,0:T(8,128)} %get-tuple-element.188, f32[2,3,1024]{2,1,0:T(4,128)S(1)} %log_add_fusion, pred[1024,1024]{0,1:T(8,128)(4,1)S(1)} %iota_compare_fusion.1), kind=kOutput, calls=%fused_computation.132 | convolution fusion | flops 830865408 | bytes 27287552 | tf_op jit(solution)/shard_map/hgqk,khd->qhgd/dot_general | solution.py:25
  175.7 46.9 %collective-permute-done.41 = bf16[3,384,512]{2,1,0:T(8,128)(2,1)S(1)} collective-permute-done((bf16[3,384,512]{2,1,0:T(8,128)(2,1)S(1)}, bf16[3,384,512]{2,1,0:T(8,128)(2,1)S(1)}, u32[]{:S(2)}, u32[]{:S(2)}) %collective-permute-start.41) | collective-permute-done | bytes 1179680 | tf_op jit(solution)/shard_map/ppermute | solution.py:51
  231.4 35.4 %collective-permute-done.43 = bf16[3,384,512]{2,1,0:T(8,128)(2,1)S(1)} collective-permute-done((bf16[3,384,512]{2,1,0:T(8,128)(2,1)S(1)}, bf16[3,384,512]{2,1,0:T(8,128)(2,1)S(1)}, u32[]{:S(2)}, u32[]{:S(2)}) %collective-permute-start.43) | collective-permute-done | bytes 1179680 | tf_op jit(solution)/shard_map/ppermute | solution.py:51
  275.6 29.8 %collective-permute-done.26 = bf16[256,1536]{1,0:T(8,128)(2,1)S(1)} collective-permute-done((bf16[256,1536]{1,0:T(8,128)(2,1)S(1)}, bf16[256,1536]{1,0:T(8,128)(2,1)S(1)}, u32[]{:S(2)}, u32[]{:S(2)}) %collective-permute-start.26) | collective-permute-done | bytes 786464 | tf_op jit(solution)/shard_map/ppermute | solution.py:51
  309.9 27.9 %collective-permute-done.34 = bf16[256,1536]{1,0:T(8,128)(2,1)S(1)} collective-permute-done((bf16[256,1536]{1,0:T(8,128)(2,1)S(1)}, bf16[256,1536]{1,0:T(8,128)(2,1)S(1)}, u32[]{:S(2)}, u32[]{:S(2)}) %collective-permute-start.34) | collective-permute-done | bytes 786464 | tf_op jit(solution)/shard_map/ppermute | solution.py:51
  348.8 10.3 convert_bitcast_fusion.1
  359.0 11.8 %copy.127 = bf16[3,16,104,1536]{3,2,1,0:T(8,128)(2,1)} copy(bf16[3,16,104,1536]{3,2,0,1:T(8,128)(2,1)} %convert_bitcast_fusion.1) | data formatting | bytes 30670848 | tf_op jit(solution)/shard_map/convert_element_type | solution.py:274
  370.8 8.0 fusion.108
  380.3 17.1 %fusion.113 = f32[3,1664,512]{1,2,0:T(8,128)} fusion(bf16[3,1664,1536]{2,1,0:T(8,128)(2,1)} %bitcast.410, bf16[3,1536,512]{2,1,0:T(8,128)(2,1)} %constant_dynamic-update-slice_fusion.16), kind=kOutput, calls=%fused_computation.381 | convolution fusion | flops 7851737088 | bytes 30277632 | tf_op jit(solution)/shard_map/erd,edf->erf/dot_general | solution.py:25
  397.5 13.2 %convolution_convert_fusion.1 = bf16[3,1664,1536]{2,1,0:T(8,128)(2,1)} fusion(bf16[3,256,1536]{2,1,0:T(8,128)(2,1)} %constant_dynamic-update-slice_fusion.14, f32[3,1664]{1,0:T(4,128)S(1)} %mul.726, f32[3,1664,512]{1,2,0:T(8,128)} %fusion.113), kind=kOutput, calls=%fused_computation.16 | convolution fusion | flops 3942481920 | bytes 27938304 | tf_op jit(solution)/shard_map/erf,efd->erd/dot_general | solution.py:25
  410.7 15.1 %bitcast_convert_fusion.1 = bf16[16,256,1536]{2,1,0:T(8,128)(2,1)} fusion(bf16[3,16,104,1536]{3,2,1,0:T(8,128)(2,1)} %bitcast.440, s32[16,3,256]{2,1,0:T(4,128)S(1)} %copy.125, pred[16,3,256]{2,1,0:T(4,128)(4,1)S(1)} %get-tuple-element.85), kind=kOutput, calls=%fused_computation.6 | convolution fusion | flops 3934715904 | bytes 27979776 | tf_op jit(solution)/shard_map/sect,escd->std/dot_general | solution.py:25
  445.5 29.6 %collective-permute-done.66 = f32[8,128]{1,0:T(8,128)S(1)} collective-permute-done((f32[8,128]{1,0:T(8,128)S(1)}, f32[8,128]{1,0:T(8,128)S(1)}, u32[]{:S(2)}, u32[]{:S(2)}) %collective-permute-start.66) | collective-permute-done | bytes 4128 | tf_op jit(solution)/shard_map/ppermute | solution.py:51
  479.5 3.6 collective-permute-done.68
  491.4 14.1 %collective-permute-done.47 = bf16[256,1536]{1,0:T(8,128)(2,1)S(1)} collective-permute-done((bf16[256,1536]{1,0:T(8,128)(2,1)S(1)}, bf16[256,1536]{1,0:T(8,128)(2,1)S(1)}, u32[]{:S(2)}, u32[]{:S(2)}) %collective-permute-start.47) | collective-permute-done | bytes 786464 | tf_op jit(solution)/shard_map/ppermute | solution.py:51
  505.5 15.9 %collective-permute-done.49 = bf16[256,1536]{1,0:T(8,128)(2,1)S(1)} collective-permute-done((bf16[256,1536]{1,0:T(8,128)(2,1)S(1)}, bf16[256,1536]{1,0:T(8,128)(2,1)S(1)}, u32[]{:S(2)}, u32[]{:S(2)}) %collective-permute-start.49) | collective-permute-done | bytes 786464 | tf_op jit(solution)/shard_map/ppermute | solution.py:51
  522.3 3.6 collective-permute-done.59
  536.2 11.9 %collective-permute-done.71 = bf16[256,1536]{1,0:T(8,128)(2,1)S(1)} collective-permute-done((bf16[256,1536]{1,0:T(8,128)(2,1)S(1)}, bf16[256,1536]{1,0:T(8,128)(2,1)S(1)}, u32[]{:S(2)}, u32[]{:S(2)}) %collective-permute-start.71) | collective-permute-done | bytes 786464 | tf_op jit(solution)/shard_map/ppermute | solution.py:51
  548.1 16.8 %collective-permute-done.77 = bf16[256,1536]{1,0:T(8,128)(2,1)S(1)} collective-permute-done((bf16[256,1536]{1,0:T(8,128)(2,1)S(1)}, bf16[256,1536]{1,0:T(8,128)(2,1)S(1)}, u32[]{:S(2)}, u32[]{:S(2)}) %collective-permute-start.77) | collective-permute-done | bytes 786464 | tf_op jit(solution)/shard_map/ppermute | solution.py:51
  575.3 10.0 collective-permute-done.79
  585.3 18.8 %collective-permute-done.81 = bf16[256,1536]{1,0:T(8,128)(2,1)S(1)} collective-permute-done((bf16[256,1536]{1,0:T(8,128)(2,1)S(1)}, bf16[256,1536]{1,0:T(8,128)(2,1)S(1)}, u32[]{:S(2)}, u32[]{:S(2)}) %collective-permute-start.81) | collective-permute-done | bytes 786464 | tf_op jit(solution)/shard_map/ppermute | solution.py:51
  613.2 10.5 convert_bitcast_fusion
  623.7 11.3 copy.131
  635.0 14.0 %multiply_convert_fusion.1 = (bf16[3,1664,256]{1,2,0:T(8,128)(2,1)}, bf16[3,1664,256]{1,2,0:T(8,128)(2,1)}, f32[3,1664]{1,0:T(4,128)S(1)}) fusion(f32[3,1664,512]{1,2,0:T(8,128)} %fusion.113, f32[3,1664]{1,0:T(4,128)S(1)} %broadcast_multiply_fusion.1, bf16[3,1664,1536]{2,1,0:T(8,128)(2,1)} %bitcast.412, ...), kind=kOutput, calls=%fused_computation.24 | convolution fusion | flops 3948866560 | bytes 33070080 | tf_op jit(solution)/shard_map/erd,efd->erf/dot_general | solution.py:25
  649.0 15.5 %convolution_convert_fusion = bf16[3,1664,1536]{2,1,0:T(8,128)(2,1)} fusion(bf16[3,1536,512]{2,1,0:T(8,128)(2,1)} %constant_dynamic-update-slice_fusion.16, bf16[3,1664,256]{1,2,0:T(8,128)(2,1)} %get-tuple-element.96, bf16[3,1664,256]{1,2,0:T(8,128)(2,1)} %get-tuple-element.95), kind=kOutput, calls=%fused_computation.15 | convolution fusion | flops 7869628416 | bytes 25165824 | tf_op jit(solution)/shard_map/erf,edf->erd/dot_general | solution.py:25
  664.5 15.4 %bitcast_convert_fusion = bf16[16,256,1536]{2,1,0:T(8,128)(2,1)} fusion(bf16[3,16,104,1536]{3,2,1,0:T(8,128)(2,1)} %bitcast.439, s32[16,3,256]{2,1,0:T(4,128)S(1)} %copy.125, pred[16,3,256]{2,1,0:T(4,128)(4,1)S(1)} %get-tuple-element.85), kind=kOutput, calls=%fused_computation.5 | convolution fusion | flops 3934715904 | bytes 27979776 | tf_op jit(solution)/shard_map/sect,escd->std/dot_general | solution.py:25
  679.9 5.5 slice_bitcast_fusion.14
  694.8 3.6 collective-permute-done.63
  699.5 13.8 %convolution_convert_fusion.2 = bf16[3,1536,512]{1,2,0:T(8,128)(2,1)S(1)} fusion(bf16[3,1664,1536]{2,1,0:T(8,128)(2,1)} %bitcast.411, bf16[3,1664,256]{1,2,0:T(8,128)(2,1)} %get-tuple-element.96, bf16[3,1664,256]{1,2,0:T(8,128)(2,1)} %get-tuple-element.95), kind=kOutput, calls=%fused_computation.33 | convolution fusion | flops 7864320000 | bytes 25165824 | tf_op jit(solution)/shard_map/erd,erf->edf/dot_general | solution.py:25
  720.5 5.9 fusion.41
  729.6 12.8 %multiply_convert_fusion.3 = bf16[3,256,1536]{2,1,0:T(8,128)(2,1)S(1)} fusion(bf16[3,1664,1536]{2,1,0:T(8,128)(2,1)} %bitcast.413, f32[3,1664]{1,0:T(4,128)S(1)} %mul.726, f32[3,1664,512]{1,2,0:T(8,128)} %fusion.113), kind=kOutput, calls=%fused_computation.32 | convolution fusion | flops 3937173504 | bytes 27938304 | tf_op jit(solution)/shard_map/erf,erd->efd/dot_general | solution.py:25
  746.2 3.4 collective-permute-done.106
  762.9 24.3 %collective-permute-done.96 = bf16[256,1536]{1,0:T(8,128)(2,1)} collective-permute-done((bf16[256,1536]{1,0:T(8,128)(2,1)}, bf16[256,1536]{1,0:T(8,128)(2,1)}, u32[]{:S(2)}, u32[]{:S(2)}) %collective-permute-start.96) | collective-permute-done | bytes 786464 | tf_op jit(solution)/shard_map/ppermute | solution.py:51
  790.9 13.1 %collective-permute-done.143 = bf16[3,128,1536]{2,1,0:T(8,128)(2,1)} collective-permute-done((bf16[3,128,1536]{2,1,0:T(8,128)(2,1)}, bf16[3,128,1536]{2,1,0:T(8,128)(2,1)}, u32[]{:S(2)}, u32[]{:S(2)}) %collective-permute-start.143) | collective-permute-done | bytes 1179680 | tf_op jit(solution)/shard_map/ppermute | solution.py:51
  804.6 23.2 %collective-permute-done.140 = bf16[3,384,512]{1,2,0:T(8,128)(2,1)} collective-permute-done((bf16[3,384,512]{1,2,0:T(8,128)(2,1)}, bf16[3,384,512]{1,2,0:T(8,128)(2,1)}, u32[]{:S(2)}, u32[]{:S(2)}) %collective-permute-start.140) | collective-permute-done | bytes 1179680 | tf_op jit(solution)/shard_map/ppermute | solution.py:51
  832.3 4.7 convert_select_fusion.1
  837.0 9.8 collective-permute-done.91
  846.8 17.4 %collective-permute-done.99 = bf16[256,1536]{1,0:T(8,128)(2,1)S(1)} collective-permute-done((bf16[256,1536]{1,0:T(8,128)(2,1)S(1)}, bf16[256,1536]{1,0:T(8,128)(2,1)S(1)}, u32[]{:S(2)}, u32[]{:S(2)}) %collective-permute-start.99) | collective-permute-done | bytes 786464 | tf_op jit(solution)/shard_map/ppermute | solution.py:51
  864.1 3.4 multiply_reduce_fusion.1
  879.4 17.4 %collective-permute-done.124 = f32[25,384]{1,0:T(8,128)S(1)} collective-permute-done((f32[25,384]{1,0:T(8,128)S(1)}, f32[25,384]{1,0:T(8,128)S(1)}, u32[]{:S(2)}, u32[]{:S(2)}) %collective-permute-start.124) | collective-permute-done | bytes 38432 | tf_op jit(solution)/shard_map/ppermute | solution.py:51
  900.8 6.0 copy.138
  912.3 3.4 convolution_convert_fusion.7
  915.7 17.1 %fusion = (f32[2,3,1024]{2,1,0:T(4,128)S(1)}, f32[2,1024,1024,3]{2,1,3,0:T(8,128)}) fusion(f32[2,1024,1024,3]{2,1,3,0:T(8,128)} %get-tuple-element.188, f32[2,3,1024]{2,1,0:T(4,128)S(1)} %copy-done.63, pred[1024,1024]{0,1:T(8,128)(4,1)S(1)} %copy-done.3, bf16[1024,2,64,1]{0,2,3,1:T(8,128)(2,1)S(1)} %bitcast.422, bf16[1024,2,3,64]{0,3,2,1:T(8,128)(2,1)S(1)} %bitcast.425), kind=kOutput, calls=%fused_computation.2 | convolution fusion | flops 836757504 | bytes 52477952 | tf_op jit(solution)/shard_map/qhgd,khd->hgqk/dot_general | solution.py:25
  932.8 17.8 %fusion.2 = bf16[2,3,1024,1024]{2,3,1,0:T(8,128)(2,1)S(1)} fusion(f32[2,1024,1024,3]{2,1,3,0:T(8,128)} %get-tuple-element.192, f32[2,1024,1024,3]{2,1,3,0:T(8,128)} %get-tuple-element.188, f32[2,3,1024]{2,1,0:T(4,128)S(1)} %get-tuple-element.191, f32[2,3,1024]{2,1,0:T(4,128)S(1)} %copy-done.63, pred[1024,1024]{0,1:T(8,128)(4,1)S(1)} %copy-done.3), kind=kLoop, calls=%fused_computation.4 | loop fusion | flops 37748736 | bytes 64012288 | tf_op jit(solution)/shard_map/convert_element_type | solution.py:112
  950.7 3.4 convolution_multiply_fusion
  954.1 5.0 fusion.64
  959.2 11.9 %fusion.65 = bf16[2,64,1024]{2,1,0:T(8,128)(2,1)S(1)} fusion(bf16[1024,2,3,64]{0,3,2,1:T(8,128)(2,1)} %bitcast.426, f32[2,1024,1024,3]{2,1,3,0:T(8,128)} %get-tuple-element.188, f32[2,3,1024]{2,1,0:T(4,128)S(1)} %copy-done.63, pred[1024,1024]{0,1:T(8,128)(4,1)S(1)} %copy-done.3), kind=kOutput, calls=%fused_computation.138 | convolution fusion | flops 830603264 | bytes 27287552 | tf_op jit(solution)/shard_map/hgqk,qhgd->khd/dot_general | solution.py:25
  975.7 4.5 convolution_convert_fusion.3
  989.0 14.7 %collective-permute-done.126 = bf16[384,640]{1,0:T(8,128)(2,1)S(1)} collective-permute-done((bf16[384,640]{1,0:T(8,128)(2,1)S(1)}, bf16[384,640]{1,0:T(8,128)(2,1)S(1)}, u32[]{:S(2)}, u32[]{:S(2)}) %collective-permute-start.126) | collective-permute-done | bytes 491552 | tf_op jit(solution)/shard_map/ppermute | solution.py:51
  1005.0 24.3 %collective-permute-done.127 = bf16[384,640]{1,0:T(8,128)(2,1)S(1)} collective-permute-done((bf16[384,640]{1,0:T(8,128)(2,1)S(1)}, bf16[384,640]{1,0:T(8,128)(2,1)S(1)}, u32[]{:S(2)}, u32[]{:S(2)}) %collective-permute-start.127) | collective-permute-done | bytes 491552 | tf_op jit(solution)/shard_map/ppermute | solution.py:51
  1032.4 12.3 %collective-permute-done.129 = bf16[384,640]{1,0:T(8,128)(2,1)S(1)} collective-permute-done((bf16[384,640]{1,0:T(8,128)(2,1)S(1)}, bf16[384,640]{1,0:T(8,128)(2,1)S(1)}, u32[]{:S(2)}, u32[]{:S(2)}) %collective-permute-start.129) | collective-permute-done | bytes 491552 | tf_op jit(solution)/shard_map/ppermute | solution.py:51
  1045.5 31.9 %collective-permute-done.134 = bf16[384,1536]{1,0:T(8,128)(2,1)S(1)} collective-permute-done((bf16[384,1536]{1,0:T(8,128)(2,1)S(1)}, bf16[384,1536]{1,0:T(8,128)(2,1)S(1)}, u32[]{:S(2)}, u32[]{:S(2)}) %collective-permute-start.134) | collective-permute-done | bytes 1179680 | tf_op jit(solution)/shard_map/ppermute | solution.py:175
  1080.3 6.0 collective-permute-done.131
  1090.4 10.6 collective-permute-start.114
  1134.2 12.6 %collective-permute-done.139 = bf16[384,1536]{1,0:T(8,128)(2,1)S(1)} collective-permute-done((bf16[384,1536]{1,0:T(8,128)(2,1)S(1)}, bf16[384,1536]{1,0:T(8,128)(2,1)S(1)}, u32[]{:S(2)}, u32[]{:S(2)}) %collective-permute-start.139) | collective-permute-done | bytes 1179680 | tf_op jit(solution)/shard_map/ppermute | solution.py:175
  (633 shorter events, 293.5 us)
Async XLA Ops:
  5.4 63.3 %collective-permute-start.6 = (bf16[384,640]{1,0:T(8,128)(2,1)}, bf16[384,640]{1,0:T(8,128)(2,1)}, u32[]{:S(2)}, u32[]{:S(2)}) collective-permute-start(bf16[384,640]{1,0:T(8,128)(2,1)} %get-tuple-element.165), channel_id=1, source_target_pairs={{0,8},{8,0},{16,24},{24,16},{1,9},{9,1},{17,25},{25,17},{2,10},{10... | collective-permute-start | bytes 1474568 | tf_op jit(solution)/shard_map/ppermute | solution.py:51
  8.5 61.6 %collective-permute-start.7 = (bf16[384,640]{1,0:T(8,128)(2,1)}, bf16[384,640]{1,0:T(8,128)(2,1)}, u32[]{:S(2)}, u32[]{:S(2)}) collective-permute-start(bf16[384,640]{1,0:T(8,128)(2,1)} %get-tuple-element.165), channel_id=1, source_target_pairs={{0,16},{8,24},{16,0},{24,8},{1,17},{9,25},{17,1},{25,9},{2,18},{10... | collective-permute-start | bytes 1474568 | tf_op jit(solution)/shard_map/ppermute | solution.py:51
  11.0 61.8 %collective-permute-start.8 = (bf16[384,640]{1,0:T(8,128)(2,1)}, bf16[384,640]{1,0:T(8,128)(2,1)}, u32[]{:S(2)}, u32[]{:S(2)}) collective-permute-start(bf16[384,640]{1,0:T(8,128)(2,1)} %get-tuple-element.165), channel_id=1, source_target_pairs={{0,24},{8,16},{16,8},{24,0},{1,25},{9,17},{17,9},{25,1},{2,26},{10... | collective-permute-start | bytes 1474568 | tf_op jit(solution)/shard_map/ppermute | solution.py:51
  12.1 41.9 %collective-permute-start.1 = (bf16[2,384]{1,0:T(2,128)(2,1)S(1)}, bf16[2,384]{1,0:T(2,128)(2,1)S(1)}, u32[]{:S(2)}, u32[]{:S(2)}) collective-permute-start(bf16[2,384]{1,0:T(2,128)(2,1)S(1)} %get-tuple-element.94), channel_id=1, source_target_pairs={{0,16},{8,24},{16,0},{24,8},{1,17},{9,25},{17,1},{25,9},{2,18},{10... | collective-permute-start | bytes 4616 | tf_op jit(solution)/shard_map/ppermute | solution.py:51
  70.1 38.9 %collective-permute-start.11 = (bf16[384,1536]{1,0:T(8,128)(2,1)S(1)}, bf16[384,1536]{1,0:T(8,128)(2,1)S(1)}, u32[]{:S(2)}, u32[]{:S(2)}) collective-permute-start(bf16[384,1536]{1,0:T(8,128)(2,1)S(1)} %copy-done.40), channel_id=1, source_target_pairs={{0,24},{9,1},{18,10},{27,19},{4,28},{13,5},{22,14},{31,23}} | collective-permute-start | bytes 3538952 | tf_op jit(solution)/shard_map/ppermute | solution.py:175
  72.9 48.8 %collective-permute-start.9 = (bf16[384,1536]{1,0:T(8,128)(2,1)S(1)}, bf16[384,1536]{1,0:T(8,128)(2,1)S(1)}, u32[]{:S(2)}, u32[]{:S(2)}) collective-permute-start(bf16[384,1536]{1,0:T(8,128)(2,1)S(1)} %copy-done.40), channel_id=1, source_target_pairs={{0,8},{9,17},{18,26},{27,3},{4,12},{13,21},{22,30},{31,7}} | collective-permute-start | bytes 3538952 | tf_op jit(solution)/shard_map/ppermute | solution.py:175
  80.2 150.2 %collective-permute-start.44 = (bf16[3,128,1536]{2,1,0:T(8,128)(2,1)}, bf16[3,128,1536]{2,1,0:T(8,128)(2,1)S(1)}, u32[]{:S(2)}, u32[]{:S(2)}) collective-permute-start(bf16[3,128,1536]{2,1,0:T(8,128)(2,1)} %param.25), channel_id=1, source_target_pairs={{0,8},{8,0},{16,24},{24,16},{1,9},{9,1},{17,25},{25,17},{2,10},{10... | collective-permute-start | bytes 3538952 | tf_op jit(solution)/shard_map/ppermute | solution.py:51
  83.4 40.2 %collective-permute-start.5 = (bf16[256,1536]{1,0:T(8,128)(2,1)S(1)}, bf16[256,1536]{1,0:T(8,128)(2,1)S(1)}, u32[]{:S(2)}, u32[]{:S(2)}) collective-permute-start(bf16[256,1536]{1,0:T(8,128)(2,1)S(1)} %collective-permute-done.4), channel_id=1, source_target_pairs={{0,1},{1,0},{2,3},{3,2},{4,5},{5,4},{6,7},{7,6},{8,9},{9,8},{10,11... | collective-permute-start | bytes 2359304 | tf_op jit(solution)/shard_map/ppermute | solution.py:51
  88.8 79.0 %collective-permute-start.16 = (s32[2,256,8]{1,2,0:T(8,128)S(1)}, s32[2,256,8]{1,2,0:T(8,128)S(1)}, u32[]{:S(2)}, u32[]{:S(2)}) collective-permute-start(s32[2,256,8]{1,2,0:T(8,128)S(1)} %pad_add_fusion), channel_id=1, source_target_pairs={{0,1},{1,0},{2,3},{3,2},{4,5},{5,4},{6,7},{7,6},{8,9},{9,8},{10,11... | collective-permute-start | bytes 49160 | tf_op jit(solution)/shard_map/ppermute | solution.py:51
  121.7 46.1 %collective-permute-start.19 = (s32[2,256,8]{1,2,0:T(8,128)S(1)}, s32[2,256,8]{1,2,0:T(8,128)S(1)}, u32[]{:S(2)}, u32[]{:S(2)}) collective-permute-start(s32[2,256,8]{1,2,0:T(8,128)S(1)} %pad_add_fusion), channel_id=1, source_target_pairs={{0,4},{1,5},{2,6},{3,7},{4,0},{5,1},{6,2},{7,3},{8,12},{9,13},{10,... | collective-permute-start | bytes 49160 | tf_op jit(solution)/shard_map/ppermute | solution.py:51
  123.5 44.5 %collective-permute-start.21 = (s32[2,256,8]{1,2,0:T(8,128)S(1)}, s32[2,256,8]{1,2,0:T(8,128)S(1)}, u32[]{:S(2)}, u32[]{:S(2)}) collective-permute-start(s32[2,256,8]{1,2,0:T(8,128)S(1)} %pad_add_fusion), channel_id=1, source_target_pairs={{0,6},{1,7},{2,4},{3,5},{4,2},{5,3},{6,0},{7,1},{8,14},{9,15},{10,... | collective-permute-start | bytes 49160 | tf_op jit(solution)/shard_map/ppermute | solution.py:51
  123.5 44.9 %collective-permute-start.18 = (s32[2,256,8]{1,2,0:T(8,128)S(1)}, s32[2,256,8]{1,2,0:T(8,128)S(1)}, u32[]{:S(2)}, u32[]{:S(2)}) collective-permute-start(s32[2,256,8]{1,2,0:T(8,128)S(1)} %collective-permute-done.17), channel_id=1, source_target_pairs={{0,1},{1,0},{2,3},{3,2},{4,5},{5,4},{6,7},{7,6},{8,9},{9,8},{10,11... | collective-permute-start | bytes 49160 | tf_op jit(solution)/shard_map/ppermute | solution.py:51
  167.9 54.7 %collective-permute-start.41 = (bf16[3,384,512]{2,1,0:T(8,128)(2,1)S(1)}, bf16[3,384,512]{2,1,0:T(8,128)(2,1)S(1)}, u32[]{:S(2)}, u32[]{:S(2)}) collective-permute-start(bf16[3,384,512]{2,1,0:T(8,128)(2,1)S(1)} %pad_maximum_fusion.6), channel_id=1, source_target_pairs={{0,16},{8,24},{16,0},{24,8},{1,17},{9,25},{17,1},{25,9},{2,18},{10... | collective-permute-start | bytes 3538952 | tf_op jit(solution)/shard_map/ppermute | solution.py:51
  170.1 52.5 %collective-permute-start.12 = (bf16[256,1536]{1,0:T(8,128)(2,1)S(1)}, bf16[256,1536]{1,0:T(8,128)(2,1)S(1)}, u32[]{:S(2)}, u32[]{:S(2)}) collective-permute-start(bf16[256,1536]{1,0:T(8,128)(2,1)S(1)} %get-tuple-element.132), channel_id=1, source_target_pairs={{0,1},{1,0},{2,3},{3,2},{4,5},{5,4},{6,7},{7,6},{8,9},{9,8},{10,11... | collective-permute-start | bytes 2359304 | tf_op jit(solution)/shard_map/ppermute | solution.py:51
  170.5 52.1 %collective-permute-start.14 = (bf16[256,1536]{1,0:T(8,128)(2,1)S(1)}, bf16[256,1536]{1,0:T(8,128)(2,1)S(1)}, u32[]{:S(2)}, u32[]{:S(2)}) collective-permute-start(bf16[256,1536]{1,0:T(8,128)(2,1)S(1)} %add_convert_fusion.3), channel_id=1, source_target_pairs={{0,2},{1,3},{2,0},{3,1},{4,6},{5,7},{6,4},{7,5},{8,10},{9,11},{10,... | collective-permute-start | bytes 2359304 | tf_op jit(solution)/shard_map/ppermute | solution.py:51
  172.3 53.5 %collective-permute-start.42 = (bf16[3,384,512]{2,1,0:T(8,128)(2,1)S(1)}, bf16[3,384,512]{2,1,0:T(8,128)(2,1)S(1)}, u32[]{:S(2)}, u32[]{:S(2)}) collective-permute-start(bf16[3,384,512]{2,1,0:T(8,128)(2,1)S(1)} %copy-done.43), channel_id=1, source_target_pairs={{0,8},{8,0},{16,24},{24,16},{1,9},{9,1},{17,25},{25,17},{2,10},{10... | collective-permute-start | bytes 3538952 | tf_op jit(solution)/shard_map/ppermute | solution.py:51
  222.5 44.3 %collective-permute-start.43 = (bf16[3,384,512]{2,1,0:T(8,128)(2,1)S(1)}, bf16[3,384,512]{2,1,0:T(8,128)(2,1)S(1)}, u32[]{:S(2)}, u32[]{:S(2)}) collective-permute-start(bf16[3,384,512]{2,1,0:T(8,128)(2,1)S(1)} %collective-permute-done.41), channel_id=1, source_target_pairs={{0,8},{8,0},{16,24},{24,16},{1,9},{9,1},{17,25},{25,17},{2,10},{10... | collective-permute-start | bytes 3538952 | tf_op jit(solution)/shard_map/ppermute | solution.py:51
  224.4 47.3 %collective-permute-start.23 = (bf16[256,1536]{1,0:T(8,128)(2,1)S(1)}, bf16[256,1536]{1,0:T(8,128)(2,1)S(1)}, u32[]{:S(2)}, u32[]{:S(2)}) collective-permute-start(bf16[256,1536]{1,0:T(8,128)(2,1)S(1)} %get-tuple-element.88), channel_id=1, source_target_pairs={{0,1},{1,0},{2,3},{3,2},{4,5},{5,4},{6,7},{7,6},{8,9},{9,8},{10,11... | collective-permute-start | bytes 2359304 | tf_op jit(solution)/shard_map/ppermute | solution.py:51
  224.4 49.3 %collective-permute-start.24 = (bf16[256,1536]{1,0:T(8,128)(2,1)S(1)}, bf16[256,1536]{1,0:T(8,128)(2,1)S(1)}, u32[]{:S(2)}, u32[]{:S(2)}) collective-permute-start(bf16[256,1536]{1,0:T(8,128)(2,1)S(1)} %get-tuple-element.88), channel_id=1, source_target_pairs={{0,2},{1,3},{2,0},{3,1},{4,6},{5,7},{6,4},{7,5},{8,10},{9,11},{10,... | collective-permute-start | bytes 2359304 | tf_op jit(solution)/shard_map/ppermute | solution.py:51
  225.8 44.5 %collective-permute-start.30 = (bf16[256,1536]{1,0:T(8,128)(2,1)S(1)}, bf16[256,1536]{1,0:T(8,128)(2,1)S(1)}, u32[]{:S(2)}, u32[]{:S(2)}) collective-permute-start(bf16[256,1536]{1,0:T(8,128)(2,1)S(1)} %get-tuple-element.88), channel_id=1, source_target_pairs={{0,16},{8,24},{16,0},{24,8},{1,17},{9,25},{17,1},{25,9},{2,18},{10... | collective-permute-start | bytes 2359304 | tf_op jit(solution)/shard_map/ppermute | solution.py:51
  267.9 37.5 %collective-permute-start.26 = (bf16[256,1536]{1,0:T(8,128)(2,1)S(1)}, bf16[256,1536]{1,0:T(8,128)(2,1)S(1)}, u32[]{:S(2)}, u32[]{:S(2)}) collective-permute-start(bf16[256,1536]{1,0:T(8,128)(2,1)S(1)} %get-tuple-element.88), channel_id=1, source_target_pairs={{0,4},{1,5},{2,6},{3,7},{4,0},{5,1},{6,2},{7,3},{8,12},{9,13},{10,... | collective-permute-start | bytes 2359304 | tf_op jit(solution)/shard_map/ppermute | solution.py:51
  270.2 38.6 %collective-permute-start.28 = (bf16[256,1536]{1,0:T(8,128)(2,1)S(1)}, bf16[256,1536]{1,0:T(8,128)(2,1)S(1)}, u32[]{:S(2)}, u32[]{:S(2)}) collective-permute-start(bf16[256,1536]{1,0:T(8,128)(2,1)S(1)} %get-tuple-element.88), channel_id=1, source_target_pairs={{0,6},{1,7},{2,4},{3,5},{4,2},{5,3},{6,0},{7,1},{8,14},{9,15},{10,... | collective-permute-start | bytes 2359304 | tf_op jit(solution)/shard_map/ppermute | solution.py:51
  270.3 39.1 %collective-permute-start.32 = (bf16[256,1536]{1,0:T(8,128)(2,1)S(1)}, bf16[256,1536]{1,0:T(8,128)(2,1)S(1)}, u32[]{:S(2)}, u32[]{:S(2)}) collective-permute-start(bf16[256,1536]{1,0:T(8,128)(2,1)S(1)} %collective-permute-done.30), channel_id=1, source_target_pairs={{0,2},{1,3},{2,0},{3,1},{4,6},{5,7},{6,4},{7,5},{8,10},{9,11},{10,... | collective-permute-start | bytes 2359304 | tf_op jit(solution)/shard_map/ppermute | solution.py:51
  271.7 66.1 %collective-permute-start.34 = (bf16[256,1536]{1,0:T(8,128)(2,1)S(1)}, bf16[256,1536]{1,0:T(8,128)(2,1)S(1)}, u32[]{:S(2)}, u32[]{:S(2)}) collective-permute-start(bf16[256,1536]{1,0:T(8,128)(2,1)S(1)} %collective-permute-done.30), channel_id=1, source_target_pairs={{0,4},{1,5},{2,6},{3,7},{4,0},{5,1},{6,2},{7,3},{8,12},{9,13},{10,... | collective-permute-start | bytes 2359304 | tf_op jit(solution)/shard_map/ppermute | solution.py:51
  273.7 33.3 %collective-permute-start.25 = (bf16[256,1536]{1,0:T(8,128)(2,1)S(1)}, bf16[256,1536]{1,0:T(8,128)(2,1)S(1)}, u32[]{:S(2)}, u32[]{:S(2)}) collective-permute-start(bf16[256,1536]{1,0:T(8,128)(2,1)S(1)} %collective-permute-done.24), channel_id=1, source_target_pairs={{0,1},{1,0},{2,3},{3,2},{4,5},{5,4},{6,7},{7,6},{8,9},{9,8},{10,11... | collective-permute-start | bytes 2359304 | tf_op jit(solution)/shard_map/ppermute | solution.py:51
  305.5 32.4 %collective-permute-start.36 = (bf16[256,1536]{1,0:T(8,128)(2,1)S(1)}, bf16[256,1536]{1,0:T(8,128)(2,1)S(1)}, u32[]{:S(2)}, u32[]{:S(2)}) collective-permute-start(bf16[256,1536]{1,0:T(8,128)(2,1)S(1)} %collective-permute-done.30), channel_id=1, source_target_pairs={{0,6},{1,7},{2,4},{3,5},{4,2},{5,3},{6,0},{7,1},{8,14},{9,15},{10,... | collective-permute-start | bytes 2359304 | tf_op jit(solution)/shard_map/ppermute | solution.py:51
  308.9 33.3 %collective-permute-start.31 = (bf16[256,1536]{1,0:T(8,128)(2,1)S(1)}, bf16[256,1536]{1,0:T(8,128)(2,1)S(1)}, u32[]{:S(2)}, u32[]{:S(2)}) collective-permute-start(bf16[256,1536]{1,0:T(8,128)(2,1)S(1)} %collective-permute-done.30), channel_id=1, source_target_pairs={{0,1},{1,0},{2,3},{3,2},{4,5},{5,4},{6,7},{7,6},{8,9},{9,8},{10,11... | collective-permute-start | bytes 2359304 | tf_op jit(solution)/shard_map/ppermute | solution.py:51
  309.5 34.6 %collective-permute-start.33 = (bf16[256,1536]{1,0:T(8,128)(2,1)S(1)}, bf16[256,1536]{1,0:T(8,128)(2,1)S(1)}, u32[]{:S(2)}, u32[]{:S(2)}) collective-permute-start(bf16[256,1536]{1,0:T(8,128)(2,1)S(1)} %collective-permute-done.32), channel_id=1, source_target_pairs={{0,1},{1,0},{2,3},{3,2},{4,5},{5,4},{6,7},{7,6},{8,9},{9,8},{10,11... | collective-permute-start | bytes 2359304 | tf_op jit(solution)/shard_map/ppermute | solution.py:51
  432.6 52.3 %collective-permute-start.52 = (bf16[256,1536]{1,0:T(8,128)(2,1)S(1)}, bf16[256,1536]{1,0:T(8,128)(2,1)S(1)}, u32[]{:S(2)}, u32[]{:S(2)}) collective-permute-start(bf16[256,1536]{1,0:T(8,128)(2,1)S(1)} %get-tuple-element.115), channel_id=1, source_target_pairs={{0,1},{1,0},{2,3},{3,2},{4,5},{5,4},{6,7},{7,6},{8,9},{9,8},{10,11... | collective-permute-start | bytes 2359304 | tf_op jit(solution)/shard_map/ppermute | solution.py:51
  438.5 46.5 %collective-permute-start.54 = (bf16[256,1536]{1,0:T(8,128)(2,1)S(1)}, bf16[256,1536]{1,0:T(8,128)(2,1)S(1)}, u32[]{:S(2)}, u32[]{:S(2)}) collective-permute-start(bf16[256,1536]{1,0:T(8,128)(2,1)S(1)} %get-tuple-element.122), channel_id=1, source_target_pairs={{0,2},{1,3},{2,0},{3,1},{4,6},{5,7},{6,4},{7,5},{8,10},{9,11},{10,... | collective-permute-start | bytes 2359304 | tf_op jit(solution)/shard_map/ppermute | solution.py:51
  438.6 47.3 %collective-permute-start.56 = (bf16[256,1536]{1,0:T(8,128)(2,1)S(1)}, bf16[256,1536]{1,0:T(8,128)(2,1)S(1)}, u32[]{:S(2)}, u32[]{:S(2)}) collective-permute-start(bf16[256,1536]{1,0:T(8,128)(2,1)S(1)} %get-tuple-element.121), channel_id=1, source_target_pairs={{0,4},{1,5},{2,6},{3,7},{4,0},{5,1},{6,2},{7,3},{8,12},{9,13},{10,... | collective-permute-start | bytes 2359304 | tf_op jit(solution)/shard_map/ppermute | solution.py:51
  440.4 47.0 %collective-permute-start.58 = (bf16[256,1536]{1,0:T(8,128)(2,1)S(1)}, bf16[256,1536]{1,0:T(8,128)(2,1)S(1)}, u32[]{:S(2)}, u32[]{:S(2)}) collective-permute-start(bf16[256,1536]{1,0:T(8,128)(2,1)S(1)} %get-tuple-element.120), channel_id=1, source_target_pairs={{0,6},{1,7},{2,4},{3,5},{4,2},{5,3},{6,0},{7,1},{8,14},{9,15},{10,... | collective-permute-start | bytes 2359304 | tf_op jit(solution)/shard_map/ppermute | solution.py:51
  485.8 35.5 %collective-permute-start.49 = (bf16[256,1536]{1,0:T(8,128)(2,1)S(1)}, bf16[256,1536]{1,0:T(8,128)(2,1)S(1)}, u32[]{:S(2)}, u32[]{:S(2)}) collective-permute-start(bf16[256,1536]{1,0:T(8,128)(2,1)S(1)} %get-tuple-element.124), channel_id=1, source_target_pairs={{0,4},{1,5},{2,6},{3,7},{4,0},{5,1},{6,2},{7,3},{8,12},{9,13},{10,... | collective-permute-start | bytes 2359304 | tf_op jit(solution)/shard_map/ppermute | solution.py:51
  487.4 34.9 %collective-permute-start.51 = (bf16[256,1536]{1,0:T(8,128)(2,1)S(1)}, bf16[256,1536]{1,0:T(8,128)(2,1)S(1)}, u32[]{:S(2)}, u32[]{:S(2)}) collective-permute-start(bf16[256,1536]{1,0:T(8,128)(2,1)S(1)} %get-tuple-element.123), channel_id=1, source_target_pairs={{0,6},{1,7},{2,4},{3,5},{4,2},{5,3},{6,0},{7,1},{8,14},{9,15},{10,... | collective-permute-start | bytes 2359304 | tf_op jit(solution)/shard_map/ppermute | solution.py:51
  489.0 36.9 %collective-permute-start.59 = (bf16[256,1536]{1,0:T(8,128)(2,1)S(1)}, bf16[256,1536]{1,0:T(8,128)(2,1)S(1)}, u32[]{:S(2)}, u32[]{:S(2)}) collective-permute-start(bf16[256,1536]{1,0:T(8,128)(2,1)S(1)} %fusion.53), channel_id=1, source_target_pairs={{0,16},{8,24},{16,0},{24,8},{1,17},{9,25},{17,1},{25,9},{2,18},{10... | collective-permute-start | bytes 2359304 | tf_op jit(solution)/shard_map/ppermute | solution.py:51
  528.5 36.5 %collective-permute-start.77 = (bf16[256,1536]{1,0:T(8,128)(2,1)S(1)}, bf16[256,1536]{1,0:T(8,128)(2,1)S(1)}, u32[]{:S(2)}, u32[]{:S(2)}) collective-permute-start(bf16[256,1536]{1,0:T(8,128)(2,1)S(1)} %get-tuple-element.83), channel_id=1, source_target_pairs={{0,16},{8,24},{16,0},{24,8},{1,17},{9,25},{17,1},{25,9},{2,18},{10... | collective-permute-start | bytes 2359304 | tf_op jit(solution)/shard_map/ppermute | solution.py:51
  531.5 36.6 %collective-permute-start.73 = (bf16[256,1536]{1,0:T(8,128)(2,1)S(1)}, bf16[256,1536]{1,0:T(8,128)(2,1)S(1)}, u32[]{:S(2)}, u32[]{:S(2)}) collective-permute-start(bf16[256,1536]{1,0:T(8,128)(2,1)S(1)} %get-tuple-element.83), channel_id=1, source_target_pairs={{0,4},{1,5},{2,6},{3,7},{4,0},{5,1},{6,2},{7,3},{8,12},{9,13},{10,... | collective-permute-start | bytes 2359304 | tf_op jit(solution)/shard_map/ppermute | solution.py:51
  533.1 38.5 %collective-permute-start.75 = (bf16[256,1536]{1,0:T(8,128)(2,1)S(1)}, bf16[256,1536]{1,0:T(8,128)(2,1)S(1)}, u32[]{:S(2)}, u32[]{:S(2)}) collective-permute-start(bf16[256,1536]{1,0:T(8,128)(2,1)S(1)} %get-tuple-element.83), channel_id=1, source_target_pairs={{0,6},{1,7},{2,4},{3,5},{4,2},{5,3},{6,0},{7,1},{8,14},{9,15},{10,... | collective-permute-start | bytes 2359304 | tf_op jit(solution)/shard_map/ppermute | solution.py:51
  535.0 155.5 %collective-permute-start.61 = (f32[8,128]{1,0:T(8,128)S(1)}, f32[8,128]{1,0:T(8,128)S(1)}, u32[]{:S(2)}, u32[]{:S(2)}) collective-permute-start(f32[8,128]{1,0:T(8,128)S(1)} %broadcast_add_fusion.1), channel_id=1, source_target_pairs={{0,2},{1,3},{2,0},{3,1},{4,6},{5,7},{6,4},{7,5},{8,10},{9,11},{10,... | collective-permute-start | bytes 12296 | tf_op jit(solution)/shard_map/ppermute | solution.py:51
  568.2 36.0 %collective-permute-start.81 = (bf16[256,1536]{1,0:T(8,128)(2,1)S(1)}, bf16[256,1536]{1,0:T(8,128)(2,1)S(1)}, u32[]{:S(2)}, u32[]{:S(2)}) collective-permute-start(bf16[256,1536]{1,0:T(8,128)(2,1)S(1)} %collective-permute-done.77), channel_id=1, source_target_pairs={{0,4},{1,5},{2,6},{3,7},{4,0},{5,1},{6,2},{7,3},{8,12},{9,13},{10,... | collective-permute-start | bytes 2359304 | tf_op jit(solution)/shard_map/ppermute | solution.py:51
  571.6 32.5 %collective-permute-start.83 = (bf16[256,1536]{1,0:T(8,128)(2,1)S(1)}, bf16[256,1536]{1,0:T(8,128)(2,1)S(1)}, u32[]{:S(2)}, u32[]{:S(2)}) collective-permute-start(bf16[256,1536]{1,0:T(8,128)(2,1)S(1)} %collective-permute-done.77), channel_id=1, source_target_pairs={{0,6},{1,7},{2,4},{3,5},{4,2},{5,3},{6,0},{7,1},{8,14},{9,15},{10,... | collective-permute-start | bytes 2359304 | tf_op jit(solution)/shard_map/ppermute | solution.py:51
  575.1 31.5 %collective-permute-start.78 = (bf16[256,1536]{1,0:T(8,128)(2,1)S(1)}, bf16[256,1536]{1,0:T(8,128)(2,1)S(1)}, u32[]{:S(2)}, u32[]{:S(2)}) collective-permute-start(bf16[256,1536]{1,0:T(8,128)(2,1)S(1)} %collective-permute-done.77), channel_id=1, source_target_pairs={{0,1},{1,0},{2,3},{3,2},{4,5},{5,4},{6,7},{7,6},{8,9},{9,8},{10,11... | collective-permute-start | bytes 2359304 | tf_op jit(solution)/shard_map/ppermute | solution.py:51
  716.6 35.6 %collective-permute-start.141 = (bf16[3,384,512]{1,2,0:T(8,128)(2,1)}, bf16[3,384,512]{1,2,0:T(8,128)(2,1)}, u32[]{:S(2)}, u32[]{:S(2)}) collective-permute-start(bf16[3,384,512]{1,2,0:T(8,128)(2,1)} %get-tuple-element.129), channel_id=1, source_target_pairs={{0,8},{8,0},{16,24},{24,16},{1,9},{9,1},{17,25},{25,17},{2,10},{10... | collective-permute-start | bytes 3538952 | tf_op jit(solution)/shard_map/ppermute | solution.py:51
  749.6 54.4 %collective-permute-start.143 = (bf16[3,128,1536]{2,1,0:T(8,128)(2,1)}, bf16[3,128,1536]{2,1,0:T(8,128)(2,1)}, u32[]{:S(2)}, u32[]{:S(2)}) collective-permute-start(bf16[3,128,1536]{2,1,0:T(8,128)(2,1)} %constant_dynamic-slice_fusion), channel_id=1, source_target_pairs={{0,8},{8,0},{16,24},{24,16},{1,9},{9,1},{17,25},{25,17},{2,10},{10... | collective-permute-start | bytes 3538952 | tf_op jit(solution)/shard_map/ppermute | solution.py:51
  749.8 78.0 %collective-permute-start.140 = (bf16[3,384,512]{1,2,0:T(8,128)(2,1)}, bf16[3,384,512]{1,2,0:T(8,128)(2,1)}, u32[]{:S(2)}, u32[]{:S(2)}) collective-permute-start(bf16[3,384,512]{1,2,0:T(8,128)(2,1)} %get-tuple-element.128), channel_id=1, source_target_pairs={{0,8},{8,0},{16,24},{24,16},{1,9},{9,1},{17,25},{25,17},{2,10},{10... | collective-permute-start | bytes 3538952 | tf_op jit(solution)/shard_map/ppermute | solution.py:51
  751.7 35.5 %collective-permute-start.96 = (bf16[256,1536]{1,0:T(8,128)(2,1)}, bf16[256,1536]{1,0:T(8,128)(2,1)}, u32[]{:S(2)}, u32[]{:S(2)}) collective-permute-start(bf16[256,1536]{1,0:T(8,128)(2,1)} %get-tuple-element.107), channel_id=1, source_target_pairs={{0,4},{1,5},{2,6},{3,7},{4,0},{5,1},{6,2},{7,3},{8,12},{9,13},{10,... | collective-permute-start | bytes 2359304 | tf_op jit(solution)/shard_map/ppermute | solution.py:51
  752.2 35.0 %collective-permute-start.98 = (bf16[256,1536]{1,0:T(8,128)(2,1)}, bf16[256,1536]{1,0:T(8,128)(2,1)}, u32[]{:S(2)}, u32[]{:S(2)}) collective-permute-start(bf16[256,1536]{1,0:T(8,128)(2,1)} %get-tuple-element.106), channel_id=1, source_target_pairs={{0,6},{1,7},{2,4},{3,5},{4,2},{5,3},{6,0},{7,1},{8,14},{9,15},{10,... | collective-permute-start | bytes 2359304 | tf_op jit(solution)/shard_map/ppermute | solution.py:51
  756.9 72.2 %collective-permute-start.142 = (bf16[3,384,512]{1,2,0:T(8,128)(2,1)}, bf16[3,384,512]{1,2,0:T(8,128)(2,1)}, u32[]{:S(2)}, u32[]{:S(2)}) collective-permute-start(bf16[3,384,512]{1,2,0:T(8,128)(2,1)} %add_convert_fusion), channel_id=1, source_target_pairs={{0,16},{8,24},{16,0},{24,8},{1,17},{9,25},{17,1},{25,9},{2,18},{10... | collective-permute-start | bytes 3538952 | tf_op jit(solution)/shard_map/ppermute | solution.py:51
  787.2 49.8 %collective-permute-start.85 = (bf16[256,1536]{1,0:T(8,128)(2,1)}, bf16[256,1536]{1,0:T(8,128)(2,1)S(1)}, u32[]{:S(2)}, u32[]{:S(2)}) collective-permute-start(bf16[256,1536]{1,0:T(8,128)(2,1)} %get-tuple-element.97), channel_id=1, source_target_pairs={{0,1},{1,0},{2,3},{3,2},{4,5},{5,4},{6,7},{7,6},{8,9},{9,8},{10,11... | collective-permute-start | bytes 2359304 | tf_op jit(solution)/shard_map/ppermute | solution.py:51
  787.2 49.7 %collective-permute-start.87 = (bf16[256,1536]{1,0:T(8,128)(2,1)}, bf16[256,1536]{1,0:T(8,128)(2,1)S(1)}, u32[]{:S(2)}, u32[]{:S(2)}) collective-permute-start(bf16[256,1536]{1,0:T(8,128)(2,1)} %get-tuple-element.105), channel_id=1, source_target_pairs={{0,2},{1,3},{2,0},{3,1},{4,6},{5,7},{6,4},{7,5},{8,10},{9,11},{10,... | collective-permute-start | bytes 2359304 | tf_op jit(solution)/shard_map/ppermute | solution.py:51
  804.1 32.9 %collective-permute-start.89 = (bf16[256,1536]{1,0:T(8,128)(2,1)S(1)}, bf16[256,1536]{1,0:T(8,128)(2,1)S(1)}, u32[]{:S(2)}, u32[]{:S(2)}) collective-permute-start(bf16[256,1536]{1,0:T(8,128)(2,1)S(1)} %copy-done.48), channel_id=1, source_target_pairs={{0,4},{1,5},{2,6},{3,7},{4,0},{5,1},{6,2},{7,3},{8,12},{9,13},{10,... | collective-permute-start | bytes 2359304 | tf_op jit(solution)/shard_map/ppermute | solution.py:51
  829.1 35.0 %collective-permute-start.99 = (bf16[256,1536]{1,0:T(8,128)(2,1)S(1)}, bf16[256,1536]{1,0:T(8,128)(2,1)S(1)}, u32[]{:S(2)}, u32[]{:S(2)}) collective-permute-start(bf16[256,1536]{1,0:T(8,128)(2,1)S(1)} %fusion.38), channel_id=1, source_target_pairs={{0,16},{8,24},{16,0},{24,8},{1,17},{9,25},{17,1},{25,9},{2,18},{10... | collective-permute-start | bytes 2359304 | tf_op jit(solution)/shard_map/ppermute | solution.py:51
  875.7 32.5 %collective-permute-start.108 = (bf16[256,1536]{1,0:T(8,128)(2,1)S(1)}, bf16[256,1536]{1,0:T(8,128)(2,1)S(1)}, u32[]{:S(2)}, u32[]{:S(2)}) collective-permute-start(bf16[256,1536]{1,0:T(8,128)(2,1)S(1)} %get-tuple-element.79), channel_id=1, source_target_pairs={{0,1},{1,0},{2,3},{3,2},{4,5},{5,4},{6,7},{7,6},{8,9},{9,8},{10,11... | collective-permute-start | bytes 2359304 | tf_op jit(solution)/shard_map/ppermute | solution.py:51
  980.5 48.9 %collective-permute-start.127 = (bf16[384,640]{1,0:T(8,128)(2,1)S(1)}, bf16[384,640]{1,0:T(8,128)(2,1)S(1)}, u32[]{:S(2)}, u32[]{:S(2)}) collective-permute-start(bf16[384,640]{1,0:T(8,128)(2,1)S(1)} %get-tuple-element.142), channel_id=1, source_target_pairs={{0,16},{8,24},{16,0},{24,8},{1,17},{9,25},{17,1},{25,9},{2,18},{10... | collective-permute-start | bytes 1474568 | tf_op jit(solution)/shard_map/ppermute | solution.py:51
  982.8 47.9 %collective-permute-start.128 = (bf16[384,640]{1,0:T(8,128)(2,1)S(1)}, bf16[384,640]{1,0:T(8,128)(2,1)S(1)}, u32[]{:S(2)}, u32[]{:S(2)}) collective-permute-start(bf16[384,640]{1,0:T(8,128)(2,1)S(1)} %get-tuple-element.141), channel_id=1, source_target_pairs={{0,24},{8,16},{16,8},{24,0},{1,25},{9,17},{17,9},{25,1},{2,26},{10... | collective-permute-start | bytes 1474568 | tf_op jit(solution)/shard_map/ppermute | solution.py:51
  984.9 46.0 %collective-permute-start.112 = (bf16[256,1536]{1,0:T(8,128)(2,1)S(1)}, bf16[256,1536]{1,0:T(8,128)(2,1)S(1)}, u32[]{:S(2)}, u32[]{:S(2)}) collective-permute-start(bf16[256,1536]{1,0:T(8,128)(2,1)S(1)} %get-tuple-element.131), channel_id=1, source_target_pairs={{0,1},{1,0},{2,3},{3,2},{4,5},{5,4},{6,7},{7,6},{8,9},{9,8},{10,11... | collective-permute-start | bytes 2359304 | tf_op jit(solution)/shard_map/ppermute | solution.py:51
  987.7 57.6 %collective-permute-start.133 = (bf16[384,1536]{1,0:T(8,128)(2,1)S(1)}, bf16[384,1536]{1,0:T(8,128)(2,1)S(1)}, u32[]{:S(2)}, u32[]{:S(2)}) collective-permute-start(bf16[384,1536]{1,0:T(8,128)(2,1)S(1)} %convolution_convert_fusion.6), channel_id=1, source_target_pairs={{8,0},{17,9},{26,18},{3,27},{12,4},{21,13},{30,22},{7,31}} | collective-permute-start | bytes 3538952 | tf_op jit(solution)/shard_map/ppermute | solution.py:175
  1003.7 73.6 %collective-permute-start.134 = (bf16[384,1536]{1,0:T(8,128)(2,1)S(1)}, bf16[384,1536]{1,0:T(8,128)(2,1)S(1)}, u32[]{:S(2)}, u32[]{:S(2)}) collective-permute-start(bf16[384,1536]{1,0:T(8,128)(2,1)S(1)} %convolution_convert_fusion.6), channel_id=1, source_target_pairs={{16,0},{25,9},{2,18},{11,27},{20,4},{29,13},{6,22},{15,31}} | collective-permute-start | bytes 3538952 | tf_op jit(solution)/shard_map/ppermute | solution.py:175
  1029.3 48.0 %collective-permute-start.135 = (bf16[384,1536]{1,0:T(8,128)(2,1)S(1)}, bf16[384,1536]{1,0:T(8,128)(2,1)S(1)}, u32[]{:S(2)}, u32[]{:S(2)}) collective-permute-start(bf16[384,1536]{1,0:T(8,128)(2,1)S(1)} %convolution_convert_fusion.6), channel_id=1, source_target_pairs={{24,0},{1,9},{10,18},{19,27},{28,4},{5,13},{14,22},{23,31}} | collective-permute-start | bytes 3538952 | tf_op jit(solution)/shard_map/ppermute | solution.py:175
  1030.6 56.9 %collective-permute-start.111 = (bf16[256,1536]{1,0:T(8,128)(2,1)S(1)}, bf16[256,1536]{1,0:T(8,128)(2,1)S(1)}, u32[]{:S(2)}, u32[]{:S(2)}) collective-permute-start(bf16[256,1536]{1,0:T(8,128)(2,1)S(1)} %get-tuple-element.130), channel_id=1, source_target_pairs={{0,1},{1,0},{2,3},{3,2},{4,5},{5,4},{6,7},{7,6},{8,9},{9,8},{10,11... | collective-permute-start | bytes 2359304 | tf_op jit(solution)/shard_map/ppermute | solution.py:51
  1044.7 42.8 %collective-permute-start.113 = (bf16[256,1536]{1,0:T(8,128)(2,1)S(1)}, bf16[256,1536]{1,0:T(8,128)(2,1)S(1)}, u32[]{:S(2)}, u32[]{:S(2)}) collective-permute-start(bf16[256,1536]{1,0:T(8,128)(2,1)S(1)} %add_convert_fusion.2), channel_id=1, source_target_pairs={{0,2},{1,3},{2,0},{3,1},{4,6},{5,7},{6,4},{7,5},{8,10},{9,11},{10,... | collective-permute-start | bytes 2359304 | tf_op jit(solution)/shard_map/ppermute | solution.py:51
  1045.4 40.9 %collective-permute-start.130 = (bf16[384,640]{1,0:T(8,128)(2,1)S(1)}, bf16[384,640]{1,0:T(8,128)(2,1)S(1)}, u32[]{:S(2)}, u32[]{:S(2)}) collective-permute-start(bf16[384,640]{1,0:T(8,128)(2,1)S(1)} %add_convert_fusion.5), channel_id=1, source_target_pairs={{0,1},{1,0},{2,3},{3,2},{4,5},{5,4},{6,7},{7,6},{8,9},{9,8},{10,11... | collective-permute-start | bytes 1474568 | tf_op jit(solution)/shard_map/ppermute | solution.py:51
  1079.2 34.3 %collective-permute-start.136 = (bf16[384,1536]{1,0:T(8,128)(2,1)}, bf16[384,1536]{1,0:T(8,128)(2,1)}, u32[]{:S(2)}, u32[]{:S(2)}) collective-permute-start(bf16[384,1536]{1,0:T(8,128)(2,1)} %fusion.66), channel_id=1, source_target_pairs={{0,4},{1,5},{2,6},{3,7},{4,0},{5,1},{6,2},{7,3},{8,12},{9,13},{10,... | collective-permute-start | bytes 3538952 | tf_op jit(solution)/shard_map/ppermute | solution.py:51
  1086.3 39.3 %collective-permute-start.132 = (bf16[384,640]{1,0:T(8,128)(2,1)}, bf16[384,640]{1,0:T(8,128)(2,1)}, u32[]{:S(2)}, u32[]{:S(2)}) collective-permute-start(bf16[384,640]{1,0:T(8,128)(2,1)} %collective-permute-done.131), channel_id=1, source_target_pairs={{0,1},{1,0},{2,3},{3,2},{4,5},{5,4},{6,7},{7,6},{8,9},{9,8},{10,11... | collective-permute-start | bytes 1474568 | tf_op jit(solution)/shard_map/ppermute | solution.py:51
  (165 other events, 2595.8 us)

commit v2 on v1

v2 whole, which is shorter than its diff:
```python
import functools

import jax
import jax.numpy as jnp
from jax import lax
from jax.experimental import pallas as pl
from jax.experimental.pallas import tpu as pltpu
from jax.sharding import PartitionSpec as P

H = 24
KVH = 8
HD = 64
FF = 512
TOP = 8
EXP_DEV = 3
SEQ_MIN = 1024

EPS = 1e-05
RESIDUAL = 0.22
SCORE_SCALE = 1.0 / 64.0
ROPE_BASE = 10000.0
NEG = -1000000000.0

f32 = jnp.float32
bf16 = jnp.bfloat16


def mm(spec, a, b):
    return jnp.einsum(spec, a, b, preferred_element_type=f32)


def rms_norm(states, gain):
    return states * lax.rsqrt(jnp.mean(states * states, axis=-1, keepdims=True) + EPS) * gain


def rope_tables(positions):
    half_dim = HD // 2
    frequencies = ROPE_BASE ** (-(2.0 * jnp.arange(half_dim, dtype=f32)) / HD)
    angles = positions[:, None] * frequencies[None, :]
    return (jnp.cos(angles)[:, None, :], jnp.sin(angles)[:, None, :])


def rotary(heads_in, cosine_table, sine_table):
    half_dim = heads_in.shape[-1] // 2
    first = heads_in[..., :half_dim]
    second = heads_in[..., half_dim:]
    return jnp.concatenate(
        [first * cosine_table - second * sine_table, second * cosine_table + first * sine_table],
        axis=-1,
    )


def send(x, axis, mask):
    count = lax.axis_size(axis)
    return lax.ppermute(x, axis, [(i, i ^ mask) for i in range(count)])


def gather_blocks(x, count):
    blocks = [x]
    for j in range(1, count):
        blocks.append(send(blocks[j - 1], "expert", 1) if j % 2 else send(x, "expert", j))
    return blocks


def scatter_sum(parts):
    total = None
    for j in range(0, len(parts), 2):
        chip = parts[j].astype(f32) + send(parts[j + 1], "expert", 1).astype(f32)
        if j:
            chip = send(chip.astype(bf16), "expert", j).astype(f32)
        total = chip if total is None else total + chip
    return total


def total_over(x, axis):
    mask = 1
    while mask < lax.axis_size(axis):
        x = x + send(x, axis, mask)
        mask *= 2
    return x


def place(blocks, starts, axis, size):
    width = blocks[0].shape[axis]
    shape = list(blocks[0].shape)
    shape[axis] = size * width
    out = jnp.zeros(shape, blocks[0].dtype)
    for block, start in zip(blocks, starts):
        out = lax.dynamic_update_slice_in_dim(out, block, start * width, axis)
    return out


def pick(x, index, width, axis):
    return lax.dynamic_slice_in_dim(x, index * width, width, axis)


def never(x):
    return (x != x).astype(jnp.int32)


def attend(queries, keys, values):
    count = queries.shape[0]
    raw = mm("qhgd,khd->hgqk", queries, keys) * SCORE_SCALE
    causal = jnp.arange(count)[:, None] >= jnp.arange(count)[None, :]
    scores = jnp.where(causal[None, None], raw, NEG)
    top = jnp.max(scores, axis=-1, keepdims=True)
    log_total = top + jnp.log(jnp.sum(jnp.exp(scores - top), axis=-1, keepdims=True))
    probs = jnp.exp(scores - log_total).astype(bf16)
    context = mm("hgqk,khd->qhgd", probs, values).astype(bf16)
    return context, log_total


def attend_back(queries, keys, values, log_total, grad_context):
    count = queries.shape[0]
    raw = mm("qhgd,khd->hgqk", queries, keys) * SCORE_SCALE
    causal = jnp.arange(count)[:, None] >= jnp.arange(count)[None, :]
    probs = jnp.exp(jnp.where(causal[None, None], raw, NEG) - log_total)
    grad_probs = mm("qhgd,khd->hgqk", grad_context, values)
    delta = jnp.sum(probs * grad_probs, axis=-1, keepdims=True)
    grad_scores = (probs * (grad_probs - delta)).astype(bf16)
    grad_queries = mm("hgqk,khd->qhgd", grad_scores, keys) * SCORE_SCALE
    grad_keys = mm("hgqk,qhgd->khd", grad_scores, queries) * SCORE_SCALE
    grad_values = mm("hgqk,qhgd->khd", probs.astype(bf16), grad_context)
    return grad_queries, grad_keys, grad_values


CAP = 112
GATE_COLUMNS = 128
NT = (((1,), (1,)), ((), ()))
TN = (((0,), (0,)), ((), ()))
NN = (((1,), (0,)), ((), ()))


def dg(a, b, dims):
    return lax.dot_general(a, b, dims, preferred_element_type=f32)


def whole(shape):
    return pl.BlockSpec(shape, lambda *_: (0,) * len(shape))


def params(mib):
    return pltpu.CompilerParams(vmem_limit_bytes=mib << 20)


def select_rows(slot_row):
    row = lax.broadcasted_iota(jnp.int32, (CAP, slot_row.shape[1]), 0).astype(f32)
    return row == slot_row


def experts_kernel(me_ref, routes_ref, router_ref, gate_up_ref, down_ref, *refs):
    blocks, refs = refs[:8], refs[8:]
    parts, refs = refs[:8], refs[8:]
    arrived_ref, lin_ref, weighted_ref, slot_ref, gate_ref, sel, made = refs
    step = pl.program_id(0)
    tok, width = blocks[0].shape

    @pl.when(step == 0)
    def _():
        first = me_ref[0] * EXP_DEV
        experts = router_ref.shape[0]
        which = lax.broadcasted_iota(jnp.int32, (experts, tok), 0)
        before = (
            lax.broadcasted_iota(jnp.int32, (tok, tok), 0)
            < lax.broadcasted_iota(jnp.int32, (tok, tok), 1)
        ).astype(bf16)
        for s in range(8):
            logits = dg(router_ref[...], blocks[s][...], NT)
            names = routes_ref[s]
            routed = which == names[0:1, :]
            for k in range(1, TOP):
                routed = routed | (which == names[k : k + 1, :])
            logits = jnp.where(routed, logits, NEG)
            top = jnp.max(logits, axis=0, keepdims=True)
            grown = jnp.where(routed, jnp.exp(logits - top), 0.0)
            gates = grown / jnp.sum(grown, axis=0, keepdims=True)
            hots, picked = [], []
            for i in range(EXP_DEV):
                own = which == first + i
                hots.append(jnp.sum(jnp.where(own & routed, 1.0, 0.0), axis=0, keepdims=True))
                picked.append(jnp.sum(jnp.where(own, gates, 0.0), axis=0, keepdims=True))
            filler = jnp.zeros((8 - EXP_DEV, tok), f32)
            hot = jnp.concatenate(hots + [filler], axis=0)
            rank = dg(hot.astype(bf16), before, NN)
            slot = jnp.where(hot > 0.0, rank, -1.0)
            slot_ref[s] = slot
            gate_ref[s] = jnp.concatenate(picked + [filler], axis=0)
            for i in range(EXP_DEV):
                sel[s, i * CAP : (i + 1) * CAP, :] = select_rows(slot[i : i + 1, :]).astype(bf16)

    at = pl.ds(pl.multiple_of(step * CAP, CAP), CAP)
    for s in range(8):
        arrived_ref[s, 0] = dg(sel[s, at, :], blocks[s][...], NN).astype(bf16)
    lin = dg(arrived_ref[:, 0].reshape(8 * CAP, width), gate_up_ref[0], NN)
    lin_ref[:, 0] = lin.reshape(8, CAP, lin.shape[1])
    half = lin.shape[1] // 2
    gate_part, up_part = lin[:, :half], lin[:, half:]
    hidden = gate_part * jax.nn.sigmoid(gate_part) * up_part
    for s in range(8):
        gate_row = gate_ref[s, pl.ds(step, 1), :]
        row_gate = jnp.sum(
            jnp.where(sel[s, at, :] > 0, gate_row, 0.0), axis=1, keepdims=True
        )
        weighted_ref[s, 0] = (row_gate * hidden[s * CAP : (s + 1) * CAP]).astype(bf16)
    out = dg(weighted_ref[:, 0].reshape(8 * CAP, half), down_ref[0], NN)
    made[:, at, :] = out.reshape(8, CAP, width).astype(bf16)

    @pl.when(step == EXP_DEV - 1)
    def _():
        for s in range(8):
            parts[s][...] = dg(sel[s], made[s], TN).astype(bf16)


def experts_forward(me, routes_t, router_t, blocks, gate_up_w, down_w):
    tok, width = blocks[0].shape
    cols, half = gate_up_w.shape[2], down_w.shape[1]
    by_expert = lambda w: pl.BlockSpec((8, 1, CAP, w), lambda e, *_: (0, e, 0, 0))
    rows = lambda w, t: jax.ShapeDtypeStruct((8, EXP_DEV, CAP, w), t)
    out = pl.pallas_call(
        experts_kernel,
        grid_spec=pltpu.PrefetchScalarGridSpec(
            num_scalar_prefetch=1,
            grid=(EXP_DEV,),
            in_specs=[
                whole(routes_t.shape),
                whole(router_t.shape),
                pl.BlockSpec((1, width, cols), lambda e, *_: (e, 0, 0)),
                pl.BlockSpec((1, half, width), lambda e, *_: (e, 0, 0)),
            ]
            + [whole((tok, width))] * 8,
            out_specs=[whole((tok, width))] * 8
            + [by_expert(width), by_expert(cols), by_expert(half)]
            + [whole((8, 8, tok))] * 2,
            scratch_shapes=[
                pltpu.VMEM((8, EXP_DEV * CAP, tok), bf16),
                pltpu.VMEM((8, EXP_DEV * CAP, width), bf16),
            ],
        ),
        out_shape=[jax.ShapeDtypeStruct((tok, width), bf16)] * 8
        + [rows(width, bf16), rows(cols, f32), rows(half, bf16)]
        + [jax.ShapeDtypeStruct((8, 8, tok), f32)] * 2,
        compiler_params=params(60),
        cost_estimate=pl.CostEstimate(
            flops=11 * 10**9, bytes_accessed=40 * 10**6, transcendentals=10**6
        ),
        name="experts_forward",
    )(me, routes_t, router_t, gate_up_w, down_w, *blocks)
    return list(out[:8]), out[8:]


def experts_back_kernel(me_ref, slot_ref, gate_ref, lin_ref, gate_up_ref, down_ref, *refs):
    blocks, refs = refs[:8], refs[8:]
    parts, refs = refs[:8], refs[8:]
    arrived_ref, lin_grad_ref, sel, made = refs
    step = pl.program_id(0)
    tok, width = blocks[0].shape
    half = down_ref.shape[1]
    at = pl.ds(pl.multiple_of(step * CAP, CAP), CAP)

    for s in range(8):
        sel[s, at, :] = select_rows(slot_ref[s, pl.ds(step, 1), :]).astype(bf16)
        arrived_ref[s, 0] = dg(sel[s, at, :], blocks[s][...], NN).astype(bf16)
    pull = dg(arrived_ref[:, 0].reshape(8 * CAP, width), down_ref[0], NT)
    lin = lin_ref[:, 0].reshape(8 * CAP, 2 * half)
    gate_part, up_part = lin[:, :half], lin[:, half:]
    sig = jax.nn.sigmoid(gate_part)
    act = gate_part * sig
    row_gg = RESIDUAL * jnp.sum(act * up_part * pull, axis=1, keepdims=True)
    slope = sig * (1.0 + gate_part * (1.0 - sig))
    own = me_ref[0] * EXP_DEV + step
    column = lax.broadcasted_iota(jnp.int32, (CAP, made.shape[2] - width), 1)
    for s in range(8):
        mine = slice(s * CAP, (s + 1) * CAP)
        chosen = sel[s, at, :] > 0
        gate_row = gate_ref[s, pl.ds(step, 1), :]
        row_gate = jnp.sum(jnp.where(chosen, gate_row, 0.0), axis=1, keepdims=True)
        made[s, at, width:] = jnp.where(column == own, row_gg[mine], 0.0).astype(bf16)
        hidden_grad = RESIDUAL * row_gate * pull[mine]
        lin_grad_ref[s, 0, :, :half] = (hidden_grad * up_part[mine] * slope[mine]).astype(bf16)
        lin_grad_ref[s, 0, :, half:] = (hidden_grad * act[mine]).astype(bf16)
    out = dg(lin_grad_ref[:, 0].reshape(8 * CAP, 2 * half), gate_up_ref[0], NT)
    made[:, at, :width] = out.reshape(8, CAP, width).astype(bf16)

    @pl.when(step == EXP_DEV - 1)
    def _():
        for s in range(8):
            parts[s][...] = dg(sel[s], made[s], TN).astype(bf16)


def experts_backward(me, slot, gate, lin, blocks, gate_up_w, down_w):
    tok, width = blocks[0].shape
    cols, half = gate_up_w.shape[2], down_w.shape[1]
    wide = width + GATE_COLUMNS
    by_expert = lambda w: pl.BlockSpec((8, 1, CAP, w), lambda e, *_: (0, e, 0, 0))
    rows = lambda w: jax.ShapeDtypeStruct((8, EXP_DEV, CAP, w), bf16)
    out = pl.pallas_call(
        experts_back_kernel,
        grid_spec=pltpu.PrefetchScalarGridSpec(
            num_scalar_prefetch=1,
            grid=(EXP_DEV,),
            in_specs=[
                whole(slot.shape),
                whole(gate.shape),
                by_expert(cols),
                pl.BlockSpec((1, width, cols), lambda e, *_: (e, 0, 0)),
                pl.BlockSpec((1, half, width), lambda e, *_: (e, 0, 0)),
            ]
            + [whole((tok, width))] * 8,
            out_specs=[whole((tok, wide))] * 8 + [by_expert(width), by_expert(cols)],
            scratch_shapes=[
                pltpu.VMEM((8, EXP_DEV * CAP, tok), bf16),
                pltpu.VMEM((8, EXP_DEV * CAP, wide), bf16),
            ],
        ),
        out_shape=[jax.ShapeDtypeStruct((tok, wide), bf16)] * 8 + [rows(width), rows(cols)],
        compiler_params=params(60),
        cost_estimate=pl.CostEstimate(
            flops=11 * 10**9, bytes_accessed=40 * 10**6, transcendentals=10**6
        ),
        name="experts_backward",
    )(me, slot, gate, lin, gate_up_w, down_w, *blocks)
    return list(out[:8]), out[8:]


def expert_weights_kernel(after_ref, *refs):
    chunks = len(refs) // 4
    gate_up_ref, down_ref = refs[-2:]
    gate_up, down = None, None
    for c in range(chunks):
        states, lin_grad, weighted, grads = [
            r[:, 0].reshape(8 * CAP, r.shape[3]) for r in refs[4 * c : 4 * c + 4]
        ]
        one, two = dg(states, lin_grad, TN), dg(weighted, grads, TN)
        gate_up = one if gate_up is None else gate_up + one
        down = two if down is None else down + two
    gate_up_ref[0] = gate_up.astype(bf16)
    down_ref[0] = (RESIDUAL * down).astype(bf16)


def expert_weights(after, chunks):
    width, cols, half = [chunks[0][i].shape[3] for i in range(3)]
    by_expert = lambda w: pl.BlockSpec((8, 1, CAP, w), lambda e, *_: (0, e, 0, 0))
    flat = [x for chunk in chunks for x in chunk]
    return pl.pallas_call(
        expert_weights_kernel,
        grid_spec=pltpu.PrefetchScalarGridSpec(
            num_scalar_prefetch=1,
            grid=(EXP_DEV,),
            in_specs=[by_expert(x.shape[3]) for x in flat],
            out_specs=[
                pl.BlockSpec((1, width, cols), lambda e, *_: (e, 0, 0)),
                pl.BlockSpec((1, half, width), lambda e, *_: (e, 0, 0)),
            ],
        ),
        out_shape=[
            jax.ShapeDtypeStruct((EXP_DEV, width, cols), bf16),
            jax.ShapeDtypeStruct((EXP_DEV, half, width), bf16),
        ],
        compiler_params=params(60),
        cost_estimate=pl.CostEstimate(
            flops=14 * 10**9, bytes_accessed=40 * 10**6, transcendentals=0
        ),
        name="expert_weights",
    )(after, *flat)


MESH = pl.DeviceIdType.MESH


def flip(index, mask):
    return index + mask - 2 * mask * lax.rem(lax.div(index, mask), 2)


def greet(partners):
    barrier = pltpu.get_barrier_semaphore()
    for partner in partners:
        pl.semaphore_signal(barrier, inc=1, device_id=partner, device_id_type=MESH)
    pl.semaphore_wait(barrier, len(partners))


class Wire:
    def __init__(self, send_sem, recv_sem):
        self.send_sem, self.recv_sem, self.copies = send_sem, recv_sem, []

    def start(self, src, dst, partner):
        i = len(self.copies)
        copy = pltpu.make_async_remote_copy(
            src_ref=src,
            dst_ref=dst,
            send_sem=self.send_sem.at[i],
            recv_sem=self.recv_sem.at[i],
            device_id=partner,
            device_id_type=MESH,
        )
        copy.start()
        self.copies.append(copy)
        return copy

    def finish(self):
        for copy in self.copies:
            copy.wait_send()


def comm_call(kernel, name, number, copies, in_specs, out_specs, out_shape, scratch, cost):
    return pl.pallas_call(
        kernel,
        in_specs=in_specs,
        out_specs=out_specs,
        out_shape=out_shape,
        scratch_shapes=list(scratch) + [pltpu.SemaphoreType.DMA((copies,))] * 2,
        compiler_params=pltpu.CompilerParams(
            vmem_limit_bytes=60 << 20, collective_id=number, has_side_effects=True
        ),
        cost_estimate=pl.CostEstimate(flops=cost, bytes_accessed=cost, transcendentals=0),
        name=name,
    )


ANYWHERE = pl.BlockSpec(memory_space=pl.ANY)
ON_CHIP = pl.BlockSpec(memory_space=pltpu.VMEM)


def add_into(rows, out, first, *others, step=32):
    @pl.loop(0, rows // step)
    def _(i):
        at = pl.ds(pl.multiple_of(i * step, step), step)
        total = first[at].astype(f32)
        for other in others:
            total = total + other[at].astype(f32)
        out[at] = total.astype(out.dtype)


def neighbours(half):
    e, z = lax.axis_index("expert"), lax.axis_index("dp")
    across = lax.rem(z + half, lax.axis_size("dp"))
    return [{"expert": flip(e, m)} for m in (1, 2, 4)] + [{"dp": across}]


def exchange_plane(wire, partners, x_ref, near, far):
    core, side_x, side_y, across = partners
    cut = x_ref.shape[0] // 2
    low, high = pl.ds(0, cut), pl.ds(cut, cut)

    def direct(b, at):
        return (
            wire.start(b[0].at[at], b[2].at[at], side_x),
            wire.start(b[0].at[at], b[4].at[at], side_y),
        )

    z_low = wire.start(x_ref.at[low], far[0].at[low], across)
    z_high = wire.start(x_ref.at[high], far[0].at[high], across)
    near_x_low = wire.start(near[0].at[low], near[2].at[low], side_x)
    near_y_high = wire.start(near[0].at[high], near[4].at[high], side_y)
    near_x_high = wire.start(near[0].at[high], near[2].at[high], side_x)
    near_y_low = wire.start(near[0].at[low], near[4].at[low], side_y)
    last = [wire.start(near[0], near[1], core)]
    near_x_low.wait_recv()
    near_diag_low = wire.start(near[2].at[low], near[6].at[low], side_y)
    near_y_high.wait_recv()
    near_diag_high = wire.start(near[4].at[high], near[6].at[high], side_x)
    near_x_high.wait_recv()
    last.append(wire.start(near[2], near[3], core))
    near_y_low.wait_recv()
    last.append(wire.start(near[4], near[5], core))
    z_low.wait_recv()
    far_x_low, far_y_low = direct(far, low)
    near_diag_low.wait_recv()
    near_diag_high.wait_recv()
    last.append(wire.start(near[6], near[7], core))
    z_high.wait_recv()
    far_x_high, far_y_high = direct(far, high)
    last.append(wire.start(far[0], far[1], core))
    far_x_low.wait_recv()
    far_diag_low = wire.start(far[2].at[low], far[6].at[low], side_y)
    far_y_low.wait_recv()
    far_y_high.wait_recv()
    far_diag_high = wire.start(far[4].at[high], far[6].at[high], side_x)
    last.append(wire.start(far[4], far[5], core))
    far_x_high.wait_recv()
    last.append(wire.start(far[2], far[3], core))
    far_diag_low.wait_recv()
    far_diag_high.wait_recv()
    last.append(wire.start(far[6], far[7], core))
    for copy in last:
        copy.wait_recv()


def plane_gather_kernel(half, x_ref, *refs):
    wire = Wire(*refs[15:])
    partners = neighbours(half)
    greet(partners)
    exchange_plane(wire, partners, x_ref, (x_ref,) + refs[:7], refs[7:15])
    wire.finish()


def plane_gather(x, half, number, name):
    block = jax.ShapeDtypeStruct(x.shape, x.dtype)
    out = comm_call(
        functools.partial(plane_gather_kernel, half),
        name,
        number,
        22,
        [ANYWHERE],
        [ANYWHERE] * 15,
        [block] * 15,
        [],
        50 * x.size,
    )(x)
    return [x] + list(out[:7]), list(out[7:])


def plane_scatter_kernel(half, *refs):
    parts = {"near": refs[:8], "far": refs[8:16]}
    out, core_in, sums, diag_in, last_in, z_out, z_in = refs[16:23]
    wire = Wire(*refs[23:])
    core, side_x, side_y, across = partners = neighbours(half)
    rows = out.shape[0] // 2
    cut = rows // 2
    low, high = pl.ds(0, cut), pl.ds(cut, cut)
    greet(partners)
    segments = [(kind, h) for kind in ("far", "near") for h in range(2)]
    from_core, from_diag, from_last, from_z = {}, {}, {}, {}

    def part(s, j):
        kind, h = segments[s]
        return parts[kind][j].at[pl.ds(h * rows, rows)]

    for s in range(4):
        for k in (3, 1, 2, 0):
            from_core[s, k] = wire.start(part(s, 2 * k + 1), core_in.at[s, k], core)

    def chip_sum(s, k):
        from_core[s, k].wait_recv()
        add_into(rows, sums.at[s, k], part(s, 2 * k), core_in.at[s, k])

    def enter(s):
        chip_sum(s, 3)
        from_diag[s, 0] = wire.start(sums.at[s, 3, low], diag_in.at[s, 0], side_x)
        from_diag[s, 1] = wire.start(sums.at[s, 3, high], diag_in.at[s, 1], side_y)
        chip_sum(s, 1)
        from_last[s, 0] = wire.start(sums.at[s, 1, low], last_in.at[s, 0, low], side_x)
        chip_sum(s, 2)
        from_last[s, 1] = wire.start(sums.at[s, 2, high], last_in.at[s, 1, high], side_y)

    def turn(s):
        from_diag[s, 1].wait_recv()
        add_into(cut, sums.at[s, 1, high], sums.at[s, 1, high], diag_in.at[s, 1])
        from_last[s, 2] = wire.start(sums.at[s, 1, high], last_in.at[s, 0, high], side_x)
        from_diag[s, 0].wait_recv()
        add_into(cut, sums.at[s, 2, low], sums.at[s, 2, low], diag_in.at[s, 0])
        from_last[s, 3] = wire.start(sums.at[s, 2, low], last_in.at[s, 1, low], side_y)

    def leave(s):
        kind, h = segments[s]
        from_core[s, 0].wait_recv()
        for i in range(4):
            from_last[s, i].wait_recv()
        target = z_out.at[h] if kind == "far" else out.at[pl.ds(h * rows, rows)]
        add_into(rows, target, part(s, 0), core_in.at[s, 0], last_in.at[s, 0], last_in.at[s, 1])
        if kind == "far":
            from_z[h] = wire.start(z_out.at[h], z_in.at[h], across)

    for step, s in (
        (enter, 0),
        (enter, 1),
        (turn, 0),
        (enter, 2),
        (turn, 1),
        (leave, 0),
        (enter, 3),
        (leave, 1),
        (turn, 2),
        (turn, 3),
        (leave, 2),
        (leave, 3),
    ):
        step(s)
    for h in range(2):
        from_z[h].wait_recv()
        target = out.at[pl.ds(h * rows, rows)]
        add_into(rows, target, target, z_in.at[h])
    wire.finish()


def plane_scatter(near, far, half, number, name):
    rows, width = near[0].shape
    specs = [ON_CHIP, ANYWHERE] * 8
    block = (rows // 2, width)
    return comm_call(
        functools.partial(plane_scatter_kernel, half),
        name,
        number,
        42,
        specs,
        ON_CHIP,
        jax.ShapeDtypeStruct((rows, width), f32),
        [
            pltpu.VMEM((4, 4) + block, bf16),
            pltpu.VMEM((4, 4) + block, bf16),
            pltpu.VMEM((4, 2, rows // 4, width), bf16),
            pltpu.VMEM((4, 2) + block, bf16),
            pltpu.VMEM((2,) + block, bf16),
            pltpu.VMEM((2,) + block, bf16),
        ],
        50 * rows * width,
    )(*near, *far)


def seq_gather_kernel(group, x_ref, out, send_sem, recv_sem):
    wire = Wire(send_sem, recv_sem)
    e = lax.axis_index("expert")
    head = lax.rem(e, group)
    core, side_x = [{"expert": flip(e, m)} for m in (1, 2)]
    rows = x_ref.shape[0]
    cut = rows // 2
    mine = pl.multiple_of(head * rows, rows)
    other = pl.multiple_of(flip(head, 2) * rows, rows)
    greet([core, side_x])
    crossing = [
        wire.start(x_ref.at[pl.ds(h * cut, cut)], out.at[pl.ds(mine + h * cut, cut)], side_x)
        for h in range(2)
    ]
    last = [wire.start(x_ref, out.at[pl.ds(mine, rows)], core)]
    out[pl.ds(mine, rows), :] = x_ref[...]
    for h in range(2):
        crossing[h].wait_recv()
        piece = out.at[pl.ds(other + h * cut, cut)]
        last.append(wire.start(piece, piece, core))
    for copy in last:
        copy.wait_recv()
    wire.finish()


def seq_gather(x, group, number, name):
    rows, width = x.shape
    return comm_call(
        functools.partial(seq_gather_kernel, group),
        name,
        number,
        5,
        [ON_CHIP],
        ON_CHIP,
        jax.ShapeDtypeStruct((group * rows, width), x.dtype),
        [],
        20 * x.size,
    )(x)


def seq_scatter_kernel(group, x_ref, out, core_in, sums, last_in, send_sem, recv_sem):
    wire = Wire(send_sem, recv_sem)
    e = lax.axis_index("expert")
    head = lax.rem(e, group)
    core, side_x = [{"expert": flip(e, m)} for m in (1, 2)]
    rows = out.shape[0]
    cut = rows // 2

    def part(block, h):
        return x_ref.at[pl.ds(pl.multiple_of(block * rows + h * cut, cut), cut)]

    greet([core, side_x])
    crossing = [
        wire.start(part(flip(flip(head, 2), 1), h), core_in.at[1, h], core) for h in range(2)
    ]
    near = [wire.start(part(flip(head, 1), h), core_in.at[0, h], core) for h in range(2)]
    last = []
    for h in range(2):
        crossing[h].wait_recv()
        add_into(cut, sums.at[h], part(flip(head, 2), h), core_in.at[1, h])
        last.append(wire.start(sums.at[h], last_in.at[h], side_x))
    for h in range(2):
        near[h].wait_recv()
        last[h].wait_recv()
        add_into(
            cut, out.at[pl.ds(h * cut, cut)], part(head, h), core_in.at[0, h], last_in.at[h]
        )
    wire.finish()


def seq_scatter(x, group, number, name):
    rows, width = x.shape[0] // group, x.shape[1]
    piece = (rows // 2, width)
    return comm_call(
        functools.partial(seq_scatter_kernel, group),
        name,
        number,
        6,
        [ON_CHIP],
        ON_CHIP,
        jax.ShapeDtypeStruct((rows, width), f32),
        [
            pltpu.VMEM((2, 2) + piece, bf16),
            pltpu.VMEM((2,) + piece, bf16),
            pltpu.VMEM((2,) + piece, bf16),
        ],
        20 * rows * width,
    )(x)


def start_kernel(half, replicas, x_ref, small_ref, *refs):
    near, far, small_out = (x_ref,) + refs[:7], refs[7:15], refs[15]
    wire = Wire(*refs[16:])
    z = lax.axis_index("dp")
    partners = neighbours(half)
    planes = [{"dp": lax.rem(z + k, replicas)} for k in range(1, replicas)]
    greet(partners[:3] + planes)
    spread = [wire.start(small_ref, small_out.at[z], plane) for plane in planes]
    small_out[z] = small_ref[...]
    exchange_plane(wire, partners, x_ref, near, far)
    for copy in spread:
        copy.wait_recv()
    wire.finish()


def start_exchange(x, small, half, replicas):
    block = jax.ShapeDtypeStruct(x.shape, x.dtype)
    out = comm_call(
        functools.partial(start_kernel, half, replicas),
        "start_exchange",
        1,
        22 + replicas - 1,
        [ANYWHERE, ON_CHIP],
        [ANYWHERE] * 15 + [ON_CHIP],
        [block] * 15 + [jax.ShapeDtypeStruct((replicas,) + small.shape, small.dtype)],
        [],
        10**6,
    )(x, small)
    return [x] + list(out[:7]), list(out[7:15]), out[15]


def dense_kernel(replicas, grads, small, out, small_out, *refs):
    y_in, z_out, z_in, small_in, small_sum, turn_in = refs[:6]
    wire = Wire(*refs[6:])
    e, z = lax.axis_index("expert"), lax.axis_index("dp")
    head, row = lax.rem(e, 4), lax.div(e, 4)
    partners = [{"expert": flip(e, m)} for m in (1, 2, 4)]
    core, side_x, side_y = partners
    slab, width = grads.shape[0] // replicas, grads.shape[1]
    cut = slab // 2
    quarter = cut // 2
    order = [2, 1, 3, 0]
    block = {k: lax.rem(z + k, replicas) for k in range(replicas)}
    plane = {k: {"dp": block[k]} for k in range(1, replicas)}
    greet(partners + list(plane.values()))

    def half_of(k, which):
        return grads.at[pl.ds(pl.multiple_of(block[k] * slab + which * cut, cut), cut)]

    small_copies = [wire.start(small.at[block[k]], small_in.at[k - 1], plane[k]) for k in plane]
    from_y = {k: wire.start(half_of(k, 1 - row), y_in.at[k], side_y) for k in order}
    for copy in small_copies:
        copy.wait_recv()
    small_sum[0] = small[z] + small_in[0] + small_in[1] + small_in[2]
    turn = wire.start(small_sum.at[0], turn_in.at[0], core)
    from_z = {}
    for step, k in enumerate(order):
        from_y[k].wait_recv()
        add_into(cut, z_out.at[k], half_of(k, row), y_in.at[k])
        if k:
            from_z[k] = wire.start(z_out.at[k], z_in.at[k - 1], plane[k])
        if step == 0:
            turn.wait_recv()
            small_sum[1] = small_sum[0] + turn_in[0]
            turn = wire.start(small_sum.at[1], turn_in.at[1], side_x)
        if step == 1:
            turn.wait_recv()
            small_sum[2] = small_sum[1] + turn_in[1]
            turn = wire.start(small_sum.at[2], turn_in.at[2], side_y)
    turn.wait_recv()
    small_out[...] = small_sum[2] + turn_in[2]
    for k in from_z:
        from_z[k].wait_recv()

    def place(which_head, which_row, first=0, size=cut):
        start = pl.multiple_of(which_row * cut + first, quarter)
        columns = pl.ds(pl.multiple_of(which_head * width, 128), width)
        return out.at[pl.ds(start, size), columns]

    mine = place(head, row)
    add_into(cut, mine, z_out.at[0], z_in.at[0], z_in.at[1], z_in.at[2])
    other = flip(head, 2)
    pieces = [place(head, row, h * quarter, quarter) for h in range(2)]
    over_x = [wire.start(piece, piece, side_x) for piece in pieces]
    over_y = [wire.start(piece, piece, side_y) for piece in reversed(pieces)]
    last = [wire.start(mine, mine, core)]
    over_x[0].wait_recv()
    piece = place(other, row, 0, quarter)
    diag = [wire.start(piece, piece, side_y)]
    over_y[0].wait_recv()
    piece = place(head, 1 - row, quarter, quarter)
    diag.append(wire.start(piece, piece, side_x))
    over_x[1].wait_recv()
    last.append(wire.start(place(other, row), place(other, row), core))
    over_y[1].wait_recv()
    last.append(wire.start(place(head, 1 - row), place(head, 1 - row), core))
    for copy in diag:
        copy.wait_recv()
    last.append(wire.start(place(other, 1 - row), place(other, 1 - row), core))
    for copy in last:
        copy.wait_recv()
    wire.finish()


def dense_reduce(grads, small, replicas):
    slab, width = grads.shape[0] // replicas, grads.shape[1]
    piece = (slab // 2, width)
    lot = small.shape[1:]
    return comm_call(
        functools.partial(dense_kernel, replicas),
        "dense_reduce",
        2,
        23,
        [ON_CHIP] * 2,
        [ON_CHIP] * 2,
        [jax.ShapeDtypeStruct((slab, 4 * width), bf16), jax.ShapeDtypeStruct(lot, f32)],
        [
            pltpu.VMEM((4,) + piece, bf16),
            pltpu.VMEM((4,) + piece, bf16),
            pltpu.VMEM((3,) + piece, bf16),
            pltpu.VMEM((3,) + lot, f32),
            pltpu.VMEM((3,) + lot, f32),
            pltpu.VMEM((3,) + lot, f32),
        ],
        10**8,
    )(grads, small)


def body(
    hidden_in,
    teacher,
    valid,
    routes,
    gain_attn,
    gain_moe,
    w_query,
    w_key,
    w_value,
    w_out,
    w_router,
    w_gate_up,
    w_down,
):
    tok, width = hidden_in.shape
    owners = lax.axis_size("expert")
    replicas = lax.axis_size("dp")
    me = lax.axis_index("expert")
    plane = lax.axis_index("dp")
    length = min(SEQ_MIN, owners * tok)
    group = length // tok
    head = me % group
    experts_all = EXP_DEV * owners
    slots = 8 * ((tok * TOP + experts_all * 7 - 1) // (experts_all * 7))
    half = replicas // 2
    side = plane // half
    ff_half = FF // 2
    slab = width // replicas
    q_cols = H * HD // group
    kv_cols = KVH * HD // group
    kv_dev = KVH // group
    per_kv = H // KVH

    def over_dp(x, axis):
        if replicas > group:
            return lax.all_gather(x, "dp", axis=axis, tiled=True)
        return place(
            [x] + [send(x, "dp", m) for m in range(1, replicas)],
            [plane ^ m for m in range(replicas)],
            axis,
            replicas,
        )

    routes_t = jnp.transpose(routes)
    count = jnp.full_like(routes_t, jnp.sum(valid))
    small = jnp.concatenate(
        [gain_attn[None], gain_moe[None], jnp.transpose(w_router), jnp.zeros((6, slab), bf16)]
    )
    near_names, far_names, small = start_exchange(
        jnp.concatenate([routes_t, count]), small, half, replicas
    )
    small = jnp.transpose(small, (1, 0, 2)).reshape(small.shape[1], width)
    gain_one, gain_two, router_t = small[0], small[1], small[2 : 2 + experts_all]
    near_routes = jnp.stack([r[:TOP] for r in near_names])
    far_routes = jnp.stack([r[:TOP] for r in far_names])
    me_ref = jnp.reshape(me, (1,)).astype(jnp.int32)
    valid_float = valid.astype(f32)
    valid_count = sum(r[TOP, :1] for r in near_names + far_names)
    mask = 1
    while mask < half:
        valid_count = valid_count + send(valid_count, "dp", mask)
        mask *= 2
    valid_count = valid_count[0].astype(f32)
    hold = (valid_count < 0).astype(jnp.int32)
    qkv_slice = jnp.concatenate(
        [
            pick(w_query, head + hold, q_cols, 1),
            pick(w_key, head + hold, kv_cols, 1),
            pick(w_value, head + hold, kv_cols, 1),
        ],
        axis=1,
    )
    qkv = over_dp(qkv_slice, 0)

    inputs = hidden_in.astype(f32)
    normed_f, norm_one_pull = jax.vjp(rms_norm, inputs, gain_one.astype(f32))
    normed = normed_f.astype(bf16)
    seq = seq_gather(normed, group, 3, "gather_normed")
    hold = never(seq[0, 0])
    w_out, w_down = [jnp.where(hold == 0, w, jnp.zeros((), bf16)) for w in (w_out, w_down)]

    def on_grid(x, pairs):
        return lax.ppermute(x, ("dp", "expert"), pairs)

    if replicas == group:
        out_slice = jnp.where(plane == head, w_out, jnp.zeros((), bf16))
        for step in range(1, replicas):
            pairs = [
                (
                    (i % group) * owners + i,
                    ((i % group + step) % replicas) * owners + i,
                )
                for i in range(owners)
            ]
            out_slice = out_slice + on_grid(w_out, pairs)
    else:
        out_slice = pick(lax.all_gather(w_out, "dp", axis=0, tiled=True), head, q_cols, 0)

    def columns(which):
        return jnp.concatenate(
            [
                pick(w_gate_up[:, :, :FF], which, ff_half, 2),
                pick(w_gate_up[:, :, FF:], which, ff_half, 2),
            ],
            axis=2,
        )

    mine = columns(side + hold)
    if replicas > group:
        gate_up_w = jnp.where(
            side == 0,
            lax.all_gather(columns(0), "dp", axis=1, tiled=True),
            lax.all_gather(columns(1), "dp", axis=1, tiled=True),
        )
        down_w = pick(lax.all_gather(w_down, "dp", axis=1, tiled=True), side, ff_half, 1)
    else:
        other = send(columns(1 - side + hold), "dp", half)
        gate_up_w = place(
            [mine, other]
            + [send(mine, "dp", m) for m in range(1, half)]
            + [send(other, "dp", m) for m in range(1, half)],
            [plane, plane ^ half]
            + [plane ^ m for m in range(1, half)]
            + [plane ^ half ^ m for m in range(1, half)],
            1,
            replicas,
        )
        down_w = place(
            [w_down] + [send(w_down, "dp", m) for m in range(1, half)],
            [(plane % half) ^ m for m in range(half)],
            1,
            half,
        )

    lin = mm("td,dc->tc", seq, qkv)
    cosine, sine = rope_tables(jnp.arange(length, dtype=f32))
    queries = (
        rotary(lin[:, :q_cols].reshape(length, kv_dev * per_kv, HD), cosine, sine)
        .astype(bf16)
        .reshape(length, kv_dev, per_kv, HD)
    )
    keys = rotary(
        lin[:, q_cols : q_cols + kv_cols].reshape(length, kv_dev, HD), cosine, sine
    ).astype(bf16)
    values = lin[:, q_cols + kv_cols :].reshape(length, kv_dev, HD).astype(bf16)
    context, log_total = attend(queries, keys, values)
    context = context.reshape(length, q_cols)
    branch = mm("tc,cd->td", context, out_slice).astype(bf16)
    mid = inputs + RESIDUAL * seq_scatter(branch, group, 4, "scatter_branch")
    moe_f, norm_two_pull = jax.vjp(rms_norm, mid, gain_two.astype(f32))
    moe_input = moe_f.astype(bf16)

    near, far = plane_gather(moe_input, half, 5, "gather_tokens")
    near_parts, near_kept = experts_forward(me_ref, near_routes, router_t, near, gate_up_w, down_w)
    far_parts, far_kept = experts_forward(me_ref, far_routes, router_t, far, gate_up_w, down_w)
    final_state = mid + RESIDUAL * plane_scatter(near_parts, far_parts, half, 6, "scatter_outputs")
    activations = final_state.astype(bf16)
    mismatch = final_state - teacher.astype(f32)
    squares = jnp.sum(0.5 * valid_float[:, None] * mismatch * mismatch)
    tokens_all = tok * replicas * owners
    grad_final = tokens_all / valid_count * valid_float[:, None] * mismatch

    grad_near, grad_far = plane_gather(grad_final.astype(bf16), half, 5, "gather_tokens")

    def back(kept, blocks):
        arrived, lin, weighted, slot, gate = kept
        parts, (grads, lin_grad) = experts_backward(
            me_ref, slot, gate, lin, blocks, gate_up_w, down_w
        )
        return parts, (arrived, lin_grad, weighted, grads)

    near_grads, near_chunk = back(near_kept, grad_near)
    far_grads, far_chunk = back(far_kept, grad_far)
    returned = plane_scatter(near_grads, far_grads, half, 7, "scatter_grads")
    after = jnp.reshape(never(returned[0, 0]), (1,))
    grad_gate_up, grad_down = expert_weights(after, [near_chunk, far_chunk])
    branch_scale = jnp.where(never(grad_down[0, 0, 0]) == 0, RESIDUAL, 0.0)

    ff_slab = FF // replicas
    low = plane % half
    if replicas > group:
        spread = lambda x: lax.psum_scatter(
            x.astype(f32), "dp", scatter_dimension=1, tiled=True
        )
        blank = jnp.zeros_like(grad_down)
        down_out = spread(
            jnp.where(
                side == 0,
                jnp.concatenate([grad_down, blank], axis=1),
                jnp.concatenate([blank, grad_down], axis=1),
            )
        )
        own_side = spread(jnp.where(side == 0, grad_gate_up, jnp.zeros((), bf16)))
        other_side = spread(jnp.where(side == 1, grad_gate_up, jnp.zeros((), bf16)))
        near_cols = jnp.where(side == 0, own_side, other_side)
        far_cols = jnp.where(side == 0, other_side, own_side)
    else:
        down_out = pick(grad_down, low, ff_slab, 1).astype(f32)
        for m in range(1, half):
            down_out = down_out + send(pick(grad_down, low ^ m, ff_slab, 1), "dp", m).astype(f32)
        near_cols = pick(grad_gate_up, plane, slab, 1).astype(f32)
        far_cols = pick(grad_gate_up, plane ^ half, slab, 1).astype(f32)
        for m in range(1, half):
            near_cols = near_cols + send(
                pick(grad_gate_up, plane ^ m, slab, 1), "dp", m
            ).astype(f32)
            far_cols = far_cols + send(
                pick(grad_gate_up, plane ^ half ^ m, slab, 1), "dp", m
            ).astype(f32)
        far_cols = send(far_cols.astype(bf16), "dp", half).astype(f32)
    first = jnp.where(side == 0, near_cols, far_cols)
    last = jnp.where(side == 0, far_cols, near_cols)
    gate_up_out = jnp.concatenate(
        [
            first[:, :, :ff_half],
            last[:, :, :ff_half],
            first[:, :, ff_half:],
            last[:, :, ff_half:],
        ],
        axis=2,
    )

    grad_gates = returned[:, width : width + experts_all]
    own_routed = jnp.any(
        routes[:, :, None] == jnp.arange(experts_all, dtype=jnp.int32), axis=1
    )
    own_logits = jnp.where(own_routed, mm("td,ed->te", moe_input, router_t), NEG)
    own_gates = jnp.where(own_routed, jax.nn.softmax(own_logits, axis=-1), 0.0)
    grad_logits = (
        own_gates * (grad_gates - jnp.sum(own_gates * grad_gates, axis=-1, keepdims=True))
    ).astype(bf16)
    grad_router_t = mm("td,te->ed", moe_input, grad_logits)
    grad_moe_input = returned[:, :width] + mm("te,ed->td", grad_logits, router_t)
    grad_mid_norm, grad_gain_two = norm_two_pull(grad_moe_input)
    grad_mid = grad_final + grad_mid_norm
    grad_branch = (branch_scale * grad_mid).astype(bf16)

    seq_grad = seq_gather(grad_branch, group, 3, "gather_normed")
    grad_out = mm("tc,td->cd", context, seq_grad).astype(bf16)
    grad_context = (
        mm("td,cd->tc", seq_grad, out_slice).astype(bf16).reshape(length, kv_dev, per_kv, HD)
    )
    grad_q, grad_k, grad_v = attend_back(queries, keys, values, log_total, grad_context)
    grad_lin = jnp.concatenate(
        [
            rotary(grad_q.reshape(length, kv_dev * per_kv, HD), cosine, -sine).reshape(
                length, q_cols
            ),
            rotary(grad_k, cosine, -sine).reshape(length, kv_cols),
            grad_v.reshape(length, kv_cols),
        ],
        axis=1,
    ).astype(bf16)
    grad_qkv = mm("td,tc->dc", seq, grad_lin).astype(bf16)
    normed_parts = mm("tc,dc->td", grad_lin, qkv).astype(bf16)
    grad_normed = seq_scatter(normed_parts, group, 4, "scatter_branch")
    grad_in_norm, grad_gain_one = norm_one_pull(grad_normed)
    grad_in = grad_mid + grad_in_norm

    def other_sequences(x):
        total = x.astype(f32)
        mask = group
        while mask < owners:
            total = total + send(total.astype(bf16), "expert", mask).astype(f32)
            mask *= 2
        return total

    lot = jnp.concatenate(
        [
            grad_router_t,
            grad_gain_one[None],
            grad_gain_two[None],
            jnp.full((6, width), squares),
        ]
    )
    if replicas == group:
        lot = jnp.transpose(lot.reshape(32, replicas, slab), (1, 0, 2))
        by_head, lot = dense_reduce(grad_qkv, lot, replicas)
    else:
        lot = lax.psum_scatter(lot, "dp", scatter_dimension=1, tiled=True)
        lot = lax.psum(lot, "expert")
        qkv_sum = lax.psum_scatter(
            grad_qkv.astype(f32), "dp", scatter_dimension=0, tiled=True
        )
        qkv_sum = other_sequences(qkv_sum).astype(bf16)
        by_head = place(
            gather_blocks(qkv_sum, group),
            [head ^ j for j in range(group)],
            1,
            group,
        )
    def of_heads(first, count):
        wide = q_cols + 2 * kv_cols
        return jnp.concatenate(
            [by_head[:, h * wide + first : h * wide + first + count] for h in range(group)], axis=1
        ).astype(f32)

    g_query = of_heads(0, q_cols)
    g_key = of_heads(q_cols, kv_cols)
    g_value = of_heads(q_cols + kv_cols, kv_cols)
    g_router, g_one, g_two = (
        jnp.transpose(lot[:experts_all]),
        lot[experts_all],
        lot[experts_all + 1],
    )
    loss_value = lot[experts_all + 2, 0] / (valid_count * width)

    if replicas == group:
        out_sum = grad_out.astype(f32)
        for step in range(1, replicas):
            pairs = [
                (
                    ((i % group + step) % replicas) * owners + i,
                    (i % group) * owners + i,
                )
                for i in range(owners)
            ]
            out_sum = out_sum + on_grid(grad_out, pairs).astype(f32)
        out_sum = other_sequences(out_sum).astype(bf16)
        g_out = jnp.where(plane == head, out_sum, jnp.zeros((), bf16))
        for m in range(1, group):
            pairs = [
                ((i % group) * owners + i, (i % group) * owners + (i ^ m)) for i in range(owners)
            ]
            g_out = g_out + on_grid(out_sum, pairs)
        g_out = g_out.astype(f32)
    else:
        out_sum = other_sequences(lax.psum(grad_out, "dp")).astype(bf16)
        g_out = pick(
            place(
                gather_blocks(out_sum, group), [head ^ j for j in range(group)], 0, group
            ),
            plane,
            slab,
            0,
        ).astype(f32)

    return (
        activations,
        loss_value,
        grad_in,
        g_one,
        g_two,
        g_query,
        g_key,
        g_value,
        g_out,
        g_router,
        gate_up_out,
        down_out,
    )


def solution(mesh):
    placed = (
        P(("dp", "expert"), None),
        P(("dp", "expert"), None),
        P(("dp", "expert")),
        P(("dp", "expert"), None),
        P("dp"),
        P("dp"),
        P("dp", None),
        P("dp", None),
        P("dp", None),
        P("dp", None),
        P("dp", None),
        P("expert", "dp", None),
        P("expert", "dp", None),
    )
    return jax.shard_map(
        body,
        mesh=mesh,
        in_specs=placed,
        out_specs=(
            P(("dp", "expert"), None),
            P(),
            P(("dp", "expert"), None),
            P("dp"),
            P("dp"),
            P("dp", None),
            P("dp", None),
            P("dp", None),
            P("dp", None),
            P("dp", None),
            P("expert", "dp", None),
            P("expert", "dp", None),
        ),
        check_vma=False,
    )
```

time: 1160 us -> 983 us (0.85)
  Pallas kernels: 0 us -> 557 us
  waiting for transfers between devices: 566 us -> 65.1 us
  matrix products: 229 us -> 90.4 us
  starting transfers between devices: 134 us -> 83.6 us
  local copies, waits for them, and re-layouts: 121 us -> 75.7 us
  between operations: 6.04 us -> 18.7 us
    pallas_call x0 -> x15, Pallas kernels: none -> 557 us  [the longest x2 147 us: plane_scatter(): comm_call(functools.partial(plane_scatter_kernel, half), name, number, 42...]
    ppermute x135 -> x13, waiting for transfers between devices: 480 us -> 65 us  [send(): return lax.ppermute(x, axis, [(i, i ^ mask) for i in range(count)])]
    dot_general x26 -> x15, matrix products: 229 us -> 90.4 us  [mm(): return jnp.einsum(spec, a, b, preferred_element_type=f32)]
    ppermute x9, waiting for transfers between devices: 85.7 us -> 0.02 us  [on_grid(): return lax.ppermute(x, ('dp', 'expert'), pairs)]
    ppermute x135 -> x13, starting transfers between devices: 119 us -> 64.5 us  [send(): return lax.ppermute(x, axis, [(i, i ^ mask) for i in range(count)])]
    unnamed x207 -> x167, local copies, waits for them, and re-layouts: 39.1 us -> 15.3 us
    slice x4 -> x23, local copies, waits for them, and re-layouts: 2.34 us -> 25.7 us  [the longest x15 17.4 us: body(): valid_count = sum((r[TOP, :1] for r in near_names + far_names))]
    convert_element_type x3 -> x2, local copies, waits for them, and re-layouts: 23.1 us -> 0.02 us  [the longest x1 0.01 us: body(): normed_f, norm_one_pull = jax.vjp(rms_norm, inputs, gain_one.astype(f32))]
  transfers between devices with their start and end apart: 144 -> 22, of which waited for: 54 -> 5; matrix products, arithmetic and copies ran while one was open for 24% -> 21% of each run, Pallas kernels for 0% -> 17%
where the time goes in v2:
time: 983 us; the launch traced here: 975 us
  Pallas kernels  557 us (57%)
  matrix products  90.4 us (9%)
  other arithmetic  84 us (9%)
  starting transfers between devices  83.6 us (9%)
  local copies, waits for them, and re-layouts  75.7 us (8%)
  waiting for transfers between devices  65.1 us (7%)
  between operations  18.7 us (2%)
    pallas_call x2, Pallas kernels, plane_scatter(): comm_call(functools.partial(plane_scatter_kernel, half), name, number, 42...  147 us
    pallas_call x2, Pallas kernels, plane_gather(): comm_call(functools.partial(plane_gather_kernel, half), name, number, 22,...  116 us
    dot_general x15, matrix products, mm(): return jnp.einsum(spec, a, b, preferred_element_type=f32)  90.4 us
    ppermute x13, waiting for transfers between devices, send(): return lax.ppermute(x, axis, [(i, i ^ mask) for i in range(count)])  65 us
    ppermute x13, starting transfers between devices, send(): return lax.ppermute(x, axis, [(i, i ^ mask) for i in range(count)])  64.5 us
    pallas_call x1, Pallas kernels, dense_reduce(): comm_call(functools.partial(dense_kernel, replicas), 'dense_reduce', 2, 2...  56.8 us
    pallas_call x2, Pallas kernels, experts_backward(): pl.pallas_call(experts_back_kernel, grid_spec=pltpu.PrefetchScalarGridSpe...  50.8 us
    pallas_call x2, Pallas kernels, seq_scatter(): comm_call(functools.partial(seq_scatter_kernel, group), name, number, 6,...  48.2 us
  transfers between devices with their start and end apart: 22, of which 5 were waited for; matrix products, arithmetic and copies ran while one was open for 21% of the time, Pallas kernels for 17%

profile of v2, /device:TPU:0, one launch (start us, length us, event | category | flops | bytes accessed | tf_op | source)
XLA Modules:
  0.0 974.5 jit_solution(6696503643897976552)
XLA Ops:
  3.4 1.9 concatenate.62.x_ref
  6.9 21.0 %start_exchange.1 = (s32[16,256]{1,0:T(8,128)}, s32[16,256]{1,0:T(8,128)}, s32[16,256]{1,0:T(8,128)}, s32[16,256]{1,0:T(8,128)}, s32[16,256]{1,0:T(8,128)}, /*in...) custom-call(s32[16,256]{1,0:T(8,128)} %concatenate.62.x_ref, ...), custom_call_target="tpu_custom_call" | custom-call | flops 1000000 | bytes 1000000 | tf_op jit(solution)/shard_map/start_exchange/pallas_call | solution.py:716
  31.2 2.3 fusion.7.x_ref
  33.5 24.1 %gather_normed.2 = bf16[1024,1536]{1,0:T(8,128)(2,1)} custom-call(bf16[256,1536]{1,0:T(8,128)(2,1)} %fusion.7.x_ref), custom_call_target="tpu_custom_call" | custom-call | flops 7864320 | bytes 7864320 | tf_op jit(solution)/shard_map/gather_normed/pallas_call | solution.py:636
  61.3 3.5 collective-permute-start.4
  64.8 2.3 collective-permute-start.5
  99.7 3.0 fusion.39
  118.8 2.0 collective-permute-start.1
  120.8 2.6 broadcast_in_dim.94
  126.2 3.6 collective-permute-start.3
  131.3 2.6 collective-permute-done.1
  133.9 4.9 collective-permute-start.6
  138.8 1.9 constant_dynamic-update-slice_fusion.24
  140.6 19.7 %collective-permute-done.2 = bf16[384,640]{1,0:T(8,128)(2,1)S(1)} collective-permute-done((bf16[384,640]{1,0:T(8,128)(2,1)}, bf16[384,640]{1,0:T(8,128)(2,1)S(1)}, u32[]{:S(2)}, u32[]{:S(2)}) %collective-permute-start.2) | collective-permute-done | bytes 491552 | tf_op jit(solution)/shard_map/ppermute | solution.py:55
  161.1 46.6 %collective-permute-start.8 = (bf16[3,384,512]{2,1,0:T(8,128)(2,1)}, bf16[3,384,512]{2,1,0:T(8,128)(2,1)}, u32[]{:S(2)}, u32[]{:S(2)}) collective-permute-start(bf16[3,384,512]{2,1,0:T(8,128)(2,1)} %get-tuple-element.246), channel_id=1, source_target_pairs={{0,8},{8,0},{16,24},{24,16},{1,9},{9,1},{17,25},{25,17},{2,10},{10... | collective-permute-start | bytes 3538952 | tf_op jit(solution)/shard_map/ppermute | solution.py:55
  208.5 4.7 fusion.44
  216.0 10.7 %fusion.4 = (f32[2,3,1024]{2,1,0:T(4,128)S(1)}, f32[2,1024,1024,3]{2,1,3,0:T(8,128)}) fusion(pred[1024,1024]{0,1:T(8,128)(4,1)S(1)} %iota_compare_fusion, bf16[1024,2,3,32]{0,3,2,1:T(8,128)(2,1)S(1)} %bitcast.164, bf16[1024,2,3,32]{0,3,2,1:T(8,128)(2,1)S(1)} %bitcast.162, bf16[1024,2,32]{0,2,1:T(8,128)(2,1)S(1)} %get-tuple-element.255, ...), kind=kOutput, calls=%fused_computation.9 | convolution fusion | flops 826271744 | bytes 27287552 | tf_op jit(solution)/shard_map/qhgd,khd->hgqk/dot_general | solution.py:29
  226.7 11.4 %exponential_reduce_fusion = f32[2,3,1024]{2,1,0:T(4,128)S(1)} fusion(f32[2,1024,1024,3]{2,1,3,0:T(8,128)} %get-tuple-element.264, f32[2,3,1024]{2,1,0:T(4,128)S(1)} %get-tuple-element.263, pred[1024,1024]{0,1:T(8,128)(4,1)S(1)} %iota_compare_fusion), kind=kLoop, calls=%fused_computation.7 | loop fusion | flops 25159680 | bytes 26263552 | tf_op jit(solution)/shard_map/reduce_sum | solution.py:107
  238.2 11.6 %convolution_convert_fusion.5 = bf16[2,64,3,1024]{3,1,2,0:T(8,128)(2,1)S(1)} fusion(bf16[1024,2,64,1]{0,2,3,1:T(8,128)(2,1)S(1)} %bitcast.166, f32[2,1024,1024,3]{2,1,3,0:T(8,128)} %get-tuple-element.264, f32[2,3,1024]{2,1,0:T(4,128)S(1)} %log_add_fusion, pred[1024,1024]{0,1:T(8,128)(4,1)S(1)} %iota_compare_fusion), kind=kOutput, calls=%fused_computation.51 | convolution fusion | flops 830865408 | bytes 27287552 | tf_op jit(solution)/shard_map/hgqk,khd->qhgd/dot_general | solution.py:29
  250.0 2.1 add_add_fusion.2
  253.1 3.5 convolution_convert_fusion.1.x_ref
  256.6 22.9 %scatter_branch.2 = f32[256,1536]{1,0:T(8,128)} custom-call(bf16[1024,1536]{1,0:T(8,128)(2,1)} %convolution_convert_fusion.1.x_ref), custom_call_target="tpu_custom_call" | custom-call | flops 7864320 | bytes 7864320 | tf_op jit(solution)/shard_map/scatter_branch/pallas_call | solution.py:682
  279.5 1.7 multiply_reduce_fusion.2
  281.3 1.9 collective-permute-start.9
  284.3 58.7 %gather_tokens.2 = (bf16[256,1536]{1,0:T(8,128)(2,1)}, bf16[256,1536]{1,0:T(8,128)(2,1)}, bf16[256,1536]{1,0:T(8,128)(2,1)}, bf16[256,1536]{1,0:T(8,128)(2,1)}, ...) custom-call(bf16[256,1536]{1,0:T(8,128)(2,1)} %multiply_convert_fusi, ...), custom_call_target="tpu_custom_call" | custom-call | flops 19660800 | bytes 19660800 | tf_op jit(solution)/shard_map/gather_tokens/pallas_call | solution.py:498
  344.8 2.4 constant_dynamic-update-slice_fusion.20
  347.2 2.4 constant_dynamic-update-slice_fusion.19
  349.5 2.4 constant_dynamic-update-slice_fusion.16.down_ref
  353.0 23.3 %experts_forward.2 = (bf16[256,1536]{1,0:T(8,128)(2,1)}, bf16[256,1536]{1,0:T(8,128)(2,1)}, bf16[256,1536]{1,0:T(8,128)(2,1)}, bf16[256,1536]{1,0:T(8,128)(2,1)}...) custom-call(s32[1]{0:T(128)} %bitcast.33.me_ref, ...), custom_call_target="tpu_custom_call" | custom-call | flops 11000000512 | bytes 40000000 | tf_op jit(solution)/shard_map/experts_forward/pallas_call | solution.py:219
  376.3 23.6 %experts_forward.3 = (bf16[256,1536]{1,0:T(8,128)(2,1)}, bf16[256,1536]{1,0:T(8,128)(2,1)}, bf16[256,1536]{1,0:T(8,128)(2,1)}, bf16[256,1536]{1,0:T(8,128)(2,1)}...) custom-call(s32[1]{0:T(128)} %bitcast.33.me_ref, ...), custom_call_target="tpu_custom_call" | custom-call | flops 11000000512 | bytes 40000000 | tf_op jit(solution)/shard_map/experts_forward/pallas_call | solution.py:219
  399.9 75.7 %scatter_outputs.1 = f32[256,1536]{1,0:T(8,128)} custom-call(bf16[256,1536]{1,0:T(8,128)(2,1)} %get-tuple-element.131.refs_0_, bf16[256,1536]{1,0:T(8,128)(2,1)} %get-tuple-element.132.refs_1_, bf16[256,1536]{1,0:T(8,128)(2,1)} %get-tuple-element.133.refs_2_, bf16[256,1536]{1,0:T(8,128)(2,1)} %get-tuple-element.134.refs_3_, ...), custom_call_target="tpu_custom_call" | custom-call | flops 19660800 | bytes 19660800 | tf_op jit(solution)/shard_map/scatter_outputs/pallas_call | solution.py:589
  475.6 3.0 multiply_convert_fusion.2.x_ref.refs_0_
  478.6 57.5 %gather_tokens.3 = (bf16[256,1536]{1,0:T(8,128)(2,1)}, bf16[256,1536]{1,0:T(8,128)(2,1)}, bf16[256,1536]{1,0:T(8,128)(2,1)}, bf16[256,1536]{1,0:T(8,128)(2,1)}, ...) custom-call(bf16[256,1536]{1,0:T(8,128)(2,1)} %multiply_convert_fusi, ...), custom_call_target="tpu_custom_call" | custom-call | flops 19660800 | bytes 19660800 | tf_op jit(solution)/shard_map/gather_tokens/pallas_call | solution.py:498
  536.2 25.4 %experts_backward.2 = (bf16[256,1664]{1,0:T(8,128)(2,1)}, bf16[256,1664]{1,0:T(8,128)(2,1)}, bf16[256,1664]{1,0:T(8,128)(2,1)}, bf16[256,1664]{1,0:T(8,128)(2,1)...) custom-call(s32[1]{0:T(128)} %bitcast.33.me_ref, ...), custom_call_target="tpu_custom_call" | custom-call | flops 11000000512 | bytes 40000000 | tf_op jit(solution)/shard_map/experts_backward/pallas_call | solution.py:296
  561.6 25.4 %experts_backward.3 = (bf16[256,1664]{1,0:T(8,128)(2,1)}, bf16[256,1664]{1,0:T(8,128)(2,1)}, bf16[256,1664]{1,0:T(8,128)(2,1)}, bf16[256,1664]{1,0:T(8,128)(2,1)...) custom-call(s32[1]{0:T(128)} %bitcast.33.me_ref, ...), custom_call_target="tpu_custom_call" | custom-call | flops 11000000512 | bytes 40000000 | tf_op jit(solution)/shard_map/experts_backward/pallas_call | solution.py:296
  586.9 71.7 %scatter_grads.1 = f32[256,1664]{1,0:T(8,128)} custom-call(bf16[256,1664]{1,0:T(8,128)(2,1)} %get-tuple-element.165.refs_0_, bf16[256,1664]{1,0:T(8,128)(2,1)} %get-tuple-element.166.refs_1_, bf16[256,1664]{1,0:T(8,128)(2,1)} %get-tuple-element.167.refs_2_, bf16[256,1664]{1,0:T(8,128)(2,1)} %get-tuple-element.168.refs_3_, ...), custom_call_target="tpu_custom_call" | custom-call | flops 21299200 | bytes 21299200 | tf_op jit(solution)/shard_map/scatter_grads/pallas_call | solution.py:589
  661.1 21.6 %expert_weights.1 = (bf16[3,1536,512]{2,1,0:T(8,128)(2,1)}, bf16[3,256,1536]{2,1,0:T(8,128)(2,1)}) custom-call(s32[1]{0:T(128)} %bitcast.54.after_ref, bf16[8,3,112,1536]{3,2,1,0:T(8,128)(2,1)} %get-tuple-element.192.refs_0_, bf16[8,3,112,512]{3,2,1,0:T(8,128)(2,1)} %get-tuple-element.193.refs_1_, bf16[8,3,112,256]{3,2,1,0:T(8,128)(2,1)} %get-tuple-element.194.refs_2_, ...), custom_call_target="tpu_custom_call" | custom-call | flops 14000000000 | bytes 40000000 | tf_op jit(solution)/shard_map/expert_weights/pallas_call | solution.py:344
  682.8 2.6 constant_dynamic-slice_fusion
  687.7 3.7 multiply_reduce_fusion
  692.7 2.5 multiply_convert_fusion
  695.2 24.0 %gather_normed.3 = bf16[1024,1536]{1,0:T(8,128)(2,1)} custom-call(bf16[256,1536]{1,0:T(8,128)(2,1)} %get-tuple-element.213.x_ref), custom_call_target="tpu_custom_call" | custom-call | flops 7864320 | bytes 7864320 | tf_op jit(solution)/shard_map/gather_normed/pallas_call | solution.py:636
  719.3 4.7 convolution_convert_fusion.3
  727.8 1.9 fusion.43
  731.2 17.4 %fusion = (f32[2,3,1024]{2,1,0:T(4,128)S(1)}, f32[2,1024,1024,3]{2,1,3,0:T(8,128)}) fusion(f32[2,1024,1024,3]{2,1,3,0:T(8,128)} %get-tuple-element.264, f32[2,3,1024]{2,1,0:T(4,128)S(1)} %log_add_fusion, pred[1024,1024]{0,1:T(8,128)(4,1)S(1)} %iota_compare_fusion, bf16[1024,2,64,1]{0,2,3,1:T(8,128)(2,1)S(1)} %bitcast.167, ...), kind=kOutput, calls=%fused_computation.2 | convolution fusion | flops 836757504 | bytes 52477952 | tf_op jit(solution)/shard_map/qhgd,khd->hgqk/dot_general | solution.py:29
  748.7 18.0 %fusion.2 = bf16[2,3,1024,1024]{2,3,1,0:T(8,128)(2,1)S(1)} fusion(f32[2,1024,1024,3]{2,1,3,0:T(8,128)} %get-tuple-element.269, f32[2,1024,1024,3]{2,1,3,0:T(8,128)} %get-tuple-element.264, f32[2,3,1024]{2,1,0:T(4,128)S(1)} %get-tuple-element.268, f32[2,3,1024]{2,1,0:T(4,128)S(1)} %log_add_fusion, pred[1024,1024]{0,1:T(8,128)(4,1)} %copy-done.2), kind=kLoop, calls=%fused_computation.4 | loop fusion | flops 37748736 | bytes 64012288 | tf_op jit(solution)/shard_map/convert_element_type | solution.py:120
  766.7 3.4 convolution_multiply_fusion
  770.1 5.9 fusion.15
  776.0 11.9 %fusion.16 = bf16[2,64,1024]{2,1,0:T(8,128)(2,1)S(1)} fusion(bf16[1024,2,3,64]{0,3,2,1:T(8,128)(2,1)} %bitcast.171, f32[2,1024,1024,3]{2,1,3,0:T(8,128)} %get-tuple-element.264, f32[2,3,1024]{2,1,0:T(4,128)S(1)} %log_add_fusion, pred[1024,1024]{0,1:T(8,128)(4,1)S(1)} %copy-done.3), kind=kOutput, calls=%fused_computation.57 | convolution fusion | flops 830603264 | bytes 27287552 | tf_op jit(solution)/shard_map/hgqk,qhgd->khd/dot_general | solution.py:29
  789.7 4.1 convolution_convert_fusion.x_ref
  793.8 3.8 convolution_convert_fusion.2.grads
  797.7 4.5 collective-permute-start.21
  803.8 25.3 %scatter_branch.3 = f32[256,1536]{1,0:T(8,128)} custom-call(bf16[1024,1536]{1,0:T(8,128)(2,1)} %convolution_convert_fusion.x_ref), custom_call_target="tpu_custom_call" | custom-call | flops 7864320 | bytes 7864320 | tf_op jit(solution)/shard_map/scatter_branch/pallas_call | solution.py:682
  829.2 1.9 fusion.13
  832.6 56.8 %dense_reduce.1 = (bf16[384,2560]{1,0:T(8,128)(2,1)}, f32[32,384]{1,0:T(8,128)}) custom-call(bf16[1536,640]{1,0:T(8,128)(2,1)} %convolution_convert_fusion.2.grads, f32[4,32,384]{2,1,0:T(8,128)} %maximum_bitcast_fusion.1.small), custom_call_target="tpu_custom_call" | custom-call | flops 100000000 | bytes 100000000 | tf_op jit(solution)/shard_map/dense_reduce/pallas_call | solution.py:807
  896.9 4.0 fusion.17
  904.0 3.9 collective-permute-start.18
  910.2 2.1 add_convert_fusion
  912.6 3.0 convert_add_fusion.1
  915.6 13.9 %collective-permute-done.14 = bf16[384,1536]{1,0:T(8,128)(2,1)} collective-permute-done((bf16[384,1536]{1,0:T(8,128)(2,1)}, bf16[384,1536]{1,0:T(8,128)(2,1)}, u32[]{:S(2)}, u32[]{:S(2)}) %collective-permute-start.14) | collective-permute-done | bytes 1179680 | tf_op jit(solution)/shard_map/ppermute | solution.py:55
  929.5 3.4 add_convert_fusion.1
  937.5 16.0 %collective-permute-done.18 = bf16[3,384,512]{2,1,0:T(8,128)(2,1)S(1)} collective-permute-done((bf16[3,384,512]{2,1,0:T(8,128)(2,1)S(1)}, bf16[3,384,512]{2,1,0:T(8,128)(2,1)S(1)}, u32[]{:S(2)}, u32[]{:S(2)}) %collective-permute-start.18) | collective-permute-done | bytes 1179680 | tf_op jit(solution)/shard_map/ppermute | solution.py:55
  953.6 12.8 %collective-permute-done.20 = bf16[3,384,512]{2,1,0:T(8,128)(2,1)S(1)} collective-permute-done((bf16[3,384,512]{2,1,0:T(8,128)(2,1)S(1)}, bf16[3,384,512]{2,1,0:T(8,128)(2,1)S(1)}, u32[]{:S(2)}, u32[]{:S(2)}) %collective-permute-start.20) | collective-permute-done | bytes 1179680 | tf_op jit(solution)/shard_map/ppermute | solution.py:55
  966.3 2.0 convert_select_fusion.1
  968.7 2.8 pad_maximum_fusion
  (286 shorter events, 93.8 us)
Async XLA Ops:
  0.6 116.1 %copy-start = (bf16[384,1536]{1,0:T(8,128)(2,1)S(1)}, bf16[384,1536]{1,0:T(8,128)(2,1)}, u32[]{:S(2)}) copy-start(bf16[384,1536]{1,0:T(8,128)(2,1)} %param.19) | copy-start | bytes 3538948
  33.5 26.7 %copy-start.15 = (bf16[384,1536]{1,0:T(8,128)(2,1)S(1)}, bf16[384,1536]{1,0:T(8,128)(2,1)}, u32[]{:S(2)}) copy-start(bf16[384,1536]{1,0:T(8,128)(2,1)} %param.22) | copy-start | bytes 3538948
  57.7 17.8 %copy-start.72 = (s32[16,256]{1,0:T(8,128)S(1)}, s32[16,256]{1,0:T(8,128)}, u32[]{:S(2)}) copy-start(s32[16,256]{1,0:T(8,128)} %get-tuple-element.116) | copy-start | bytes 49156
  60.2 37.0 %copy-start.52 = (s32[256,8]{0,1:T(8,128)S(1)}, s32[256,8]{0,1:T(8,128)}, u32[]{:S(2)}) copy-start(s32[256,8]{0,1:T(8,128)} %param.16) | copy-start | bytes 24580
  60.2 37.6 %copy-start.51 = (bf16[4,32,384]{2,1,0:T(8,128)(2,1)S(1)}, bf16[4,32,384]{2,1,0:T(8,128)(2,1)}, u32[]{:S(2)}) copy-start(bf16[4,32,384]{2,1,0:T(8,128)(2,1)} %get-tuple-element.108) | copy-start | bytes 294916
  61.3 188.5 %collective-permute-start.4 = (bf16[384,1536]{1,0:T(8,128)(2,1)}, bf16[384,1536]{1,0:T(8,128)(2,1)}, u32[]{:S(2)}, u32[]{:S(2)}) collective-permute-start(bf16[384,1536]{1,0:T(8,128)(2,1)} %broadcast_select_fusion.1), channel_id=1, source_target_pairs={{0,8},{9,17},{18,26},{27,3},{4,12},{13,21},{22,30},{31,7}} | collective-permute-start | bytes 3538952 | tf_op jit(solution)/shard_map/ppermute | solution.py:910
  64.8 185.1 %collective-permute-start.5 = (bf16[384,1536]{1,0:T(8,128)(2,1)}, bf16[384,1536]{1,0:T(8,128)(2,1)}, u32[]{:S(2)}, u32[]{:S(2)}) collective-permute-start(bf16[384,1536]{1,0:T(8,128)(2,1)} %broadcast_select_fusion.1), channel_id=1, source_target_pairs={{0,16},{9,25},{18,2},{27,11},{4,20},{13,29},{22,6},{31,15}} | collective-permute-start | bytes 3538952 | tf_op jit(solution)/shard_map/ppermute | solution.py:910
  94.7 21.4 %collective-permute-start = (s32[1]{0:T(128)}, s32[1]{0:T(128)}, u32[]{:S(2)}, u32[]{:S(2)}) collective-permute-start(s32[1]{0:T(128)} %add.226), channel_id=1, source_target_pairs={{0,8},{8,0},{16,24},{24,16},{1,9},{9,1},{17,25},{25,17},{2,10},{10... | collective-permute-start | bytes 20 | tf_op jit(solution)/shard_map/ppermute | solution.py:55
  96.4 634.8 %copy-start.2 = (pred[1024,1024]{0,1:T(8,128)(4,1)}, pred[1024,1024]{0,1:T(8,128)(4,1)S(1)}, u32[]{:S(2)}) copy-start(pred[1024,1024]{0,1:T(8,128)(4,1)S(1)} %iota_compare_fusion) | copy-start | bytes 3145732
  99.6 115.4 %copy-start.17 = (f32[1024,32]{0,1:T(8,128)}, f32[1024,32]{0,1:T(8,128)S(1)}, u32[]{:S(2)}) copy-start(f32[1024,32]{0,1:T(8,128)S(1)} %get-tuple-element.262) | copy-start | bytes 393220
  99.7 5.5 copy-start.67
  99.7 6.0 copy-start.66
  99.7 6.6 copy-start.65
  99.7 7.2 copy-start.64
  99.7 7.8 copy-start.63
  99.7 8.4 copy-start.62
  99.7 9.0 copy-start.61
  99.7 9.6 copy-start.60
  118.8 15.1 %collective-permute-start.1 = (bf16[384,640]{1,0:T(8,128)(2,1)}, bf16[384,640]{1,0:T(8,128)(2,1)}, u32[]{:S(2)}, u32[]{:S(2)}) collective-permute-start(bf16[384,640]{1,0:T(8,128)(2,1)} %get-tuple-element.256), channel_id=1, source_target_pairs={{0,8},{8,0},{16,24},{24,16},{1,9},{9,1},{17,25},{25,17},{2,10},{10... | collective-permute-start | bytes 1474568 | tf_op jit(solution)/shard_map/ppermute | solution.py:55
  125.0 6.3 copy-start.59
  125.0 35.3 %collective-permute-start.2 = (bf16[384,640]{1,0:T(8,128)(2,1)}, bf16[384,640]{1,0:T(8,128)(2,1)S(1)}, u32[]{:S(2)}, u32[]{:S(2)}) collective-permute-start(bf16[384,640]{1,0:T(8,128)(2,1)} %get-tuple-element.256), channel_id=1, source_target_pairs={{0,16},{8,24},{16,0},{24,8},{1,17},{9,25},{17,1},{25,9},{2,18},{10... | collective-permute-start | bytes 1474568 | tf_op jit(solution)/shard_map/ppermute | solution.py:55
  126.2 35.0 %collective-permute-start.3 = (bf16[384,640]{1,0:T(8,128)(2,1)}, bf16[384,640]{1,0:T(8,128)(2,1)S(1)}, u32[]{:S(2)}, u32[]{:S(2)}) collective-permute-start(bf16[384,640]{1,0:T(8,128)(2,1)} %get-tuple-element.256), channel_id=1, source_target_pairs={{0,24},{8,16},{16,8},{24,0},{1,25},{9,17},{17,9},{25,1},{2,26},{10... | collective-permute-start | bytes 1474568 | tf_op jit(solution)/shard_map/ppermute | solution.py:55
  133.9 116.0 %collective-permute-start.6 = (bf16[384,1536]{1,0:T(8,128)(2,1)}, bf16[384,1536]{1,0:T(8,128)(2,1)S(1)}, u32[]{:S(2)}, u32[]{:S(2)}) collective-permute-start(bf16[384,1536]{1,0:T(8,128)(2,1)} %broadcast_select_fusion.1), channel_id=1, source_target_pairs={{0,24},{9,1},{18,10},{27,19},{4,28},{13,5},{22,14},{31,23}} | collective-permute-start | bytes 3538952 | tf_op jit(solution)/shard_map/ppermute | solution.py:910
  160.3 121.0 %collective-permute-start.7 = (bf16[3,384,512]{2,1,0:T(8,128)(2,1)}, bf16[3,384,512]{2,1,0:T(8,128)(2,1)}, u32[]{:S(2)}, u32[]{:S(2)}) collective-permute-start(bf16[3,384,512]{2,1,0:T(8,128)(2,1)} %pad_maximum_fusion.3), channel_id=1, source_target_pairs={{0,16},{8,24},{16,0},{24,8},{1,17},{9,25},{17,1},{25,9},{2,18},{10... | collective-permute-start | bytes 3538952 | tf_op jit(solution)/shard_map/ppermute | solution.py:55
  161.1 186.0 %collective-permute-start.8 = (bf16[3,384,512]{2,1,0:T(8,128)(2,1)}, bf16[3,384,512]{2,1,0:T(8,128)(2,1)}, u32[]{:S(2)}, u32[]{:S(2)}) collective-permute-start(bf16[3,384,512]{2,1,0:T(8,128)(2,1)} %get-tuple-element.246), channel_id=1, source_target_pairs={{0,8},{8,0},{16,24},{24,16},{1,9},{9,1},{17,25},{25,17},{2,10},{10... | collective-permute-start | bytes 3538952 | tf_op jit(solution)/shard_map/ppermute | solution.py:55
  214.8 23.4 %copy-start.39 = (bf16[1024,128]{0,1:T(8,128)(2,1)}, bf16[1024,128]{0,1:T(8,128)(2,1)S(1)}, u32[]{:S(2)}) copy-start(bf16[1024,128]{0,1:T(8,128)(2,1)S(1)} %slice.363) | copy-start | bytes 786436
  215.0 11.7 %copy-start.31 = (bf16[1024,6,32]{0,2,1:T(8,128)(2,1)}, bf16[1024,6,32]{0,2,1:T(8,128)(2,1)S(1)}, u32[]{:S(2)}) copy-start(bf16[1024,6,32]{0,2,1:T(8,128)(2,1)S(1)} %get-tuple-element.244) | copy-start | bytes 1179652
  215.1 11.7 %copy-start.32 = (bf16[1024,6,32]{0,2,1:T(8,128)(2,1)}, bf16[1024,6,32]{0,2,1:T(8,128)(2,1)S(1)}, u32[]{:S(2)}) copy-start(bf16[1024,6,32]{0,2,1:T(8,128)(2,1)S(1)} %get-tuple-element.245) | copy-start | bytes 1179652
  216.0 10.7 %copy-start.43 = (bf16[1024,2,32]{0,2,1:T(8,128)(2,1)}, bf16[1024,2,32]{0,2,1:T(8,128)(2,1)S(1)}, u32[]{:S(2)}) copy-start(bf16[1024,2,32]{0,2,1:T(8,128)(2,1)S(1)} %get-tuple-element.254) | copy-start | bytes 393220
  216.0 10.7 %copy-start.45 = (bf16[1024,2,32]{0,2,1:T(8,128)(2,1)}, bf16[1024,2,32]{0,2,1:T(8,128)(2,1)S(1)}, u32[]{:S(2)}) copy-start(bf16[1024,2,32]{0,2,1:T(8,128)(2,1)S(1)} %get-tuple-element.255) | copy-start | bytes 393220
  238.2 11.7 %copy-start.16 = (bf16[384,1536]{1,0:T(8,128)(2,1)S(1)}, bf16[384,1536]{1,0:T(8,128)(2,1)}, u32[]{:S(2)}) copy-start(bf16[384,1536]{1,0:T(8,128)(2,1)} %param.22) | copy-start | bytes 3538948
  249.8 99.7 %collective-permute-start.10 = (bf16[3,128,1536]{2,1,0:T(8,128)(2,1)}, bf16[3,128,1536]{2,1,0:T(8,128)(2,1)}, u32[]{:S(2)}, u32[]{:S(2)}) collective-permute-start(bf16[3,128,1536]{2,1,0:T(8,128)(2,1)} %get-tuple-element.218), channel_id=1, source_target_pairs={{0,8},{8,0},{16,24},{24,16},{1,9},{9,1},{17,25},{25,17},{2,10},{10... | collective-permute-start | bytes 3538952 | tf_op jit(solution)/shard_map/ppermute | solution.py:55
  256.6 22.9 %copy-start.6 = (bf16[256,1536]{1,0:T(8,128)(2,1)S(1)}, bf16[256,1536]{1,0:T(8,128)(2,1)}, u32[]{:S(2)}) copy-start(bf16[256,1536]{1,0:T(8,128)(2,1)} %param.13) | copy-start | bytes 2359300
  281.3 70.6 %collective-permute-start.9 = (bf16[3,384,512]{2,1,0:T(8,128)(2,1)}, bf16[3,384,512]{2,1,0:T(8,128)(2,1)S(1)}, u32[]{:S(2)}, u32[]{:S(2)}) collective-permute-start(bf16[3,384,512]{2,1,0:T(8,128)(2,1)} %collective-permute-done.7), channel_id=1, source_target_pairs={{0,8},{8,0},{16,24},{24,16},{1,9},{9,1},{17,25},{25,17},{2,10},{10... | collective-permute-start | bytes 3538952 | tf_op jit(solution)/shard_map/ppermute | solution.py:55
  283.2 59.8 %copy-start.47 = (pred[256,24]{1,0:T(32,128)(4,1)S(1)}, pred[256,24]{1,0:T(32,128)(4,1)}, u32[]{:S(2)}) copy-start(pred[256,24]{1,0:T(32,128)(4,1)} %copy.44) | copy-start | bytes 18436
  283.2 59.8 %copy-start.53 = (bf16[4,3,8,384]{3,2,0,1:T(8,128)(2,1)S(1)}, bf16[4,3,8,384]{3,2,0,1:T(8,128)(2,1)}, u32[]{:S(2)}) copy-start(bf16[4,3,8,384]{3,2,0,1:T(8,128)(2,1)} %copy.59) | copy-start | bytes 221188
  399.9 75.7 %copy-start.21 = (bf16[256,1536]{1,0:T(8,128)(2,1)S(1)}, bf16[256,1536]{1,0:T(8,128)(2,1)}, u32[]{:S(2)}) copy-start(bf16[256,1536]{1,0:T(8,128)(2,1)} %param.14) | copy-start | bytes 2359300
  719.2 8.6 copy-start.10
  719.3 10.5 %copy-start.20 = (bf16[1024,1536]{1,0:T(8,128)(2,1)S(1)}, bf16[1024,1536]{1,0:T(8,128)(2,1)}, u32[]{:S(2)}) copy-start(bf16[1024,1536]{1,0:T(8,128)(2,1)} %gather_normed.3) | copy-start | bytes 9437188
  719.3 10.5 %copy-start.36 = (bf16[384,1536]{1,0:T(8,128)(2,1)S(1)}, bf16[384,1536]{1,0:T(8,128)(2,1)}, u32[]{:S(2)}) copy-start(bf16[384,1536]{1,0:T(8,128)(2,1)} %copy-done.35) | copy-start | bytes 3538948
  723.9 172.9 %collective-permute-start.11 = (bf16[384,1536]{1,0:T(8,128)(2,1)}, bf16[384,1536]{1,0:T(8,128)(2,1)}, u32[]{:S(2)}, u32[]{:S(2)}) collective-permute-start(bf16[384,1536]{1,0:T(8,128)(2,1)} %convolution_convert_fusion.3), channel_id=1, source_target_pairs={{8,0},{17,9},{26,18},{3,27},{12,4},{21,13},{30,22},{7,31}} | collective-permute-start | bytes 3538952 | tf_op jit(solution)/shard_map/ppermute | solution.py:910
  725.2 171.7 %collective-permute-start.12 = (bf16[384,1536]{1,0:T(8,128)(2,1)}, bf16[384,1536]{1,0:T(8,128)(2,1)}, u32[]{:S(2)}, u32[]{:S(2)}) collective-permute-start(bf16[384,1536]{1,0:T(8,128)(2,1)} %convolution_convert_fusion.3), channel_id=1, source_target_pairs={{16,0},{25,9},{2,18},{11,27},{20,4},{29,13},{6,22},{15,31}} | collective-permute-start | bytes 3538952 | tf_op jit(solution)/shard_map/ppermute | solution.py:910
  726.5 170.4 %collective-permute-start.13 = (bf16[384,1536]{1,0:T(8,128)(2,1)}, bf16[384,1536]{1,0:T(8,128)(2,1)}, u32[]{:S(2)}, u32[]{:S(2)}) collective-permute-start(bf16[384,1536]{1,0:T(8,128)(2,1)} %convolution_convert_fusion.3), channel_id=1, source_target_pairs={{24,0},{1,9},{10,18},{19,27},{28,4},{5,13},{14,22},{23,31}} | collective-permute-start | bytes 3538952 | tf_op jit(solution)/shard_map/ppermute | solution.py:910
  731.2 17.4 %copy-start.41 = (bf16[1024,384]{0,1:T(8,128)(2,1)}, bf16[1024,384]{0,1:T(8,128)(2,1)S(1)}, u32[]{:S(2)}) copy-start(bf16[1024,384]{0,1:T(8,128)(2,1)S(1)} %convolution_convert_fusion.4) | copy-start | bytes 2359300
  748.6 18.0 %copy-start.44 = (bf16[1024,2,32]{0,2,1:T(8,128)(2,1)S(1)}, bf16[1024,2,32]{0,2,1:T(8,128)(2,1)}, u32[]{:S(2)}) copy-start(bf16[1024,2,32]{0,2,1:T(8,128)(2,1)} %copy-done.43) | copy-start | bytes 393220
  748.6 18.0 %copy-start.46 = (bf16[1024,2,32]{0,2,1:T(8,128)(2,1)S(1)}, bf16[1024,2,32]{0,2,1:T(8,128)(2,1)}, u32[]{:S(2)}) copy-start(bf16[1024,2,32]{0,2,1:T(8,128)(2,1)} %copy-done.45) | copy-start | bytes 393220
  770.1 5.9 copy-start.3
  776.0 11.9 %copy-start.11 = (f32[2,64,3,1024]{3,1,2,0:T(8,128)S(1)}, f32[2,64,3,1024]{3,1,2,0:T(8,128)}, u32[]{:S(2)}) copy-start(f32[2,64,3,1024]{3,1,2,0:T(8,128)} %convolution_multiply_fusion) | copy-start | bytes 4718596
  776.0 11.9 %copy-start.18 = (f32[1024,32]{0,1:T(8,128)S(1)}, f32[1024,32]{0,1:T(8,128)}, u32[]{:S(2)}) copy-start(f32[1024,32]{0,1:T(8,128)} %copy-done.17) | copy-start | bytes 393220
  776.0 11.9 %copy-start.37 = (f32[1024,32]{0,1:T(8,128)S(1)}, f32[1024,32]{0,1:T(8,128)}, u32[]{:S(2)}) copy-start(f32[1024,32]{0,1:T(8,128)} %get-tuple-element.260) | copy-start | bytes 393220
  789.0 13.2 %slice-start = ((s8[4718592]{0:T(1024)(128)(4,1)}), s8[4194304]{0:T(1024)(128)(4,1)S(1)}, s32[]{:S(2)}) async-start(s8[4718592]{0:T(1024)(128)(4,1)} %bitcast.159), calls=%async_computation | async-start | bytes 8388608
  789.7 12.5 %slice-start.1 = ((s8[4718592]{0:T(1024)(128)(4,1)}), s8[524288]{0:T(1024)(128)(4,1)S(1)}, s32[]{:S(2)}) async-start(s8[4718592]{0:T(1024)(128)(4,1)} %bitcast.159), calls=%async_computation.1 | async-start | bytes 1048576
  797.7 114.7 %collective-permute-start.21 = (bf16[3,128,1536]{2,1,0:T(8,128)(2,1)}, bf16[3,128,1536]{2,1,0:T(8,128)(2,1)}, u32[]{:S(2)}, u32[]{:S(2)}) collective-permute-start(bf16[3,128,1536]{2,1,0:T(8,128)(2,1)} %constant_dynamic-slice_fusion), channel_id=1, source_target_pairs={{0,8},{8,0},{16,24},{24,16},{1,9},{9,1},{17,25},{25,17},{2,10},{10... | collective-permute-start | bytes 3538952 | tf_op jit(solution)/shard_map/ppermute | solution.py:55
  803.8 106.4 %collective-permute-start.19 = (bf16[3,384,512]{2,1,0:T(8,128)(2,1)}, bf16[3,384,512]{2,1,0:T(8,128)(2,1)}, u32[]{:S(2)}, u32[]{:S(2)}) collective-permute-start(bf16[3,384,512]{2,1,0:T(8,128)(2,1)} %get-tuple-element.222), channel_id=1, source_target_pairs={{0,8},{8,0},{16,24},{24,16},{1,9},{9,1},{17,25},{25,17},{2,10},{10... | collective-permute-start | bytes 3538952 | tf_op jit(solution)/shard_map/ppermute | solution.py:55
  803.8 25.4 %copy-start.50 = (f32[1536]{0:T(1024)S(1)}, f32[1536]{0:T(1024)}, u32[]{:S(2)}) copy-start(f32[1536]{0:T(1024)} %copy-done.49) | copy-start | bytes 18436
  803.8 25.4 %copy-start.56 = (f32[256]{0:T(256)S(1)}, f32[256]{0:T(256)}, u32[]{:S(2)}) copy-start(f32[256]{0:T(256)} %copy-done.55) | copy-start | bytes 3076
  832.6 59.6 %copy-start.58 = (f32[256]{0:T(256)S(1)}, f32[256]{0:T(256)}, u32[]{:S(2)}) copy-start(f32[256]{0:T(256)} %copy-done.57) | copy-start | bytes 3076
  896.9 7.1 copy-start.33
  900.9 28.6 %collective-permute-start.14 = (bf16[384,1536]{1,0:T(8,128)(2,1)}, bf16[384,1536]{1,0:T(8,128)(2,1)}, u32[]{:S(2)}, u32[]{:S(2)}) collective-permute-start(bf16[384,1536]{1,0:T(8,128)(2,1)} %fusion.17), channel_id=1, source_target_pairs={{0,4},{1,5},{2,6},{3,7},{4,0},{5,1},{6,2},{7,3},{8,12},{9,13},{10,... | collective-permute-start | bytes 3538952 | tf_op jit(solution)/shard_map/ppermute | solution.py:55
  904.0 49.6 %collective-permute-start.18 = (bf16[3,384,512]{2,1,0:T(8,128)(2,1)S(1)}, bf16[3,384,512]{2,1,0:T(8,128)(2,1)S(1)}, u32[]{:S(2)}, u32[]{:S(2)}) collective-permute-start(bf16[3,384,512]{2,1,0:T(8,128)(2,1)S(1)} %copy-done.33), channel_id=1, source_target_pairs={{0,8},{8,0},{16,24},{24,16},{1,9},{9,1},{17,25},{25,17},{2,10},{10... | collective-permute-start | bytes 3538952 | tf_op jit(solution)/shard_map/ppermute | solution.py:55
  912.3 54.0 %collective-permute-start.20 = (bf16[3,384,512]{2,1,0:T(8,128)(2,1)S(1)}, bf16[3,384,512]{2,1,0:T(8,128)(2,1)S(1)}, u32[]{:S(2)}, u32[]{:S(2)}) collective-permute-start(bf16[3,384,512]{2,1,0:T(8,128)(2,1)S(1)} %add_convert_fusion), channel_id=1, source_target_pairs={{0,16},{8,24},{16,0},{24,8},{1,17},{9,25},{17,1},{25,9},{2,18},{10... | collective-permute-start | bytes 3538952 | tf_op jit(solution)/shard_map/ppermute | solution.py:55
  932.9 38.6 %collective-permute-start.15 = (bf16[384,1536]{1,0:T(8,128)(2,1)S(1)}, bf16[384,1536]{1,0:T(8,128)(2,1)S(1)}, u32[]{:S(2)}, u32[]{:S(2)}) collective-permute-start(bf16[384,1536]{1,0:T(8,128)(2,1)S(1)} %add_convert_fusion.1), channel_id=1, source_target_pairs={{0,1},{9,8},{18,19},{27,26},{4,5},{13,12},{22,23},{31,30}} | collective-permute-start | bytes 3538952 | tf_op jit(solution)/shard_map/ppermute | solution.py:910
  934.5 37.0 %collective-permute-start.16 = (bf16[384,1536]{1,0:T(8,128)(2,1)S(1)}, bf16[384,1536]{1,0:T(8,128)(2,1)S(1)}, u32[]{:S(2)}, u32[]{:S(2)}) collective-permute-start(bf16[384,1536]{1,0:T(8,128)(2,1)S(1)} %add_convert_fusion.1), channel_id=1, source_target_pairs={{0,2},{9,11},{18,16},{27,25},{4,6},{13,15},{22,20},{31,29}} | collective-permute-start | bytes 3538952 | tf_op jit(solution)/shard_map/ppermute | solution.py:910
  936.2 35.4 %collective-permute-start.17 = (bf16[384,1536]{1,0:T(8,128)(2,1)S(1)}, bf16[384,1536]{1,0:T(8,128)(2,1)S(1)}, u32[]{:S(2)}, u32[]{:S(2)}) collective-permute-start(bf16[384,1536]{1,0:T(8,128)(2,1)S(1)} %add_convert_fusion.1), channel_id=1, source_target_pairs={{0,3},{9,10},{18,17},{27,24},{4,7},{13,14},{22,21},{31,28}} | collective-permute-start | bytes 3538952 | tf_op jit(solution)/shard_map/ppermute | solution.py:910
  (35 other events, 89.2 us)

commit v3 on v2

--- a/solution.py
+++ b/solution.py
@@ -148,10 +148,10 @@
     return row == slot_row
 
 
-def experts_kernel(me_ref, routes_ref, router_ref, gate_up_ref, down_ref, *refs):
-    blocks, refs = refs[:8], refs[8:]
+def experts_kernel(me_ref, router_ref, gate_up_ref, down_ref, *refs):
+    blocks, routes, refs = refs[:8], refs[8:16], refs[16:]
     parts, refs = refs[:8], refs[8:]
-    arrived_ref, lin_ref, weighted_ref, slot_ref, gate_ref, sel, made = refs
+    arrived_ref, lin_ref, weighted_ref, slot_ref, gate_ref, count_ref, sel, made = refs
     step = pl.program_id(0)
     tok, width = blocks[0].shape
 
@@ -164,9 +164,11 @@
             lax.broadcasted_iota(jnp.int32, (tok, tok), 0)
             < lax.broadcasted_iota(jnp.int32, (tok, tok), 1)
         ).astype(bf16)
+        count = jnp.zeros(count_ref.shape, jnp.int32)
         for s in range(8):
             logits = dg(router_ref[...], blocks[s][...], NT)
-            names = routes_ref[s]
+            names = routes[s][...]
+            count = count + names[TOP:]
             routed = which == names[0:1, :]
             for k in range(1, TOP):
                 routed = routed | (which == names[k : k + 1, :])
@@ -187,6 +189,7 @@
             gate_ref[s] = jnp.concatenate(picked + [filler], axis=0)
             for i in range(EXP_DEV):
                 sel[s, i * CAP : (i + 1) * CAP, :] = select_rows(slot[i : i + 1, :]).astype(bf16)
+        count_ref[...] = count
 
     at = pl.ds(pl.multiple_of(step * CAP, CAP), CAP)
     for s in range(8):
@@ -211,7 +214,7 @@
             parts[s][...] = dg(sel[s], made[s], TN).astype(bf16)
 
 
-def experts_forward(me, routes_t, router_t, blocks, gate_up_w, down_w):
+def experts_forward(me, routes, router_t, blocks, gate_up_w, down_w):
     tok, width = blocks[0].shape
     cols, half = gate_up_w.shape[2], down_w.shape[1]
     by_expert = lambda w: pl.BlockSpec((8, 1, CAP, w), lambda e, *_: (0, e, 0, 0))
@@ -222,15 +225,16 @@
             num_scalar_prefetch=1,
             grid=(EXP_DEV,),
             in_specs=[
-                whole(routes_t.shape),
                 whole(router_t.shape),
                 pl.BlockSpec((1, width, cols), lambda e, *_: (e, 0, 0)),
                 pl.BlockSpec((1, half, width), lambda e, *_: (e, 0, 0)),
             ]
-            + [whole((tok, width))] * 8,
+            + [whole((tok, width))] * 8
+            + [whole(routes[0].shape)] * 8,
             out_specs=[whole((tok, width))] * 8
             + [by_expert(width), by_expert(cols), by_expert(half)]
-            + [whole((8, 8, tok))] * 2,
+            + [whole((8, 8, tok))] * 2
+            + [whole((8, tok))],
             scratch_shapes=[
                 pltpu.VMEM((8, EXP_DEV * CAP, tok), bf16),
                 pltpu.VMEM((8, EXP_DEV * CAP, width), bf16),
@@ -238,14 +242,15 @@
         ),
         out_shape=[jax.ShapeDtypeStruct((tok, width), bf16)] * 8
         + [rows(width, bf16), rows(cols, f32), rows(half, bf16)]
-        + [jax.ShapeDtypeStruct((8, 8, tok), f32)] * 2,
+        + [jax.ShapeDtypeStruct((8, 8, tok), f32)] * 2
+        + [jax.ShapeDtypeStruct((8, tok), jnp.int32)],
         compiler_params=params(60),
         cost_estimate=pl.CostEstimate(
             flops=11 * 10**9, bytes_accessed=40 * 10**6, transcendentals=10**6
         ),
         name="experts_forward",
-    )(me, routes_t, router_t, gate_up_w, down_w, *blocks)
-    return list(out[:8]), out[8:]
+    )(me, router_t, gate_up_w, down_w, *blocks, *routes)
+    return list(out[:8]), out[8:13], out[13]
 
 
 def experts_back_kernel(me_ref, slot_ref, gate_ref, lin_ref, gate_up_ref, down_ref, *refs):
@@ -401,7 +406,9 @@
             copy.wait_send()
 
 
-def comm_call(kernel, name, number, copies, in_specs, out_specs, out_shape, scratch, cost):
+def comm_call(
+    kernel, name, number, copies, in_specs, out_specs, out_shape, scratch, cost, aliases={}
+):
     return pl.pallas_call(
         kernel,
         in_specs=in_specs,
@@ -412,6 +419,7 @@
             vmem_limit_bytes=60 << 20, collective_id=number, has_side_effects=True
         ),
         cost_estimate=pl.CostEstimate(flops=cost, bytes_accessed=cost, transcendentals=0),
+        input_output_aliases=aliases,
         name=name,
     )
 
@@ -430,83 +438,277 @@
         out[at] = total.astype(out.dtype)
 
 
+def plane_places():
+    z = lax.axis_index("dp")
+    return z, flip(z, 1), lax.rem(z + 2, 4), lax.div(z, 2), lax.rem(z, 2)
+
+
+def stripe(index, size):
+    return pl.ds(pl.multiple_of(index * size, size), size)
+
+
+class WeightsIn:
+    def __init__(self, wire, experts, w_gate_up, w_down, gate_up, down, stage, stage_down, sems):
+        z, beside, opposite, side, low = plane_places()
+        slab, part = w_gate_up.shape[1], gate_up.shape[2] // 2
+        rows = w_down.shape[1]
+        self.wire, self.gate_up, self.slab, self.opposite = wire, gate_up, slab, opposite
+        self.beside = {"dp": beside}
+        self.crossing, self.arriving, self.stores = [], [], []
+
+        def columns(i, which, p):
+            return w_gate_up.at[i, :, stripe(2 * p + which, part)]
+
+        def spot(i, p):
+            return gate_up.at[i, stripe(z, slab), pl.ds(p * part, part)]
+
+        self.loads = loads = []
+        for n, i in enumerate(experts):
+            for p in range(2):
+                loads.append(
+                    pltpu.make_async_copy(
+                        columns(i, side, p),
+                        stage.at[n, :, pl.ds(p * part, part)],
+                        sems.at[n, p],
+                    )
+                )
+            loads.append(pltpu.make_async_copy(w_down.at[i], stage_down.at[n], sems.at[n, 2]))
+            for load in loads[-3:]:
+                load.start()
+            self.crossing.append(
+                (
+                    i,
+                    [
+                        wire.start(columns(i, 1 - side, p), spot(i, p), {"dp": opposite})
+                        for p in range(2)
+                    ],
+                )
+            )
+            for p in range(2):
+                self.arriving.append(wire.start(columns(i, side, p), spot(i, p), self.beside))
+            here = down.at[i, stripe(low, rows)]
+            self.arriving.append(wire.start(w_down.at[i], here, self.beside))
+            self.stores.append(
+                pltpu.make_async_copy(
+                    stage.at[n], gate_up.at[i, stripe(z, slab)], sems.at[n, 3]
+                )
+            )
+            self.stores.append(pltpu.make_async_copy(stage_down.at[n], here, sems.at[n, 4]))
+
+    def finish(self):
+        for load in self.loads:
+            load.wait()
+        for store in self.stores:
+            store.start()
+        for i, copies in self.crossing:
+            for copy in copies:
+                copy.wait_recv()
+            piece = self.gate_up.at[i, stripe(self.opposite, self.slab)]
+            self.arriving.append(self.wire.start(piece, piece, self.beside))
+        for copy in self.arriving:
+            copy.wait_recv()
+        for store in self.stores:
+            store.wait()
+
+
+def weights_scratch(count, slab, columns, rows, width):
+    return [
+        pltpu.VMEM((count, slab, columns), bf16),
+        pltpu.VMEM((count, rows, width), bf16),
+        pltpu.SemaphoreType.DMA((count, 5)),
+    ]
+
+
+class GradsOut:
+    def __init__(self, wire, i, grad_gate_up, grad_down, out, out_down, got, own, downs, sems):
+        z, beside, opposite, side, low = plane_places()
+        slab, rows = out.shape[0], out_down.shape[0]
+        self.wire, self.side, self.across = wire, side, {"dp": opposite}
+        self.out, self.out_down, self.got, self.own, self.downs = out, out_down, got, own, downs
+
+        def slab_of(plane):
+            return grad_gate_up.at[i, stripe(plane, slab)]
+
+        def rows_of(which):
+            return grad_down.at[i, stripe(which, rows)]
+
+        to = {"dp": beside}
+        self.loads = [
+            pltpu.make_async_copy(slab_of(opposite), own.at[0], sems.at[0]),
+            pltpu.make_async_copy(slab_of(z), own.at[1], sems.at[1]),
+            pltpu.make_async_copy(rows_of(low), downs.at[0], sems.at[2]),
+        ]
+        for load in self.loads:
+            load.start()
+        self.copies = [
+            wire.start(slab_of(flip(opposite, 1)), got.at[0], to),
+            wire.start(slab_of(beside), got.at[1], to),
+            wire.start(rows_of(1 - low), downs.at[1], to),
+        ]
+
+    def cross(self):
+        self.loads[0].wait()
+        self.copies[0].wait_recv()
+        slab = self.out.shape[0]
+        add_into(slab, self.own.at[2], self.own.at[0], self.got.at[0])
+        self.copies.append(self.wire.start(self.own.at[2], self.got.at[2], self.across))
+
+    def finish(self):
+        part = self.out.shape[1] // 4
+        slab = self.out.shape[0]
+        self.loads[1].wait()
+        self.copies[1].wait_recv()
+        self.copies[3].wait_recv()
+        out, got, own, side = self.out, self.got, self.own, self.side
+
+        @pl.loop(0, slab // 32)
+        def _(r):
+            at = pl.ds(pl.multiple_of(r * 32, 32), 32)
+            for p in range(2):
+                lanes = pl.ds(p * part, part)
+                total = own[1, at, lanes].astype(f32) + got[1, at, lanes].astype(f32)
+                out[at, stripe(2 * p + side, part)] = total.astype(bf16)
+                out[at, stripe(2 * p + 1 - side, part)] = got[2, at, lanes]
+
+        self.loads[2].wait()
+        self.copies[2].wait_recv()
+        add_into(self.out_down.shape[0], self.out_down, self.downs.at[0], self.downs.at[1])
+
+
+def grads_scratch(slab, columns, rows, width):
+    return [
+        pltpu.VMEM((3, slab, columns), bf16),
+        pltpu.VMEM((3, slab, columns), bf16),
+        pltpu.VMEM((2, rows, width), bf16),
+        pltpu.SemaphoreType.DMA((3,)),
+    ]
+
+
+def grads_shapes(grad_gate_up, grad_down):
+    slab, columns = grad_gate_up.shape[1] // 4, grad_gate_up.shape[2]
+    rows, width = grad_down.shape[1] // 2, grad_down.shape[2]
+    return (
+        [jax.ShapeDtypeStruct((slab, 2 * columns), bf16), jax.ShapeDtypeStruct((rows, width), bf16)],
+        grads_scratch(slab, columns, rows, width),
+    )
+
+
 def neighbours(half):
     e, z = lax.axis_index("expert"), lax.axis_index("dp")
     across = lax.rem(z + half, lax.axis_size("dp"))
     return [{"expert": flip(e, m)} for m in (1, 2, 4)] + [{"dp": across}]
 
 
-def exchange_plane(wire, partners, x_ref, near, far):
+class Several:
+    def __init__(self, copies):
+        self.copies = copies
+
+    def wait_recv(self):
+        for copy in self.copies:
+            copy.wait_recv()
+
+
+def exchange_plane(wire, partners, near, far, begin=None):
     core, side_x, side_y, across = partners
-    cut = x_ref.shape[0] // 2
-    low, high = pl.ds(0, cut), pl.ds(cut, cut)
-
-    def direct(b, at):
-        return (
-            wire.start(b[0].at[at], b[2].at[at], side_x),
-            wire.start(b[0].at[at], b[4].at[at], side_y),
-        )
-
-    z_low = wire.start(x_ref.at[low], far[0].at[low], across)
-    z_high = wire.start(x_ref.at[high], far[0].at[high], across)
-    near_x_low = wire.start(near[0].at[low], near[2].at[low], side_x)
-    near_y_high = wire.start(near[0].at[high], near[4].at[high], side_y)
-    near_x_high = wire.start(near[0].at[high], near[2].at[high], side_x)
-    near_y_low = wire.start(near[0].at[low], near[4].at[low], side_y)
-    last = [wire.start(near[0], near[1], core)]
+
+    def cut(ref, h):
+        rows = ref.shape[0] // 2
+        return ref.at[pl.ds(h * rows, rows)]
+
+    def start(src, dst, to, h=None):
+        if h is not None:
+            src, dst = [[cut(ref, h) for ref in refs] for refs in (src, dst)]
+        return Several([wire.start(x, y, to) for x, y in zip(src, dst)])
+
+    z_low = start(near[0], far[0], across, 0)
+    z_high = start(near[0], far[0], across, 1)
+    near_x_low = start(near[0], near[2], side_x, 0)
+    near_y_high = start(near[0], near[4], side_y, 1)
+    near_x_high = start(near[0], near[2], side_x, 1)
+    near_y_low = start(near[0], near[4], side_y, 0)
+    last = [start(near[0], near[1], core)]
+    cargo = begin() if begin else None
     near_x_low.wait_recv()
-    near_diag_low = wire.start(near[2].at[low], near[6].at[low], side_y)
+    near_diag_low = start(near[2], near[6], side_y, 0)
     near_y_high.wait_recv()
-    near_diag_high = wire.start(near[4].at[high], near[6].at[high], side_x)
+    near_diag_high = start(near[4], near[6], side_x, 1)
     near_x_high.wait_recv()
-    last.append(wire.start(near[2], near[3], core))
+    last.append(start(near[2], near[3], core))
     near_y_low.wait_recv()
-    last.append(wire.start(near[4], near[5], core))
+    last.append(start(near[4], near[5], core))
     z_low.wait_recv()
-    far_x_low, far_y_low = direct(far, low)
+    far_x_low = start(far[0], far[2], side_x, 0)
+    far_y_low = start(far[0], far[4], side_y, 0)
     near_diag_low.wait_recv()
     near_diag_high.wait_recv()
-    last.append(wire.start(near[6], near[7], core))
+    last.append(start(near[6], near[7], core))
     z_high.wait_recv()
-    far_x_high, far_y_high = direct(far, high)
-    last.append(wire.start(far[0], far[1], core))
+    far_x_high = start(far[0], far[2], side_x, 1)
+    far_y_high = start(far[0], far[4], side_y, 1)
+    last.append(start(far[0], far[1], core))
     far_x_low.wait_recv()
-    far_diag_low = wire.start(far[2].at[low], far[6].at[low], side_y)
+    far_diag_low = start(far[2], far[6], side_y, 0)
     far_y_low.wait_recv()
     far_y_high.wait_recv()
-    far_diag_high = wire.start(far[4].at[high], far[6].at[high], side_x)
-    last.append(wire.start(far[4], far[5], core))
+    far_diag_high = start(far[4], far[6], side_x, 1)
+    last.append(start(far[4], far[5], core))
     far_x_high.wait_recv()
-    last.append(wire.start(far[2], far[3], core))
+    last.append(start(far[2], far[3], core))
     far_diag_low.wait_recv()
     far_diag_high.wait_recv()
-    last.append(wire.start(far[6], far[7], core))
+    last.append(start(far[6], far[7], core))
     for copy in last:
         copy.wait_recv()
-
-
-def plane_gather_kernel(half, x_ref, *refs):
-    wire = Wire(*refs[15:])
+    if cargo:
+        cargo.finish()
+
+
+def plane_gather_kernel(half, experts, count, *refs):
+    inputs, refs = refs[:count], refs[count:]
+    if experts:
+        (w_gate_up, w_down), refs = refs[:2], refs[4:]
+    outs, refs = refs[: 15 * count], refs[15 * count :]
+    near = [list(inputs)] + [list(outs[j * count : (j + 1) * count]) for j in range(7)]
+    far = [list(outs[j * count : (j + 1) * count]) for j in range(7, 15)]
+    wire = Wire(*refs[-2:])
     partners = neighbours(half)
-    greet(partners)
-    exchange_plane(wire, partners, x_ref, (x_ref,) + refs[:7], refs[7:15])
+    begin = None
+    if experts:
+        greet(partners + [{"dp": plane_places()[1]}])
+        begin = lambda: WeightsIn(wire, experts, w_gate_up, w_down, *refs[:5])
+    else:
+        greet(partners)
+    exchange_plane(wire, partners, near, far, begin)
     wire.finish()
 
 
-def plane_gather(x, half, number, name):
-    block = jax.ShapeDtypeStruct(x.shape, x.dtype)
+def plane_gather(inputs, half, number, name, experts=(), weights=(), filled=()):
+    count, size = len(inputs), inputs[0].size
+    blocks = [jax.ShapeDtypeStruct(x.shape, x.dtype) for x in inputs]
+    scratch, aliases = [], {}
+    if experts:
+        (w_gate_up, w_down), (gate_up, down) = weights, filled
+        scratch = weights_scratch(
+            len(experts), w_gate_up.shape[1], gate_up.shape[2], w_down.shape[1], down.shape[2]
+        )
+        aliases = {count + 2: 15 * count, count + 3: 15 * count + 1}
     out = comm_call(
-        functools.partial(plane_gather_kernel, half),
+        functools.partial(plane_gather_kernel, half, experts, count),
         name,
         number,
-        22,
-        [ANYWHERE],
-        [ANYWHERE] * 15,
-        [block] * 15,
-        [],
-        50 * x.size,
-    )(x)
-    return [x] + list(out[:7]), list(out[7:])
+        22 * count + 6 * len(experts),
+        [ANYWHERE] * (count + len(weights) + len(filled)),
+        [ANYWHERE] * (15 * count + len(filled)),
+        blocks * 15 + [jax.ShapeDtypeStruct(x.shape, x.dtype) for x in filled],
+        scratch,
+        80 * size,
+        aliases,
+    )(*inputs, *weights, *filled)
+    pairs = []
+    for n, x in enumerate(inputs):
+        own = out[n : 15 * count : count]
+        pairs.append(([x] + list(own[:7]), list(own[7:])))
+    return pairs, out[15 * count :]
 
 
 def plane_scatter_kernel(half, *refs):
@@ -606,28 +808,38 @@
     )(*near, *far)
 
 
-def seq_gather_kernel(group, x_ref, out, send_sem, recv_sem):
-    wire = Wire(send_sem, recv_sem)
+def chip_partners():
     e = lax.axis_index("expert")
-    head = lax.rem(e, group)
-    core, side_x = [{"expert": flip(e, m)} for m in (1, 2)]
+    return [{"expert": flip(e, m)} for m in (1, 2)]
+
+
+def exchange_seq(wire, group, x_ref, out, between=None):
+    head = lax.rem(lax.axis_index("expert"), group)
+    core, side_x = chip_partners()
     rows = x_ref.shape[0]
     cut = rows // 2
     mine = pl.multiple_of(head * rows, rows)
     other = pl.multiple_of(flip(head, 2) * rows, rows)
-    greet([core, side_x])
     crossing = [
         wire.start(x_ref.at[pl.ds(h * cut, cut)], out.at[pl.ds(mine + h * cut, cut)], side_x)
         for h in range(2)
     ]
     last = [wire.start(x_ref, out.at[pl.ds(mine, rows)], core)]
     out[pl.ds(mine, rows), :] = x_ref[...]
+    if between:
+        between()
     for h in range(2):
         crossing[h].wait_recv()
         piece = out.at[pl.ds(other + h * cut, cut)]
         last.append(wire.start(piece, piece, core))
     for copy in last:
         copy.wait_recv()
+
+
+def seq_gather_kernel(group, x_ref, out, send_sem, recv_sem):
+    wire = Wire(send_sem, recv_sem)
+    greet(chip_partners())
+    exchange_seq(wire, group, x_ref, out)
     wire.finish()
 
 
@@ -646,18 +858,15 @@
     )(x)
 
 
-def seq_scatter_kernel(group, x_ref, out, core_in, sums, last_in, send_sem, recv_sem):
-    wire = Wire(send_sem, recv_sem)
-    e = lax.axis_index("expert")
-    head = lax.rem(e, group)
-    core, side_x = [{"expert": flip(e, m)} for m in (1, 2)]
+def sum_seq(wire, group, x_ref, out, core_in, sums, last_in):
+    head = lax.rem(lax.axis_index("expert"), group)
+    core, side_x = chip_partners()
     rows = out.shape[0]
     cut = rows // 2
 
     def part(block, h):
         return x_ref.at[pl.ds(pl.multiple_of(block * rows + h * cut, cut), cut)]
 
-    greet([core, side_x])
     crossing = [
         wire.start(part(flip(flip(head, 2), 1), h), core_in.at[1, h], core) for h in range(2)
     ]
@@ -673,12 +882,26 @@
         add_into(
             cut, out.at[pl.ds(h * cut, cut)], part(head, h), core_in.at[0, h], last_in.at[h]
         )
+
+
+def seq_scatter_kernel(group, x_ref, out, core_in, sums, last_in, send_sem, recv_sem):
+    wire = Wire(send_sem, recv_sem)
+    greet(chip_partners())
+    sum_seq(wire, group, x_ref, out, core_in, sums, last_in)
     wire.finish()
+
+
+def seq_scratch(rows, width):
+    piece = (rows // 2, width)
+    return [
+        pltpu.VMEM((2, 2) + piece, bf16),
+        pltpu.VMEM((2,) + piece, bf16),
+        pltpu.VMEM((2,) + piece, bf16),
+    ]
 
 
 def seq_scatter(x, group, number, name):
     rows, width = x.shape[0] // group, x.shape[1]
-    piece = (rows // 2, width)
     return comm_call(
         functools.partial(seq_scatter_kernel, group),
         name,
@@ -687,49 +910,211 @@
         [ON_CHIP],
         ON_CHIP,
         jax.ShapeDtypeStruct((rows, width), f32),
-        [
-            pltpu.VMEM((2, 2) + piece, bf16),
-            pltpu.VMEM((2,) + piece, bf16),
-            pltpu.VMEM((2,) + piece, bf16),
-        ],
+        seq_scratch(rows, width),
         20 * rows * width,
     )(x)
 
 
-def start_kernel(half, replicas, x_ref, small_ref, *refs):
-    near, far, small_out = (x_ref,) + refs[:7], refs[7:15], refs[15]
-    wire = Wire(*refs[16:])
+def entry_kernel(group, x_ref, qkv_in, out_in, seq, qkv, out_slice, send_sem, recv_sem):
+    wire = Wire(send_sem, recv_sem)
+    e, z = lax.axis_index("expert"), lax.axis_index("dp")
+    head, row = lax.rem(e, group), lax.div(e, group)
+    side_y = {"expert": flip(e, 4)}
+    block = [lax.rem(z + k, 4) for k in range(4)]
+    planes = [{"dp": b} for b in block]
+    slab = qkv_in.shape[0]
+    cut = slab // 2
+    greet(chip_partners() + [side_y] + planes[1:])
+    mine = pl.ds(pl.multiple_of(row * cut, cut), cut)
+
+    def spot(plane):
+        return qkv.at[pl.ds(pl.multiple_of(plane * slab + row * cut, cut), cut)]
+
+    from_z = [wire.start(qkv_in.at[mine], spot(z), planes[k]) for k in (1, 2, 3)]
+    owner = z == head
+
+    def out_copy(n, to, at):
+        return pltpu.make_async_remote_copy(
+            src_ref=out_in.at[at] if n < 3 else out_slice.at[at],
+            dst_ref=out_slice.at[at],
+            send_sem=send_sem.at[12 + n],
+            recv_sem=recv_sem.at[12 if n < 3 else 13],
+            device_id=to,
+            device_id_type=MESH,
+        )
+
+    spread = [out_copy(k - 1, planes[k], mine) for k in (1, 2, 3)]
+    swap = out_copy(3, side_y, mine)
+
+    @pl.when(owner)
+    def _():
+        for copy in spread:
+            copy.start()
+        out_slice[...] = out_in[...]
+
+    qkv[pl.ds(pl.multiple_of(z * slab, slab), slab), :] = qkv_in[...]
+    from_y = []
+
+    def relay():
+        for k in (1, 3, 2):
+            from_z[k - 1].wait_recv()
+            piece = spot(block[4 - k])
+            from_y.append(wire.start(piece, piece, side_y))
+
+    exchange_seq(wire, group, x_ref, seq, relay)
+    for copy in from_y:
+        copy.wait_recv()
+
+    @pl.when(owner)
+    def _():
+        for copy in spread:
+            copy.wait_send()
+
+    @pl.when(jnp.logical_not(owner))
+    def _():
+        spread[0].wait_recv()
+        swap.start()
+        swap.wait()
+
+    wire.finish()
+
+
+def attention_entry(x, qkv_slice, w_out, group):
+    rows, width = x.shape
+    slab, columns = qkv_slice.shape
+    return comm_call(
+        functools.partial(entry_kernel, group),
+        "attention_entry",
+        8,
+        16,
+        [ON_CHIP] * 3,
+        [ON_CHIP] * 3,
+        [
+            jax.ShapeDtypeStruct((group * rows, width), bf16),
+            jax.ShapeDtypeStruct((4 * slab, columns), bf16),
+            jax.ShapeDtypeStruct((slab, width), bf16),
+        ],
+        [],
+        40 * x.size,
+    )(x, qkv_slice, w_out)
+
+
+def scatter_weights_kernel(group, experts, x_ref, w_gate_up, w_down, out, gate_up, down, *refs):
+    wire = Wire(*refs[6:])
+    _, beside, opposite, _, _ = plane_places()
+    greet(chip_partners() + [{"dp": beside}, {"dp": opposite}])
+    cargo = WeightsIn(wire, experts, w_gate_up, w_down, gate_up, down, *refs[3:6])
+    sum_seq(wire, group, x_ref, out, *refs[:3])
+    cargo.finish()
+    wire.finish()
+
+
+def seq_scatter_weights(x, group, experts, w_gate_up, w_down):
+    rows, width = x.shape[0] // group, x.shape[1]
+    count, slab, columns = w_gate_up.shape
+    ff_rows = w_down.shape[1]
+    return comm_call(
+        functools.partial(scatter_weights_kernel, group, experts),
+        "scatter_branch_weights",
+        9,
+        6 + 6 * len(experts),
+        [ON_CHIP, ANYWHERE, ANYWHERE],
+        [ON_CHIP, ANYWHERE, ANYWHERE],
+        [
+            jax.ShapeDtypeStruct((rows, width), f32),
+            jax.ShapeDtypeStruct((count, 4 * slab, columns // 2), bf16),
+            jax.ShapeDtypeStruct((count, 2 * ff_rows, width), bf16),
+        ],
+        seq_scratch(rows, width)
+        + weights_scratch(len(experts), slab, columns // 2, ff_rows, width),
+        40 * rows * width,
+    )(x, w_gate_up, w_down)
+
+
+def gather_grads_kernel(group, i, x_ref, grad_gate_up, grad_down, seq, out, out_down, *refs):
+    wire = Wire(*refs[4:])
+    _, beside, opposite, _, _ = plane_places()
+    greet(chip_partners() + [{"dp": beside}, {"dp": opposite}])
+    cargo = GradsOut(wire, i, grad_gate_up, grad_down, out, out_down, *refs[:4])
+    exchange_seq(wire, group, x_ref, seq, cargo.cross)
+    cargo.finish()
+    wire.finish()
+
+
+def seq_gather_grads(x, group, i, grad_gate_up, grad_down):
+    rows, width = x.shape
+    shapes, scratch = grads_shapes(grad_gate_up, grad_down)
+    return comm_call(
+        functools.partial(gather_grads_kernel, group, i),
+        "gather_branch_grads",
+        10,
+        9,
+        [ON_CHIP, ANYWHERE, ANYWHERE],
+        [ON_CHIP] * 3,
+        [jax.ShapeDtypeStruct((group * rows, width), x.dtype)] + shapes,
+        scratch,
+        40 * x.size,
+    )(x, grad_gate_up, grad_down)
+
+
+def scatter_grads_kernel(group, i, x_ref, grad_gate_up, grad_down, total, out, out_down, *refs):
+    wire = Wire(*refs[7:])
+    _, beside, opposite, _, _ = plane_places()
+    greet(chip_partners() + [{"dp": beside}, {"dp": opposite}])
+    cargo = GradsOut(wire, i, grad_gate_up, grad_down, out, out_down, *refs[3:7])
+    sum_seq(wire, group, x_ref, total, *refs[:3])
+    cargo.cross()
+    cargo.finish()
+    wire.finish()
+
+
+def seq_scatter_grads(x, group, i, grad_gate_up, grad_down):
+    rows, width = x.shape[0] // group, x.shape[1]
+    shapes, scratch = grads_shapes(grad_gate_up, grad_down)
+    return comm_call(
+        functools.partial(scatter_grads_kernel, group, i),
+        "scatter_normed_grads",
+        11,
+        10,
+        [ON_CHIP, ANYWHERE, ANYWHERE],
+        [ON_CHIP] * 3,
+        [jax.ShapeDtypeStruct((rows, width), f32)] + shapes,
+        seq_scratch(rows, width) + scratch,
+        40 * rows * width,
+    )(x, grad_gate_up, grad_down)
+
+
+def start_kernel(replicas, small_ref, small_out, send_sem, recv_sem):
+    wire = Wire(send_sem, recv_sem)
     z = lax.axis_index("dp")
-    partners = neighbours(half)
     planes = [{"dp": lax.rem(z + k, replicas)} for k in range(1, replicas)]
-    greet(partners[:3] + planes)
+    greet(planes)
     spread = [wire.start(small_ref, small_out.at[z], plane) for plane in planes]
     small_out[z] = small_ref[...]
-    exchange_plane(wire, partners, x_ref, near, far)
     for copy in spread:
         copy.wait_recv()
     wire.finish()
 
 
-def start_exchange(x, small, half, replicas):
-    block = jax.ShapeDtypeStruct(x.shape, x.dtype)
-    out = comm_call(
-        functools.partial(start_kernel, half, replicas),
+def start_exchange(small, replicas):
+    return comm_call(
+        functools.partial(start_kernel, replicas),
         "start_exchange",
         1,
-        22 + replicas - 1,
-        [ANYWHERE, ON_CHIP],
-        [ANYWHERE] * 15 + [ON_CHIP],
-        [block] * 15 + [jax.ShapeDtypeStruct((replicas,) + small.shape, small.dtype)],
+        replicas - 1,
+        [ON_CHIP],
+        ON_CHIP,
+        jax.ShapeDtypeStruct((replicas,) + small.shape, small.dtype),
         [],
         10**6,
-    )(x, small)
-    return [x] + list(out[:7]), list(out[7:15]), out[15]
-
-
-def dense_kernel(replicas, grads, small, out, small_out, *refs):
+    )(small)
+
+
+def dense_kernel(
+    replicas, i, grads, small, grad_gate_up, grad_down, out, small_out, cargo_out, cargo_down, *refs
+):
     y_in, z_out, z_in, small_in, small_sum, turn_in = refs[:6]
-    wire = Wire(*refs[6:])
+    wire = Wire(*refs[10:])
     e, z = lax.axis_index("expert"), lax.axis_index("dp")
     head, row = lax.rem(e, 4), lax.div(e, 4)
     partners = [{"expert": flip(e, m)} for m in (1, 2, 4)]
@@ -747,6 +1132,7 @@
 
     small_copies = [wire.start(small.at[block[k]], small_in.at[k - 1], plane[k]) for k in plane]
     from_y = {k: wire.start(half_of(k, 1 - row), y_in.at[k], side_y) for k in order}
+    cargo = GradsOut(wire, i, grad_gate_up, grad_down, cargo_out, cargo_down, *refs[6:10])
     for copy in small_copies:
         copy.wait_recv()
     small_sum[0] = small[z] + small_in[0] + small_in[1] + small_in[2]
@@ -767,6 +1153,7 @@
             turn = wire.start(small_sum.at[2], turn_in.at[2], side_y)
     turn.wait_recv()
     small_out[...] = small_sum[2] + turn_in[2]
+    cargo.cross()
     for k in from_z:
         from_z[k].wait_recv()
 
@@ -797,21 +1184,23 @@
     last.append(wire.start(place(other, 1 - row), place(other, 1 - row), core))
     for copy in last:
         copy.wait_recv()
+    cargo.finish()
     wire.finish()
 
 
-def dense_reduce(grads, small, replicas):
+def dense_reduce(grads, small, replicas, i, grad_gate_up, grad_down):
     slab, width = grads.shape[0] // replicas, grads.shape[1]
     piece = (slab // 2, width)
     lot = small.shape[1:]
+    shapes, scratch = grads_shapes(grad_gate_up, grad_down)
     return comm_call(
-        functools.partial(dense_kernel, replicas),
+        functools.partial(dense_kernel, replicas, i),
         "dense_reduce",
         2,
-        23,
-        [ON_CHIP] * 2,
-        [ON_CHIP] * 2,
-        [jax.ShapeDtypeStruct((slab, 4 * width), bf16), jax.ShapeDtypeStruct(lot, f32)],
+        27,
+        [ON_CHIP] * 2 + [ANYWHERE] * 2,
+        [ON_CHIP] * 4,
+        [jax.ShapeDtypeStruct((slab, 4 * width), bf16), jax.ShapeDtypeStruct(lot, f32)] + shapes,
         [
             pltpu.VMEM((4,) + piece, bf16),
             pltpu.VMEM((4,) + piece, bf16),
@@ -819,9 +1208,10 @@
             pltpu.VMEM((3,) + lot, f32),
             pltpu.VMEM((3,) + lot, f32),
             pltpu.VMEM((3,) + lot, f32),
-        ],
+        ]
+        + scratch,
         10**8,
-    )(grads, small)
+    )(grads, small, grad_gate_up, grad_down)
 
 
 def body(
@@ -873,91 +1263,34 @@
     small = jnp.concatenate(
         [gain_attn[None], gain_moe[None], jnp.transpose(w_router), jnp.zeros((6, slab), bf16)]
     )
-    near_names, far_names, small = start_exchange(
-        jnp.concatenate([routes_t, count]), small, half, replicas
-    )
+    names = jnp.concatenate([routes_t, count])
+    small = start_exchange(small, replicas)
     small = jnp.transpose(small, (1, 0, 2)).reshape(small.shape[1], width)
     gain_one, gain_two, router_t = small[0], small[1], small[2 : 2 + experts_all]
-    near_routes = jnp.stack([r[:TOP] for r in near_names])
-    far_routes = jnp.stack([r[:TOP] for r in far_names])
     me_ref = jnp.reshape(me, (1,)).astype(jnp.int32)
     valid_float = valid.astype(f32)
-    valid_count = sum(r[TOP, :1] for r in near_names + far_names)
-    mask = 1
-    while mask < half:
-        valid_count = valid_count + send(valid_count, "dp", mask)
-        mask *= 2
-    valid_count = valid_count[0].astype(f32)
-    hold = (valid_count < 0).astype(jnp.int32)
     qkv_slice = jnp.concatenate(
         [
-            pick(w_query, head + hold, q_cols, 1),
-            pick(w_key, head + hold, kv_cols, 1),
-            pick(w_value, head + hold, kv_cols, 1),
+            pick(w_query, head, q_cols, 1),
+            pick(w_key, head, kv_cols, 1),
+            pick(w_value, head, kv_cols, 1),
         ],
         axis=1,
     )
-    qkv = over_dp(qkv_slice, 0)
-
     inputs = hidden_in.astype(f32)
     normed_f, norm_one_pull = jax.vjp(rms_norm, inputs, gain_one.astype(f32))
     normed = normed_f.astype(bf16)
-    seq = seq_gather(normed, group, 3, "gather_normed")
-    hold = never(seq[0, 0])
-    w_out, w_down = [jnp.where(hold == 0, w, jnp.zeros((), bf16)) for w in (w_out, w_down)]
+    compact = replicas == group
 
     def on_grid(x, pairs):
         return lax.ppermute(x, ("dp", "expert"), pairs)
 
-    if replicas == group:
-        out_slice = jnp.where(plane == head, w_out, jnp.zeros((), bf16))
-        for step in range(1, replicas):
-            pairs = [
-                (
-                    (i % group) * owners + i,
-                    ((i % group + step) % replicas) * owners + i,
-                )
-                for i in range(owners)
-            ]
-            out_slice = out_slice + on_grid(w_out, pairs)
+    if compact:
+        seq, qkv, out_slice = attention_entry(normed, qkv_slice, w_out, group)
     else:
+        seq = seq_gather(normed, group, 3, "gather_normed")
+        qkv = over_dp(qkv_slice, 0)
         out_slice = pick(lax.all_gather(w_out, "dp", axis=0, tiled=True), head, q_cols, 0)
-
-    def columns(which):
-        return jnp.concatenate(
-            [
-                pick(w_gate_up[:, :, :FF], which, ff_half, 2),
-                pick(w_gate_up[:, :, FF:], which, ff_half, 2),
-            ],
-            axis=2,
-        )
-
-    mine = columns(side + hold)
-    if replicas > group:
-        gate_up_w = jnp.where(
-            side == 0,
-            lax.all_gather(columns(0), "dp", axis=1, tiled=True),
-            lax.all_gather(columns(1), "dp", axis=1, tiled=True),
-        )
-        down_w = pick(lax.all_gather(w_down, "dp", axis=1, tiled=True), side, ff_half, 1)
-    else:
-        other = send(columns(1 - side + hold), "dp", half)
-        gate_up_w = place(
-            [mine, other]
-            + [send(mine, "dp", m) for m in range(1, half)]
-            + [send(other, "dp", m) for m in range(1, half)],
-            [plane, plane ^ half]
-            + [plane ^ m for m in range(1, half)]
-            + [plane ^ half ^ m for m in range(1, half)],
-            1,
-            replicas,
-        )
-        down_w = place(
-            [w_down] + [send(w_down, "dp", m) for m in range(1, half)],
-            [(plane % half) ^ m for m in range(half)],
-            1,
-            half,
-        )
 
     lin = mm("td,dc->tc", seq, qkv)
     cosine, sine = rope_tables(jnp.arange(length, dtype=f32))
@@ -973,13 +1306,44 @@
     context, log_total = attend(queries, keys, values)
     context = context.reshape(length, q_cols)
     branch = mm("tc,cd->td", context, out_slice).astype(bf16)
-    mid = inputs + RESIDUAL * seq_scatter(branch, group, 4, "scatter_branch")
+    if compact:
+        summed, gate_up_w, down_w = seq_scatter_weights(branch, group, (0,), w_gate_up, w_down)
+    else:
+        summed = seq_scatter(branch, group, 4, "scatter_branch")
+        gate_up_all = lax.all_gather(w_gate_up, "dp", axis=1, tiled=True)
+        gate_up_w = jnp.concatenate(
+            [pick(gate_up_all, p * 2 + side, ff_half, 2) for p in range(2)], axis=2
+        )
+        down_w = pick(lax.all_gather(w_down, "dp", axis=1, tiled=True), side, ff_half, 1)
+    mid = inputs + RESIDUAL * summed
     moe_f, norm_two_pull = jax.vjp(rms_norm, mid, gain_two.astype(f32))
     moe_input = moe_f.astype(bf16)
 
-    near, far = plane_gather(moe_input, half, 5, "gather_tokens")
-    near_parts, near_kept = experts_forward(me_ref, near_routes, router_t, near, gate_up_w, down_w)
-    far_parts, far_kept = experts_forward(me_ref, far_routes, router_t, far, gate_up_w, down_w)
+    if compact:
+        blocks, (gate_up_w, down_w) = plane_gather(
+            [moe_input, names],
+            half,
+            12,
+            "gather_all",
+            (1, 2),
+            (w_gate_up, w_down),
+            (gate_up_w, down_w),
+        )
+    else:
+        blocks, _ = plane_gather([moe_input, names], half, 13, "gather_names")
+    (near, far), (near_names, far_names) = blocks
+    near_parts, near_kept, near_count = experts_forward(
+        me_ref, near_names, router_t, near, gate_up_w, down_w
+    )
+    far_parts, far_kept, far_count = experts_forward(
+        me_ref, far_names, router_t, far, gate_up_w, down_w
+    )
+    valid_count = near_count[0, :1] + far_count[0, :1]
+    mask = 1
+    while mask < half:
+        valid_count = valid_count + send(valid_count, "dp", mask)
+        mask *= 2
+    valid_count = valid_count[0].astype(f32)
     final_state = mid + RESIDUAL * plane_scatter(near_parts, far_parts, half, 6, "scatter_outputs")
     activations = final_state.astype(bf16)
     mismatch = final_state - teacher.astype(f32)
@@ -987,7 +1351,7 @@
     tokens_all = tok * replicas * owners
     grad_final = tokens_all / valid_count * valid_float[:, None] * mismatch
 
-    grad_near, grad_far = plane_gather(grad_final.astype(bf16), half, 5, "gather_tokens")
+    ((grad_near, grad_far),), _ = plane_gather([grad_final.astype(bf16)], half, 5, "gather_tokens")
 
     def back(kept, blocks):
         arrived, lin, weighted, slot, gate = kept
@@ -1002,50 +1366,6 @@
     after = jnp.reshape(never(returned[0, 0]), (1,))
     grad_gate_up, grad_down = expert_weights(after, [near_chunk, far_chunk])
     branch_scale = jnp.where(never(grad_down[0, 0, 0]) == 0, RESIDUAL, 0.0)
-
-    ff_slab = FF // replicas
-    low = plane % half
-    if replicas > group:
-        spread = lambda x: lax.psum_scatter(
-            x.astype(f32), "dp", scatter_dimension=1, tiled=True
-        )
-        blank = jnp.zeros_like(grad_down)
-        down_out = spread(
-            jnp.where(
-                side == 0,
-                jnp.concatenate([grad_down, blank], axis=1),
-                jnp.concatenate([blank, grad_down], axis=1),
-            )
-        )
-        own_side = spread(jnp.where(side == 0, grad_gate_up, jnp.zeros((), bf16)))
-        other_side = spread(jnp.where(side == 1, grad_gate_up, jnp.zeros((), bf16)))
-        near_cols = jnp.where(side == 0, own_side, other_side)
-        far_cols = jnp.where(side == 0, other_side, own_side)
-    else:
-        down_out = pick(grad_down, low, ff_slab, 1).astype(f32)
-        for m in range(1, half):
-            down_out = down_out + send(pick(grad_down, low ^ m, ff_slab, 1), "dp", m).astype(f32)
-        near_cols = pick(grad_gate_up, plane, slab, 1).astype(f32)
-        far_cols = pick(grad_gate_up, plane ^ half, slab, 1).astype(f32)
-        for m in range(1, half):
-            near_cols = near_cols + send(
-                pick(grad_gate_up, plane ^ m, slab, 1), "dp", m
-            ).astype(f32)
-            far_cols = far_cols + send(
-                pick(grad_gate_up, plane ^ half ^ m, slab, 1), "dp", m
-            ).astype(f32)
-        far_cols = send(far_cols.astype(bf16), "dp", half).astype(f32)
-    first = jnp.where(side == 0, near_cols, far_cols)
-    last = jnp.where(side == 0, far_cols, near_cols)
-    gate_up_out = jnp.concatenate(
-        [
-            first[:, :, :ff_half],
-            last[:, :, :ff_half],
-            first[:, :, ff_half:],
-            last[:, :, ff_half:],
-        ],
-        axis=2,
-    )
 
     grad_gates = returned[:, width : width + experts_all]
     own_routed = jnp.any(
@@ -1062,8 +1382,25 @@
     grad_mid = grad_final + grad_mid_norm
     grad_branch = (branch_scale * grad_mid).astype(bf16)
 
-    seq_grad = seq_gather(grad_branch, group, 3, "gather_normed")
+    done = []
+    if compact:
+        seq_grad, *part = seq_gather_grads(grad_branch, group, 0, grad_gate_up, grad_down)
+        done.append(part)
+    else:
+        seq_grad = seq_gather(grad_branch, group, 3, "gather_normed")
     grad_out = mm("tc,td->cd", context, seq_grad).astype(bf16)
+    if compact:
+        out_sum = grad_out.astype(f32)
+        for step in range(1, replicas):
+            pairs = [
+                (
+                    ((i % group + step) % replicas) * owners + i,
+                    (i % group) * owners + i,
+                )
+                for i in range(owners)
+            ]
+            out_sum = out_sum + on_grid(grad_out, pairs).astype(f32)
+        entered = jnp.where(never(out_sum[0, 0]) == 0, 1.0, 0.0)
     grad_context = (
         mm("td,cd->tc", seq_grad, out_slice).astype(bf16).reshape(length, kv_dev, per_kv, HD)
     )
@@ -1079,8 +1416,13 @@
         axis=1,
     ).astype(bf16)
     grad_qkv = mm("td,tc->dc", seq, grad_lin).astype(bf16)
-    normed_parts = mm("tc,dc->td", grad_lin, qkv).astype(bf16)
-    grad_normed = seq_scatter(normed_parts, group, 4, "scatter_branch")
+    normed_parts = mm("tc,dc->td", grad_lin, qkv)
+    normed_parts = (entered * normed_parts if compact else normed_parts).astype(bf16)
+    if compact:
+        grad_normed, *part = seq_scatter_grads(normed_parts, group, 1, grad_gate_up, grad_down)
+        done.append(part)
+    else:
+        grad_normed = seq_scatter(normed_parts, group, 4, "scatter_branch")
     grad_in_norm, grad_gain_one = norm_one_pull(grad_normed)
     grad_in = grad_mid + grad_in_norm
 
@@ -1100,49 +1442,7 @@
             jnp.full((6, width), squares),
         ]
     )
-    if replicas == group:
-        lot = jnp.transpose(lot.reshape(32, replicas, slab), (1, 0, 2))
-        by_head, lot = dense_reduce(grad_qkv, lot, replicas)
-    else:
-        lot = lax.psum_scatter(lot, "dp", scatter_dimension=1, tiled=True)
-        lot = lax.psum(lot, "expert")
-        qkv_sum = lax.psum_scatter(
-            grad_qkv.astype(f32), "dp", scatter_dimension=0, tiled=True
-        )
-        qkv_sum = other_sequences(qkv_sum).astype(bf16)
-        by_head = place(
-            gather_blocks(qkv_sum, group),
-            [head ^ j for j in range(group)],
-            1,
-            group,
-        )
-    def of_heads(first, count):
-        wide = q_cols + 2 * kv_cols
-        return jnp.concatenate(
-            [by_head[:, h * wide + first : h * wide + first + count] for h in range(group)], axis=1
-        ).astype(f32)
-
-    g_query = of_heads(0, q_cols)
-    g_key = of_heads(q_cols, kv_cols)
-    g_value = of_heads(q_cols + kv_cols, kv_cols)
-    g_router, g_one, g_two = (
-        jnp.transpose(lot[:experts_all]),
-        lot[experts_all],
-        lot[experts_all + 1],
-    )
-    loss_value = lot[experts_all + 2, 0] / (valid_count * width)
-
-    if replicas == group:
-        out_sum = grad_out.astype(f32)
-        for step in range(1, replicas):
-            pairs = [
-                (
-                    ((i % group + step) % replicas) * owners + i,
-                    (i % group) * owners + i,
-                )
-                for i in range(owners)
-            ]
-            out_sum = out_sum + on_grid(grad_out, pairs).astype(f32)
+    if compact:
         out_sum = other_sequences(out_sum).astype(bf16)
         g_out = jnp.where(plane == head, out_sum, jnp.zeros((), bf16))
         for m in range(1, group):
@@ -1151,6 +1451,13 @@
             ]
             g_out = g_out + on_grid(out_sum, pairs)
         g_out = g_out.astype(f32)
+        lot = jnp.where(never(out_sum[0, 0]) == 0, lot, 0.0)
+        lot = jnp.transpose(lot.reshape(32, replicas, slab), (1, 0, 2))
+        by_head, lot, *part = dense_reduce(
+            grad_qkv, lot, replicas, 2, grad_gate_up, grad_down
+        )
+        done.append(part)
+        gate_up_out, down_out = [jnp.stack(x).astype(f32) for x in zip(*done)]
     else:
         out_sum = other_sequences(lax.psum(grad_out, "dp")).astype(bf16)
         g_out = pick(
@@ -1161,6 +1468,53 @@
             slab,
             0,
         ).astype(f32)
+        lot = lax.psum_scatter(lot, "dp", scatter_dimension=1, tiled=True)
+        lot = lax.psum(lot, "expert")
+        qkv_sum = lax.psum_scatter(
+            grad_qkv.astype(f32), "dp", scatter_dimension=0, tiled=True
+        )
+        qkv_sum = other_sequences(qkv_sum).astype(bf16)
+        by_head = place(
+            gather_blocks(qkv_sum, group), [head ^ j for j in range(group)], 1, group
+        )
+        spread = lambda x: lax.psum_scatter(
+            x.astype(f32), "dp", scatter_dimension=1, tiled=True
+        )
+        blank = jnp.zeros_like(grad_down)
+        down_out = spread(
+            jnp.where(
+                side == 0,
+                jnp.concatenate([grad_down, blank], axis=1),
+                jnp.concatenate([blank, grad_down], axis=1),
+            )
+        )
+        first = spread(jnp.where(side == 0, grad_gate_up, jnp.zeros((), bf16)))
+        last = spread(jnp.where(side == 1, grad_gate_up, jnp.zeros((), bf16)))
+        gate_up_out = jnp.concatenate(
+            [
+                first[:, :, :ff_half],
+                last[:, :, :ff_half],
+                first[:, :, ff_half:],
+                last[:, :, ff_half:],
+            ],
+            axis=2,
+        )
+
+    def of_heads(first, count):
+        wide = q_cols + 2 * kv_cols
+        return jnp.concatenate(
+            [by_head[:, h * wide + first : h * wide + first + count] for h in range(group)], axis=1
+        ).astype(f32)
+
+    g_query = of_heads(0, q_cols)
+    g_key = of_heads(q_cols, kv_cols)
+    g_value = of_heads(q_cols + kv_cols, kv_cols)
+    g_router, g_one, g_two = (
+        jnp.transpose(lot[:experts_all]),
+        lot[experts_all],
+        lot[experts_all + 1],
+    )
+    loss_value = lot[experts_all + 2, 0] / (valid_count * width)
 
     return (
         activations,

time: 983 us -> 900 us (0.916)
  Pallas kernels: 557 us -> 678 us
  starting transfers between devices: 83.6 us -> 16 us
  waiting for transfers between devices: 65.1 us -> 0.02 us
  local copies, waits for them, and re-layouts: 75.7 us -> 25.7 us
  other arithmetic: 84 us -> 73.8 us
    pallas_call x8, Pallas kernels: 290 us -> 420 us  [the longest x2 153 us: plane_gather(): comm_call(functools.partial(plane_gather_kernel, half, experts, count), n...]
    ppermute x13 -> x2, waiting for transfers between devices: 65 us -> 0.01 us  [send(): return lax.ppermute(x, axis, [(i, i ^ mask) for i in range(count)])]
    ppermute x13 -> x2, starting transfers between devices: 64.5 us -> 5.51 us  [send(): return lax.ppermute(x, axis, [(i, i ^ mask) for i in range(count)])]
    slice x19 -> x4, local copies, waits for them, and re-layouts: 21.9 us -> 3.51 us  [the longest x2 2.45 us: body(): valid_count = near_count[0, :1] + far_count[0, :1]]
    dynamic_update_slice x7 -> x0, local copies, waits for them, and re-layouts: 11.7 us -> none  [place(): out = lax.dynamic_update_slice_in_dim(out, block, start * width, axis)]
  transfers between devices with their start and end apart: 22 -> 8, of which waited for: 5 -> 0; matrix products, arithmetic and copies ran while one was open for 21% -> 10% of each run, Pallas kernels for 17% -> 21%
where the time goes in v3:
time: 900 us; the launch traced here: 894 us
  Pallas kernels  678 us (75%)
  matrix products  89.8 us (10%)
  other arithmetic  73.8 us (8%)
  local copies, waits for them, and re-layouts  25.7 us (3%)
  starting transfers between devices  16 us (2%)
  between operations  10.8 us (1%)
    pallas_call x2, Pallas kernels, plane_gather(): comm_call(functools.partial(plane_gather_kernel, half, experts, count), n...  153 us
    pallas_call x2, Pallas kernels, plane_scatter(): comm_call(functools.partial(plane_scatter_kernel, half), name, number, 42...  139 us
    dot_general x15, matrix products, mm(): return jnp.einsum(spec, a, b, preferred_element_type=f32)  89.8 us
    pallas_call x1, Pallas kernels, dense_reduce(): comm_call(functools.partial(dense_kernel, replicas, i), 'dense_reduce', 2...  68.4 us
    pallas_call x1, Pallas kernels, seq_scatter_weights(): comm_call(functools.partial(scatter_weights_kernel, group, experts), 'sca...  59.7 us
    pallas_call x2, Pallas kernels, experts_backward(): pl.pallas_call(experts_back_kernel, grid_spec=pltpu.PrefetchScalarGridSpe...  51.1 us
    pallas_call x1, Pallas kernels, seq_scatter_grads(): comm_call(functools.partial(scatter_grads_kernel, group, i), 'scatter_nor...  47.8 us
    pallas_call x2, Pallas kernels, experts_forward(): pl.pallas_call(experts_kernel, grid_spec=pltpu.PrefetchScalarGridSpec(num...  47 us
  transfers between devices with their start and end apart: 8, of which 0 were waited for; matrix products, arithmetic and copies ran while one was open for 10% of the time, Pallas kernels for 21%

profile of v3, /device:TPU:0, one launch (start us, length us, event | category | flops | bytes accessed | tf_op | source)
XLA Modules:
  0.0 894.3 jit_solution(18289476083738898786)
XLA Ops:
  2.3 1.4 maximum_maximum_fusion.small_ref
  3.7 9.3 %start_exchange.1 = bf16[4,32,384]{2,1,0:T(8,128)(2,1)} custom-call(bf16[32,384]{1,0:T(8,128)(2,1)} %maximum_maximum_fusion.small_ref), custom_call_target="tpu_custom_call" | custom-call | flops 1000000 | bytes 1000000 | tf_op jit(solution)/shard_map/start_exchange/pallas_call | solution.py:1100
  13.9 1.4 fusion.12
  18.3 41.7 %attention_entry.1 = (bf16[1024,1536]{1,0:T(8,128)(2,1)}, bf16[1536,640]{1,0:T(8,128)(2,1)}, bf16[384,1536]{1,0:T(8,128)(2,1)}) custom-call(bf16[256,1536]{1,0:T(8,128)(2,1)} %fusion.7.x_ref, bf16[384,640]{1,0:T(8,128)(2,1)} %pad_maximum_fusion.7.qkv_in, bf16[384,1536]{1,0:T(8,128)(2,1)} %out_in.1), custom_call_target="tpu_custom_call" | custom-call | flops 15728640 | bytes 15728640 | tf_op jit(solution)/shard_map/attention_entry/pallas_call | solution.py:985
  60.0 4.7 fusion.42
  67.0 1.2 fusion.24
  68.8 10.7 %fusion.4 = (f32[2,3,1024]{2,1,0:T(4,128)S(1)}, f32[2,1024,1024,3]{2,1,3,0:T(8,128)}) fusion(pred[1024,1024]{0,1:T(8,128)(4,1)S(1)} %iota_compare_fusion, bf16[1024,2,3,32]{0,3,2,1:T(8,128)(2,1)S(1)} %bitcast.120, bf16[1024,2,3,32]{0,3,2,1:T(8,128)(2,1)S(1)} %bitcast.118, bf16[1024,2,32]{0,2,1:T(8,128)(2,1)S(1)} %get-tuple-element.273, ...), kind=kOutput, calls=%fused_computation.9 | convolution fusion | flops 826271744 | bytes 27287552 | tf_op jit(solution)/shard_map/qhgd,khd->hgqk/dot_general | solution.py:29
  79.5 11.4 %exponential_reduce_fusion = f32[2,3,1024]{2,1,0:T(4,128)S(1)} fusion(f32[2,1024,1024,3]{2,1,3,0:T(8,128)} %get-tuple-element.280, f32[2,3,1024]{2,1,0:T(4,128)S(1)} %get-tuple-element.279, pred[1024,1024]{0,1:T(8,128)(4,1)S(1)} %iota_compare_fusion), kind=kLoop, calls=%fused_computation.7 | loop fusion | flops 25159680 | bytes 26263552 | tf_op jit(solution)/shard_map/reduce_sum | solution.py:107
  91.0 11.6 %convolution_convert_fusion.4 = bf16[2,64,3,1024]{3,1,2,0:T(8,128)(2,1)S(1)} fusion(bf16[1024,2,64,1]{0,2,3,1:T(8,128)(2,1)S(1)} %bitcast.122, f32[2,1024,1024,3]{2,1,3,0:T(8,128)} %get-tuple-element.280, f32[2,3,1024]{2,1,0:T(4,128)S(1)} %log_add_fusion, pred[1024,1024]{0,1:T(8,128)(4,1)S(1)} %iota_compare_fusion), kind=kOutput, calls=%fused_computation.46 | convolution fusion | flops 830865408 | bytes 27287552 | tf_op jit(solution)/shard_map/hgqk,khd->qhgd/dot_general | solution.py:29
  103.6 3.5 convolution_convert_fusion.x_ref
  107.1 59.7 %scatter_branch_weights.1 = (f32[256,1536]{1,0:T(8,128)}, bf16[3,1536,512]{2,1,0:T(8,128)(2,1)}, bf16[3,256,1536]{2,1,0:T(8,128)(2,1)}) custom-call(bf16[1024,1536]{1,0:T(8,128)(2,1)} %convolution_convert_fusion.x_ref, bf16[3,384,1024]{2,1,0:T(8,128)(2,1)} %refs_2_.1, bf16[3,128,1536]{2,1,0:T(8,128)(2,1)} %refs_3_.1), custom_call_target="tpu_custom_call" | custom-call | flops 15728640 | bytes 15728640 | tf_op jit(solution)/shard_map/scatter_branch_weights/pallas_call | solution.py:1016
  166.8 1.8 multiply_reduce_fusion.2
  170.4 1.3 concatenate.59.refs_1_.refs_8_
  172.7 92.9 %gather_all.1 = (bf16[256,1536]{1,0:T(8,128)(2,1)}, s32[16,256]{1,0:T(8,128)}, bf16[256,1536]{1,0:T(8,128)(2,1)}, s32[16,256]{1,0:T(8,128)}, bf16[256,1536]{1,0:...) custom-call(bf16[256,1536]{1,0:T(8,128)(2,1)} %multiply_convert_fusi, ...), custom_call_target="tpu_custom_call", output_to_operand_aliasing={{30}: (4, {}), {31}: (5, {})} | custom-call | flops 31457280 | bytes 31457280 | tf_op jit(solution)/shard_map/gather_all/pallas_call | solution.py:695
  265.6 23.3 %experts_forward.3 = (bf16[256,1536]{1,0:T(8,128)(2,1)}, bf16[256,1536]{1,0:T(8,128)(2,1)}, bf16[256,1536]{1,0:T(8,128)(2,1)}, bf16[256,1536]{1,0:T(8,128)(2,1)}...) custom-call(s32[1]{0:T(128)} %bitcast.14.me_ref, ...), custom_call_target="tpu_custom_call" | custom-call | flops 11000000512 | bytes 40000000 | tf_op jit(solution)/shard_map/experts_forward/pallas_call | solution.py:222
  288.9 1.3 slice.132
  290.2 23.7 %experts_forward.2 = (bf16[256,1536]{1,0:T(8,128)(2,1)}, bf16[256,1536]{1,0:T(8,128)(2,1)}, bf16[256,1536]{1,0:T(8,128)(2,1)}, bf16[256,1536]{1,0:T(8,128)(2,1)}...) custom-call(s32[1]{0:T(128)} %bitcast.14.me_ref, ...), custom_call_target="tpu_custom_call" | custom-call | flops 11000000512 | bytes 40000000 | tf_op jit(solution)/shard_map/experts_forward/pallas_call | solution.py:222
  313.8 1.2 slice.131
  316.4 3.9 collective-permute-start
  321.7 69.1 %scatter_outputs.1 = f32[256,1536]{1,0:T(8,128)} custom-call(bf16[256,1536]{1,0:T(8,128)(2,1)} %get-tuple-element.147.refs_0_, bf16[256,1536]{1,0:T(8,128)(2,1)} %get-tuple-element.148.refs_1_, bf16[256,1536]{1,0:T(8,128)(2,1)} %get-tuple-element.149.refs_2_, bf16[256,1536]{1,0:T(8,128)(2,1)} %get-tuple-element.150.refs_3_, ...), custom_call_target="tpu_custom_call" | custom-call | flops 19660800 | bytes 19660800 | tf_op jit(solution)/shard_map/scatter_outputs/pallas_call | solution.py:791
  391.5 2.8 multiply_convert_fusion.3.refs_0_
  394.3 59.9 %gather_tokens.1 = (bf16[256,1536]{1,0:T(8,128)(2,1)}, bf16[256,1536]{1,0:T(8,128)(2,1)}, bf16[256,1536]{1,0:T(8,128)(2,1)}, bf16[256,1536]{1,0:T(8,128)(2,1)}, ...) custom-call(bf16[256,1536]{1,0:T(8,128)(2,1)} %multiply_convert_fusi, ...), custom_call_target="tpu_custom_call" | custom-call | flops 31457280 | bytes 31457280 | tf_op jit(solution)/shard_map/gather_tokens/pallas_call | solution.py:695
  454.2 25.7 %experts_backward.2 = (bf16[256,1664]{1,0:T(8,128)(2,1)}, bf16[256,1664]{1,0:T(8,128)(2,1)}, bf16[256,1664]{1,0:T(8,128)(2,1)}, bf16[256,1664]{1,0:T(8,128)(2,1)...) custom-call(s32[1]{0:T(128)} %bitcast.14.me_ref, ...), custom_call_target="tpu_custom_call" | custom-call | flops 11000000512 | bytes 40000000 | tf_op jit(solution)/shard_map/experts_backward/pallas_call | solution.py:301
  479.9 25.4 %experts_backward.3 = (bf16[256,1664]{1,0:T(8,128)(2,1)}, bf16[256,1664]{1,0:T(8,128)(2,1)}, bf16[256,1664]{1,0:T(8,128)(2,1)}, bf16[256,1664]{1,0:T(8,128)(2,1)...) custom-call(s32[1]{0:T(128)} %bitcast.14.me_ref, ...), custom_call_target="tpu_custom_call" | custom-call | flops 11000000512 | bytes 40000000 | tf_op jit(solution)/shard_map/experts_backward/pallas_call | solution.py:301
  505.4 69.7 %scatter_grads.1 = f32[256,1664]{1,0:T(8,128)} custom-call(bf16[256,1664]{1,0:T(8,128)(2,1)} %get-tuple-element.191.refs_0_, bf16[256,1664]{1,0:T(8,128)(2,1)} %get-tuple-element.192.refs_1_, bf16[256,1664]{1,0:T(8,128)(2,1)} %get-tuple-element.193.refs_2_, bf16[256,1664]{1,0:T(8,128)(2,1)} %get-tuple-element.194.refs_3_, ...), custom_call_target="tpu_custom_call" | custom-call | flops 21299200 | bytes 21299200 | tf_op jit(solution)/shard_map/scatter_grads/pallas_call | solution.py:791
  577.4 4.7 multiply_reduce_fusion
  583.4 21.6 %expert_weights.1 = (bf16[3,1536,512]{2,1,0:T(8,128)(2,1)}, bf16[3,256,1536]{2,1,0:T(8,128)(2,1)}) custom-call(s32[1]{0:T(128)} %bitcast.21.after_ref, bf16[8,3,112,1536]{3,2,1,0:T(8,128)(2,1)} %get-tuple-element.218.refs_0_, bf16[8,3,112,512]{3,2,1,0:T(8,128)(2,1)} %get-tuple-element.219.refs_1_, bf16[8,3,112,256]{3,2,1,0:T(8,128)(2,1)} %get-tuple-element.220.refs_2_, ...), custom_call_target="tpu_custom_call" | custom-call | flops 14000000000 | bytes 40000000 | tf_op jit(solution)/shard_map/expert_weights/pallas_call | solution.py:349
  605.0 1.2 slice.134
  607.5 4.5 multiply_convert_fusion.1
  612.1 40.1 %gather_branch_grads.1 = (bf16[1024,1536]{1,0:T(8,128)(2,1)}, bf16[384,1024]{1,0:T(8,128)(2,1)}, bf16[128,1536]{1,0:T(8,128)(2,1)}) custom-call(bf16[256,1536]{1,0:T(8,128)(2,1)} %get-tuple-element.249.x_ref, bf16[3,1536,512]{2,1,0:T(8,128)(2,1)} %get-tuple-element.227.grad_gate_up, bf16[3,256,1536]{2,1,0:T(8,128)(2,1)} %get-tuple-element.226.grad_down), custom_call_target="tpu_custom_call" | custom-call | flops 15728640 | bytes 15728640 | tf_op jit(solution)/shard_map/gather_branch_grads/pallas_call | solution.py:1047
  652.2 4.5 convolution_convert_fusion.2
  656.6 1.3 collective-permute-start.1
  657.9 1.3 collective-permute-start.2
  659.2 1.3 collective-permute-start.3
  660.5 2.0 fusion.41
  662.5 1.4 convolution_convert_fusion.3
  663.9 17.3 %fusion = (f32[2,3,1024]{2,1,0:T(4,128)S(1)}, f32[2,1024,1024,3]{2,1,3,0:T(8,128)}) fusion(f32[2,1024,1024,3]{2,1,3,0:T(8,128)} %get-tuple-element.280, f32[2,3,1024]{2,1,0:T(4,128)S(1)} %copy-done.32, pred[1024,1024]{0,1:T(8,128)(4,1)S(1)} %iota_compare_fusion, bf16[1024,2,64,1]{0,2,3,1:T(8,128)(2,1)S(1)} %bitcast.123, ...), kind=kOutput, calls=%fused_computation.2 | convolution fusion | flops 836757504 | bytes 52477952 | tf_op jit(solution)/shard_map/qhgd,khd->hgqk/dot_general | solution.py:29
  681.3 17.5 %fusion.2 = bf16[2,3,1024,1024]{2,3,1,0:T(8,128)(2,1)S(1)} fusion(f32[2,1024,1024,3]{2,1,3,0:T(8,128)} %get-tuple-element.285, f32[2,1024,1024,3]{2,1,3,0:T(8,128)} %get-tuple-element.280, f32[2,3,1024]{2,1,0:T(4,128)S(1)} %get-tuple-element.284, f32[2,3,1024]{2,1,0:T(4,128)S(1)} %copy-done.32, pred[1024,1024]{0,1:T(8,128)(4,1)S(1)} %iota_compare_fusion), kind=kLoop, calls=%fused_computation.4 | loop fusion | flops 37748736 | bytes 64012288 | tf_op jit(solution)/shard_map/convert_element_type | solution.py:120
  698.8 3.4 convolution_multiply_fusion
  702.2 5.0 fusion.15
  707.3 12.5 %fusion.16 = bf16[2,64,1024]{2,1,0:T(8,128)(2,1)} fusion(bf16[1024,2,3,64]{0,3,2,1:T(8,128)(2,1)} %bitcast.130, f32[2,1024,1024,3]{2,1,3,0:T(8,128)} %get-tuple-element.280, f32[2,3,1024]{2,1,0:T(4,128)S(1)} %copy-done.32, pred[1024,1024]{0,1:T(8,128)(4,1)S(1)} %iota_compare_fusion), kind=kOutput, calls=%fused_computation.52 | convolution fusion | flops 830603264 | bytes 27287552 | tf_op jit(solution)/shard_map/hgqk,qhgd->khd/dot_general | solution.py:29
  722.1 1.6 copy-done.53
  723.7 3.8 convolution_convert_fusion.1.grads
  727.6 4.1 fusion.36
  731.7 1.6 collective-permute-start.4
  735.1 4.2 multiply_convert_fusion.x_ref
  739.3 47.8 %scatter_normed_grads.1 = (f32[256,1536]{1,0:T(8,128)}, bf16[384,1024]{1,0:T(8,128)(2,1)}, bf16[128,1536]{1,0:T(8,128)(2,1)}) custom-call(bf16[1024,1536]{1,0:T(8,128)(2,1)} %multiply_convert_fusion.x_ref, bf16[3,1536,512]{2,1,0:T(8,128)(2,1)} %get-tuple-element.227.grad_gate_up, bf16[3,256,1536]{2,1,0:T(8,128)(2,1)} %get-tuple-element.226.grad_down), custom_call_target="tpu_custom_call" | custom-call | flops 15728640 | bytes 15728640 | tf_op jit(solution)/shard_map/scatter_normed_grads/pallas_call | solution.py:1074
  787.2 1.9 fusion.13
  789.1 3.4 fusion.11
  792.6 1.6 add_convert_fusion
  794.8 2.2 collective-permute-start.5
  797.1 2.0 collective-permute-start.6
  799.1 2.3 collective-permute-start.7
  803.5 68.4 %dense_reduce.1 = (bf16[384,2560]{1,0:T(8,128)(2,1)}, f32[32,384]{1,0:T(8,128)}, bf16[384,1024]{1,0:T(8,128)(2,1)}, bf16[128,1536]{1,0:T(8,128)(2,1)}) custom-call(bf16[1536,640]{1,0:T(8,128)(2,1)} %convolution_convert_fusion.1.grads, f32[4,32,384]{2,1,0:T(8,128)} %fusion.19.small, bf16[3,1536,512]{2,1,0:T(8,128)(2,1)} %get-tuple-element.227.grad_gate_up, ...), custom_call_target="tpu_custom_call" | custom-call | flops 100000000 | bytes 100000000 | tf_op jit(solution)/shard_map/dense_reduce/pallas_call | solution.py:1196
  871.9 1.4 slice_bitcast_fusion.1
  873.3 1.2 slice.143
  874.5 2.1 fusion.38
  877.3 2.1 maximum_convert_fusion.4
  879.4 2.0 maximum_convert_fusion.3
  881.4 1.4 slice_reduce_fusion
  882.8 2.6 maximum_convert_fusion
  886.6 1.6 maximum_convert_fusion.2
  888.2 1.7 maximum_convert_fusion.1
  889.9 3.0 add_convert_fusion.1
  (177 shorter events, 21.3 us)
Async XLA Ops:
  0.6 14.7 %copy-start = (bf16[384,1536]{1,0:T(8,128)(2,1)S(1)}, bf16[384,1536]{1,0:T(8,128)(2,1)}, u32[]{:S(2)}) copy-start(bf16[384,1536]{1,0:T(8,128)(2,1)} %param.19) | copy-start | bytes 3538948
  0.7 14.7 %copy-start.2 = (bf16[256,1536]{1,0:T(8,128)(2,1)S(1)}, bf16[256,1536]{1,0:T(8,128)(2,1)}, u32[]{:S(2)}) copy-start(bf16[256,1536]{1,0:T(8,128)(2,1)} %param.13) | copy-start | bytes 2359300
  13.9 4.4 copy-start.36
  15.3 3.0 copy-start.45
  15.3 3.0 copy-start.41
  64.7 1.5 copy-start.10
  64.9 1.4 copy-start.30
  66.3 24.7 %copy-start.15 = (bf16[1024,128]{0,1:T(8,128)(2,1)}, bf16[1024,128]{0,1:T(8,128)(2,1)S(1)}, u32[]{:S(2)}) copy-start(bf16[1024,128]{0,1:T(8,128)(2,1)S(1)} %slice.205) | copy-start | bytes 786436
  66.3 2.1 slice-start
  68.4 11.1 %copy-start.12 = (bf16[1024,6,32]{0,2,1:T(8,128)(2,1)}, bf16[1024,6,32]{0,2,1:T(8,128)(2,1)S(1)}, u32[]{:S(2)}) copy-start(bf16[1024,6,32]{0,2,1:T(8,128)(2,1)S(1)} %get-tuple-element.268) | copy-start | bytes 1179652
  68.4 11.1 %copy-start.13 = (bf16[1024,6,32]{0,2,1:T(8,128)(2,1)}, bf16[1024,6,32]{0,2,1:T(8,128)(2,1)S(1)}, u32[]{:S(2)}) copy-start(bf16[1024,6,32]{0,2,1:T(8,128)(2,1)S(1)} %get-tuple-element.269) | copy-start | bytes 1179652
  68.8 10.7 %copy-start.23 = (bf16[1024,2,32]{0,2,1:T(8,128)(2,1)}, bf16[1024,2,32]{0,2,1:T(8,128)(2,1)S(1)}, u32[]{:S(2)}) copy-start(bf16[1024,2,32]{0,2,1:T(8,128)(2,1)S(1)} %get-tuple-element.272) | copy-start | bytes 393220
  68.8 10.7 %copy-start.25 = (bf16[1024,2,32]{0,2,1:T(8,128)(2,1)}, bf16[1024,2,32]{0,2,1:T(8,128)(2,1)S(1)}, u32[]{:S(2)}) copy-start(bf16[1024,2,32]{0,2,1:T(8,128)(2,1)S(1)} %get-tuple-element.273) | copy-start | bytes 393220
  91.0 11.6 %copy-start.31 = (f32[2,3,1024]{2,1,0:T(4,128)}, f32[2,3,1024]{2,1,0:T(4,128)S(1)}, u32[]{:S(2)}) copy-start(f32[2,3,1024]{2,1,0:T(4,128)S(1)} %log_add_fusion) | copy-start | bytes 73732
  91.0 12.5 %copy-start.56 = (bf16[384,1536]{1,0:T(8,128)(2,1)S(1)}, bf16[384,1536]{1,0:T(8,128)(2,1)}, u32[]{:S(2)}) copy-start(bf16[384,1536]{1,0:T(8,128)(2,1)} %get-tuple-element.127) | copy-start | bytes 3538948
  166.7 2.4 copy-start.50
  166.7 3.0 copy-start.35
  166.7 3.6 copy-start.40
  169.1 96.5 %copy-start.43 = (f32[256]{0:T(256)}, f32[256]{0:T(256)S(1)}, u32[]{:S(2)}) copy-start(f32[256]{0:T(256)S(1)} %fusion.28) | copy-start | bytes 3076
  290.2 30.9 %copy-start.4 = (bf16[256,1536]{1,0:T(8,128)(2,1)S(1)}, bf16[256,1536]{1,0:T(8,128)(2,1)}, u32[]{:S(2)}) copy-start(bf16[256,1536]{1,0:T(8,128)(2,1)} %multiply_convert_fusion.2.refs_0_) | copy-start | bytes 2359300
  290.2 30.9 %copy-start.38 = (bf16[4,3,8,384]{3,2,0,1:T(8,128)(2,1)S(1)}, bf16[4,3,8,384]{3,2,0,1:T(8,128)(2,1)}, u32[]{:S(2)}) copy-start(bf16[4,3,8,384]{3,2,0,1:T(8,128)(2,1)} %copy.61) | copy-start | bytes 221188
  316.4 74.4 %collective-permute-start = (s32[1]{0:T(128)}, s32[1]{0:T(128)}, u32[]{:S(2)}, u32[]{:S(2)}) collective-permute-start(s32[1]{0:T(128)} %bitcast.19), channel_id=1, source_target_pairs={{0,8},{8,0},{16,24},{24,16},{1,9},{9,1},{17,25},{25,17},{2,10},{10... | collective-permute-start | bytes 20 | tf_op jit(solution)/shard_map/ppermute | solution.py:55
  321.6 69.8 %copy-start.51 = (s32[256]{0:T(256)S(1)}, s32[256]{0:T(256)}, u32[]{:S(2)}) copy-start(s32[256]{0:T(256)} %param.15) | copy-start | bytes 3076
  505.3 70.9 %copy-start.34 = (pred[256,24]{1,0:T(32,128)(4,1)S(1)}, pred[256,24]{1,0:T(32,128)(4,1)}, u32[]{:S(2)}) copy-start(pred[256,24]{1,0:T(32,128)(4,1)} %copy-done.33) | copy-start | bytes 18436
  505.3 72.0 %copy-start.39 = (bf16[4,3,8,384]{3,2,0,1:T(8,128)(2,1)S(1)}, bf16[4,3,8,384]{3,2,0,1:T(8,128)(2,1)}, u32[]{:S(2)}) copy-start(bf16[4,3,8,384]{3,2,0,1:T(8,128)(2,1)} %copy.61) | copy-start | bytes 221188
  505.3 72.0 %copy-start.44 = (f32[256]{0:T(256)S(1)}, f32[256]{0:T(256)}, u32[]{:S(2)}) copy-start(f32[256]{0:T(256)} %copy-done.43) | copy-start | bytes 3076
  577.4 4.7 copy-start.48
  612.1 40.1 %copy-start.59 = (bf16[2,64,3,1024]{3,1,2,0:T(8,128)(2,1)S(1)}, bf16[2,64,3,1024]{3,1,2,0:T(8,128)(2,1)}, u32[]{:S(2)}) copy-start(bf16[2,64,3,1024]{3,1,2,0:T(8,128)(2,1)} %copy-done.58) | copy-start | bytes 2359300
  652.1 10.3 %copy-start.54 = (bf16[1024,1536]{1,0:T(8,128)(2,1)S(1)}, bf16[1024,1536]{1,0:T(8,128)(2,1)}, u32[]{:S(2)}) copy-start(bf16[1024,1536]{1,0:T(8,128)(2,1)} %get-tuple-element.228) | copy-start | bytes 9437188
  652.1 10.3 %copy-start.57 = (bf16[384,1536]{1,0:T(8,128)(2,1)S(1)}, bf16[384,1536]{1,0:T(8,128)(2,1)}, u32[]{:S(2)}) copy-start(bf16[384,1536]{1,0:T(8,128)(2,1)} %get-tuple-element.127) | copy-start | bytes 3538948
  656.6 71.0 %collective-permute-start.1 = (bf16[384,1536]{1,0:T(8,128)(2,1)}, bf16[384,1536]{1,0:T(8,128)(2,1)}, u32[]{:S(2)}, u32[]{:S(2)}) collective-permute-start(bf16[384,1536]{1,0:T(8,128)(2,1)} %convolution_convert_fusion.2), channel_id=1, source_target_pairs={{8,0},{17,9},{26,18},{3,27},{12,4},{21,13},{30,22},{7,31}} | collective-permute-start | bytes 3538952 | tf_op jit(solution)/shard_map/ppermute | solution.py:1286
  657.9 69.7 %collective-permute-start.2 = (bf16[384,1536]{1,0:T(8,128)(2,1)}, bf16[384,1536]{1,0:T(8,128)(2,1)}, u32[]{:S(2)}, u32[]{:S(2)}) collective-permute-start(bf16[384,1536]{1,0:T(8,128)(2,1)} %convolution_convert_fusion.2), channel_id=1, source_target_pairs={{16,0},{25,9},{2,18},{11,27},{20,4},{29,13},{6,22},{15,31}} | collective-permute-start | bytes 3538952 | tf_op jit(solution)/shard_map/ppermute | solution.py:1286
  659.2 68.4 %collective-permute-start.3 = (bf16[384,1536]{1,0:T(8,128)(2,1)}, bf16[384,1536]{1,0:T(8,128)(2,1)}, u32[]{:S(2)}, u32[]{:S(2)}) collective-permute-start(bf16[384,1536]{1,0:T(8,128)(2,1)} %convolution_convert_fusion.2), channel_id=1, source_target_pairs={{24,0},{1,9},{10,18},{19,27},{28,4},{5,13},{14,22},{23,31}} | collective-permute-start | bytes 3538952 | tf_op jit(solution)/shard_map/ppermute | solution.py:1286
  662.5 1.4 copy-start.16
  662.5 1.4 copy-start.32
  663.9 17.3 %copy-start.20 = (bf16[1024,384]{0,1:T(8,128)(2,1)}, bf16[1024,384]{0,1:T(8,128)(2,1)S(1)}, u32[]{:S(2)}) copy-start(bf16[1024,384]{0,1:T(8,128)(2,1)S(1)} %convolution_convert_fusion.3) | copy-start | bytes 2359300
  681.2 17.5 %copy-start.24 = (bf16[1024,2,32]{0,2,1:T(8,128)(2,1)S(1)}, bf16[1024,2,32]{0,2,1:T(8,128)(2,1)}, u32[]{:S(2)}) copy-start(bf16[1024,2,32]{0,2,1:T(8,128)(2,1)} %copy-done.23) | copy-start | bytes 393220
  681.3 17.5 %copy-start.26 = (bf16[1024,2,32]{0,2,1:T(8,128)(2,1)S(1)}, bf16[1024,2,32]{0,2,1:T(8,128)(2,1)}, u32[]{:S(2)}) copy-start(bf16[1024,2,32]{0,2,1:T(8,128)(2,1)} %copy-done.25) | copy-start | bytes 393220
  707.3 12.5 %copy-start.22 = (f32[24,1536]{1,0:T(8,128)S(1)}, f32[24,1536]{1,0:T(8,128)}, u32[]{:S(2)}) copy-start(f32[24,1536]{1,0:T(8,128)} %fusion.41) | copy-start | bytes 442372
  707.3 13.2 %copy-start.49 = (f32[1536]{0:T(1024)S(1)}, f32[1536]{0:T(1024)}, u32[]{:S(2)}) copy-start(f32[1536]{0:T(1024)} %get-tuple-element.238) | copy-start | bytes 18436
  707.3 14.4 %copy-start.9 = (f32[1024,32]{0,1:T(8,128)S(1)}, f32[1024,32]{0,1:T(8,128)}, u32[]{:S(2)}) copy-start(f32[1024,32]{0,1:T(8,128)} %copy-done.8) | copy-start | bytes 393220
  707.3 14.4 %copy-start.14 = (f32[1024,32]{0,1:T(8,128)S(1)}, f32[1024,32]{0,1:T(8,128)}, u32[]{:S(2)}) copy-start(f32[1024,32]{0,1:T(8,128)} %get-tuple-element.276) | copy-start | bytes 393220
  719.8 2.0 copy-start.5
  721.8 1.9 copy-start.53
  721.8 1.9 copy-start.60
  727.6 7.6 copy-start.55
  731.7 60.9 %collective-permute-start.4 = (bf16[384,1536]{1,0:T(8,128)(2,1)}, bf16[384,1536]{1,0:T(8,128)(2,1)}, u32[]{:S(2)}, u32[]{:S(2)}) collective-permute-start(bf16[384,1536]{1,0:T(8,128)(2,1)} %get-tuple-element.247), channel_id=1, source_target_pairs={{0,4},{1,5},{2,6},{3,7},{4,0},{5,1},{6,2},{7,3},{8,12},{9,13},{10,... | collective-permute-start | bytes 3538952 | tf_op jit(solution)/shard_map/ppermute | solution.py:55
  739.3 47.9 %copy-start.3 = (bf16[256,1536]{1,0:T(8,128)(2,1)S(1)}, bf16[256,1536]{1,0:T(8,128)(2,1)}, u32[]{:S(2)}) copy-start(bf16[256,1536]{1,0:T(8,128)(2,1)} %param.13) | copy-start | bytes 2359300
  739.3 47.9 %copy-start.37 = (f32[1536]{0:T(1024)S(1)}, f32[1536]{0:T(1024)}, u32[]{:S(2)}) copy-start(f32[1536]{0:T(1024)} %copy-done.36) | copy-start | bytes 18436
  739.3 47.9 %copy-start.42 = (f32[256]{0:T(256)S(1)}, f32[256]{0:T(256)}, u32[]{:S(2)}) copy-start(f32[256]{0:T(256)} %copy-done.41) | copy-start | bytes 3076
  787.2 2.0 copy-start.46
  792.6 10.2 %copy-start.21 = (f32[3,4,8,384]{3,2,0,1:T(8,128)S(1)}, f32[3,4,8,384]{3,2,0,1:T(8,128)}, u32[]{:S(2)}) copy-start(f32[3,4,8,384]{3,2,0,1:T(8,128)} %copy.63) | copy-start | bytes 442372
  792.6 10.2 %copy-start.52 = (f32[32]{0:T(128)S(1)}, f32[32]{0:T(128)}, u32[]{:S(2)}) copy-start(f32[32]{0:T(128)} %pad.22.clone) | copy-start | bytes 388
  794.2 77.7 %copy-start.6 = (bf16[384,1536]{1,0:T(8,128)(2,1)}, bf16[384,1536]{1,0:T(8,128)(2,1)S(1)}, u32[]{:S(2)}) copy-start(bf16[384,1536]{1,0:T(8,128)(2,1)S(1)} %add_convert_fusion) | copy-start | bytes 3538948
  794.8 95.1 %collective-permute-start.5 = (bf16[384,1536]{1,0:T(8,128)(2,1)S(1)}, bf16[384,1536]{1,0:T(8,128)(2,1)S(1)}, u32[]{:S(2)}, u32[]{:S(2)}) collective-permute-start(bf16[384,1536]{1,0:T(8,128)(2,1)S(1)} %add_convert_fusion), channel_id=1, source_target_pairs={{0,1},{9,8},{18,19},{27,26},{4,5},{13,12},{22,23},{31,30}} | collective-permute-start | bytes 3538952 | tf_op jit(solution)/shard_map/ppermute | solution.py:1286
  797.1 92.8 %collective-permute-start.6 = (bf16[384,1536]{1,0:T(8,128)(2,1)S(1)}, bf16[384,1536]{1,0:T(8,128)(2,1)S(1)}, u32[]{:S(2)}, u32[]{:S(2)}) collective-permute-start(bf16[384,1536]{1,0:T(8,128)(2,1)S(1)} %add_convert_fusion), channel_id=1, source_target_pairs={{0,2},{9,11},{18,16},{27,25},{4,6},{13,15},{22,20},{31,29}} | collective-permute-start | bytes 3538952 | tf_op jit(solution)/shard_map/ppermute | solution.py:1286
  799.1 90.8 %collective-permute-start.7 = (bf16[384,1536]{1,0:T(8,128)(2,1)S(1)}, bf16[384,1536]{1,0:T(8,128)(2,1)}, u32[]{:S(2)}, u32[]{:S(2)}) collective-permute-start(bf16[384,1536]{1,0:T(8,128)(2,1)S(1)} %add_convert_fusion), channel_id=1, source_target_pairs={{0,3},{9,10},{18,17},{27,24},{4,7},{13,14},{22,21},{31,28}} | collective-permute-start | bytes 3538952 | tf_op jit(solution)/shard_map/ppermute | solution.py:1286
  877.3 5.5 copy-start.17
  877.3 5.5 copy-start.18
  877.3 5.5 copy-start.19
  882.8 2.6 copy-start.11
  885.4 1.2 copy-start.29
  888.2 1.7 copy-start.7
  889.9 3.0 copy-start.1
  (6 other events, 4.8 us)

commit v4 on v3

--- a/solution.py
+++ b/solution.py
@@ -36,18 +36,8 @@
 def rope_tables(positions):
     half_dim = HD // 2
     frequencies = ROPE_BASE ** (-(2.0 * jnp.arange(half_dim, dtype=f32)) / HD)
-    angles = positions[:, None] * frequencies[None, :]
-    return (jnp.cos(angles)[:, None, :], jnp.sin(angles)[:, None, :])
-
-
-def rotary(heads_in, cosine_table, sine_table):
-    half_dim = heads_in.shape[-1] // 2
-    first = heads_in[..., :half_dim]
-    second = heads_in[..., half_dim:]
-    return jnp.concatenate(
-        [first * cosine_table - second * sine_table, second * cosine_table + first * sine_table],
-        axis=-1,
-    )
+    angles = frequencies[:, None] * positions[None, :]
+    return jnp.cos(angles), jnp.sin(angles)
 
 
 def send(x, axis, mask):
@@ -96,32 +86,6 @@
 
 def never(x):
     return (x != x).astype(jnp.int32)
-
-
-def attend(queries, keys, values):
-    count = queries.shape[0]
-    raw = mm("qhgd,khd->hgqk", queries, keys) * SCORE_SCALE
-    causal = jnp.arange(count)[:, None] >= jnp.arange(count)[None, :]
-    scores = jnp.where(causal[None, None], raw, NEG)
-    top = jnp.max(scores, axis=-1, keepdims=True)
-    log_total = top + jnp.log(jnp.sum(jnp.exp(scores - top), axis=-1, keepdims=True))
-    probs = jnp.exp(scores - log_total).astype(bf16)
-    context = mm("hgqk,khd->qhgd", probs, values).astype(bf16)
-    return context, log_total
-
-
-def attend_back(queries, keys, values, log_total, grad_context):
-    count = queries.shape[0]
-    raw = mm("qhgd,khd->hgqk", queries, keys) * SCORE_SCALE
-    causal = jnp.arange(count)[:, None] >= jnp.arange(count)[None, :]
-    probs = jnp.exp(jnp.where(causal[None, None], raw, NEG) - log_total)
-    grad_probs = mm("qhgd,khd->hgqk", grad_context, values)
-    delta = jnp.sum(probs * grad_probs, axis=-1, keepdims=True)
-    grad_scores = (probs * (grad_probs - delta)).astype(bf16)
-    grad_queries = mm("hgqk,khd->qhgd", grad_scores, keys) * SCORE_SCALE
-    grad_keys = mm("hgqk,qhgd->khd", grad_scores, queries) * SCORE_SCALE
-    grad_values = mm("hgqk,qhgd->khd", probs.astype(bf16), grad_context)
-    return grad_queries, grad_keys, grad_values
 
 
 CAP = 112
@@ -448,13 +412,26 @@
 
 
 class WeightsIn:
-    def __init__(self, wire, experts, w_gate_up, w_down, gate_up, down, stage, stage_down, sems):
+    def __init__(
+        self,
+        wire,
+        experts,
+        w_gate_up,
+        w_down,
+        gate_up,
+        down,
+        stage,
+        stage_down,
+        sems,
+        direct=False,
+    ):
         z, beside, opposite, side, low = plane_places()
         slab, part = w_gate_up.shape[1], gate_up.shape[2] // 2
         rows = w_down.shape[1]
         self.wire, self.gate_up, self.slab, self.opposite = wire, gate_up, slab, opposite
         self.beside = {"dp": beside}
         self.crossing, self.arriving, self.stores = [], [], []
+        self.direct = direct
 
         def columns(i, which, p):
             return w_gate_up.at[i, :, stripe(2 * p + which, part)]
@@ -475,6 +452,10 @@
             loads.append(pltpu.make_async_copy(w_down.at[i], stage_down.at[n], sems.at[n, 2]))
             for load in loads[-3:]:
                 load.start()
+            if direct:
+                corner = {"dp": flip(opposite, 1)}
+                for p in range(2):
+                    self.arriving.append(wire.start(columns(i, 1 - side, p), spot(i, p), corner))
             self.crossing.append(
                 (
                     i,
@@ -503,6 +484,8 @@
         for i, copies in self.crossing:
             for copy in copies:
                 copy.wait_recv()
+            if self.direct:
+                continue
             piece = self.gate_up.at[i, stripe(self.opposite, self.slab)]
             self.arriving.append(self.wire.start(piece, piece, self.beside))
         for copy in self.arriving:
@@ -813,7 +796,7 @@
     return [{"expert": flip(e, m)} for m in (1, 2)]
 
 
-def exchange_seq(wire, group, x_ref, out, between=None):
+def exchange_seq(wire, group, x_ref, out, between=None, steps=()):
     head = lax.rem(lax.axis_index("expert"), group)
     core, side_x = chip_partners()
     rows = x_ref.shape[0]
@@ -829,9 +812,13 @@
     if between:
         between()
     for h in range(2):
+        if steps:
+            steps[h]()
         crossing[h].wait_recv()
         piece = out.at[pl.ds(other + h * cut, cut)]
         last.append(wire.start(piece, piece, core))
+    if steps:
+        steps[2]()
     for copy in last:
         copy.wait_recv()
 
@@ -858,7 +845,7 @@
     )(x)
 
 
-def sum_seq(wire, group, x_ref, out, core_in, sums, last_in):
+def sum_seq(wire, group, x_ref, out, core_in, sums, last_in, between=None):
     head = lax.rem(lax.axis_index("expert"), group)
     core, side_x = chip_partners()
     rows = out.shape[0]
@@ -876,6 +863,8 @@
         crossing[h].wait_recv()
         add_into(cut, sums.at[h], part(flip(head, 2), h), core_in.at[1, h])
         last.append(wire.start(sums.at[h], last_in.at[h], side_x))
+    if between:
+        between()
     for h in range(2):
         near[h].wait_recv()
         last[h].wait_recv()
@@ -920,62 +909,94 @@
     e, z = lax.axis_index("expert"), lax.axis_index("dp")
     head, row = lax.rem(e, group), lax.div(e, group)
     side_y = {"expert": flip(e, 4)}
-    block = [lax.rem(z + k, 4) for k in range(4)]
-    planes = [{"dp": b} for b in block]
+    top = 3
     slab = qkv_in.shape[0]
     cut = slab // 2
-    greet(chip_partners() + [side_y] + planes[1:])
+    greet(chip_partners() + [side_y] + [{"dp": lax.rem(z + k, 4)} for k in range(1, 4)])
     mine = pl.ds(pl.multiple_of(row * cut, cut), cut)
 
     def spot(plane):
         return qkv.at[pl.ds(pl.multiple_of(plane * slab + row * cut, cut), cut)]
 
-    from_z = [wire.start(qkv_in.at[mine], spot(z), planes[k]) for k in (1, 2, 3)]
-    owner = z == head
-
-    def out_copy(n, to, at):
+    def copy(n, src, dst, to):
         return pltpu.make_async_remote_copy(
-            src_ref=out_in.at[at] if n < 3 else out_slice.at[at],
-            dst_ref=out_slice.at[at],
-            send_sem=send_sem.at[12 + n],
-            recv_sem=recv_sem.at[12 if n < 3 else 13],
+            src_ref=src,
+            dst_ref=dst,
+            send_sem=send_sem.at[n],
+            recv_sem=recv_sem.at[n],
             device_id=to,
             device_id_type=MESH,
         )
 
-    spread = [out_copy(k - 1, planes[k], mine) for k in (1, 2, 3)]
-    swap = out_copy(3, side_y, mine)
+    up, down = {"dp": lax.rem(z + 1, 4)}, {"dp": lax.rem(z + 3, 4)}
+    hops = []
+    for sign, to in ((1, up), (-1, down)):
+        for d in (1, 2, 3):
+            n = 5 + len(hops) * 2
+            held, got = lax.rem(z - sign * (d - 1) + 8, 4), lax.rem(z - sign * d + 8, 4)
+            source = qkv_in.at[mine] if d == 1 else spot(held)
+            edge = z < top if sign > 0 else z > 0
+            held_there = z >= d - 1 if sign > 0 else z <= top - (d - 1)
+            arrives = z >= d if sign > 0 else z <= top - d
+            hops.append(
+                (
+                    jnp.logical_and(edge, held_there),
+                    arrives,
+                    copy(n, source, spot(held), to),
+                    copy(n + 1, spot(got), spot(got), side_y),
+                )
+            )
+    for sends, _, hop, _ in (hops[0], hops[3]):
+        pl.when(sends)(hop.start)
+
+    owner = z == head
+    out_up = copy(17, out_slice.at[mine], out_slice.at[mine], up)
+    out_down = copy(18, out_slice.at[mine], out_slice.at[mine], down)
+    own_up = copy(17, out_in.at[mine], out_slice.at[mine], up)
+    own_down = copy(18, out_in.at[mine], out_slice.at[mine], down)
+    swap = copy(19, out_slice.at[mine], out_slice.at[mine], side_y)
+    pl.when(jnp.logical_and(owner, z < top))(own_up.start)
+    pl.when(jnp.logical_and(owner, z > 0))(own_down.start)
 
     @pl.when(owner)
     def _():
-        for copy in spread:
-            copy.start()
         out_slice[...] = out_in[...]
 
     qkv[pl.ds(pl.multiple_of(z * slab, slab), slab), :] = qkv_in[...]
-    from_y = []
-
-    def relay():
-        for k in (1, 3, 2):
-            from_z[k - 1].wait_recv()
-            piece = spot(block[4 - k])
-            from_y.append(wire.start(piece, piece, side_y))
-
-    exchange_seq(wire, group, x_ref, seq, relay)
-    for copy in from_y:
-        copy.wait_recv()
-
-    @pl.when(owner)
-    def _():
-        for copy in spread:
-            copy.wait_send()
-
-    @pl.when(jnp.logical_not(owner))
-    def _():
-        spread[0].wait_recv()
-        swap.start()
-        swap.wait()
-
+
+    def relay(d):
+        for way in (0, 3):
+            _, arrives, hop, across = hops[way + d]
+
+            @pl.when(arrives)
+            def _():
+                hop.wait_recv()
+                across.start()
+
+            if d < 2:
+                sends, _, following, _ = hops[way + d + 1]
+                pl.when(sends)(following.start)
+
+        @pl.when(z == head + d + 1)
+        def _():
+            out_up.wait_recv()
+            pl.when(z < top)(out_up.start)
+            swap.start()
+
+        @pl.when(z == head - d - 1)
+        def _():
+            out_down.wait_recv()
+            pl.when(z > 0)(out_down.start)
+            swap.start()
+
+    steps = [functools.partial(relay, d) for d in range(3)]
+    exchange_seq(wire, group, x_ref, seq, steps=steps)
+    for sends, arrives, hop, across in hops:
+        pl.when(arrives)(across.wait)
+        pl.when(sends)(hop.wait_send)
+    pl.when(jnp.logical_not(owner))(swap.wait)
+    pl.when(jnp.logical_and(z >= head, z < top))(out_up.wait_send)
+    pl.when(jnp.logical_and(z <= head, z > 0))(out_down.wait_send)
     wire.finish()
 
 
@@ -986,7 +1007,7 @@
         functools.partial(entry_kernel, group),
         "attention_entry",
         8,
-        16,
+        20,
         [ON_CHIP] * 3,
         [ON_CHIP] * 3,
         [
@@ -1002,8 +1023,8 @@
 def scatter_weights_kernel(group, experts, x_ref, w_gate_up, w_down, out, gate_up, down, *refs):
     wire = Wire(*refs[6:])
     _, beside, opposite, _, _ = plane_places()
-    greet(chip_partners() + [{"dp": beside}, {"dp": opposite}])
-    cargo = WeightsIn(wire, experts, w_gate_up, w_down, gate_up, down, *refs[3:6])
+    greet(chip_partners() + [{"dp": p} for p in (beside, opposite, flip(opposite, 1))])
+    cargo = WeightsIn(wire, experts, w_gate_up, w_down, gate_up, down, *refs[3:6], direct=True)
     sum_seq(wire, group, x_ref, out, *refs[:3])
     cargo.finish()
     wire.finish()
@@ -1017,7 +1038,7 @@
         functools.partial(scatter_weights_kernel, group, experts),
         "scatter_branch_weights",
         9,
-        6 + 6 * len(experts),
+        6 + 7 * len(experts),
         [ON_CHIP, ANYWHERE, ANYWHERE],
         [ON_CHIP, ANYWHERE, ANYWHERE],
         [
@@ -1062,8 +1083,7 @@
     _, beside, opposite, _, _ = plane_places()
     greet(chip_partners() + [{"dp": beside}, {"dp": opposite}])
     cargo = GradsOut(wire, i, grad_gate_up, grad_down, out, out_down, *refs[3:7])
-    sum_seq(wire, group, x_ref, total, *refs[:3])
-    cargo.cross()
+    sum_seq(wire, group, x_ref, total, *refs[:3], cargo.cross)
     cargo.finish()
     wire.finish()
 
@@ -1212,6 +1232,90 @@
         + scratch,
         10**8,
     )(grads, small, grad_gate_up, grad_down)
+
+
+STRIP = 256
+
+
+def strips(ref_rows):
+    return [(b * STRIP, (b + 1) * STRIP) for b in range(ref_rows // STRIP)]
+
+
+def head_rows(index):
+    return pl.ds(pl.multiple_of(index * HD, HD), HD)
+
+
+def scores_of(keys, queries, first):
+    raw = dg(keys, queries, TN)
+    key = lax.broadcasted_iota(jnp.int32, raw.shape, 0)
+    query = lax.broadcasted_iota(jnp.int32, raw.shape, 1) + first
+    raw = jnp.where(key <= query, raw, NEG)
+    grown = jnp.exp(raw - jnp.max(raw, axis=0, keepdims=True))
+    return grown * (1.0 / jnp.sum(grown, axis=0, keepdims=True))
+
+
+def attend_kernel(q_ref, k_ref, v_ref, out_ref):
+    group = q_ref.shape[0] // k_ref.shape[0]
+
+    @pl.loop(0, q_ref.shape[0] // HD)
+    def _(h):
+        mine, shared = head_rows(h), head_rows(lax.div(h, group))
+        for first, last in strips(q_ref.shape[1]):
+            probs = scores_of(k_ref[shared, :last], q_ref[mine, first:last], first)
+            out = dg(v_ref[shared, :last], probs.astype(bf16), NN)
+            out_ref[mine, first:last] = out.astype(bf16)
+
+
+def attend_back_kernel(q_ref, k_ref, v_ref, grad_ref, dq_ref, dk_ref, dv_ref):
+    group = q_ref.shape[0] // k_ref.shape[0]
+    dk_ref[...] = jnp.zeros_like(dk_ref)
+    dv_ref[...] = jnp.zeros_like(dv_ref)
+
+    @pl.loop(0, q_ref.shape[0] // HD)
+    def _(h):
+        mine, shared = head_rows(h), head_rows(lax.div(h, group))
+        for first, last in strips(q_ref.shape[1]):
+            queries, grad = q_ref[mine, first:last], grad_ref[mine, first:last]
+            keys = k_ref[shared, :last]
+            probs = scores_of(keys, queries, first)
+            grad_probs = dg(v_ref[shared, :last], grad, TN)
+            delta = jnp.sum(probs * grad_probs, axis=0, keepdims=True)
+            grad_scores = (probs * (grad_probs - delta)).astype(bf16)
+            dq_ref[mine, first:last] = dg(keys, grad_scores, NN) * SCORE_SCALE
+            dk_ref[shared, :last] += dg(queries, grad_scores, NT)
+            dv_ref[shared, :last] += dg(grad, probs.astype(bf16), NT)
+
+
+def on_chip_call(kernel, name, inputs, shapes, flops):
+    return pl.pallas_call(
+        kernel,
+        in_specs=[ON_CHIP] * len(inputs),
+        out_specs=[ON_CHIP] * len(shapes),
+        out_shape=shapes,
+        compiler_params=params(60),
+        cost_estimate=pl.CostEstimate(
+            flops=flops, bytes_accessed=10**7, transcendentals=4 * 10**6
+        ),
+        name=name,
+    )(*inputs)
+
+
+def attend(queries, keys, values):
+    shapes = [jax.ShapeDtypeStruct(queries.shape, bf16)]
+    return on_chip_call(attend_kernel, "attend", (queries, keys, values), shapes, 10**10)[0]
+
+
+def attend_back(queries, keys, values, grad_context):
+    shapes = [jax.ShapeDtypeStruct(x.shape, f32) for x in (queries, keys, values)]
+    inputs = (queries, keys, values, grad_context)
+    return on_chip_call(attend_back_kernel, "attend_back", inputs, shapes, 3 * 10**10)
+
+
+def turned(x, cosine, sine):
+    x = x.reshape(-1, 2, HD // 2, x.shape[1])
+    first, second = x[:, 0], x[:, 1]
+    out = jnp.stack([first * cosine - second * sine, second * cosine + first * sine], axis=1)
+    return out.reshape(-1, x.shape[3])
 
 
 def body(
@@ -1245,8 +1349,6 @@
     slab = width // replicas
     q_cols = H * HD // group
     kv_cols = KVH * HD // group
-    kv_dev = KVH // group
-    per_kv = H // KVH
 
     def over_dp(x, axis):
         if replicas > group:
@@ -1292,20 +1394,13 @@
         qkv = over_dp(qkv_slice, 0)
         out_slice = pick(lax.all_gather(w_out, "dp", axis=0, tiled=True), head, q_cols, 0)
 
-    lin = mm("td,dc->tc", seq, qkv)
+    lin = mm("td,dc->ct", seq, qkv)
     cosine, sine = rope_tables(jnp.arange(length, dtype=f32))
-    queries = (
-        rotary(lin[:, :q_cols].reshape(length, kv_dev * per_kv, HD), cosine, sine)
-        .astype(bf16)
-        .reshape(length, kv_dev, per_kv, HD)
-    )
-    keys = rotary(
-        lin[:, q_cols : q_cols + kv_cols].reshape(length, kv_dev, HD), cosine, sine
-    ).astype(bf16)
-    values = lin[:, q_cols + kv_cols :].reshape(length, kv_dev, HD).astype(bf16)
-    context, log_total = attend(queries, keys, values)
-    context = context.reshape(length, q_cols)
-    branch = mm("tc,cd->td", context, out_slice).astype(bf16)
+    queries = turned(lin[:q_cols], cosine, sine).astype(bf16) * jnp.asarray(SCORE_SCALE, bf16)
+    keys = turned(lin[q_cols : q_cols + kv_cols], cosine, sine).astype(bf16)
+    values = lin[q_cols + kv_cols :].astype(bf16)
+    context = attend(queries, keys, values)
+    branch = mm("ct,cd->td", context, out_slice).astype(bf16)
     if compact:
         summed, gate_up_w, down_w = seq_scatter_weights(branch, group, (0,), w_gate_up, w_down)
     else:
@@ -1388,7 +1483,7 @@
         done.append(part)
     else:
         seq_grad = seq_gather(grad_branch, group, 3, "gather_normed")
-    grad_out = mm("tc,td->cd", context, seq_grad).astype(bf16)
+    grad_out = mm("ct,td->cd", context, seq_grad).astype(bf16)
     if compact:
         out_sum = grad_out.astype(f32)
         for step in range(1, replicas):
@@ -1401,22 +1496,13 @@
             ]
             out_sum = out_sum + on_grid(grad_out, pairs).astype(f32)
         entered = jnp.where(never(out_sum[0, 0]) == 0, 1.0, 0.0)
-    grad_context = (
-        mm("td,cd->tc", seq_grad, out_slice).astype(bf16).reshape(length, kv_dev, per_kv, HD)
-    )
-    grad_q, grad_k, grad_v = attend_back(queries, keys, values, log_total, grad_context)
+    grad_context = mm("td,cd->ct", seq_grad, out_slice).astype(bf16)
+    grad_q, grad_k, grad_v = attend_back(queries, keys, values, grad_context)
     grad_lin = jnp.concatenate(
-        [
-            rotary(grad_q.reshape(length, kv_dev * per_kv, HD), cosine, -sine).reshape(
-                length, q_cols
-            ),
-            rotary(grad_k, cosine, -sine).reshape(length, kv_cols),
-            grad_v.reshape(length, kv_cols),
-        ],
-        axis=1,
+        [turned(grad_q, cosine, -sine), turned(grad_k, cosine, -sine), grad_v]
     ).astype(bf16)
-    grad_qkv = mm("td,tc->dc", seq, grad_lin).astype(bf16)
-    normed_parts = mm("tc,dc->td", grad_lin, qkv)
+    grad_qkv = mm("td,ct->dc", seq, grad_lin).astype(bf16)
+    normed_parts = mm("ct,dc->td", grad_lin, qkv)
     normed_parts = (entered * normed_parts if compact else normed_parts).astype(bf16)
     if compact:
         grad_normed, *part = seq_scatter_grads(normed_parts, group, 1, grad_gate_up, grad_down)

time: 900 us -> 853 us (0.948)
  matrix products: 89.8 us -> 30.5 us
  other arithmetic: 73.8 us -> 48.7 us
  Pallas kernels: 678 us -> 702 us
  waiting for transfers between devices: 0.02 us -> 12.4 us
    dot_general x15 -> x9, matrix products: 89.8 us -> 30.5 us  [mm(): return jnp.einsum(spec, a, b, preferred_element_type=f32)]
    pallas_call x1 -> x3, Pallas kernels: 41.7 us -> 75.9 us  [the longest x2 39.2 us: on_chip_call(): pl.pallas_call(kernel, in_specs=[ON_CHIP] * len(inputs), out_specs=[ON_CH...]
    convert_element_type x1 -> x0, other arithmetic: 17.5 us -> none  [attend_back(): grad_scores = (probs * (grad_probs - delta)).astype(bf16)]
    ppermute x6, waiting for transfers between devices: 0.02 us -> 12.4 us  [on_grid(): return lax.ppermute(x, ('dp', 'expert'), pairs)]
    reduce_sum x1 -> x0, other arithmetic: 11.4 us -> none  [attend(): jnp.sum(jnp.exp(scores - top), axis=-1, keepdims=True)]
  transfers between devices with their start and end apart: 8 -> 8, of which waited for: 0 -> 1; matrix products, arithmetic and copies ran while one was open for 10% -> 5% of each run, Pallas kernels for 21% -> 24%
where the time goes in v4:
time: 853 us; the launch traced here: 847 us
  Pallas kernels  702 us (82%)
  other arithmetic  48.7 us (6%)
  matrix products  30.5 us (4%)
  local copies, waits for them, and re-layouts  26 us (3%)
  starting transfers between devices  17.2 us (2%)
  waiting for transfers between devices  12.4 us (1%)
  between operations  10.7 us (1%)
    pallas_call x2, Pallas kernels, plane_gather(): comm_call(functools.partial(plane_gather_kernel, half, experts, count), n...  157 us
    pallas_call x2, Pallas kernels, plane_scatter(): comm_call(functools.partial(plane_scatter_kernel, half), name, number, 42...  137 us
    pallas_call x1, Pallas kernels, dense_reduce(): comm_call(functools.partial(dense_kernel, replicas, i), 'dense_reduce', 2...  73.3 us
    pallas_call x1, Pallas kernels, seq_scatter_weights(): comm_call(functools.partial(scatter_weights_kernel, group, experts), 'sca...  51.7 us
    pallas_call x2, Pallas kernels, experts_backward(): pl.pallas_call(experts_back_kernel, grid_spec=pltpu.PrefetchScalarGridSpe...  50.9 us
    pallas_call x2, Pallas kernels, experts_forward(): pl.pallas_call(experts_kernel, grid_spec=pltpu.PrefetchScalarGridSpec(num...  46.7 us
    pallas_call x1, Pallas kernels, seq_gather_grads(): comm_call(functools.partial(gather_grads_kernel, group, i), 'gather_branc...  40 us
    pallas_call x2, Pallas kernels, on_chip_call(): pl.pallas_call(kernel, in_specs=[ON_CHIP] * len(inputs), out_specs=[ON_CH...  39.2 us
  transfers between devices with their start and end apart: 8, of which 1 were waited for; matrix products, arithmetic and copies ran while one was open for 5% of the time, Pallas kernels for 24%

profile of v4, /device:TPU:0, one launch (start us, length us, event | category | flops | bytes accessed | tf_op | source)
XLA Modules:
  0.0 847.2 jit_solution(7665827043895290444)
XLA Ops:
  2.3 1.4 maximum_maximum_fusion.small_ref
  3.7 9.3 %start_exchange.1 = bf16[4,32,384]{2,1,0:T(8,128)(2,1)} custom-call(bf16[32,384]{1,0:T(8,128)(2,1)} %maximum_maximum_fusion.small_ref), custom_call_target="tpu_custom_call" | custom-call | flops 1000000 | bytes 1000000 | tf_op jit(solution)/shard_map/start_exchange/pallas_call | solution.py:1120
  13.9 1.4 fusion.7
  15.3 1.1 fusion.2.x_ref
  18.3 36.7 %attention_entry.1 = (bf16[1024,1536]{1,0:T(8,128)(2,1)}, bf16[1536,640]{1,0:T(8,128)(2,1)}, bf16[384,1536]{1,0:T(8,128)(2,1)}) custom-call(bf16[256,1536]{1,0:T(8,128)(2,1)} %fusion.2.x_ref, bf16[384,640]{1,0:T(8,128)(2,1)} %pad_maximum_fusion.4.qkv_in, bf16[384,1536]{1,0:T(8,128)(2,1)} %out_in.1), custom_call_target="tpu_custom_call" | custom-call | flops 15728640 | bytes 15728640 | tf_op jit(solution)/shard_map/attention_entry/pallas_call | solution.py:1006
  55.0 4.7 fusion.28
  59.8 1.4 copy-done.6
  64.3 1.0 maximum_multiply_fusion
  65.3 15.9 %attend.1 = bf16[384,1024]{1,0:T(8,128)(2,1)} custom-call(bf16[384,1024]{1,0:T(8,128)(2,1)} %bitcast.57, bf16[128,1024]{1,0:T(8,128)(2,1)} %bitcast.69, bf16[128,1024]{1,0:T(8,128)(2,1)} %slice.205.v_ref), custom_call_target="tpu_custom_call" | custom-call | flops 10000000000 | bytes 10000000 | tf_op jit(solution)/shard_map/attend/pallas_call | solution.py:1290
  81.2 4.6 convolution_convert_fusion.x_ref
  85.8 51.7 %scatter_branch_weights.1 = (f32[256,1536]{1,0:T(8,128)}, bf16[3,1536,512]{2,1,0:T(8,128)(2,1)}, bf16[3,256,1536]{2,1,0:T(8,128)(2,1)}) custom-call(bf16[1024,1536]{1,0:T(8,128)(2,1)} %convolution_convert_fusion.x_ref, bf16[3,384,1024]{2,1,0:T(8,128)(2,1)} %refs_2_.1, bf16[3,128,1536]{2,1,0:T(8,128)(2,1)} %refs_3_.1), custom_call_target="tpu_custom_call" | custom-call | flops 15728640 | bytes 15728640 | tf_op jit(solution)/shard_map/scatter_branch_weights/pallas_call | solution.py:1037
  137.5 1.8 multiply_reduce_fusion.2
  141.2 1.3 concatenate.34.refs_1_.refs_8_
  142.4 1.1 multiply_convert_fusion.2.refs_0_
  143.5 95.9 %gather_all.1 = (bf16[256,1536]{1,0:T(8,128)(2,1)}, s32[16,256]{1,0:T(8,128)}, bf16[256,1536]{1,0:T(8,128)(2,1)}, s32[16,256]{1,0:T(8,128)}, bf16[256,1536]{1,0:...) custom-call(bf16[256,1536]{1,0:T(8,128)(2,1)} %multiply_convert_fusi, ...), custom_call_target="tpu_custom_call", output_to_operand_aliasing={{30}: (4, {}), {31}: (5, {})} | custom-call | flops 31457280 | bytes 31457280 | tf_op jit(solution)/shard_map/gather_all/pallas_call | solution.py:678
  239.4 23.1 %experts_forward.3 = (bf16[256,1536]{1,0:T(8,128)(2,1)}, bf16[256,1536]{1,0:T(8,128)(2,1)}, bf16[256,1536]{1,0:T(8,128)(2,1)}, bf16[256,1536]{1,0:T(8,128)(2,1)}...) custom-call(s32[1]{0:T(128)} %bitcast.6.me_ref, ...), custom_call_target="tpu_custom_call" | custom-call | flops 11000000512 | bytes 40000000 | tf_op jit(solution)/shard_map/experts_forward/pallas_call | solution.py:186
  262.5 1.3 slice.132
  263.8 23.6 %experts_forward.2 = (bf16[256,1536]{1,0:T(8,128)(2,1)}, bf16[256,1536]{1,0:T(8,128)(2,1)}, bf16[256,1536]{1,0:T(8,128)(2,1)}, bf16[256,1536]{1,0:T(8,128)(2,1)}...) custom-call(s32[1]{0:T(128)} %bitcast.6.me_ref, ...), custom_call_target="tpu_custom_call" | custom-call | flops 11000000512 | bytes 40000000 | tf_op jit(solution)/shard_map/experts_forward/pallas_call | solution.py:186
  287.4 1.2 slice.131
  289.9 4.0 collective-permute-start
  295.2 64.7 %scatter_outputs.1 = f32[256,1536]{1,0:T(8,128)} custom-call(bf16[256,1536]{1,0:T(8,128)(2,1)} %get-tuple-element.150.refs_0_, bf16[256,1536]{1,0:T(8,128)(2,1)} %get-tuple-element.151.refs_1_, bf16[256,1536]{1,0:T(8,128)(2,1)} %get-tuple-element.152.refs_2_, bf16[256,1536]{1,0:T(8,128)(2,1)} %get-tuple-element.153.refs_3_, ...), custom_call_target="tpu_custom_call" | custom-call | flops 19660800 | bytes 19660800 | tf_op jit(solution)/shard_map/scatter_outputs/pallas_call | solution.py:774
  360.7 2.8 multiply_convert_fusion.3.refs_0_
  363.5 60.7 %gather_tokens.1 = (bf16[256,1536]{1,0:T(8,128)(2,1)}, bf16[256,1536]{1,0:T(8,128)(2,1)}, bf16[256,1536]{1,0:T(8,128)(2,1)}, bf16[256,1536]{1,0:T(8,128)(2,1)}, ...) custom-call(bf16[256,1536]{1,0:T(8,128)(2,1)} %multiply_convert_fusi, ...), custom_call_target="tpu_custom_call" | custom-call | flops 31457280 | bytes 31457280 | tf_op jit(solution)/shard_map/gather_tokens/pallas_call | solution.py:678
  424.2 25.7 %experts_backward.2 = (bf16[256,1664]{1,0:T(8,128)(2,1)}, bf16[256,1664]{1,0:T(8,128)(2,1)}, bf16[256,1664]{1,0:T(8,128)(2,1)}, bf16[256,1664]{1,0:T(8,128)(2,1)...) custom-call(s32[1]{0:T(128)} %bitcast.6.me_ref, ...), custom_call_target="tpu_custom_call" | custom-call | flops 11000000512 | bytes 40000000 | tf_op jit(solution)/shard_map/experts_backward/pallas_call | solution.py:265
  449.9 25.2 %experts_backward.3 = (bf16[256,1664]{1,0:T(8,128)(2,1)}, bf16[256,1664]{1,0:T(8,128)(2,1)}, bf16[256,1664]{1,0:T(8,128)(2,1)}, bf16[256,1664]{1,0:T(8,128)(2,1)...) custom-call(s32[1]{0:T(128)} %bitcast.6.me_ref, ...), custom_call_target="tpu_custom_call" | custom-call | flops 11000000512 | bytes 40000000 | tf_op jit(solution)/shard_map/experts_backward/pallas_call | solution.py:265
  475.1 72.1 %scatter_grads.1 = f32[256,1664]{1,0:T(8,128)} custom-call(bf16[256,1664]{1,0:T(8,128)(2,1)} %get-tuple-element.194.refs_0_, bf16[256,1664]{1,0:T(8,128)(2,1)} %get-tuple-element.195.refs_1_, bf16[256,1664]{1,0:T(8,128)(2,1)} %get-tuple-element.196.refs_2_, bf16[256,1664]{1,0:T(8,128)(2,1)} %get-tuple-element.197.refs_3_, ...), custom_call_target="tpu_custom_call" | custom-call | flops 21299200 | bytes 21299200 | tf_op jit(solution)/shard_map/scatter_grads/pallas_call | solution.py:774
  547.2 1.2 slice.133
  548.4 1.1 multiply_reduce_fusion.3
  549.6 4.7 multiply_reduce_fusion
  555.6 21.6 %expert_weights.1 = (bf16[3,1536,512]{2,1,0:T(8,128)(2,1)}, bf16[3,256,1536]{2,1,0:T(8,128)(2,1)}) custom-call(s32[1]{0:T(128)} %bitcast.10.after_ref, bf16[8,3,112,1536]{3,2,1,0:T(8,128)(2,1)} %get-tuple-element.221.refs_0_, bf16[8,3,112,512]{3,2,1,0:T(8,128)(2,1)} %get-tuple-element.222.refs_1_, bf16[8,3,112,256]{3,2,1,0:T(8,128)(2,1)} %get-tuple-element.223.refs_2_, ...), custom_call_target="tpu_custom_call" | custom-call | flops 14000000000 | bytes 40000000 | tf_op jit(solution)/shard_map/expert_weights/pallas_call | solution.py:313
  577.2 1.2 slice.134
  579.7 4.5 multiply_convert_fusion.1
  584.2 40.0 %gather_branch_grads.1 = (bf16[1024,1536]{1,0:T(8,128)(2,1)}, bf16[384,1024]{1,0:T(8,128)(2,1)}, bf16[128,1536]{1,0:T(8,128)(2,1)}) custom-call(bf16[256,1536]{1,0:T(8,128)(2,1)} %get-tuple-element.255.x_ref, bf16[3,1536,512]{2,1,0:T(8,128)(2,1)} %get-tuple-element.230.grad_gate_up, bf16[3,256,1536]{2,1,0:T(8,128)(2,1)} %get-tuple-element.229.grad_down), custom_call_target="tpu_custom_call" | custom-call | flops 15728640 | bytes 15728640 | tf_op jit(solution)/shard_map/gather_branch_grads/pallas_call | solution.py:1068
  624.3 4.5 convolution_convert_fusion.2
  628.8 1.3 collective-permute-start.1
  630.1 1.3 collective-permute-start.2
  631.4 1.3 collective-permute-start.3
  632.7 1.3 fusion.27
  634.0 2.3 convolution_convert_fusion.3.grad_ref
  636.9 23.3 %attend_back.1 = (f32[384,1024]{1,0:T(8,128)}, f32[128,1024]{1,0:T(8,128)}, f32[128,1024]{1,0:T(8,128)}) custom-call(bf16[384,1024]{1,0:T(8,128)(2,1)} %bitcast.58, bf16[128,1024]{1,0:T(8,128)(2,1)} %bitcast.70, bf16[128,1024]{1,0:T(8,128)(2,1)} %slice.205.v_ref, bf16[384,1024]{1,0:T(8,128)(2,1)} %convolution_convert_fusion.3.grad_ref), custom_call_target="tpu_custom_call" | custom-call | flops 30000001024 | bytes 10000000 | tf_op jit(solution)/shard_map/attend_back/pallas_call | solution.py:1290
  660.2 1.9 convert.46
  664.0 1.1 subtract_convert_fusion.2
  666.1 1.0 copy-done.37
  667.1 3.8 convolution_convert_fusion.1.grads
  671.0 12.3 %collective-permute-done.2 = bf16[384,1536]{1,0:T(8,128)(2,1)} collective-permute-done((bf16[384,1536]{1,0:T(8,128)(2,1)}, bf16[384,1536]{1,0:T(8,128)(2,1)}, u32[]{:S(2)}, u32[]{:S(2)}) %collective-permute-start.2) | collective-permute-done | bytes 1179680 | tf_op jit(solution)/shard_map/ppermute | solution.py:1388
  683.3 3.0 fusion.22
  686.3 2.4 collective-permute-start.4
  690.5 4.1 multiply_convert_fusion.x_ref
  694.6 39.1 %scatter_normed_grads.1 = (f32[256,1536]{1,0:T(8,128)}, bf16[384,1024]{1,0:T(8,128)(2,1)}, bf16[128,1536]{1,0:T(8,128)(2,1)}) custom-call(bf16[1024,1536]{1,0:T(8,128)(2,1)} %multiply_convert_fusion.x_ref, bf16[3,1536,512]{2,1,0:T(8,128)(2,1)} %get-tuple-element.230.grad_gate_up, bf16[3,256,1536]{2,1,0:T(8,128)(2,1)} %get-tuple-element.229.grad_down), custom_call_target="tpu_custom_call" | custom-call | flops 15728640 | bytes 15728640 | tf_op jit(solution)/shard_map/scatter_normed_grads/pallas_call | solution.py:1094
  733.7 2.6 fusion.8
  737.6 3.1 fusion.6
  740.8 1.7 add_convert_fusion
  743.0 2.4 collective-permute-start.5
  745.4 2.3 collective-permute-start.6
  747.7 2.3 collective-permute-start.7
  752.2 73.3 %dense_reduce.1 = (bf16[384,2560]{1,0:T(8,128)(2,1)}, f32[32,384]{1,0:T(8,128)}, bf16[384,1024]{1,0:T(8,128)(2,1)}, bf16[128,1536]{1,0:T(8,128)(2,1)}) custom-call(bf16[1536,640]{1,0:T(8,128)(2,1)} %convolution_convert_fusion.1.grads, f32[4,32,384]{2,1,0:T(8,128)} %fusion.10.small, bf16[3,1536,512]{2,1,0:T(8,128)(2,1)} %get-tuple-element.230.grad_gate_up, ...), custom_call_target="tpu_custom_call" | custom-call | flops 100000000 | bytes 100000000 | tf_op jit(solution)/shard_map/dense_reduce/pallas_call | solution.py:1216
  825.5 1.4 slice_bitcast_fusion.1
  826.9 1.2 slice.143
  828.1 1.3 fusion.24
  831.9 1.4 slice_reduce_fusion
  833.3 4.3 maximum_convert_fusion
  838.8 1.6 maximum_convert_fusion.2
  840.4 1.7 maximum_convert_fusion.1
  842.1 3.7 add_convert_fusion.1
  (136 shorter events, 20.4 us)
Async XLA Ops:
  0.6 14.6 %copy-start = (bf16[384,1536]{1,0:T(8,128)(2,1)S(1)}, bf16[384,1536]{1,0:T(8,128)(2,1)}, u32[]{:S(2)}) copy-start(bf16[384,1536]{1,0:T(8,128)(2,1)} %param.19) | copy-start | bytes 3538948
  0.7 14.7 %copy-start.2 = (bf16[256,1536]{1,0:T(8,128)(2,1)S(1)}, bf16[256,1536]{1,0:T(8,128)(2,1)}, u32[]{:S(2)}) copy-start(bf16[256,1536]{1,0:T(8,128)(2,1)} %param.13) | copy-start | bytes 2359300
  13.9 3.6 copy-start.19
  15.2 3.0 copy-start.30
  15.3 3.0 copy-start.26
  59.7 1.5 copy-start.6
  59.8 2.2 copy-start.14
  61.9 1.4 slice-start
  65.3 15.9 %copy-start.40 = (bf16[384,1536]{1,0:T(8,128)(2,1)S(1)}, bf16[384,1536]{1,0:T(8,128)(2,1)}, u32[]{:S(2)}) copy-start(bf16[384,1536]{1,0:T(8,128)(2,1)} %get-tuple-element.130) | copy-start | bytes 3538948
  137.5 2.4 copy-start.34
  137.5 3.0 copy-start.17
  137.5 3.6 copy-start.23
  139.3 0.6 copy-start.31
  139.9 99.5 %copy-start.28 = (f32[256]{0:T(256)}, f32[256]{0:T(256)S(1)}, u32[]{:S(2)}) copy-start(f32[256]{0:T(256)S(1)} %fusion.19) | copy-start | bytes 3076
  263.8 30.9 %copy-start.5 = (bf16[256,1536]{1,0:T(8,128)(2,1)S(1)}, bf16[256,1536]{1,0:T(8,128)(2,1)}, u32[]{:S(2)}) copy-start(bf16[256,1536]{1,0:T(8,128)(2,1)} %multiply_convert_fusion.2.refs_0_) | copy-start | bytes 2359300
  263.8 30.9 %copy-start.21 = (bf16[4,3,8,384]{3,2,0,1:T(8,128)(2,1)S(1)}, bf16[4,3,8,384]{3,2,0,1:T(8,128)(2,1)}, u32[]{:S(2)}) copy-start(bf16[4,3,8,384]{3,2,0,1:T(8,128)(2,1)} %copy.41) | copy-start | bytes 221188
  289.9 70.1 %collective-permute-start = (s32[1]{0:T(128)}, s32[1]{0:T(128)}, u32[]{:S(2)}, u32[]{:S(2)}) collective-permute-start(s32[1]{0:T(128)} %bitcast.8), channel_id=1, source_target_pairs={{0,8},{8,0},{16,24},{24,16},{1,9},{9,1},{17,25},{25,17},{2,10},{10... | collective-permute-start | bytes 20 | tf_op jit(solution)/shard_map/ppermute | solution.py:45
  294.0 0.6 copy-start.15
  295.2 65.4 %copy-start.35 = (s32[256]{0:T(256)S(1)}, s32[256]{0:T(256)}, u32[]{:S(2)}) copy-start(s32[256]{0:T(256)} %param.15) | copy-start | bytes 3076
  475.1 73.3 %copy-start.16 = (pred[256,24]{1,0:T(32,128)(4,1)S(1)}, pred[256,24]{1,0:T(32,128)(4,1)}, u32[]{:S(2)}) copy-start(pred[256,24]{1,0:T(32,128)(4,1)} %copy-done.15) | copy-start | bytes 18436
  475.1 74.4 %copy-start.22 = (bf16[4,3,8,384]{3,2,0,1:T(8,128)(2,1)S(1)}, bf16[4,3,8,384]{3,2,0,1:T(8,128)(2,1)}, u32[]{:S(2)}) copy-start(bf16[4,3,8,384]{3,2,0,1:T(8,128)(2,1)} %copy.41) | copy-start | bytes 221188
  475.1 74.4 %copy-start.29 = (f32[256]{0:T(256)S(1)}, f32[256]{0:T(256)}, u32[]{:S(2)}) copy-start(f32[256]{0:T(256)} %copy-done.28) | copy-start | bytes 3076
  549.6 4.7 copy-start.32
  584.2 40.0 %copy-start.42 = (bf16[384,1024]{1,0:T(8,128)(2,1)S(1)}, bf16[384,1024]{1,0:T(8,128)(2,1)}, u32[]{:S(2)}) copy-start(bf16[384,1024]{1,0:T(8,128)(2,1)} %attend.1) | copy-start | bytes 2359300
  624.3 9.7 %copy-start.38 = (bf16[1024,1536]{1,0:T(8,128)(2,1)S(1)}, bf16[1024,1536]{1,0:T(8,128)(2,1)}, u32[]{:S(2)}) copy-start(bf16[1024,1536]{1,0:T(8,128)(2,1)} %get-tuple-element.231) | copy-start | bytes 9437188
  624.3 9.7 %copy-start.41 = (bf16[384,1536]{1,0:T(8,128)(2,1)S(1)}, bf16[384,1536]{1,0:T(8,128)(2,1)}, u32[]{:S(2)}) copy-start(bf16[384,1536]{1,0:T(8,128)(2,1)} %get-tuple-element.130) | copy-start | bytes 3538948
  628.8 42.2 %collective-permute-start.1 = (bf16[384,1536]{1,0:T(8,128)(2,1)}, bf16[384,1536]{1,0:T(8,128)(2,1)}, u32[]{:S(2)}, u32[]{:S(2)}) collective-permute-start(bf16[384,1536]{1,0:T(8,128)(2,1)} %convolution_convert_fusion.2), channel_id=1, source_target_pairs={{8,0},{17,9},{26,18},{3,27},{12,4},{21,13},{30,22},{7,31}} | collective-permute-start | bytes 3538952 | tf_op jit(solution)/shard_map/ppermute | solution.py:1388
  630.1 53.2 %collective-permute-start.2 = (bf16[384,1536]{1,0:T(8,128)(2,1)}, bf16[384,1536]{1,0:T(8,128)(2,1)}, u32[]{:S(2)}, u32[]{:S(2)}) collective-permute-start(bf16[384,1536]{1,0:T(8,128)(2,1)} %convolution_convert_fusion.2), channel_id=1, source_target_pairs={{16,0},{25,9},{2,18},{11,27},{20,4},{29,13},{6,22},{15,31}} | collective-permute-start | bytes 3538952 | tf_op jit(solution)/shard_map/ppermute | solution.py:1388
  631.4 51.9 %collective-permute-start.3 = (bf16[384,1536]{1,0:T(8,128)(2,1)}, bf16[384,1536]{1,0:T(8,128)(2,1)}, u32[]{:S(2)}, u32[]{:S(2)}) collective-permute-start(bf16[384,1536]{1,0:T(8,128)(2,1)} %convolution_convert_fusion.2), channel_id=1, source_target_pairs={{24,0},{1,9},{10,18},{19,27},{28,4},{5,13},{14,22},{23,31}} | collective-permute-start | bytes 3538952 | tf_op jit(solution)/shard_map/ppermute | solution.py:1388
  636.9 25.2 %copy-start.33 = (f32[1536]{0:T(1024)S(1)}, f32[1536]{0:T(1024)}, u32[]{:S(2)}) copy-start(f32[1536]{0:T(1024)} %get-tuple-element.244) | copy-start | bytes 18436
  660.2 4.9 copy-start.9
  665.1 1.0 copy-start.18
  665.1 2.0 copy-start.37
  671.0 19.5 %copy-start.39 = (bf16[1536,640]{1,0:T(8,128)(2,1)S(1)}, bf16[1536,640]{1,0:T(8,128)(2,1)}, u32[]{:S(2)}) copy-start(bf16[1536,640]{1,0:T(8,128)(2,1)} %get-tuple-element.128) | copy-start | bytes 5898244
  686.3 2.4 copy-start.3
  686.3 54.4 %collective-permute-start.4 = (bf16[384,1536]{1,0:T(8,128)(2,1)S(1)}, bf16[384,1536]{1,0:T(8,128)(2,1)}, u32[]{:S(2)}, u32[]{:S(2)}) collective-permute-start(bf16[384,1536]{1,0:T(8,128)(2,1)S(1)} %get-tuple-element.253), channel_id=1, source_target_pairs={{0,4},{1,5},{2,6},{3,7},{4,0},{5,1},{6,2},{7,3},{8,12},{9,13},{10,... | collective-permute-start | bytes 3538952 | tf_op jit(solution)/shard_map/ppermute | solution.py:45
  694.6 39.1 %copy-start.20 = (f32[1536]{0:T(1024)S(1)}, f32[1536]{0:T(1024)}, u32[]{:S(2)}) copy-start(f32[1536]{0:T(1024)} %copy-done.19) | copy-start | bytes 18436
  694.6 39.1 %copy-start.27 = (f32[256]{0:T(256)S(1)}, f32[256]{0:T(256)}, u32[]{:S(2)}) copy-start(f32[256]{0:T(256)} %copy-done.26) | copy-start | bytes 3076
  733.7 3.9 copy-start.7
  737.6 3.2 copy-start.4
  740.8 10.6 %copy-start.10 = (f32[3,4,8,384]{3,2,0,1:T(8,128)S(1)}, f32[3,4,8,384]{3,2,0,1:T(8,128)}, u32[]{:S(2)}) copy-start(f32[3,4,8,384]{3,2,0,1:T(8,128)} %copy.43) | copy-start | bytes 442372
  740.8 10.6 %copy-start.24 = (f32[1,4,384]{2,0,1:T(1,128)S(1)}, f32[1,4,384]{2,0,1:T(1,128)}, u32[]{:S(2)}) copy-start(f32[1,4,384]{2,0,1:T(1,128)} %concatenate.38) | copy-start | bytes 18436
  740.8 10.6 %copy-start.25 = (f32[1,4,384]{2,0,1:T(1,128)S(1)}, f32[1,4,384]{2,0,1:T(1,128)}, u32[]{:S(2)}) copy-start(f32[1,4,384]{2,0,1:T(1,128)} %concatenate.37) | copy-start | bytes 18436
  740.8 10.6 %copy-start.36 = (f32[32]{0:T(128)S(1)}, f32[32]{0:T(128)}, u32[]{:S(2)}) copy-start(f32[32]{0:T(128)} %pad.22.clone) | copy-start | bytes 388
  743.0 99.0 %collective-permute-start.5 = (bf16[384,1536]{1,0:T(8,128)(2,1)S(1)}, bf16[384,1536]{1,0:T(8,128)(2,1)}, u32[]{:S(2)}, u32[]{:S(2)}) collective-permute-start(bf16[384,1536]{1,0:T(8,128)(2,1)S(1)} %add_convert_fusion), channel_id=1, source_target_pairs={{0,1},{9,8},{18,19},{27,26},{4,5},{13,12},{22,23},{31,30}} | collective-permute-start | bytes 3538952 | tf_op jit(solution)/shard_map/ppermute | solution.py:1388
  745.4 96.7 %collective-permute-start.6 = (bf16[384,1536]{1,0:T(8,128)(2,1)S(1)}, bf16[384,1536]{1,0:T(8,128)(2,1)}, u32[]{:S(2)}, u32[]{:S(2)}) collective-permute-start(bf16[384,1536]{1,0:T(8,128)(2,1)S(1)} %add_convert_fusion), channel_id=1, source_target_pairs={{0,2},{9,11},{18,16},{27,25},{4,6},{13,15},{22,20},{31,29}} | collective-permute-start | bytes 3538952 | tf_op jit(solution)/shard_map/ppermute | solution.py:1388
  747.7 94.4 %collective-permute-start.7 = (bf16[384,1536]{1,0:T(8,128)(2,1)S(1)}, bf16[384,1536]{1,0:T(8,128)(2,1)}, u32[]{:S(2)}, u32[]{:S(2)}) collective-permute-start(bf16[384,1536]{1,0:T(8,128)(2,1)S(1)} %add_convert_fusion), channel_id=1, source_target_pairs={{0,3},{9,10},{18,17},{27,24},{4,7},{13,14},{22,21},{31,28}} | collective-permute-start | bytes 3538952 | tf_op jit(solution)/shard_map/ppermute | solution.py:1388
  833.3 4.3 copy-start.8
  837.6 1.0 copy-start.11
  837.6 1.1 copy-start.12
  837.6 1.2 copy-start.13
  842.1 3.8 copy-start.1

commit v5 on v4

--- a/solution.py
+++ b/solution.py
@@ -694,15 +694,23 @@
     return pairs, out[15 * count :]
 
 
-def plane_scatter_kernel(half, *refs):
+def plane_scatter_kernel(half, i, *refs):
     parts = {"near": refs[:8], "far": refs[8:16]}
-    out, core_in, sums, diag_in, last_in, z_out, z_in = refs[16:23]
-    wire = Wire(*refs[23:])
+    refs = refs[16:]
+    carried = ()
+    if i is not None:
+        carried, refs = refs[:2] + refs[3:5] + refs[11:15], refs[2:3] + refs[5:11] + refs[15:]
+    out, core_in, sums, diag_in, last_in, z_out, z_in = refs[:7]
+    wire = Wire(*refs[7:])
     core, side_x, side_y, across = partners = neighbours(half)
     rows = out.shape[0] // 2
     cut = rows // 2
     low, high = pl.ds(0, cut), pl.ds(cut, cut)
-    greet(partners)
+    if carried:
+        greet(partners + [{"dp": plane_places()[1]}])
+        cargo = GradsOut(wire, i, *carried)
+    else:
+        greet(partners)
     segments = [(kind, h) for kind in ("far", "near") for h in range(2)]
     from_core, from_diag, from_last, from_z = {}, {}, {}, {}
 
@@ -760,25 +768,30 @@
         (leave, 3),
     ):
         step(s)
+        if carried and (step, s) == (leave, 1):
+            cargo.cross()
     for h in range(2):
         from_z[h].wait_recv()
         target = out.at[pl.ds(h * rows, rows)]
         add_into(rows, target, target, z_in.at[h])
+    if carried:
+        cargo.finish()
     wire.finish()
 
 
-def plane_scatter(near, far, half, number, name):
+def plane_scatter(near, far, half, number, name, i=None, grads=()):
     rows, width = near[0].shape
     specs = [ON_CHIP, ANYWHERE] * 8
     block = (rows // 2, width)
+    shapes, scratch = grads_shapes(*grads) if grads else ([], [])
     return comm_call(
-        functools.partial(plane_scatter_kernel, half),
+        functools.partial(plane_scatter_kernel, half, i),
         name,
         number,
-        42,
-        specs,
-        ON_CHIP,
-        jax.ShapeDtypeStruct((rows, width), f32),
+        42 + 2 * len(grads),
+        specs + [ANYWHERE] * len(grads),
+        [ON_CHIP] * (1 + len(shapes)),
+        [jax.ShapeDtypeStruct((rows, width), f32)] + shapes,
         [
             pltpu.VMEM((4, 4) + block, bf16),
             pltpu.VMEM((4, 4) + block, bf16),
@@ -786,9 +799,10 @@
             pltpu.VMEM((4, 2) + block, bf16),
             pltpu.VMEM((2,) + block, bf16),
             pltpu.VMEM((2,) + block, bf16),
-        ],
+        ]
+        + scratch,
         50 * rows * width,
-    )(*near, *far)
+    )(*near, *far, *grads)
 
 
 def chip_partners():
@@ -1130,11 +1144,9 @@
     )(small)
 
 
-def dense_kernel(
-    replicas, i, grads, small, grad_gate_up, grad_down, out, small_out, cargo_out, cargo_down, *refs
-):
+def dense_kernel(replicas, grads, small, out, small_out, *refs):
     y_in, z_out, z_in, small_in, small_sum, turn_in = refs[:6]
-    wire = Wire(*refs[10:])
+    wire = Wire(*refs[6:])
     e, z = lax.axis_index("expert"), lax.axis_index("dp")
     head, row = lax.rem(e, 4), lax.div(e, 4)
     partners = [{"expert": flip(e, m)} for m in (1, 2, 4)]
@@ -1152,7 +1164,6 @@
 
     small_copies = [wire.start(small.at[block[k]], small_in.at[k - 1], plane[k]) for k in plane]
     from_y = {k: wire.start(half_of(k, 1 - row), y_in.at[k], side_y) for k in order}
-    cargo = GradsOut(wire, i, grad_gate_up, grad_down, cargo_out, cargo_down, *refs[6:10])
     for copy in small_copies:
         copy.wait_recv()
     small_sum[0] = small[z] + small_in[0] + small_in[1] + small_in[2]
@@ -1173,7 +1184,6 @@
             turn = wire.start(small_sum.at[2], turn_in.at[2], side_y)
     turn.wait_recv()
     small_out[...] = small_sum[2] + turn_in[2]
-    cargo.cross()
     for k in from_z:
         from_z[k].wait_recv()
 
@@ -1204,23 +1214,21 @@
     last.append(wire.start(place(other, 1 - row), place(other, 1 - row), core))
     for copy in last:
         copy.wait_recv()
-    cargo.finish()
     wire.finish()
 
 
-def dense_reduce(grads, small, replicas, i, grad_gate_up, grad_down):
+def dense_reduce(grads, small, replicas):
     slab, width = grads.shape[0] // replicas, grads.shape[1]
     piece = (slab // 2, width)
     lot = small.shape[1:]
-    shapes, scratch = grads_shapes(grad_gate_up, grad_down)
     return comm_call(
-        functools.partial(dense_kernel, replicas, i),
+        functools.partial(dense_kernel, replicas),
         "dense_reduce",
         2,
-        27,
-        [ON_CHIP] * 2 + [ANYWHERE] * 2,
-        [ON_CHIP] * 4,
-        [jax.ShapeDtypeStruct((slab, 4 * width), bf16), jax.ShapeDtypeStruct(lot, f32)] + shapes,
+        23,
+        [ON_CHIP] * 2,
+        [ON_CHIP] * 2,
+        [jax.ShapeDtypeStruct((slab, 4 * width), bf16), jax.ShapeDtypeStruct(lot, f32)],
         [
             pltpu.VMEM((4,) + piece, bf16),
             pltpu.VMEM((4,) + piece, bf16),
@@ -1228,10 +1236,9 @@
             pltpu.VMEM((3,) + lot, f32),
             pltpu.VMEM((3,) + lot, f32),
             pltpu.VMEM((3,) + lot, f32),
-        ]
-        + scratch,
+        ],
         10**8,
-    )(grads, small, grad_gate_up, grad_down)
+    )(grads, small)
 
 
 STRIP = 256
@@ -1439,7 +1446,7 @@
         valid_count = valid_count + send(valid_count, "dp", mask)
         mask *= 2
     valid_count = valid_count[0].astype(f32)
-    final_state = mid + RESIDUAL * plane_scatter(near_parts, far_parts, half, 6, "scatter_outputs")
+    final_state = mid + RESIDUAL * plane_scatter(near_parts, far_parts, half, 6, "scatter_outputs")[0]
     activations = final_state.astype(bf16)
     mismatch = final_state - teacher.astype(f32)
     squares = jnp.sum(0.5 * valid_float[:, None] * mismatch * mismatch)
@@ -1457,10 +1464,15 @@
 
     near_grads, near_chunk = back(near_kept, grad_near)
     far_grads, far_chunk = back(far_kept, grad_far)
-    returned = plane_scatter(near_grads, far_grads, half, 7, "scatter_grads")
-    after = jnp.reshape(never(returned[0, 0]), (1,))
-    grad_gate_up, grad_down = expert_weights(after, [near_chunk, far_chunk])
-    branch_scale = jnp.where(never(grad_down[0, 0, 0]) == 0, RESIDUAL, 0.0)
+    grad_gate_up, grad_down = expert_weights(me_ref, [near_chunk, far_chunk])
+    done = []
+    if compact:
+        returned, *part = plane_scatter(
+            near_grads, far_grads, half, 7, "scatter_grads", 0, (grad_gate_up, grad_down)
+        )
+        done.append(part)
+    else:
+        (returned,) = plane_scatter(near_grads, far_grads, half, 14, "scatter_rows")
 
     grad_gates = returned[:, width : width + experts_all]
     own_routed = jnp.any(
@@ -1475,11 +1487,10 @@
     grad_moe_input = returned[:, :width] + mm("te,ed->td", grad_logits, router_t)
     grad_mid_norm, grad_gain_two = norm_two_pull(grad_moe_input)
     grad_mid = grad_final + grad_mid_norm
-    grad_branch = (branch_scale * grad_mid).astype(bf16)
-
-    done = []
+    grad_branch = (RESIDUAL * grad_mid).astype(bf16)
+
     if compact:
-        seq_grad, *part = seq_gather_grads(grad_branch, group, 0, grad_gate_up, grad_down)
+        seq_grad, *part = seq_gather_grads(grad_branch, group, 1, grad_gate_up, grad_down)
         done.append(part)
     else:
         seq_grad = seq_gather(grad_branch, group, 3, "gather_normed")
@@ -1505,7 +1516,7 @@
     normed_parts = mm("ct,dc->td", grad_lin, qkv)
     normed_parts = (entered * normed_parts if compact else normed_parts).astype(bf16)
     if compact:
-        grad_normed, *part = seq_scatter_grads(normed_parts, group, 1, grad_gate_up, grad_down)
+        grad_normed, *part = seq_scatter_grads(normed_parts, group, 2, grad_gate_up, grad_down)
         done.append(part)
     else:
         grad_normed = seq_scatter(normed_parts, group, 4, "scatter_branch")
@@ -1539,10 +1550,7 @@
         g_out = g_out.astype(f32)
         lot = jnp.where(never(out_sum[0, 0]) == 0, lot, 0.0)
         lot = jnp.transpose(lot.reshape(32, replicas, slab), (1, 0, 2))
-        by_head, lot, *part = dense_reduce(
-            grad_qkv, lot, replicas, 2, grad_gate_up, grad_down
-        )
-        done.append(part)
+        by_head, lot = dense_reduce(grad_qkv, lot, replicas)
         gate_up_out, down_out = [jnp.stack(x).astype(f32) for x in zip(*done)]
     else:
         out_sum = other_sequences(lax.psum(grad_out, "dp")).astype(bf16)

time: 853 us -> 857 us (level)
  waiting for transfers between devices: 12.4 us -> 35.7 us
  Pallas kernels: 702 us -> 692 us
    ppermute x2, waiting for transfers between devices: 0.01 us -> 18.1 us  [send(): return lax.ppermute(x, axis, [(i, i ^ mask) for i in range(count)])]
    pallas_call x3, Pallas kernels: 210 us -> 200 us  [the longest x2 155 us: plane_scatter(): comm_call(functools.partial(plane_scatter_kernel, half, i), name, number,...]
  transfers between devices with their start and end apart: 8 -> 8, of which waited for: 1 -> 2; matrix products, arithmetic and copies ran while one was open for 5% -> 4% of each run, Pallas kernels for 24% -> 16%
where the time goes in v5:
time: 857 us; the launch traced here: 851 us
  Pallas kernels  692 us (81%)
  other arithmetic  44.8 us (5%)
  waiting for transfers between devices  35.7 us (4%)
  matrix products  30.3 us (4%)
  local copies, waits for them, and re-layouts  25.1 us (3%)
  starting transfers between devices  14.8 us (2%)
    pallas_call x2, Pallas kernels, plane_gather(): comm_call(functools.partial(plane_gather_kernel, half, experts, count), n...  156 us
    pallas_call x2, Pallas kernels, plane_scatter(): comm_call(functools.partial(plane_scatter_kernel, half, i), name, number,...  155 us
    pallas_call x1, Pallas kernels, seq_scatter_weights(): comm_call(functools.partial(scatter_weights_kernel, group, experts), 'sca...  51.7 us
    pallas_call x2, Pallas kernels, experts_backward(): pl.pallas_call(experts_back_kernel, grid_spec=pltpu.PrefetchScalarGridSpe...  50.6 us
    pallas_call x2, Pallas kernels, experts_forward(): pl.pallas_call(experts_kernel, grid_spec=pltpu.PrefetchScalarGridSpec(num...  47.1 us
    pallas_call x1, Pallas kernels, dense_reduce(): comm_call(functools.partial(dense_kernel, replicas), 'dense_reduce', 2, 2...  45.2 us
    pallas_call x1, Pallas kernels, seq_gather_grads(): comm_call(functools.partial(gather_grads_kernel, group, i), 'gather_branc...  41.7 us
    pallas_call x2, Pallas kernels, on_chip_call(): pl.pallas_call(kernel, in_specs=[ON_CHIP] * len(inputs), out_specs=[ON_CH...  39 us
  transfers between devices with their start and end apart: 8, of which 2 were waited for; matrix products, arithmetic and copies ran while one was open for 4% of the time, Pallas kernels for 16%

profile of v5, /device:TPU:0, one launch (start us, length us, event | category | flops | bytes accessed | tf_op | source)
XLA Modules:
  0.0 851.2 jit_solution(11977458754965467284)
XLA Ops:
  2.3 1.4 maximum_maximum_fusion.small_ref
  3.7 9.3 %start_exchange.1 = bf16[4,32,384]{2,1,0:T(8,128)(2,1)} custom-call(bf16[32,384]{1,0:T(8,128)(2,1)} %maximum_maximum_fusion.small_ref), custom_call_target="tpu_custom_call" | custom-call | flops 1000000 | bytes 1000000 | tf_op jit(solution)/shard_map/start_exchange/pallas_call | solution.py:1134
  13.9 1.4 fusion.7
  15.3 1.1 fusion.2.x_ref
  16.5 1.0 constant_dynamic-slice_fusion
  18.3 36.7 %attention_entry.1 = (bf16[1024,1536]{1,0:T(8,128)(2,1)}, bf16[1536,640]{1,0:T(8,128)(2,1)}, bf16[384,1536]{1,0:T(8,128)(2,1)}) custom-call(bf16[256,1536]{1,0:T(8,128)(2,1)} %fusion.2.x_ref, bf16[384,640]{1,0:T(8,128)(2,1)} %pad_maximum_fusion.4.qkv_in, bf16[384,1536]{1,0:T(8,128)(2,1)} %out_in.1), custom_call_target="tpu_custom_call" | custom-call | flops 15728640 | bytes 15728640 | tf_op jit(solution)/shard_map/attention_entry/pallas_call | solution.py:1020
  55.0 4.7 fusion.28
  59.8 1.4 copy-done.10
  63.5 1.0 maximum_multiply_fusion
  65.2 15.9 %attend.1 = bf16[384,1024]{1,0:T(8,128)(2,1)} custom-call(bf16[384,1024]{1,0:T(8,128)(2,1)} %bitcast.55, bf16[128,1024]{1,0:T(8,128)(2,1)} %bitcast.67, bf16[128,1024]{1,0:T(8,128)(2,1)} %slice.197.v_ref), custom_call_target="tpu_custom_call" | custom-call | flops 10000000000 | bytes 10000000 | tf_op jit(solution)/shard_map/attend/pallas_call | solution.py:1297
  81.1 4.6 convolution_convert_fusion.x_ref
  85.7 51.7 %scatter_branch_weights.1 = (f32[256,1536]{1,0:T(8,128)}, bf16[3,1536,512]{2,1,0:T(8,128)(2,1)}, bf16[3,256,1536]{2,1,0:T(8,128)(2,1)}) custom-call(bf16[1024,1536]{1,0:T(8,128)(2,1)} %convolution_convert_fusion.x_ref, bf16[3,384,1024]{2,1,0:T(8,128)(2,1)} %refs_2_.1, bf16[3,128,1536]{2,1,0:T(8,128)(2,1)} %refs_3_.1), custom_call_target="tpu_custom_call" | custom-call | flops 15728640 | bytes 15728640 | tf_op jit(solution)/shard_map/scatter_branch_weights/pallas_call | solution.py:1051
  137.4 1.8 multiply_reduce_fusion.2
  141.0 1.3 concatenate.34.refs_1_.refs_8_
  142.3 1.1 multiply_convert_fusion.2.refs_0_
  143.4 95.9 %gather_all.1 = (bf16[256,1536]{1,0:T(8,128)(2,1)}, s32[16,256]{1,0:T(8,128)}, bf16[256,1536]{1,0:T(8,128)(2,1)}, s32[16,256]{1,0:T(8,128)}, bf16[256,1536]{1,0:...) custom-call(bf16[256,1536]{1,0:T(8,128)(2,1)} %multiply_convert_fusi, ...), custom_call_target="tpu_custom_call", output_to_operand_aliasing={{30}: (4, {}), {31}: (5, {})} | custom-call | flops 31457280 | bytes 31457280 | tf_op jit(solution)/shard_map/gather_all/pallas_call | solution.py:678
  239.3 23.1 %experts_forward.2 = (bf16[256,1536]{1,0:T(8,128)(2,1)}, bf16[256,1536]{1,0:T(8,128)(2,1)}, bf16[256,1536]{1,0:T(8,128)(2,1)}, bf16[256,1536]{1,0:T(8,128)(2,1)}...) custom-call(s32[1]{0:T(128)} %bitcast.6.me_ref.after_ref, ...), custom_call_target="tpu_custom_call" | custom-call | flops 11000000512 | bytes 40000000 | tf_op jit(solution)/shard_map/experts_forward/pallas_call | solution.py:186
  262.4 1.3 slice.125
  263.6 24.0 %experts_forward.3 = (bf16[256,1536]{1,0:T(8,128)(2,1)}, bf16[256,1536]{1,0:T(8,128)(2,1)}, bf16[256,1536]{1,0:T(8,128)(2,1)}, bf16[256,1536]{1,0:T(8,128)(2,1)}...) custom-call(s32[1]{0:T(128)} %bitcast.6.me_ref.after_ref, ...), custom_call_target="tpu_custom_call" | custom-call | flops 11000000512 | bytes 40000000 | tf_op jit(solution)/shard_map/experts_forward/pallas_call | solution.py:186
  287.6 1.3 slice.126
  290.1 3.9 collective-permute-start
  295.5 64.7 %scatter_outputs.1 = f32[256,1536]{1,0:T(8,128)} custom-call(bf16[256,1536]{1,0:T(8,128)(2,1)} %get-tuple-element.151.refs_0_, bf16[256,1536]{1,0:T(8,128)(2,1)} %get-tuple-element.152.refs_1_, bf16[256,1536]{1,0:T(8,128)(2,1)} %get-tuple-element.153.refs_2_, bf16[256,1536]{1,0:T(8,128)(2,1)} %get-tuple-element.154.refs_3_, ...), custom_call_target="tpu_custom_call" | custom-call | flops 19660800 | bytes 19660800 | tf_op jit(solution)/shard_map/scatter_outputs/pallas_call | solution.py:787
  360.9 2.8 multiply_convert_fusion.3.refs_0_
  363.7 60.6 %gather_tokens.1 = (bf16[256,1536]{1,0:T(8,128)(2,1)}, bf16[256,1536]{1,0:T(8,128)(2,1)}, bf16[256,1536]{1,0:T(8,128)(2,1)}, bf16[256,1536]{1,0:T(8,128)(2,1)}, ...) custom-call(bf16[256,1536]{1,0:T(8,128)(2,1)} %multiply_convert_fusi, ...), custom_call_target="tpu_custom_call" | custom-call | flops 31457280 | bytes 31457280 | tf_op jit(solution)/shard_map/gather_tokens/pallas_call | solution.py:678
  424.3 25.2 %experts_backward.2 = (bf16[256,1664]{1,0:T(8,128)(2,1)}, bf16[256,1664]{1,0:T(8,128)(2,1)}, bf16[256,1664]{1,0:T(8,128)(2,1)}, bf16[256,1664]{1,0:T(8,128)(2,1)...) custom-call(s32[1]{0:T(128)} %bitcast.6.me_ref.after_ref, ...), custom_call_target="tpu_custom_call" | custom-call | flops 11000000512 | bytes 40000000 | tf_op jit(solution)/shard_map/experts_backward/pallas_call | solution.py:265
  449.6 25.4 %experts_backward.3 = (bf16[256,1664]{1,0:T(8,128)(2,1)}, bf16[256,1664]{1,0:T(8,128)(2,1)}, bf16[256,1664]{1,0:T(8,128)(2,1)}, bf16[256,1664]{1,0:T(8,128)(2,1)...) custom-call(s32[1]{0:T(128)} %bitcast.6.me_ref.after_ref, ...), custom_call_target="tpu_custom_call" | custom-call | flops 11000000512 | bytes 40000000 | tf_op jit(solution)/shard_map/experts_backward/pallas_call | solution.py:265
  474.9 21.4 %expert_weights.1 = (bf16[3,1536,512]{2,1,0:T(8,128)(2,1)}, bf16[3,256,1536]{2,1,0:T(8,128)(2,1)}) custom-call(s32[1]{0:T(128)} %bitcast.6.me_ref.after_ref, bf16[8,3,112,1536]{3,2,1,0:T(8,128)(2,1)} %get-tuple-element.222.refs_0_, bf16[8,3,112,512]{3,2,1,0:T(8,128)(2,1)} %get-tuple-element.223.refs_1_, bf16[8,3,112,256]{3,2,1,0:T(8,128)(2,1)} %get-tuple-element.224.refs_2_, ...), custom_call_target="tpu_custom_call" | custom-call | flops 14000000000 | bytes 40000000 | tf_op jit(solution)/shard_map/expert_weights/pallas_call | solution.py:313
  496.3 89.8 %scatter_grads.1 = (f32[256,1664]{1,0:T(8,128)}, bf16[384,1024]{1,0:T(8,128)(2,1)}, bf16[128,1536]{1,0:T(8,128)(2,1)}) custom-call(bf16[256,1664]{1,0:T(8,128)(2,1)} %get-tuple-element.195.refs_0_, bf16[256,1664]{1,0:T(8,128)(2,1)} %get-tuple-element.196.refs_1_, bf16[256,1664]{1,0:T(8,128)(2,1)} %get-tuple-element.197.refs_2_, ...), custom_call_target="tpu_custom_call" | custom-call | flops 21299200 | bytes 21299200 | tf_op jit(solution)/shard_map/scatter_grads/pallas_call | solution.py:787
  586.2 1.1 multiply_reduce_fusion.3
  587.4 3.8 multiply_reduce_fusion
  591.2 2.4 multiply_convert_fusion.1
  593.6 41.7 %gather_branch_grads.1 = (bf16[1024,1536]{1,0:T(8,128)(2,1)}, bf16[384,1024]{1,0:T(8,128)(2,1)}, bf16[128,1536]{1,0:T(8,128)(2,1)}) custom-call(bf16[256,1536]{1,0:T(8,128)(2,1)} %get-tuple-element.257.x_ref, bf16[3,1536,512]{2,1,0:T(8,128)(2,1)} %get-tuple-element.230.refs_16_.grad_gate_up, bf16[3,256,1536]{2,1,0:T(8,128)(2,1)} %get-tuple-element.231.refs_17_.grad_down), custom_call_target="tpu_custom_call" | custom-call | flops 15728640 | bytes 15728640 | tf_op jit(solution)/shard_map/gather_branch_grads/pallas_call | solution.py:1082
  635.3 4.4 convolution_convert_fusion.3.grad_ref
  639.7 2.4 convolution_convert_fusion.2
  642.2 1.3 collective-permute-start.3
  643.4 1.3 collective-permute-start.2
  644.7 1.3 collective-permute-start.1
  646.0 2.0 fusion.27
  648.0 23.1 %attend_back.1 = (f32[384,1024]{1,0:T(8,128)}, f32[128,1024]{1,0:T(8,128)}, f32[128,1024]{1,0:T(8,128)}) custom-call(bf16[384,1024]{1,0:T(8,128)(2,1)} %bitcast.56, bf16[128,1024]{1,0:T(8,128)(2,1)} %bitcast.68, bf16[128,1024]{1,0:T(8,128)(2,1)} %slice.197.v_ref, bf16[384,1024]{1,0:T(8,128)(2,1)} %convolution_convert_fusion.3.grad_ref), custom_call_target="tpu_custom_call" | custom-call | flops 30000001024 | bytes 10000000 | tf_op jit(solution)/shard_map/attend_back/pallas_call | solution.py:1297
  671.1 1.9 convert.45
  675.5 1.1 subtract_convert_fusion.2
  677.6 1.0 copy-done.47
  678.7 3.8 convolution_convert_fusion.1.grads
  682.5 17.5 %collective-permute-done.2 = bf16[384,1536]{1,0:T(8,128)(2,1)} collective-permute-done((bf16[384,1536]{1,0:T(8,128)(2,1)}, bf16[384,1536]{1,0:T(8,128)(2,1)}, u32[]{:S(2)}, u32[]{:S(2)}) %collective-permute-start.2) | collective-permute-done | bytes 1179680 | tf_op jit(solution)/shard_map/ppermute | solution.py:1395
  700.0 3.0 fusion.22
  703.0 1.4 copy-done.4
  706.2 4.1 multiply_convert_fusion.x_ref
  710.4 38.9 %scatter_normed_grads.1 = (f32[256,1536]{1,0:T(8,128)}, bf16[384,1024]{1,0:T(8,128)(2,1)}, bf16[128,1536]{1,0:T(8,128)(2,1)}) custom-call(bf16[1024,1536]{1,0:T(8,128)(2,1)} %multiply_convert_fusion.x_ref, bf16[3,1536,512]{2,1,0:T(8,128)(2,1)} %get-tuple-element.230.refs_16_.grad_gate_up, bf16[3,256,1536]{2,1,0:T(8,128)(2,1)} %get-tuple-element.231.refs_17_.grad_down), custom_call_target="tpu_custom_call" | custom-call | flops 15728640 | bytes 15728640 | tf_op jit(solution)/shard_map/scatter_normed_grads/pallas_call | solution.py:1108
  749.4 2.0 fusion.8
  752.7 3.8 maximum_convert_fusion
  756.5 1.6 maximum_convert_fusion.2
  759.2 1.6 fusion.6
  760.8 18.1 %collective-permute-done.4 = bf16[384,1536]{1,0:T(8,128)(2,1)} collective-permute-done((bf16[384,1536]{1,0:T(8,128)(2,1)S(1)}, bf16[384,1536]{1,0:T(8,128)(2,1)}, u32[]{:S(2)}, u32[]{:S(2)}) %collective-permute-start.4) | collective-permute-done | bytes 1179680 | tf_op jit(solution)/shard_map/ppermute | solution.py:45
  778.9 1.7 add_convert_fusion
  781.1 2.3 collective-permute-start.7
  783.4 2.3 collective-permute-start.6
  785.7 2.3 collective-permute-start.5
  790.2 45.2 %dense_reduce.1 = (bf16[384,2560]{1,0:T(8,128)(2,1)}, f32[32,384]{1,0:T(8,128)}) custom-call(bf16[1536,640]{1,0:T(8,128)(2,1)} %convolution_convert_fusion.1.grads, f32[4,32,384]{2,1,0:T(8,128)} %fusion.10.small), custom_call_target="tpu_custom_call" | custom-call | flops 100000000 | bytes 100000000 | tf_op jit(solution)/shard_map/dense_reduce/pallas_call | solution.py:1224
  835.3 2.0 fusion.24
  837.3 1.3 slice.135
  839.3 1.4 slice_reduce_fusion
  840.7 2.0 maximum_convert_fusion.3
  844.4 1.7 maximum_convert_fusion.1
  846.1 3.7 add_convert_fusion.1
  (154 shorter events, 19.1 us)
Async XLA Ops:
  0.6 15.8 %copy-start = (bf16[384,1536]{1,0:T(8,128)(2,1)S(1)}, bf16[384,1536]{1,0:T(8,128)(2,1)}, u32[]{:S(2)}) copy-start(bf16[384,1536]{1,0:T(8,128)(2,1)} %param.19) | copy-start | bytes 3538948
  0.7 14.6 %copy-start.2 = (bf16[256,1536]{1,0:T(8,128)(2,1)S(1)}, bf16[256,1536]{1,0:T(8,128)(2,1)}, u32[]{:S(2)}) copy-start(bf16[256,1536]{1,0:T(8,128)(2,1)} %param.13) | copy-start | bytes 2359300
  13.9 3.6 copy-start.25
  15.2 3.0 copy-start.38
  15.3 3.0 copy-start.33
  59.7 1.5 copy-start.10
  59.8 2.1 copy-start.20
  62.0 1.4 slice-start
  65.2 15.9 %copy-start.50 = (bf16[384,1536]{1,0:T(8,128)(2,1)S(1)}, bf16[384,1536]{1,0:T(8,128)(2,1)}, u32[]{:S(2)}) copy-start(bf16[384,1536]{1,0:T(8,128)(2,1)} %get-tuple-element.131) | copy-start | bytes 3538948
  137.4 2.4 copy-start.23
  137.4 3.0 copy-start.44
  137.4 3.6 copy-start.29
  139.2 0.6 copy-start.40
  139.8 99.5 %copy-start.36 = (f32[256]{0:T(256)}, f32[256]{0:T(256)S(1)}, u32[]{:S(2)}) copy-start(f32[256]{0:T(256)S(1)} %fusion.19) | copy-start | bytes 3076
  263.6 31.2 %copy-start.6 = (bf16[256,1536]{1,0:T(8,128)(2,1)S(1)}, bf16[256,1536]{1,0:T(8,128)(2,1)}, u32[]{:S(2)}) copy-start(bf16[256,1536]{1,0:T(8,128)(2,1)} %multiply_convert_fusion.2.refs_0_) | copy-start | bytes 2359300
  263.6 31.2 %copy-start.27 = (bf16[4,3,8,384]{3,2,0,1:T(8,128)(2,1)S(1)}, bf16[4,3,8,384]{3,2,0,1:T(8,128)(2,1)}, u32[]{:S(2)}) copy-start(bf16[4,3,8,384]{3,2,0,1:T(8,128)(2,1)} %copy.41) | copy-start | bytes 221188
  290.1 70.1 %collective-permute-start = (s32[1]{0:T(128)}, s32[1]{0:T(128)}, u32[]{:S(2)}, u32[]{:S(2)}) collective-permute-start(s32[1]{0:T(128)} %bitcast.8), channel_id=1, source_target_pairs={{0,8},{8,0},{16,24},{24,16},{1,9},{9,1},{17,25},{25,17},{2,10},{10... | collective-permute-start | bytes 20 | tf_op jit(solution)/shard_map/ppermute | solution.py:45
  294.2 0.6 copy-start.21
  295.4 65.4 %copy-start.45 = (s32[256]{0:T(256)S(1)}, s32[256]{0:T(256)}, u32[]{:S(2)}) copy-start(s32[256]{0:T(256)} %param.15) | copy-start | bytes 3076
  496.3 89.9 %copy-start.22 = (pred[256,24]{1,0:T(32,128)(4,1)S(1)}, pred[256,24]{1,0:T(32,128)(4,1)}, u32[]{:S(2)}) copy-start(pred[256,24]{1,0:T(32,128)(4,1)} %copy-done.21) | copy-start | bytes 18436
  496.3 91.0 %copy-start.28 = (bf16[4,3,8,384]{3,2,0,1:T(8,128)(2,1)S(1)}, bf16[4,3,8,384]{3,2,0,1:T(8,128)(2,1)}, u32[]{:S(2)}) copy-start(bf16[4,3,8,384]{3,2,0,1:T(8,128)(2,1)} %copy.41) | copy-start | bytes 221188
  496.3 91.0 %copy-start.37 = (f32[256]{0:T(256)S(1)}, f32[256]{0:T(256)}, u32[]{:S(2)}) copy-start(f32[256]{0:T(256)} %copy-done.36) | copy-start | bytes 3076
  587.3 3.8 copy-start.41
  587.3 3.8 copy-start.3
  587.4 3.8 copy-start.9
  593.6 41.7 %copy-start.51 = (bf16[384,1536]{1,0:T(8,128)(2,1)S(1)}, bf16[384,1536]{1,0:T(8,128)(2,1)}, u32[]{:S(2)}) copy-start(bf16[384,1536]{1,0:T(8,128)(2,1)} %get-tuple-element.131) | copy-start | bytes 3538948
  635.3 4.4 copy-start.48
  635.3 4.4 copy-start.52
  642.2 40.3 %collective-permute-start.3 = (bf16[384,1536]{1,0:T(8,128)(2,1)}, bf16[384,1536]{1,0:T(8,128)(2,1)}, u32[]{:S(2)}, u32[]{:S(2)}) collective-permute-start(bf16[384,1536]{1,0:T(8,128)(2,1)} %convolution_convert_fusion.2), channel_id=1, source_target_pairs={{24,0},{1,9},{10,18},{19,27},{28,4},{5,13},{14,22},{23,31}} | collective-permute-start | bytes 3538952 | tf_op jit(solution)/shard_map/ppermute | solution.py:1395
  643.4 56.6 %collective-permute-start.2 = (bf16[384,1536]{1,0:T(8,128)(2,1)}, bf16[384,1536]{1,0:T(8,128)(2,1)}, u32[]{:S(2)}, u32[]{:S(2)}) collective-permute-start(bf16[384,1536]{1,0:T(8,128)(2,1)} %convolution_convert_fusion.2), channel_id=1, source_target_pairs={{16,0},{25,9},{2,18},{11,27},{20,4},{29,13},{6,22},{15,31}} | collective-permute-start | bytes 3538952 | tf_op jit(solution)/shard_map/ppermute | solution.py:1395
  644.7 55.3 %collective-permute-start.1 = (bf16[384,1536]{1,0:T(8,128)(2,1)}, bf16[384,1536]{1,0:T(8,128)(2,1)}, u32[]{:S(2)}, u32[]{:S(2)}) collective-permute-start(bf16[384,1536]{1,0:T(8,128)(2,1)} %convolution_convert_fusion.2), channel_id=1, source_target_pairs={{8,0},{17,9},{26,18},{3,27},{12,4},{21,13},{30,22},{7,31}} | collective-permute-start | bytes 3538952 | tf_op jit(solution)/shard_map/ppermute | solution.py:1395
  648.0 25.0 %copy-start.42 = (f32[1536]{0:T(1024)S(1)}, f32[1536]{0:T(1024)}, u32[]{:S(2)}) copy-start(f32[1536]{0:T(1024)} %get-tuple-element.246) | copy-start | bytes 18436
  648.0 25.6 %copy-start.16 = (f32[24,1536]{1,0:T(8,128)S(1)}, f32[24,1536]{1,0:T(8,128)}, u32[]{:S(2)}) copy-start(f32[24,1536]{1,0:T(8,128)} %fusion.27) | copy-start | bytes 442372
  671.1 5.6 copy-start.12
  676.7 1.0 copy-start.24
  676.7 2.0 copy-start.47
  682.5 23.7 %copy-start.49 = (bf16[1536,640]{1,0:T(8,128)(2,1)S(1)}, bf16[1536,640]{1,0:T(8,128)(2,1)}, u32[]{:S(2)}) copy-start(bf16[1536,640]{1,0:T(8,128)(2,1)} %get-tuple-element.129) | copy-start | bytes 5898244
  703.0 1.4 copy-start.4
  710.4 39.0 %copy-start.26 = (f32[1536]{0:T(1024)S(1)}, f32[1536]{0:T(1024)}, u32[]{:S(2)}) copy-start(f32[1536]{0:T(1024)} %copy-done.25) | copy-start | bytes 18436
  710.4 39.0 %copy-start.34 = (f32[256]{0:T(256)S(1)}, f32[256]{0:T(256)}, u32[]{:S(2)}) copy-start(f32[256]{0:T(256)} %copy-done.33) | copy-start | bytes 3076
  749.3 2.1 copy-start.39
  749.3 3.3 copy-start.13
  749.3 3.3 copy-start.14
  751.4 27.5 %collective-permute-start.4 = (bf16[384,1536]{1,0:T(8,128)(2,1)S(1)}, bf16[384,1536]{1,0:T(8,128)(2,1)}, u32[]{:S(2)}, u32[]{:S(2)}) collective-permute-start(bf16[384,1536]{1,0:T(8,128)(2,1)S(1)} %get-tuple-element.255), channel_id=1, source_target_pairs={{0,4},{1,5},{2,6},{3,7},{4,0},{5,1},{6,2},{7,3},{8,12},{9,13},{10,... | collective-permute-start | bytes 3538952 | tf_op jit(solution)/shard_map/ppermute | solution.py:45
  752.6 3.8 copy-start.17
  752.6 3.8 copy-start.18
  752.6 3.8 copy-start.19
  756.4 2.0 copy-start.7
  756.5 2.7 copy-start.8
  756.5 2.7 copy-start.35
  756.5 2.7 copy-start.43
  759.2 19.7 %copy-start.5 = (f32[384,1536]{1,0:T(8,128)S(1)}, f32[384,1536]{1,0:T(8,128)}, u32[]{:S(2)}) copy-start(f32[384,1536]{1,0:T(8,128)} %copy-done.4) | copy-start | bytes 7077892
  760.8 28.6 %copy-start.15 = (f32[3,4,8,384]{3,2,0,1:T(8,128)S(1)}, f32[3,4,8,384]{3,2,0,1:T(8,128)}, u32[]{:S(2)}) copy-start(f32[3,4,8,384]{3,2,0,1:T(8,128)} %copy.43) | copy-start | bytes 442372
  760.8 28.6 %copy-start.31 = (f32[1,4,384]{2,0,1:T(1,128)S(1)}, f32[1,4,384]{2,0,1:T(1,128)}, u32[]{:S(2)}) copy-start(f32[1,4,384]{2,0,1:T(1,128)} %concatenate.38) | copy-start | bytes 18436
  760.8 28.6 %copy-start.32 = (f32[1,4,384]{2,0,1:T(1,128)S(1)}, f32[1,4,384]{2,0,1:T(1,128)}, u32[]{:S(2)}) copy-start(f32[1,4,384]{2,0,1:T(1,128)} %concatenate.37) | copy-start | bytes 18436
  760.8 28.6 %copy-start.46 = (f32[32]{0:T(128)S(1)}, f32[32]{0:T(128)}, u32[]{:S(2)}) copy-start(f32[32]{0:T(128)} %pad.22.clone) | copy-start | bytes 388
  781.1 65.0 %collective-permute-start.7 = (bf16[384,1536]{1,0:T(8,128)(2,1)S(1)}, bf16[384,1536]{1,0:T(8,128)(2,1)}, u32[]{:S(2)}, u32[]{:S(2)}) collective-permute-start(bf16[384,1536]{1,0:T(8,128)(2,1)S(1)} %add_convert_fusion), channel_id=1, source_target_pairs={{0,3},{9,10},{18,17},{27,24},{4,7},{13,14},{22,21},{31,28}} | collective-permute-start | bytes 3538952 | tf_op jit(solution)/shard_map/ppermute | solution.py:1395
  783.4 62.7 %collective-permute-start.6 = (bf16[384,1536]{1,0:T(8,128)(2,1)S(1)}, bf16[384,1536]{1,0:T(8,128)(2,1)}, u32[]{:S(2)}, u32[]{:S(2)}) collective-permute-start(bf16[384,1536]{1,0:T(8,128)(2,1)S(1)} %add_convert_fusion), channel_id=1, source_target_pairs={{0,2},{9,11},{18,16},{27,25},{4,6},{13,15},{22,20},{31,29}} | collective-permute-start | bytes 3538952 | tf_op jit(solution)/shard_map/ppermute | solution.py:1395
  785.7 60.4 %collective-permute-start.5 = (bf16[384,1536]{1,0:T(8,128)(2,1)S(1)}, bf16[384,1536]{1,0:T(8,128)(2,1)}, u32[]{:S(2)}, u32[]{:S(2)}) collective-permute-start(bf16[384,1536]{1,0:T(8,128)(2,1)S(1)} %add_convert_fusion), channel_id=1, source_target_pairs={{0,1},{9,8},{18,19},{27,26},{4,5},{13,12},{22,23},{31,30}} | collective-permute-start | bytes 3538952 | tf_op jit(solution)/shard_map/ppermute | solution.py:1395
  837.3 6.9 copy-start.11
  839.3 4.3 copy-start.30
  846.1 3.8 copy-start.1

commit v6 on v5

--- a/solution.py
+++ b/solution.py
@@ -1092,30 +1092,39 @@
     )(x, grad_gate_up, grad_down)
 
 
-def scatter_grads_kernel(group, i, x_ref, grad_gate_up, grad_down, total, out, out_down, *refs):
-    wire = Wire(*refs[7:])
+def scatter_grads_kernel(
+    group, i, x_ref, grad_gate_up, grad_down, once, total, out, out_down, twice, *refs
+):
+    wire = Wire(*refs[8:])
+    other = refs[7]
+    side_y = {"expert": flip(lax.axis_index("expert"), group)}
     _, beside, opposite, _, _ = plane_places()
-    greet(chip_partners() + [{"dp": beside}, {"dp": opposite}])
+    greet(chip_partners() + [side_y, {"dp": beside}, {"dp": opposite}])
+    swap = wire.start(once, other, side_y)
     cargo = GradsOut(wire, i, grad_gate_up, grad_down, out, out_down, *refs[3:7])
     sum_seq(wire, group, x_ref, total, *refs[:3], cargo.cross)
     cargo.finish()
+    swap.wait_recv()
+    add_into(once.shape[0], twice, once, other)
     wire.finish()
 
 
-def seq_scatter_grads(x, group, i, grad_gate_up, grad_down):
+def seq_scatter_grads(x, group, i, grad_gate_up, grad_down, once):
     rows, width = x.shape[0] // group, x.shape[1]
     shapes, scratch = grads_shapes(grad_gate_up, grad_down)
     return comm_call(
         functools.partial(scatter_grads_kernel, group, i),
         "scatter_normed_grads",
         11,
-        10,
-        [ON_CHIP, ANYWHERE, ANYWHERE],
-        [ON_CHIP] * 3,
-        [jax.ShapeDtypeStruct((rows, width), f32)] + shapes,
-        seq_scratch(rows, width) + scratch,
+        11,
+        [ON_CHIP, ANYWHERE, ANYWHERE, ON_CHIP],
+        [ON_CHIP] * 4,
+        [jax.ShapeDtypeStruct((rows, width), f32)]
+        + shapes
+        + [jax.ShapeDtypeStruct(once.shape, bf16)],
+        seq_scratch(rows, width) + scratch + [pltpu.VMEM(once.shape, bf16)],
         40 * rows * width,
-    )(x, grad_gate_up, grad_down)
+    )(x, grad_gate_up, grad_down, once)
 
 
 def start_kernel(replicas, small_ref, small_out, send_sem, recv_sem):
@@ -1144,7 +1153,7 @@
     )(small)
 
 
-def dense_kernel(replicas, grads, small, out, small_out, *refs):
+def dense_kernel(replicas, grads, small, once, out, small_out, g_out, *refs):
     y_in, z_out, z_in, small_in, small_sum, turn_in = refs[:6]
     wire = Wire(*refs[6:])
     e, z = lax.axis_index("expert"), lax.axis_index("dp")
@@ -1158,6 +1167,25 @@
     block = {k: lax.rem(z + k, replicas) for k in range(replicas)}
     plane = {k: {"dp": block[k]} for k in range(1, replicas)}
     greet(partners + list(plane.values()))
+
+    def hand(n, src, to):
+        return pltpu.make_async_remote_copy(
+            src_ref=src,
+            dst_ref=g_out,
+            send_sem=wire.send_sem.at[n],
+            recv_sem=wire.recv_sem.at[23],
+            device_id=to,
+            device_id_type=MESH,
+        )
+
+    owner, over = head == z, flip(head, 2) == z
+    to_core, to_x, onward = hand(23, once, core), hand(24, once, side_x), hand(25, g_out, core)
+
+    @pl.when(owner)
+    def _():
+        to_x.start()
+        to_core.start()
+        g_out[...] = once[...]
 
     def half_of(k, which):
         return grads.at[pl.ds(pl.multiple_of(block[k] * slab + which * cut, cut), cut)]
@@ -1192,6 +1220,11 @@
         columns = pl.ds(pl.multiple_of(which_head * width, 128), width)
         return out.at[pl.ds(start, size), columns]
 
+    @pl.when(over)
+    def _():
+        to_x.wait_recv()
+        onward.start()
+
     mine = place(head, row)
     add_into(cut, mine, z_out.at[0], z_in.at[0], z_in.at[1], z_in.at[2])
     other = flip(head, 2)
@@ -1214,10 +1247,17 @@
     last.append(wire.start(place(other, 1 - row), place(other, 1 - row), core))
     for copy in last:
         copy.wait_recv()
+    @pl.when(owner)
+    def _():
+        to_x.wait_send()
+        to_core.wait_send()
+
+    pl.when(over)(onward.wait_send)
+    pl.when(jnp.logical_not(jnp.logical_or(owner, over)))(to_core.wait_recv)
     wire.finish()
 
 
-def dense_reduce(grads, small, replicas):
+def dense_reduce(grads, small, once, replicas):
     slab, width = grads.shape[0] // replicas, grads.shape[1]
     piece = (slab // 2, width)
     lot = small.shape[1:]
@@ -1225,10 +1265,11 @@
         functools.partial(dense_kernel, replicas),
         "dense_reduce",
         2,
-        23,
-        [ON_CHIP] * 2,
-        [ON_CHIP] * 2,
-        [jax.ShapeDtypeStruct((slab, 4 * width), bf16), jax.ShapeDtypeStruct(lot, f32)],
+        26,
+        [ON_CHIP] * 3,
+        [ON_CHIP] * 3,
+        [jax.ShapeDtypeStruct((slab, 4 * width), bf16), jax.ShapeDtypeStruct(lot, f32)]
+        + [jax.ShapeDtypeStruct(once.shape, bf16)],
         [
             pltpu.VMEM((4,) + piece, bf16),
             pltpu.VMEM((4,) + piece, bf16),
@@ -1238,7 +1279,7 @@
             pltpu.VMEM((3,) + lot, f32),
         ],
         10**8,
-    )(grads, small)
+    )(grads, small, once)
 
 
 STRIP = 256
@@ -1506,7 +1547,6 @@
                 for i in range(owners)
             ]
             out_sum = out_sum + on_grid(grad_out, pairs).astype(f32)
-        entered = jnp.where(never(out_sum[0, 0]) == 0, 1.0, 0.0)
     grad_context = mm("td,cd->ct", seq_grad, out_slice).astype(bf16)
     grad_q, grad_k, grad_v = attend_back(queries, keys, values, grad_context)
     grad_lin = jnp.concatenate(
@@ -1514,9 +1554,11 @@
     ).astype(bf16)
     grad_qkv = mm("td,ct->dc", seq, grad_lin).astype(bf16)
     normed_parts = mm("ct,dc->td", grad_lin, qkv)
-    normed_parts = (entered * normed_parts if compact else normed_parts).astype(bf16)
+    normed_parts = normed_parts.astype(bf16)
     if compact:
-        grad_normed, *part = seq_scatter_grads(normed_parts, group, 2, grad_gate_up, grad_down)
+        grad_normed, *part, out_sum = seq_scatter_grads(
+            normed_parts, group, 2, grad_gate_up, grad_down, out_sum.astype(bf16)
+        )
         done.append(part)
     else:
         grad_normed = seq_scatter(normed_parts, group, 4, "scatter_branch")
@@ -1540,17 +1582,9 @@
         ]
     )
     if compact:
-        out_sum = other_sequences(out_sum).astype(bf16)
-        g_out = jnp.where(plane == head, out_sum, jnp.zeros((), bf16))
-        for m in range(1, group):
-            pairs = [
-                ((i % group) * owners + i, (i % group) * owners + (i ^ m)) for i in range(owners)
-            ]
-            g_out = g_out + on_grid(out_sum, pairs)
+        lot = jnp.transpose(lot.reshape(32, replicas, slab), (1, 0, 2))
+        by_head, lot, g_out = dense_reduce(grad_qkv, lot, out_sum, replicas)
         g_out = g_out.astype(f32)
-        lot = jnp.where(never(out_sum[0, 0]) == 0, lot, 0.0)
-        lot = jnp.transpose(lot.reshape(32, replicas, slab), (1, 0, 2))
-        by_head, lot = dense_reduce(grad_qkv, lot, replicas)
         gate_up_out, down_out = [jnp.stack(x).astype(f32) for x in zip(*done)]
     else:
         out_sum = other_sequences(lax.psum(grad_out, "dp")).astype(bf16)

time: 857 us -> 820 us (0.957)
  waiting for transfers between devices: 35.7 us -> 15 us
    ppermute x2 -> x1, waiting for transfers between devices: 18.1 us -> 0.01 us  [send(): return lax.ppermute(x, axis, [(i, i ^ mask) for i in range(count)])]
    ppermute x6 -> x3, waiting for transfers between devices: 17.5 us -> 15 us  [on_grid(): return lax.ppermute(x, ('dp', 'expert'), pairs)]
  transfers between devices with their start and end apart: 8 -> 4, of which waited for: 2 -> 1; matrix products, arithmetic and copies ran while one was open for 4% -> 2% of each run, Pallas kernels for 16% -> 11%
where the time goes in v6:
time: 820 us; the launch traced here: 814 us
  Pallas kernels  696 us (85%)
  other arithmetic  40.3 us (5%)
  matrix products  29.6 us (4%)
  local copies, waits for them, and re-layouts  20.3 us (2%)
  waiting for transfers between devices  15 us (2%)
    pallas_call x2, Pallas kernels, plane_gather(): comm_call(functools.partial(plane_gather_kernel, half, experts, count), n...  157 us
    pallas_call x2, Pallas kernels, plane_scatter(): comm_call(functools.partial(plane_scatter_kernel, half, i), name, number,...  155 us
    pallas_call x1, Pallas kernels, seq_scatter_weights(): comm_call(functools.partial(scatter_weights_kernel, group, experts), 'sca...  51.6 us
    pallas_call x2, Pallas kernels, experts_backward(): pl.pallas_call(experts_back_kernel, grid_spec=pltpu.PrefetchScalarGridSpe...  50.5 us
    pallas_call x1, Pallas kernels, dense_reduce(): comm_call(functools.partial(dense_kernel, replicas), 'dense_reduce', 2, 2...  47.7 us
    pallas_call x2, Pallas kernels, experts_forward(): pl.pallas_call(experts_kernel, grid_spec=pltpu.PrefetchScalarGridSpec(num...  46.9 us
    pallas_call x1, Pallas kernels, seq_gather_grads(): comm_call(functools.partial(gather_grads_kernel, group, i), 'gather_branc...  41.5 us
    pallas_call x1, Pallas kernels, seq_scatter_grads(): comm_call(functools.partial(scatter_grads_kernel, group, i), 'scatter_nor...  40 us
  transfers between devices with their start and end apart: 4, of which 1 were waited for; matrix products, arithmetic and copies ran while one was open for 2% of the time, Pallas kernels for 11%

profile of v6, /device:TPU:0, one launch (start us, length us, event | category | flops | bytes accessed | tf_op | source)
XLA Modules:
  0.0 814.5 jit_solution(11017756250649369501)
XLA Ops:
  0.7 0.8 broadcast_in_dim.19
  2.3 1.4 maximum_maximum_fusion.small_ref
  3.7 9.3 %start_exchange.1 = bf16[4,32,384]{2,1,0:T(8,128)(2,1)} custom-call(bf16[32,384]{1,0:T(8,128)(2,1)} %maximum_maximum_fusion.small_ref), custom_call_target="tpu_custom_call" | custom-call | flops 1000000 | bytes 1000000 | tf_op jit(solution)/shard_map/start_exchange/pallas_call | solution.py:1143
  13.0 0.9 fusion.15
  13.9 1.4 fusion.7
  15.3 1.1 fusion.2.x_ref
  16.4 1.0 constant_dynamic-slice_fusion
  17.4 0.8 pad_maximum_fusion.4.qkv_in
  18.3 36.7 %attention_entry.1 = (bf16[1024,1536]{1,0:T(8,128)(2,1)}, bf16[1536,640]{1,0:T(8,128)(2,1)}, bf16[384,1536]{1,0:T(8,128)(2,1)}) custom-call(bf16[256,1536]{1,0:T(8,128)(2,1)} %fusion.2.x_ref, bf16[384,640]{1,0:T(8,128)(2,1)} %pad_maximum_fusion.4.qkv_in, bf16[384,1536]{1,0:T(8,128)(2,1)} %out_in.1), custom_call_target="tpu_custom_call" | custom-call | flops 15728640 | bytes 15728640 | tf_op jit(solution)/shard_map/attention_entry/pallas_call | solution.py:1020
  54.9 4.7 fusion.26
  59.8 1.4 copy-done.7
  63.4 1.0 maximum_multiply_fusion
  65.1 15.9 %attend.1 = bf16[384,1024]{1,0:T(8,128)(2,1)} custom-call(bf16[384,1024]{1,0:T(8,128)(2,1)} %bitcast.53, bf16[128,1024]{1,0:T(8,128)(2,1)} %bitcast.65, bf16[128,1024]{1,0:T(8,128)(2,1)} %slice.187.v_ref), custom_call_target="tpu_custom_call" | custom-call | flops 10000000000 | bytes 10000000 | tf_op jit(solution)/shard_map/attend/pallas_call | solution.py:1338
  81.0 4.6 convolution_convert_fusion.1.x_ref
  85.7 51.6 %scatter_branch_weights.1 = (f32[256,1536]{1,0:T(8,128)}, bf16[3,1536,512]{2,1,0:T(8,128)(2,1)}, bf16[3,256,1536]{2,1,0:T(8,128)(2,1)}) custom-call(bf16[1024,1536]{1,0:T(8,128)(2,1)} %convolution_convert_fusion.1.x_ref, bf16[3,384,1024]{2,1,0:T(8,128)(2,1)} %refs_2_.1, bf16[3,128,1536]{2,1,0:T(8,128)(2,1)} %refs_3_.1), custom_call_target="tpu_custom_call" | custom-call | flops 15728640 | bytes 15728640 | tf_op jit(solution)/shard_map/scatter_branch_weights/pallas_call | solution.py:1051
  137.3 1.8 multiply_reduce_fusion.2
  141.0 1.3 concatenate.34.refs_1_.refs_8_
  142.2 1.1 multiply_convert_fusion.1.refs_0_
  143.3 95.9 %gather_all.1 = (bf16[256,1536]{1,0:T(8,128)(2,1)}, s32[16,256]{1,0:T(8,128)}, bf16[256,1536]{1,0:T(8,128)(2,1)}, s32[16,256]{1,0:T(8,128)}, bf16[256,1536]{1,0:...) custom-call(bf16[256,1536]{1,0:T(8,128)(2,1)} %multiply_convert_fusi, ...), custom_call_target="tpu_custom_call", output_to_operand_aliasing={{30}: (4, {}), {31}: (5, {})} | custom-call | flops 31457280 | bytes 31457280 | tf_op jit(solution)/shard_map/gather_all/pallas_call | solution.py:678
  239.2 23.1 %experts_forward.2 = (bf16[256,1536]{1,0:T(8,128)(2,1)}, bf16[256,1536]{1,0:T(8,128)(2,1)}, bf16[256,1536]{1,0:T(8,128)(2,1)}, bf16[256,1536]{1,0:T(8,128)(2,1)}...) custom-call(s32[1]{0:T(128)} %bitcast.6.me_ref.after_ref, ...), custom_call_target="tpu_custom_call" | custom-call | flops 11000000512 | bytes 40000000 | tf_op jit(solution)/shard_map/experts_forward/pallas_call | solution.py:186
  262.3 1.3 slice.119
  263.5 23.8 %experts_forward.3 = (bf16[256,1536]{1,0:T(8,128)(2,1)}, bf16[256,1536]{1,0:T(8,128)(2,1)}, bf16[256,1536]{1,0:T(8,128)(2,1)}, bf16[256,1536]{1,0:T(8,128)(2,1)}...) custom-call(s32[1]{0:T(128)} %bitcast.6.me_ref.after_ref, ...), custom_call_target="tpu_custom_call" | custom-call | flops 11000000512 | bytes 40000000 | tf_op jit(solution)/shard_map/experts_forward/pallas_call | solution.py:186
  287.3 1.3 slice.120
  289.9 4.1 collective-permute-start
  294.7 64.8 %scatter_outputs.1 = f32[256,1536]{1,0:T(8,128)} custom-call(bf16[256,1536]{1,0:T(8,128)(2,1)} %get-tuple-element.153.refs_0_, bf16[256,1536]{1,0:T(8,128)(2,1)} %get-tuple-element.154.refs_1_, bf16[256,1536]{1,0:T(8,128)(2,1)} %get-tuple-element.155.refs_2_, bf16[256,1536]{1,0:T(8,128)(2,1)} %get-tuple-element.156.refs_3_, ...), custom_call_target="tpu_custom_call" | custom-call | flops 19660800 | bytes 19660800 | tf_op jit(solution)/shard_map/scatter_outputs/pallas_call | solution.py:787
  360.2 2.8 multiply_convert_fusion.2.refs_0_
  363.0 60.7 %gather_tokens.1 = (bf16[256,1536]{1,0:T(8,128)(2,1)}, bf16[256,1536]{1,0:T(8,128)(2,1)}, bf16[256,1536]{1,0:T(8,128)(2,1)}, bf16[256,1536]{1,0:T(8,128)(2,1)}, ...) custom-call(bf16[256,1536]{1,0:T(8,128)(2,1)} %multiply_convert_fusi, ...), custom_call_target="tpu_custom_call" | custom-call | flops 31457280 | bytes 31457280 | tf_op jit(solution)/shard_map/gather_tokens/pallas_call | solution.py:678
  423.7 25.2 %experts_backward.2 = (bf16[256,1664]{1,0:T(8,128)(2,1)}, bf16[256,1664]{1,0:T(8,128)(2,1)}, bf16[256,1664]{1,0:T(8,128)(2,1)}, bf16[256,1664]{1,0:T(8,128)(2,1)...) custom-call(s32[1]{0:T(128)} %bitcast.6.me_ref.after_ref, ...), custom_call_target="tpu_custom_call" | custom-call | flops 11000000512 | bytes 40000000 | tf_op jit(solution)/shard_map/experts_backward/pallas_call | solution.py:265
  448.9 25.3 %experts_backward.3 = (bf16[256,1664]{1,0:T(8,128)(2,1)}, bf16[256,1664]{1,0:T(8,128)(2,1)}, bf16[256,1664]{1,0:T(8,128)(2,1)}, bf16[256,1664]{1,0:T(8,128)(2,1)...) custom-call(s32[1]{0:T(128)} %bitcast.6.me_ref.after_ref, ...), custom_call_target="tpu_custom_call" | custom-call | flops 11000000512 | bytes 40000000 | tf_op jit(solution)/shard_map/experts_backward/pallas_call | solution.py:265
  474.2 21.4 %expert_weights.1 = (bf16[3,1536,512]{2,1,0:T(8,128)(2,1)}, bf16[3,256,1536]{2,1,0:T(8,128)(2,1)}) custom-call(s32[1]{0:T(128)} %bitcast.6.me_ref.after_ref, bf16[8,3,112,1536]{3,2,1,0:T(8,128)(2,1)} %get-tuple-element.224.refs_0_, bf16[8,3,112,512]{3,2,1,0:T(8,128)(2,1)} %get-tuple-element.225.refs_1_, bf16[8,3,112,256]{3,2,1,0:T(8,128)(2,1)} %get-tuple-element.226.refs_2_, ...), custom_call_target="tpu_custom_call" | custom-call | flops 14000000000 | bytes 40000000 | tf_op jit(solution)/shard_map/expert_weights/pallas_call | solution.py:313
  495.6 90.0 %scatter_grads.1 = (f32[256,1664]{1,0:T(8,128)}, bf16[384,1024]{1,0:T(8,128)(2,1)}, bf16[128,1536]{1,0:T(8,128)(2,1)}) custom-call(bf16[256,1664]{1,0:T(8,128)(2,1)} %get-tuple-element.197.refs_0_, bf16[256,1664]{1,0:T(8,128)(2,1)} %get-tuple-element.198.refs_1_, bf16[256,1664]{1,0:T(8,128)(2,1)} %get-tuple-element.199.refs_2_, ...), custom_call_target="tpu_custom_call" | custom-call | flops 21299200 | bytes 21299200 | tf_op jit(solution)/shard_map/scatter_grads/pallas_call | solution.py:787
  585.7 1.1 multiply_reduce_fusion.3
  586.8 3.8 multiply_reduce_fusion
  590.7 2.4 multiply_convert_fusion
  593.1 41.5 %gather_branch_grads.1 = (bf16[1024,1536]{1,0:T(8,128)(2,1)}, bf16[384,1024]{1,0:T(8,128)(2,1)}, bf16[128,1536]{1,0:T(8,128)(2,1)}) custom-call(bf16[256,1536]{1,0:T(8,128)(2,1)} %get-tuple-element.259.x_ref, bf16[3,1536,512]{2,1,0:T(8,128)(2,1)} %get-tuple-element.232.refs_16_.grad_gate_up, bf16[3,256,1536]{2,1,0:T(8,128)(2,1)} %get-tuple-element.233.refs_17_.grad_down), custom_call_target="tpu_custom_call" | custom-call | flops 15728640 | bytes 15728640 | tf_op jit(solution)/shard_map/gather_branch_grads/pallas_call | solution.py:1082
  634.6 4.3 convolution_convert_fusion.4.grad_ref
  638.9 1.4 convolution_convert_fusion.3
  640.3 1.3 collective-permute-start.3
  641.6 1.3 collective-permute-start.2
  642.9 1.3 collective-permute-start.1
  644.2 1.3 fusion.25
  645.5 23.1 %attend_back.1 = (f32[384,1024]{1,0:T(8,128)}, f32[128,1024]{1,0:T(8,128)}, f32[128,1024]{1,0:T(8,128)}) custom-call(bf16[384,1024]{1,0:T(8,128)(2,1)} %bitcast.54, bf16[128,1024]{1,0:T(8,128)(2,1)} %bitcast.66, bf16[128,1024]{1,0:T(8,128)(2,1)} %slice.187.v_ref, bf16[384,1024]{1,0:T(8,128)(2,1)} %convolution_convert_fusion.4.grad_ref), custom_call_target="tpu_custom_call" | custom-call | flops 30000001024 | bytes 10000000 | tf_op jit(solution)/shard_map/attend_back/pallas_call | solution.py:1338
  668.6 1.9 convert.45
  670.5 1.1 subtract_convert_fusion.2
  672.3 0.8 broadcast_in_dim.25
  673.9 5.2 convolution_convert_fusion.x_ref
  679.1 3.8 convolution_convert_fusion.2.grads
  682.9 15.0 %collective-permute-done.2 = bf16[384,1536]{1,0:T(8,128)(2,1)} collective-permute-done((bf16[384,1536]{1,0:T(8,128)(2,1)S(1)}, bf16[384,1536]{1,0:T(8,128)(2,1)}, u32[]{:S(2)}, u32[]{:S(2)}) %collective-permute-start.2) | collective-permute-done | bytes 1179680 | tf_op jit(solution)/shard_map/ppermute | solution.py:1436
  697.9 3.6 add_convert_fusion.once
  701.5 40.0 %scatter_normed_grads.1 = (f32[256,1536]{1,0:T(8,128)}, bf16[384,1024]{1,0:T(8,128)(2,1)}, bf16[128,1536]{1,0:T(8,128)(2,1)}, bf16[384,1536]{1,0:T(8,128)(2,1)}) custom-call(bf16[1024,1536]{1,0:T(8,128)(2,1)} %convolution_convert_fusion.x_ref, bf16[3,1536,512]{2,1,0:T(8,128)(2,1)} %get-tuple-element.232.refs_16_.grad_gate_up, ...), custom_call_target="tpu_custom_call" | custom-call | flops 15728640 | bytes 15728640 | tf_op jit(solution)/shard_map/scatter_normed_grads/pallas_call | solution.py:1115
  741.5 1.9 fusion.8
  743.4 0.8 maximum_bitcast_fusion.small
  744.2 47.7 %dense_reduce.1 = (bf16[384,2560]{1,0:T(8,128)(2,1)}, f32[32,384]{1,0:T(8,128)}, bf16[384,1536]{1,0:T(8,128)(2,1)}) custom-call(bf16[1536,640]{1,0:T(8,128)(2,1)} %convolution_convert_fusion.2.grads, f32[4,32,384]{2,1,0:T(8,128)} %maximum_bitcast_fusion.small, bf16[384,1536]{1,0:T(8,128)(2,1)} %get-tuple-element.240.once), custom_call_target="tpu_custom_call" | custom-call | flops 100000000 | bytes 100000000 | tf_op jit(solution)/shard_map/dense_reduce/pallas_call | solution.py:1264
  791.9 1.2 slice.127
  793.1 1.4 slice_reduce_fusion
  794.5 2.4 fusion.23
  796.9 2.2 fusion.22
  799.7 1.7 convert_element_type.134
  802.1 3.1 fusion.6
  805.2 2.6 maximum_convert_fusion
  807.8 1.6 maximum_convert_fusion.2
  809.5 1.7 maximum_convert_fusion.1
  811.3 0.9 maximum_convert_fusion.3
  812.2 0.9 maximum_convert_fusion.4
  (143 shorter events, 8.8 us)
Async XLA Ops:
  0.6 15.8 %copy-start = (bf16[384,1536]{1,0:T(8,128)(2,1)S(1)}, bf16[384,1536]{1,0:T(8,128)(2,1)}, u32[]{:S(2)}) copy-start(bf16[384,1536]{1,0:T(8,128)(2,1)} %param.19) | copy-start | bytes 3538948
  0.7 14.6 %copy-start.2 = (bf16[256,1536]{1,0:T(8,128)(2,1)S(1)}, bf16[256,1536]{1,0:T(8,128)(2,1)}, u32[]{:S(2)}) copy-start(bf16[256,1536]{1,0:T(8,128)(2,1)} %param.13) | copy-start | bytes 2359300
  13.8 3.6 copy-start.31
  15.2 3.0 copy-start.40
  15.2 3.0 copy-start.36
  59.7 1.5 copy-start.7
  59.8 2.1 copy-start.28
  61.9 1.4 slice-start
  65.1 15.9 %copy-start.50 = (bf16[384,1536]{1,0:T(8,128)(2,1)S(1)}, bf16[384,1536]{1,0:T(8,128)(2,1)}, u32[]{:S(2)}) copy-start(bf16[384,1536]{1,0:T(8,128)(2,1)} %get-tuple-element.133) | copy-start | bytes 3538948
  137.3 2.4 copy-start.29
  137.3 3.0 copy-start.45
  137.3 3.6 copy-start.34
  139.1 0.6 copy-start.42
  139.7 99.5 %copy-start.38 = (f32[256]{0:T(256)}, f32[256]{0:T(256)S(1)}, u32[]{:S(2)}) copy-start(f32[256]{0:T(256)S(1)} %fusion.18) | copy-start | bytes 3076
  263.5 30.5 %copy-start.4 = (bf16[256,1536]{1,0:T(8,128)(2,1)S(1)}, bf16[256,1536]{1,0:T(8,128)(2,1)}, u32[]{:S(2)}) copy-start(bf16[256,1536]{1,0:T(8,128)(2,1)} %multiply_convert_fusion.1.refs_0_) | copy-start | bytes 2359300
  263.5 30.5 %copy-start.33 = (bf16[4,3,8,384]{3,2,0,1:T(8,128)(2,1)S(1)}, bf16[4,3,8,384]{3,2,0,1:T(8,128)(2,1)}, u32[]{:S(2)}) copy-start(bf16[4,3,8,384]{3,2,0,1:T(8,128)(2,1)} %copy.41) | copy-start | bytes 221188
  289.9 69.6 %collective-permute-start = (s32[1]{0:T(128)}, s32[1]{0:T(128)}, u32[]{:S(2)}, u32[]{:S(2)}) collective-permute-start(s32[1]{0:T(128)} %bitcast.8), channel_id=1, source_target_pairs={{0,8},{8,0},{16,24},{24,16},{1,9},{9,1},{17,25},{25,17},{2,10},{10... | collective-permute-start | bytes 20 | tf_op jit(solution)/shard_map/ppermute | solution.py:45
  294.7 65.5 %copy-start.46 = (s32[256]{0:T(256)S(1)}, s32[256]{0:T(256)}, u32[]{:S(2)}) copy-start(s32[256]{0:T(256)} %param.15) | copy-start | bytes 3076
  495.6 91.2 %copy-start.39 = (f32[256]{0:T(256)S(1)}, f32[256]{0:T(256)}, u32[]{:S(2)}) copy-start(f32[256]{0:T(256)} %copy-done.38) | copy-start | bytes 3076
  586.8 3.8 copy-start.43
  586.8 3.8 copy-start.3
  586.8 3.8 copy-start.6
  593.1 41.5 %copy-start.51 = (bf16[384,1536]{1,0:T(8,128)(2,1)S(1)}, bf16[384,1536]{1,0:T(8,128)(2,1)}, u32[]{:S(2)}) copy-start(bf16[384,1536]{1,0:T(8,128)(2,1)} %get-tuple-element.133) | copy-start | bytes 3538948
  634.6 4.4 copy-start.48
  634.6 4.3 copy-start.52
  640.3 42.6 %collective-permute-start.3 = (bf16[384,1536]{1,0:T(8,128)(2,1)S(1)}, bf16[384,1536]{1,0:T(8,128)(2,1)}, u32[]{:S(2)}, u32[]{:S(2)}) collective-permute-start(bf16[384,1536]{1,0:T(8,128)(2,1)S(1)} %convolution_convert_fusion.3), channel_id=1, source_target_pairs={{24,0},{1,9},{10,18},{19,27},{28,4},{5,13},{14,22},{23,31}} | collective-permute-start | bytes 3538952 | tf_op jit(solution)/shard_map/ppermute | solution.py:1436
  641.6 56.3 %collective-permute-start.2 = (bf16[384,1536]{1,0:T(8,128)(2,1)S(1)}, bf16[384,1536]{1,0:T(8,128)(2,1)}, u32[]{:S(2)}, u32[]{:S(2)}) collective-permute-start(bf16[384,1536]{1,0:T(8,128)(2,1)S(1)} %convolution_convert_fusion.3), channel_id=1, source_target_pairs={{16,0},{25,9},{2,18},{11,27},{20,4},{29,13},{6,22},{15,31}} | collective-permute-start | bytes 3538952 | tf_op jit(solution)/shard_map/ppermute | solution.py:1436
  642.9 55.0 %collective-permute-start.1 = (bf16[384,1536]{1,0:T(8,128)(2,1)S(1)}, bf16[384,1536]{1,0:T(8,128)(2,1)}, u32[]{:S(2)}, u32[]{:S(2)}) collective-permute-start(bf16[384,1536]{1,0:T(8,128)(2,1)S(1)} %convolution_convert_fusion.3), channel_id=1, source_target_pairs={{8,0},{17,9},{26,18},{3,27},{12,4},{21,13},{30,22},{7,31}} | collective-permute-start | bytes 3538952 | tf_op jit(solution)/shard_map/ppermute | solution.py:1436
  668.6 3.0 copy-start.8
  671.6 0.7 copy-start.44
  672.3 1.6 copy-start.49
  673.9 5.2 copy-start.30
  673.9 5.2 copy-start.47
  701.5 40.0 %copy-start.32 = (f32[1536]{0:T(1024)S(1)}, f32[1536]{0:T(1024)}, u32[]{:S(2)}) copy-start(f32[1536]{0:T(1024)} %copy-done.31) | copy-start | bytes 18436
  701.5 40.0 %copy-start.37 = (f32[256]{0:T(256)S(1)}, f32[256]{0:T(256)}, u32[]{:S(2)}) copy-start(f32[256]{0:T(256)} %copy-done.36) | copy-start | bytes 3076
  794.5 4.5 copy-start.35
  794.5 5.1 copy-start.41
  794.5 5.2 copy-start.13
  799.7 2.4 copy-start.5
  802.1 3.1 copy-start.14
  802.1 3.1 copy-start.15
  802.1 3.1 copy-start.16
  805.2 2.6 copy-start.17
  805.2 2.6 copy-start.18
  805.2 2.6 copy-start.19
  807.8 1.6 copy-start.9
  807.8 1.6 copy-start.10
  807.8 1.6 copy-start.11
  807.8 1.6 copy-start.12
  809.4 1.8 copy-start.24
  809.5 1.8 copy-start.25
  809.5 1.8 copy-start.26
  809.5 1.8 copy-start.27
  809.5 2.7 copy-start.20
  809.5 2.7 copy-start.21
  809.5 2.7 copy-start.22
  809.5 2.7 copy-start.23
  809.5 3.6 copy-start.1
